TPU v7x, 32 devices: a whole 2x2x4 slice. The times are simulated.
32 devices in a mesh: dp: 8 (over z, core), tensor: 4 (over y, x).
Axes of the slice: x: 2, y: 2, z: 4, core: 2. Of those that a mesh axis runs over, the one named last changes fastest.
Arguments:
- inputs: bfloat16 [2048, 2048], P('dp'), may hold values from -6 to 6
- segment_ids: int32 [2048], P('dp'), may hold values from 0 to 16, as said below
- first_gain: bfloat16 [2048], replicated, may hold values from 0.25 to 1.75
- first_shift: bfloat16 [2048], replicated, may hold values from -3 to 3
- project_in: bfloat16 [3, 2048, 2048], P(None, 'dp', 'tensor'), may hold values from -0.1875 to 0.1875
- query_bias: bfloat16 [2048], P('tensor'), may hold values from -3 to 3
- value_bias: bfloat16 [2048], P('tensor'), may hold values from -3 to 3
- project_out: bfloat16 [2048, 2048], P('tensor', 'dp'), may hold values from -0.75 to 0.75
- out_bias: bfloat16 [2048], replicated, may hold values from -3 to 3
- second_gain: bfloat16 [2048], replicated, may hold values from 0.25 to 1.75
- second_shift: bfloat16 [2048], replicated, may hold values from -3 to 3
- up_weight: bfloat16 [2048, 8192], P('dp', 'tensor'), may hold values from -0.125 to 0.125
- up_bias: bfloat16 [8192], P('tensor'), may hold values from -3 to 3
- down_weight: bfloat16 [8192, 2048], P('tensor', 'dp'), may hold values from -0.0625 to 0.0625
- down_bias: bfloat16 [2048], replicated, may hold values from -3 to 3
- cotangent: bfloat16 [2048, 2048], P('dp'), may hold values from -6 to 6
Outputs:
- outputs: bfloat16 [2048, 2048], P('dp')
- input_gradient: bfloat16 [2048, 2048], P('dp')
- gradient_first_gain: float32 [2048], replicated
- gradient_first_shift: float32 [2048], replicated
- gradient_project_in: float32 [3, 2048, 2048], P(None, 'dp', 'tensor')
- gradient_query_bias: float32 [2048], P('tensor')
- gradient_value_bias: float32 [2048], P('tensor')
- gradient_project_out: float32 [2048, 2048], P('tensor', 'dp')
- gradient_out_bias: float32 [2048], replicated
- gradient_second_gain: float32 [2048], replicated
- gradient_second_shift: float32 [2048], replicated
- gradient_up_weight: float32 [2048, 8192], P('dp', 'tensor')
- gradient_up_bias: float32 [8192], P('tensor')
- gradient_down_weight: float32 [8192, 2048], P('tensor', 'dp')
- gradient_down_bias: float32 [2048], replicated
Inputs may be any that keep to these rules, and one draw needn't show every extreme that they name: `segment_ids`: within each packed sequence of 256 tokens the id starts at 1 on its first token and rises by 0 or 1 from token to token, never above 16, except for a trailing run of up to a quarter of 256 tokens that are 0 (padding).
All inputs are finite; a program needn't handle non-finite values.
Results may differ from a plain program's by a relative error of at most 0.012.
The roundings to bfloat16 on the way count: a program that leaves them out, or rounds other values in their place, can miss the bound.
Values may be sent and summed in bfloat16 or wider, within the bound.
No kernel may reach another device: no remote copies, remote signals or barrier semaphores. Data moves between devices by JAX's collectives and lax.ppermute only.
A program may use at most 192 MiB of HBM per device.

v0:
```python
import jax
import jax.numpy as jnp
from jax import lax
from jax.sharding import PartitionSpec as P

DH = 128


EPSILON = 1e-05
NEGATIVE = -1e30


def normalize(values):
    center = values - jnp.mean(values, axis=-1, keepdims=True)
    inverse = lax.rsqrt(jnp.mean(center * center, axis=-1, keepdims=True) + EPSILON)
    return (center * inverse, inverse)


def norm_back(norm_grad, normed, inverse, gain):
    scaled = norm_grad * gain
    return inverse * (
        scaled
        - jnp.mean(scaled, axis=-1, keepdims=True)
        - normed * jnp.mean(scaled * normed, axis=-1, keepdims=True)
    )


def exact_gelu(values):
    return jax.nn.gelu(values, approximate=False)


def masked_scores(query_block, key_heads, segment_ids, offset, height):
    length = key_heads.shape[0]
    products = jnp.einsum(
        "qhd,khd->hqk", query_block, key_heads, preferred_element_type=jnp.float32
    )
    row_places = offset + jnp.arange(height, dtype=jnp.int32)
    places = jnp.arange(length, dtype=jnp.int32)
    allowed = (
        (segment_ids[:, None] == segment_ids[None, :])
        & (segment_ids[:, None] != 0)
        & (places[None, :] <= row_places[:, None])
    )
    allowed = allowed | (places[None, :] == row_places[:, None])
    return jnp.where(allowed[None], products * DH ** (-0.5), NEGATIVE)


def attend_forward(query_heads, key_heads, value_heads, segment_ids):
    length = query_heads.shape[0]
    height = min(512, length)

    def one_block(offset):
        scores = masked_scores(query_heads, key_heads, segment_ids, offset, height)
        largest = jnp.max(scores, axis=-1, keepdims=True)
        weights = jnp.exp(scores - largest)
        totals = jnp.sum(weights, axis=-1, keepdims=True)
        probs_low = (weights / totals).astype(jnp.bfloat16)
        mixed = jnp.einsum(
            "hqk,khd->qhd", probs_low, value_heads, preferred_element_type=jnp.float32
        )
        return (mixed.astype(jnp.bfloat16), (largest + jnp.log(totals))[..., 0])

    offsets = jnp.arange(length // height, dtype=jnp.int32) * height
    mixed, log_totals = lax.map(one_block, offsets)
    return (mixed.reshape(length, -1), log_totals)


def attend_backward(query_heads, key_heads, value_heads, segment_ids, log_totals, mixed_grad):
    length = query_heads.shape[0]
    height = min(512, length)

    def one_block(carry, item):
        key_grad, value_grad = carry
        offset, block_totals = item
        scores = masked_scores(query_heads, key_heads, segment_ids, offset, height)
        probs = jnp.exp(scores - block_totals[..., None])
        prob_grad = jnp.einsum(
            "qhd,khd->hqk", mixed_grad, value_heads, preferred_element_type=jnp.float32
        )
        score_grad = probs * (prob_grad - jnp.sum(probs * prob_grad, axis=-1, keepdims=True))
        score_low = (score_grad * DH ** (-0.5)).astype(jnp.bfloat16)
        query_grad = jnp.einsum(
            "hqk,khd->qhd", score_low, key_heads, preferred_element_type=jnp.float32
        )
        key_grad = key_grad + jnp.einsum(
            "hqk,qhd->khd", score_low, query_heads, preferred_element_type=jnp.float32
        )
        value_grad = value_grad + jnp.einsum(
            "hqk,qhd->khd",
            probs.astype(jnp.bfloat16),
            mixed_grad,
            preferred_element_type=jnp.float32,
        )
        return ((key_grad, value_grad), query_grad)

    zeros = jnp.zeros(key_heads.shape, jnp.float32)
    offsets = jnp.arange(length // height, dtype=jnp.int32) * height
    (key_grad, value_grad), query_grad = lax.scan(one_block, (zeros, zeros), (offsets, log_totals))
    return (
        query_grad.reshape(length, -1),
        key_grad.reshape(length, -1),
        value_grad.reshape(length, -1),
    )


def shards(
    inputs,
    segment_ids,
    first_gain,
    first_shift,
    project_in,
    query_bias,
    value_bias,
    project_out,
    out_bias,
    second_gain,
    second_shift,
    up_weight,
    up_bias,
    down_weight,
    down_bias,
    cotangent,
):
    full_in, full_out, full_up, full_down = (
        lax.all_gather(project_in, "dp", axis=1, tiled=True),
        lax.all_gather(project_out, "dp", axis=1, tiled=True),
        lax.all_gather(up_weight, "dp", axis=0, tiled=True),
        lax.all_gather(down_weight, "dp", axis=1, tiled=True),
    )
    length = inputs.shape[0]
    heads_here = query_bias.shape[0] // DH
    gain_one = first_gain.astype(jnp.float32)
    gain_two = second_gain.astype(jnp.float32)
    resid_in = inputs.astype(jnp.float32)
    normed_one, inverse_one = normalize(resid_in)
    first_low = (normed_one * gain_one + first_shift.astype(jnp.float32)).astype(jnp.bfloat16)
    query = (
        jnp.dot(first_low, full_in[0], preferred_element_type=jnp.float32)
        + query_bias.astype(jnp.float32)
    ).astype(jnp.bfloat16)
    key_proj = jnp.dot(first_low, full_in[1], preferred_element_type=jnp.float32).astype(
        jnp.bfloat16
    )
    value_proj = (
        jnp.dot(first_low, full_in[2], preferred_element_type=jnp.float32)
        + value_bias.astype(jnp.float32)
    ).astype(jnp.bfloat16)
    query_heads = query.reshape(length, heads_here, DH)
    key_heads = key_proj.reshape(length, heads_here, DH)
    value_heads = value_proj.reshape(length, heads_here, DH)
    mixed, log_totals = attend_forward(query_heads, key_heads, value_heads, segment_ids)
    attention_part = jnp.dot(mixed, full_out, preferred_element_type=jnp.float32)
    attention = lax.psum(attention_part, "tensor")
    hidden = resid_in + attention + out_bias.astype(jnp.float32)
    normed_two, inverse_two = normalize(hidden)
    second_low = (normed_two * gain_two + second_shift.astype(jnp.float32)).astype(jnp.bfloat16)
    upper = jnp.dot(second_low, full_up, preferred_element_type=jnp.float32) + up_bias.astype(
        jnp.float32
    )
    activated = exact_gelu(upper).astype(jnp.bfloat16)
    feed_part = jnp.dot(activated, full_down, preferred_element_type=jnp.float32)
    upstream = cotangent.astype(jnp.float32)
    grad_down = jnp.einsum("rf,rd->fd", activated, cotangent, preferred_element_type=jnp.float32)
    act_grad = jnp.einsum("rd,fd->rf", cotangent, full_down, preferred_element_type=jnp.float32)
    upper_grad = jax.vjp(exact_gelu, upper)[1](act_grad)[0]
    grad_up_bias = jnp.sum(upper_grad, axis=0)
    upper_low = upper_grad.astype(jnp.bfloat16)
    grad_up = jnp.einsum("rd,rf->df", second_low, upper_low, preferred_element_type=jnp.float32)
    second_part = jnp.einsum("rf,df->rd", upper_low, full_up, preferred_element_type=jnp.float32)
    feed = lax.psum(feed_part.astype(jnp.bfloat16), "tensor").astype(jnp.float32)
    outputs_here = (hidden + feed + down_bias.astype(jnp.float32)).astype(jnp.bfloat16)
    grad_down_bias = jnp.sum(upstream, axis=0)
    second_grad = lax.psum(second_part, "tensor")
    grad_second_gain = jnp.sum(second_grad * normed_two, axis=0)
    grad_second_shift = jnp.sum(second_grad, axis=0)
    hidden_grad = upstream + norm_back(second_grad, normed_two, inverse_two, gain_two)
    grad_out_bias = jnp.sum(hidden_grad, axis=0)
    hidden_low = hidden_grad.astype(jnp.bfloat16)
    grad_out = jnp.einsum("rh,rd->hd", mixed, hidden_low, preferred_element_type=jnp.float32)
    mixed_grad = jnp.einsum(
        "rd,hd->rh", hidden_low, full_out, preferred_element_type=jnp.float32
    ).astype(jnp.bfloat16)
    query_grad, key_grad, value_grad = attend_backward(
        query_heads,
        key_heads,
        value_heads,
        segment_ids,
        log_totals,
        mixed_grad.reshape(length, heads_here, DH),
    )
    grad_query_bias = jnp.sum(query_grad, axis=0)
    grad_value_bias = jnp.sum(value_grad, axis=0)
    stacked_low = jnp.stack([query_grad, key_grad, value_grad]).astype(jnp.bfloat16)
    grad_in = jnp.einsum("rd,jrh->jdh", first_low, stacked_low, preferred_element_type=jnp.float32)
    first_part = jnp.einsum("jrh,jdh->rd", stacked_low, full_in, preferred_element_type=jnp.float32)
    first_grad = lax.psum(first_part, "tensor")
    grad_first_gain = jnp.sum(first_grad * normed_one, axis=0)
    grad_first_shift = jnp.sum(first_grad, axis=0)
    input_gradient = (
        hidden_grad + norm_back(first_grad, normed_one, inverse_one, gain_one)
    ).astype(jnp.bfloat16)
    norms = lax.psum(
        (
            grad_first_gain,
            grad_first_shift,
            grad_out_bias,
            grad_second_gain,
            grad_second_shift,
            grad_down_bias,
        ),
        "dp",
    )
    summed = (
        lax.psum_scatter(grad_in, "dp", scatter_dimension=1, tiled=True),
        lax.psum_scatter(grad_out, "dp", scatter_dimension=1, tiled=True),
        lax.psum_scatter(grad_up, "dp", scatter_dimension=0, tiled=True),
        lax.psum_scatter(grad_down, "dp", scatter_dimension=1, tiled=True),
    )
    biases = lax.psum((grad_query_bias, grad_value_bias, grad_up_bias), "dp")
    return (
        outputs_here,
        input_gradient,
        norms[0],
        norms[1],
        summed[0],
        biases[0],
        biases[1],
        summed[1],
        norms[2],
        norms[3],
        norms[4],
        summed[2],
        biases[2],
        summed[3],
        norms[5],
    )


def solution(mesh):
    in_specs = (
        P("dp", None),
        P("dp"),
        P(),
        P(),
        P(None, "dp", "tensor"),
        P("tensor"),
        P("tensor"),
        P("tensor", "dp"),
        P(),
        P(),
        P(),
        P("dp", "tensor"),
        P("tensor"),
        P("tensor", "dp"),
        P(),
        P("dp", None),
    )
    out_specs = (
        P("dp", None),
        P("dp", None),
        P(),
        P(),
        P(None, "dp", "tensor"),
        P("tensor"),
        P("tensor"),
        P("tensor", "dp"),
        P(),
        P(),
        P(),
        P("dp", "tensor"),
        P("tensor"),
        P("tensor", "dp"),
        P(),
    )
    return jax.shard_map(shards, mesh=mesh, in_specs=in_specs, out_specs=out_specs, check_vma=False)
```

profile of v0, /device:TPU:8, one launch (start us, length us, event | category | flops | bytes accessed | tf_op | source)
XLA Modules:
  0.0 1111.8 jit_solution(16115100569589645460)
XLA Ops:
  13.5 59.9 %all-gather.5.cloned.1.call-done = bf16[3,2048,512]{2,1,0:T(8,128)(2,1)} async-done(((bf16[3,256,512]{2,1,0:T(8,128)(2,1)}), bf16[3,2048,512]{2,1,0:T(8,128)(2,1)}) %all-gather.5.cloned.1.call-update) | async-done | bytes 6291472 | tf_op jit(solution)/shard_map/all_gather | solution.py:125
  75.9 2.5 fusion.35
  82.8 25.3 %all-gather.7.cloned.1.call-done = bf16[512,2048]{1,0:T(8,128)(2,1)} async-done(((bf16[512,256]{1,0:T(8,128)(2,1)}), bf16[512,2048]{1,0:T(8,128)(2,1)}) %all-gather.7.cloned.1.call-update) | async-done | bytes 2097168 | tf_op jit(solution)/shard_map/all_gather | solution.py:126
  108.1 3.6 fusion.86
  113.3 65.4 %all-reduce.6.cloned.1.call-done = f32[256,2048]{1,0:T(8,128)} async-done(((f32[256,2048]{1,0:T(8,128)}), f32[256,2048]{1,0:T(8,128)}) %all-reduce.6.cloned.1.call-update) | async-done | bytes 2097168 | tf_op jit(solution)/shard_map/psum | solution.py:153
  181.0 78.5 %all-gather.9.cloned.1.call-done = bf16[2048,2048]{1,0:T(8,128)(2,1)} async-done(((bf16[256,2048]{1,0:T(8,128)(2,1)}), bf16[2048,2048]{1,0:T(8,128)(2,1)}) %all-gather.9.cloned.1.call-update) | async-done | bytes 8388624 | tf_op jit(solution)/shard_map/all_gather | solution.py:127
  259.6 7.1 convolution_add_fusion
  266.7 75.0 %all-gather.11.cloned.1.call-done = bf16[2048,2048]{1,0:T(8,128)(2,1)} async-done(((bf16[2048,256]{1,0:T(8,128)(2,1)}), bf16[2048,2048]{1,0:T(8,128)(2,1)}) %all-gather.11.cloned.1.call-update) | async-done | bytes 8388624 | tf_op jit(solution)/shard_map/all_gather | solution.py:128
  341.7 11.1 fusion.76
  353.8 3.7 fusion.55
  357.6 2.6 multiply_convert_fusion
  361.1 6.7 convolution_convert_fusion
  368.2 60.1 %all-reduce.10.cloned.1.call-done = f32[256,2048]{1,0:T(8,128)} async-done(((f32[256,2048]{1,0:T(8,128)}), f32[256,2048]{1,0:T(8,128)}) %all-reduce.10.cloned.1.call-update) | async-done | bytes 2097168 | tf_op jit(solution)/shard_map/psum | solution.py:173
  428.3 2.5 multiply_reduce_fusion
  430.8 53.6 %all-reduce.8.cloned.1.call-done = bf16[256,2048]{1,0:T(8,128)(2,1)} async-done(((bf16[256,2048]{1,0:T(8,128)(2,1)}), bf16[256,2048]{1,0:T(8,128)(2,1)}) %all-reduce.8.cloned.1.call-update) | async-done | bytes 1048592 | tf_op jit(solution)/shard_map/psum | solution.py:170
  484.4 4.7 fusion.78
  497.4 3.6 convolution_convert_fusion.1
  501.0 3.7 fusion.82
  509.4 6.1 convolution_bitcast_fusion.1
  515.6 7.9 convolution_bitcast_fusion
  524.5 4.2 fusion.45
  528.8 9.5 fusion.53
  539.8 8.1 fusion.87
  548.0 37.2 %all-reduce.12.cloned.1.call-done = f32[256,2048]{1,0:T(8,128)} async-done(((f32[256,2048]{1,0:T(8,128)}), f32[256,2048]{1,0:T(8,128)}) %all-reduce.12.cloned.1.call-update) | async-done | bytes 2097168 | tf_op jit(solution)/shard_map/psum | solution.py:196
  585.1 2.6 fusion.14
  587.7 27.4 %all-reduce = (f32[2048]{0:T(1024)}, f32[2048]{0:T(1024)}, f32[512]{0:T(512)}, f32[512]{0:T(512)}, f32[2048]{0:T(1024)}, /*index=5*/f32[2048]{0:T(1024)}, f32[2048]{0:T(1024)}, f32[2048]{0:T(1024)}, f32[2048]{0:T(1024)}) all-reduce(f32[2048]{0:T(1024)S(1)} %get-tuple-element.83, ...), channel_id=1, replica_groups=mesh['dp'=8,'tensor'=4] {'dp'}, use_global_device_ids=true, to_apply=%region_16.17 | all-reduce | flops 15360 | bytes 122880 | tf_op jit(solution)/shard_map/psum | solution.py:202
  615.1 3.4 fusion.13
  618.5 96.4 %reduce-scatter.5.cloned.1.call-done = f32[3,256,512]{1,2,0:T(8,128)} async-done(((f32[3,2048,512]{1,2,0:T(8,128)}), f32[3,256,512]{1,2,0:T(8,128)}) %reduce-scatter.5.cloned.1.call-update) | async-done | bytes 1572880 | tf_op jit(solution)/shard_map/reduce_scatter | solution.py:214
  715.0 3.0 copy.47
  718.0 47.2 %reduce-scatter.7.cloned.1.call-done = f32[512,256]{1,0:T(8,128)} async-done(((f32[512,2048]{1,0:T(8,128)}), f32[512,256]{1,0:T(8,128)}) %reduce-scatter.7.cloned.1.call-update) | async-done | bytes 524304 | tf_op jit(solution)/shard_map/reduce_scatter | solution.py:215
  765.2 170.3 %reduce-scatter.9.cloned.1.call-done = f32[256,2048]{1,0:T(8,128)} async-done(((f32[2048,2048]{1,0:T(8,128)}), f32[256,2048]{1,0:T(8,128)}) %reduce-scatter.9.cloned.1.call-update) | async-done | bytes 2097168 | tf_op jit(solution)/shard_map/reduce_scatter | solution.py:216
  935.5 169.4 %reduce-scatter.11.cloned.1.call-done = f32[2048,256]{1,0:T(8,128)} async-done(((f32[2048,2048]{1,0:T(8,128)}), f32[2048,256]{1,0:T(8,128)}) %reduce-scatter.11.cloned.1.call-update) | async-done | bytes 2097168 | tf_op jit(solution)/shard_map/reduce_scatter | solution.py:217
  (103 shorter events, 34.7 us)
Async XLA Ops:
  7.2 5.7 copy-start
  7.2 6.2 copy-start.19
  7.2 66.2 %all-gather.5.cloned.1.call-start = ((), (), s32[]{:S(2)}) async-start(), calls=%async_computation.4 | async-start | bytes 7077888 | tf_op jit(solution)/shard_map/all_gather | solution.py:125
  7.9 100.2 %all-gather.7.cloned.1.call-start = ((), (), s32[]{:S(2)}) async-start(), calls=%async_computation.5 | async-start | bytes 2359296 | tf_op jit(solution)/shard_map/all_gather | solution.py:126
  8.7 170.0 %all-reduce.6.cloned.1.call-start = ((), (), s32[]{:S(2)}) async-start(), calls=%async_computation.6 | async-start | bytes 4194304 | tf_op jit(solution)/shard_map/psum | solution.py:153
  75.9 2.6 copy-start.12
  78.9 2.7 copy-start.3
  81.7 0.7 copy-start.13
  82.8 29.0 %copy-start.9 = (bf16[4,128,256]{2,1,0:T(8,128)(2,1)}, bf16[4,128,256]{2,1,0:T(8,128)(2,1)S(1)}, u32[]{:S(2)}) copy-start(bf16[4,128,256]{2,1,0:T(8,128)(2,1)S(1)} %convolution_convert_fusion.3) | copy-start | bytes 786436
  111.8 1.4 copy-start.14
  111.8 1.5 copy-start.15
  111.8 1.5 copy-start.16
  111.8 1.5 copy-start.17
  111.8 147.7 %all-gather.9.cloned.1.call-start = ((), (), s32[]{:S(2)}) async-start(), calls=%async_computation.7 | async-start | bytes 9437184 | tf_op jit(solution)/shard_map/all_gather | solution.py:127
  112.4 229.3 %all-gather.11.cloned.1.call-start = ((), (), s32[]{:S(2)}) async-start(), calls=%async_computation.8 | async-start | bytes 9437184 | tf_op jit(solution)/shard_map/all_gather | solution.py:128
  113.0 315.3 %all-reduce.10.cloned.1.call-start = ((), (), s32[]{:S(2)}) async-start(), calls=%async_computation.10 | async-start | bytes 4194304 | tf_op jit(solution)/shard_map/psum | solution.py:173
  341.7 12.1 %copy-start.20 = (bf16[2048,2048]{1,0:T(8,128)(2,1)S(1)}, bf16[2048,2048]{1,0:T(8,128)(2,1)}, u32[]{:S(2)}) copy-start(bf16[2048,2048]{1,0:T(8,128)(2,1)} %all-gather.9.cloned.1.call-done) | copy-start | bytes 25165828
  352.8 1.1 copy-start.8
  357.5 126.9 %all-reduce.8.cloned.1.call-start = ((), (), s32[]{:S(2)}) async-start(), calls=%async_computation.9 | async-start | bytes 2097152 | tf_op jit(solution)/shard_map/psum | solution.py:170
  360.1 1.0 copy-start.6
  361.1 7.0 copy-start.18
  367.9 217.2 %all-reduce.12.cloned.1.call-start = ((), (), s32[]{:S(2)}) async-start(), calls=%async_computation.11 | async-start | bytes 4194304 | tf_op jit(solution)/shard_map/psum | solution.py:196
  484.4 6.0 copy-start.4
  489.1 1.3 copy-start.1
  515.5 199.5 %reduce-scatter.5.cloned.1.call-start = ((), (), s32[]{:S(2)}) async-start(), calls=%async_computation.12 | async-start | bytes 14155776 | tf_op jit(solution)/shard_map/reduce_scatter | solution.py:214
  523.5 0.9 copy-start.10
  523.5 241.7 %reduce-scatter.7.cloned.1.call-start = ((), (), s32[]{:S(2)}) async-start(), calls=%async_computation.13 | async-start | bytes 4718592 | tf_op jit(solution)/shard_map/reduce_scatter | solution.py:215
  528.7 406.8 %reduce-scatter.9.cloned.1.call-start = ((), (), s32[]{:S(2)}) async-start(), calls=%async_computation.14 | async-start | bytes 18874368 | tf_op jit(solution)/shard_map/reduce_scatter | solution.py:216
  538.3 1.2 copy-start.5
  538.3 1.5 copy-start.7
  538.3 566.6 %reduce-scatter.11.cloned.1.call-start = ((), (), s32[]{:S(2)}) async-start(), calls=%async_computation.15 | async-start | bytes 18874368 | tf_op jit(solution)/shard_map/reduce_scatter | solution.py:217
  547.9 67.1 %copy-start.2 = (f32[256,2048]{1,0:T(8,128)S(1)}, f32[256,2048]{1,0:T(8,128)}, u32[]{:S(2)}) copy-start(f32[256,2048]{1,0:T(8,128)} %copy-done.1) | copy-start | bytes 6291460
  (1 other events, 0.7 us)
Sparse Core Ops, SparseCore 0:
  9.6 63.7 all-gather.4
  75.0 33.0 all-gather.6
  111.9 66.7 all-reduce.5
  180.1 79.3 all-gather.8
  261.0 80.6 all-gather.10
  357.6 70.6 all-reduce.9
  431.9 52.4 all-reduce.7
  515.6 69.4 all-reduce.11
  587.5 127.4 reduce-scatter.4
  717.7 47.4 reduce-scatter.6
  768.1 167.3 reduce-scatter.8
  938.3 166.6 reduce-scatter.10
where the time goes:
time: 1120 us; the launch traced here: 1110 us
  waiting for transfers between devices  941 us (84%)
  matrix products  89.2 us (8%)
  blocking collectives  27.4 us (2%)
  other arithmetic  23.1 us (2%)
  local copies, waits for them, and re-layouts  15.4 us (1%)
  between operations  14.6 us (1%)
    reduce_scatter x1, waiting for transfers between devices, shards(): lax.psum_scatter(grad_up, 'dp', scatter_dimension=0, tiled=True)  170 us
    reduce_scatter x1, waiting for transfers between devices, shards(): lax.psum_scatter(grad_down, 'dp', scatter_dimension=1, tiled=True)  169 us
    reduce_scatter x1, waiting for transfers between devices, shards(): lax.psum_scatter(grad_in, 'dp', scatter_dimension=1, tiled=True)  96.4 us
    all_gather x1, waiting for transfers between devices, shards(): lax.all_gather(up_weight, 'dp', axis=0, tiled=True)  78.5 us
    all_gather x1, waiting for transfers between devices, shards(): lax.all_gather(down_weight, 'dp', axis=1, tiled=True)  75 us
    psum x1, waiting for transfers between devices, shards(): attention = lax.psum(attention_part, 'tensor')  65.4 us
    psum x1, waiting for transfers between devices, shards(): second_grad = lax.psum(second_part, 'tensor')  60.1 us
    all_gather x1, waiting for transfers between devices, shards(): lax.all_gather(project_in, 'dp', axis=1, tiled=True)  59.9 us
  transfers between devices with their start and end apart: 12, of which 12 were waited for; matrix products, arithmetic and copies ran while one was open for 7% of the time, Pallas kernels for 0%

commit v1 on v0

v1 whole, which is shorter than its diff:
```python
import jax
import jax.numpy as jnp
from jax import lax
from jax.sharding import PartitionSpec as P

DH = 128
EPSILON = 1e-05
NEGATIVE = -1e30
F32 = jnp.float32
BF16 = jnp.bfloat16


def exact_gelu(values):
    return jax.nn.gelu(values, approximate=False)


def dot(left, right, dims):
    return lax.dot_general(left, right, (dims, ((), ())), preferred_element_type=F32)


def split_at(values, pieces, axis):
    size = values.shape[axis] // pieces
    return [lax.slice_in_dim(values, i * size, (i + 1) * size, axis=axis) for i in range(pieces)]


class Places:
    def __init__(self, dp, tensor):
        self.dp, self.tensor, self.chips = dp, tensor, dp // 2
        self.rank = lax.axis_index("dp")
        self.part = lax.axis_index("tensor")
        self.chip, self.core = self.rank // 2, self.rank % 2
        chips = self.chips
        self.plus = [(i, (i // 2 + 1) % chips * 2 + i % 2) for i in range(dp)]
        self.minus = [(i, (i // 2 - 1) % chips * 2 + i % 2) for i in range(dp)]
        self.swap = [(i, i ^ 1) for i in range(dp)]

    def owner(self, place):
        other, hops = place // self.chips, place % self.chips
        return (self.chip + hops) % self.chips * 2 + (self.core ^ other)

    def place(self, owner):
        chip, core = owner // 2, owner % 2
        return (self.core ^ core) * self.chips + (chip - self.chip) % self.chips

    def features_in(self, values, axis):
        size = values.shape[axis] // self.dp
        return lax.concatenate(
            [
                lax.dynamic_slice_in_dim(values, self.owner(j) * size, size, axis)
                for j in range(self.dp)
            ],
            axis,
        )

    def features_out(self, values, axis):
        size = values.shape[axis] // self.dp
        return lax.concatenate(
            [
                lax.dynamic_slice_in_dim(values, self.place(j) * size, size, axis)
                for j in range(self.dp)
            ],
            axis,
        )

    def tokens_in(self, values):
        size = values.shape[0] // self.tensor
        return lax.concatenate(
            [
                lax.dynamic_slice_in_dim(values, (self.part ^ k) * size, size, 0)
                for k in range(self.tensor)
            ],
            0,
        )

    def send(self, values, pairs):
        return lax.ppermute(values, "dp", pairs)

    def to_peer(self, values, k):
        return lax.ppermute(values, "tensor", [(i, i ^ k) for i in range(self.tensor)])

    def gather_weight(self, block, axis):
        half = self.chips // 2
        pieces = {0: [block]}
        ahead = behind = block
        for step in range(1, half):
            behind = self.send(behind, self.plus)
            ahead = self.send(ahead, self.minus)
            pieces[self.chips - step], pieces[step] = [behind], [ahead]
        low = split_at(behind, 2, axis)[0]
        high = split_at(ahead, 2, axis)[1]
        pieces[half] = [self.send(low, self.plus), self.send(high, self.minus)]
        mine = [piece for hops in range(self.chips) for piece in pieces[hops]]
        theirs = [self.send(piece, self.swap) for piece in mine]
        return lax.concatenate(mine + theirs, axis)

    def scatter_grad(self, product, axis):
        chips, half = self.chips, self.chips // 2
        theirs = self.send(product(chips, 2 * chips).astype(BF16), self.swap)
        mine = product(0, chips) + theirs.astype(F32)
        blocks = split_at(mine, chips, axis)
        far = split_at(blocks[half].astype(BF16), 2, axis)
        low, high = self.send(far[0], self.plus), self.send(far[1], self.minus)
        for hops in range(half - 1, 0, -1):
            ahead, behind = blocks[hops], blocks[chips - hops]
            if hops == half - 1:
                a, b = split_at(ahead, 2, axis)
                ahead = lax.concatenate([a + low.astype(F32), b], axis)
                a, b = split_at(behind, 2, axis)
                behind = lax.concatenate([a, b + high.astype(F32)], axis)
            else:
                ahead, behind = ahead + low.astype(F32), behind + high.astype(F32)
            low = self.send(ahead.astype(BF16), self.plus)
            high = self.send(behind.astype(BF16), self.minus)
        return blocks[0] + low.astype(F32) + high.astype(F32)

    def scatter_tokens(self, values):
        chunks = split_at(values, self.tensor, 0)
        total = chunks[0]
        for k in range(1, self.tensor):
            total = total + self.to_peer(chunks[k].astype(BF16), k).astype(F32)
        return total

    def gather_tokens(self, chunk):
        return lax.concatenate(
            [chunk] + [self.to_peer(chunk, k) for k in range(1, self.tensor)], 0
        )

    def tokens_out(self, chunk):
        size = chunk.shape[0]
        result = jnp.zeros((size * self.tensor,) + chunk.shape[1:], chunk.dtype)
        for k in range(self.tensor):
            piece = chunk if k == 0 else self.to_peer(chunk, k)
            result = lax.dynamic_update_slice_in_dim(result, piece, (self.part ^ k) * size, 0)
        return result

    def sum_small(self, values, over_tensor):
        if over_tensor:
            values = values + sum(self.to_peer(values, k) for k in range(1, self.tensor))
        values = values + self.send(values, self.swap)
        total = values
        for hops in range(1, self.chips):
            total = total + self.send(
                values, [(i, (i // 2 + hops) % self.chips * 2 + i % 2) for i in range(self.dp)]
            )
        return total


def normalize(values):
    center = values - jnp.mean(values, axis=-1, keepdims=True)
    inverse = lax.rsqrt(jnp.mean(center * center, axis=-1, keepdims=True) + EPSILON)
    return (center * inverse, inverse)


def norm_back(norm_grad, normed, inverse, gain):
    scaled = norm_grad * gain
    return inverse * (
        scaled
        - jnp.mean(scaled, axis=-1, keepdims=True)
        - normed * jnp.mean(scaled * normed, axis=-1, keepdims=True)
    )


def mask_of(ids, places):
    allowed = (
        (ids[:, None] == ids[None, :])
        & (ids[:, None] != 0)
        & (places[None, :] <= places[:, None])
    )
    return allowed | (places[None, :] == places[:, None])


def heads_of(values):
    return values.reshape(values.shape[0], -1, DH).transpose(1, 0, 2)


def tokens_of(values):
    return values.transpose(1, 0, 2).reshape(values.shape[1], -1)


def batched(pattern, left, right):
    return jnp.einsum(pattern, left, right, preferred_element_type=F32)


def probabilities(query, key, allowed):
    scores = jnp.where(allowed[None], batched("hqd,hkd->hqk", query, key) * DH ** (-0.5), NEGATIVE)
    weights = jnp.exp(scores - jnp.max(scores, axis=-1, keepdims=True))
    return weights / jnp.sum(weights, axis=-1, keepdims=True)


def shards(
    dp,
    tensor,
    inputs,
    segment_ids,
    first_gain,
    first_shift,
    project_in,
    query_bias,
    value_bias,
    project_out,
    out_bias,
    second_gain,
    second_shift,
    up_weight,
    up_bias,
    down_weight,
    down_bias,
    cotangent,
):
    at = Places(dp, tensor)
    length = inputs.shape[0]
    own = length // tensor
    full_in = at.gather_weight(project_in, 1)
    full_out = at.gather_weight(project_out, 1)
    full_up = at.gather_weight(up_weight, 0)
    full_down = at.gather_weight(down_weight, 1)

    vectors = jnp.stack(
        [first_gain, first_shift, out_bias, second_gain, second_shift, down_bias]
    ).astype(F32)
    vectors = at.features_in(vectors, 1)
    gain_one, shift_one, bias_out, gain_two, shift_two, bias_down = [vectors[i] for i in range(6)]
    resid = at.features_in(at.tokens_in(inputs), 1)
    upstream = at.features_in(at.tokens_in(cotangent), 1)
    ids = at.tokens_in(segment_ids)
    places = at.tokens_in(jnp.arange(length, dtype=jnp.int32))
    allowed = mask_of(ids, places)

    normed_one, inverse_one = normalize(resid.astype(F32))
    first_low = (normed_one * gain_one + shift_one).astype(BF16)
    rows = ((1,), (0,))
    query = (dot(first_low, full_in[0], rows) + query_bias.astype(F32)).astype(BF16)
    key = dot(first_low, full_in[1], rows).astype(BF16)
    value = (dot(first_low, full_in[2], rows) + value_bias.astype(F32)).astype(BF16)
    query_heads, key_heads, value_heads = heads_of(query), heads_of(key), heads_of(value)
    probs = probabilities(query_heads, key_heads, allowed)
    probs_low = probs.astype(BF16)
    mixed = tokens_of(batched("hqk,hkd->hqd", probs_low, value_heads).astype(BF16))

    attention = at.scatter_tokens(dot(mixed, full_out, rows))
    hidden = resid[:own].astype(F32) + attention + bias_out
    normed_two, inverse_two = normalize(hidden)
    second_own = (normed_two * gain_two + shift_two).astype(BF16)
    second_low = at.gather_tokens(second_own)
    upper = dot(second_low, full_up, rows) + up_bias.astype(F32)
    activated = exact_gelu(upper).astype(BF16)

    act_grad = dot(upstream, full_down, ((1,), (1,)))
    upper_grad = jax.vjp(exact_gelu, upper)[1](act_grad)[0]
    upper_low = upper_grad.astype(BF16)
    second_grad = at.scatter_tokens(dot(upper_low, full_up, ((1,), (1,))))
    feed = at.scatter_tokens(dot(activated, full_down, rows))
    outputs_own = (hidden + feed + bias_down).astype(BF16)
    outputs = at.tokens_out(at.features_out(outputs_own, 1))

    upstream_own = upstream[:own].astype(F32)
    hidden_grad = upstream_own + norm_back(second_grad, normed_two, inverse_two, gain_two)
    hidden_low = at.gather_tokens(hidden_grad.astype(BF16))
    mixed_grad = dot(hidden_low, full_out, ((1,), (1,))).astype(BF16)

    mixed_heads = heads_of(mixed_grad)
    prob_grad = batched("hqd,hkd->hqk", mixed_heads, value_heads)
    score_grad = probs * (prob_grad - jnp.sum(probs * prob_grad, axis=-1, keepdims=True))
    score_low = (score_grad * DH ** (-0.5)).astype(BF16)
    query_grad = tokens_of(batched("hqk,hkd->hqd", score_low, key_heads))
    key_grad = tokens_of(batched("hqk,hqd->hkd", score_low, query_heads))
    value_grad = tokens_of(batched("hqk,hqd->hkd", probs_low, mixed_heads))
    lows = [query_grad.astype(BF16), key_grad.astype(BF16), value_grad.astype(BF16)]
    first_part = sum(dot(lows[j], full_in[j], ((1,), (1,))) for j in range(3))
    first_grad = at.scatter_tokens(first_part)
    input_grad_own = (
        hidden_grad + norm_back(first_grad, normed_one[:own], inverse_one[:own], gain_one)
    ).astype(BF16)
    input_gradient = at.tokens_out(at.features_out(input_grad_own, 1))

    size = full_up.shape[0] // dp
    over_tokens = ((0,), (0,))

    def columns(values, low, high):
        return values[:, low * size : high * size]

    grad_down = at.scatter_grad(
        lambda low, high: dot(activated, columns(upstream, low, high), over_tokens), 1
    )
    grad_up = at.scatter_grad(
        lambda low, high: dot(columns(second_low, low, high), upper_low, over_tokens), 0
    )
    grad_out = at.scatter_grad(
        lambda low, high: dot(mixed, columns(hidden_low, low, high), over_tokens), 1
    )
    stacked = jnp.stack(lows)
    grad_in = at.scatter_grad(
        lambda low, high: jnp.einsum(
            "rd,jrh->jdh", columns(first_low, low, high), stacked, preferred_element_type=F32
        ),
        1,
    )

    wide = jnp.stack(
        [
            jnp.sum(first_grad * normed_one[:own], axis=0),
            jnp.sum(first_grad, axis=0),
            jnp.sum(hidden_grad, axis=0),
            jnp.sum(second_grad * normed_two, axis=0),
            jnp.sum(second_grad, axis=0),
            jnp.sum(upstream_own, axis=0),
        ]
    )
    wide = at.sum_small(at.features_out(wide, 1), True)
    narrow = jnp.concatenate(
        [jnp.sum(query_grad, axis=0), jnp.sum(value_grad, axis=0), jnp.sum(upper_grad, axis=0)]
    )
    narrow = at.sum_small(narrow, False)
    heads = query.shape[1]
    return (
        outputs,
        input_gradient,
        wide[0],
        wide[1],
        grad_in,
        narrow[:heads],
        narrow[heads : 2 * heads],
        grad_out,
        wide[2],
        wide[3],
        wide[4],
        grad_up,
        narrow[2 * heads :],
        grad_down,
        wide[5],
    )


def solution(mesh):
    dp, tensor = mesh.shape["dp"], mesh.shape["tensor"]

    def program(*arguments):
        return shards(dp, tensor, *arguments)

    in_specs = (
        P("dp", None),
        P("dp"),
        P(),
        P(),
        P(None, "dp", "tensor"),
        P("tensor"),
        P("tensor"),
        P("tensor", "dp"),
        P(),
        P(),
        P(),
        P("dp", "tensor"),
        P("tensor"),
        P("tensor", "dp"),
        P(),
        P("dp", None),
    )
    out_specs = (
        P("dp", None),
        P("dp", None),
        P(),
        P(),
        P(None, "dp", "tensor"),
        P("tensor"),
        P("tensor"),
        P("tensor", "dp"),
        P(),
        P(),
        P(),
        P("dp", "tensor"),
        P("tensor"),
        P("tensor", "dp"),
        P(),
    )
    return jax.shard_map(program, mesh=mesh, in_specs=in_specs, out_specs=out_specs, check_vma=False)
```

time: 1120 us -> 635 us (0.57)
  waiting for transfers between devices: 941 us -> 341 us
  starting transfers between devices: 1.15 us -> 87.6 us
  local copies, waits for them, and re-layouts: 15.4 us -> 88.4 us
  blocking collectives: 27.4 us -> 0 us
  matrix products: 89.2 us -> 73.3 us
  between operations: 14.6 us -> 2.99 us
    reduce_scatter x4 -> x0, waiting for transfers between devices: 483 us -> none  [the longest x1 170 us: shards(): lax.psum_scatter(grad_up, 'dp', scatter_dimension=0, tiled=True)]
    ppermute x0 -> x91, waiting for transfers between devices: none -> 341 us  [the longest x64 303 us: send(): return lax.ppermute(values, 'dp', pairs)]
    all_gather x4 -> x0, waiting for transfers between devices: 239 us -> none  [the longest x1 78.5 us: shards(): lax.all_gather(up_weight, 'dp', axis=0, tiled=True)]
    psum x4 -> x0, waiting for transfers between devices: 216 us -> none  [the longest x1 65.4 us: shards(): attention = lax.psum(attention_part, 'tensor')]
    ppermute x0 -> x91, starting transfers between devices: none -> 87.6 us  [the longest x64 54.5 us: send(): return lax.ppermute(values, 'dp', pairs)]
    unnamed x43 -> x224, local copies, waits for them, and re-layouts: 9.33 us -> 55 us
    psum x1 -> x0, blocking collectives: 27.4 us -> none  [shards(): lax.psum((grad_first_gain, grad_first_shift, grad_out_bias, grad_second_g...]
    dot_general x20 -> x25, matrix products: 89.2 us -> 70.2 us  [the longest x18 52.1 us: dot(): lax.dot_general(left, right, (dims, ((), ())), preferred_element_type=F32)]
  transfers between devices with their start and end apart: 12 -> 91, of which waited for: 12 -> 34; matrix products, arithmetic and copies ran while one was open for 7% -> 27% of each run, Pallas kernels for 0% -> 0%
where the time goes in v1:
time: 635 us; the launch traced here: 624 us
  waiting for transfers between devices  341 us (54%)
  local copies, waits for them, and re-layouts  88.4 us (14%)
  starting transfers between devices  87.6 us (14%)
  matrix products  73.3 us (12%)
  other arithmetic  31.2 us (5%)
    ppermute x64, waiting for transfers between devices, send(): return lax.ppermute(values, 'dp', pairs)  303 us
    unnamed x224, local copies, waits for them, and re-layouts  55 us
    ppermute x64, starting transfers between devices, send(): return lax.ppermute(values, 'dp', pairs)  54.5 us
    dot_general x18, matrix products, dot(): lax.dot_general(left, right, (dims, ((), ())), preferred_element_type=F32)  52.1 us
    ppermute x27, waiting for transfers between devices, to_peer(): lax.ppermute(values, 'tensor', [(i, i ^ k) for i in range(self.tensor)])  38.2 us
    ppermute x27, starting transfers between devices, to_peer(): lax.ppermute(values, 'tensor', [(i, i ^ k) for i in range(self.tensor)])  33.1 us
  transfers between devices with their start and end apart: 91, of which 34 were waited for; matrix products, arithmetic and copies ran while one was open for 27% of the time, Pallas kernels for 0%

profile of v1, /device:TPU:8, one launch (start us, length us, event | category | flops | bytes accessed | tf_op | source)
XLA Modules:
  0.0 624.2 jit_solution(10269294732961056523)
XLA Ops:
  25.9 3.4 collective-permute-start.11
  32.4 5.1 collective-permute-done.11
  55.0 54.2 %collective-permute-done = bf16[3,256,512]{2,1,0:T(8,128)(2,1)S(1)} collective-permute-done((bf16[3,256,512]{2,1,0:T(8,128)(2,1)}, bf16[3,256,512]{2,1,0:T(8,128)(2,1)S(1)}, u32[]{:S(2)}, u32[]{:S(2)}) %collective-permute-start) | collective-permute-done | bytes 786464 | tf_op jit(solution)/shard_map/ppermute | solution.py:76
  114.8 47.8 %collective-permute-done.33 = bf16[2048,256]{1,0:T(8,128)(2,1)S(1)} collective-permute-done((bf16[2048,256]{1,0:T(8,128)(2,1)}, bf16[2048,256]{1,0:T(8,128)(2,1)S(1)}, u32[]{:S(2)}, u32[]{:S(2)}) %collective-permute-start.33) | collective-permute-done | bytes 1048608 | tf_op jit(solution)/shard_map/ppermute | solution.py:76
  165.7 16.1 %collective-permute-done.3 = bf16[3,128,512]{2,1,0:T(8,128)(2,1)S(1)} collective-permute-done((bf16[3,128,512]{2,1,0:T(8,128)(2,1)S(1)}, bf16[3,128,512]{2,1,0:T(8,128)(2,1)S(1)}, u32[]{:S(2)}, u32[]{:S(2)}) %collective-permute-start.3) | collective-permute-done | bytes 393248 | tf_op jit(solution)/shard_map/ppermute | solution.py:76
  186.1 21.2 %collective-permute-done.27 = bf16[128,2048]{1,0:T(8,128)(2,1)S(1)} collective-permute-done((bf16[128,2048]{1,0:T(8,128)(2,1)S(1)}, bf16[128,2048]{1,0:T(8,128)(2,1)S(1)}, u32[]{:S(2)}, u32[]{:S(2)}) %collective-permute-start.27) | collective-permute-done | bytes 524320 | tf_op jit(solution)/shard_map/ppermute | solution.py:76
  211.8 5.9 collective-permute-done.36
  243.0 5.1 collective-permute-done.19
  265.0 5.0 collective-permute-done.22
  270.1 5.9 convolution_add_fusion.1
  276.0 9.1 %fusion.103 = (f32[2048]{0:T(1024)}, bf16[256,2048]{1,0:T(8,128)(2,1)S(1)}, f32[256,2048]{1,0:T(8,128)S(1)}) fusion(f32[256,2048]{1,0:T(8,128)S(1)} %convolution_add_fusion.1, bf16[256,2048]{1,0:T(8,128)(2,1)} %get-tuple-element.45, bf16[2048,2048]{1,0:T(8,128)(2,1)S(1)} %copy-done.55), kind=kOutput, calls=%fused_computation.322 | convolution fusion | flops 2185754624 | bytes 14688256 | tf_op jit(solution)/shard_map/dot_general | solution.py:18
  291.5 5.7 fusion.127
  308.1 5.5 collective-permute-done.43
  342.3 3.6 fusion.118
  371.6 4.1 collective-permute-done.55
  397.4 4.8 collective-permute-done.57
  406.3 5.5 collective-permute-done.59
  419.4 4.7 collective-permute-start.70
  428.5 4.6 collective-permute-done.68
  433.6 7.3 %collective-permute-done.70 = bf16[3,128,512]{1,2,0:T(8,128)(2,1)S(1)} collective-permute-done((bf16[3,128,512]{1,2,0:T(8,128)(2,1)S(1)}, bf16[3,128,512]{1,2,0:T(8,128)(2,1)S(1)}, u32[]{:S(2)}, u32[]{:S(2)}) %collective-permute-start.70) | collective-permute-done | bytes 393248 | tf_op jit(solution)/shard_map/ppermute | solution.py:76
  445.8 3.5 fusion.134
  454.5 3.5 fusion.133
  458.3 22.6 %collective-permute-done.87 = bf16[2048,128]{0,1:T(8,128)(2,1)S(1)} collective-permute-done((bf16[2048,128]{0,1:T(8,128)(2,1)}, bf16[2048,128]{0,1:T(8,128)(2,1)S(1)}, u32[]{:S(2)}, u32[]{:S(2)}) %collective-permute-start.87) | collective-permute-done | bytes 524320 | tf_op jit(solution)/shard_map/ppermute | solution.py:76
  482.2 7.5 %collective-permute-done.89 = bf16[2048,128]{0,1:T(8,128)(2,1)S(1)} collective-permute-done((bf16[2048,128]{0,1:T(8,128)(2,1)S(1)}, bf16[2048,128]{0,1:T(8,128)(2,1)S(1)}, u32[]{:S(2)}, u32[]{:S(2)}) %collective-permute-start.89) | collective-permute-done | bytes 524320 | tf_op jit(solution)/shard_map/ppermute | solution.py:76
  492.7 10.7 %collective-permute-done.82 = bf16[128,2048]{1,0:T(8,128)(2,1)S(1)} collective-permute-done((bf16[128,2048]{1,0:T(8,128)(2,1)S(1)}, bf16[128,2048]{1,0:T(8,128)(2,1)S(1)}, u32[]{:S(2)}, u32[]{:S(2)}) %collective-permute-start.82) | collective-permute-done | bytes 524320 | tf_op jit(solution)/shard_map/ppermute | solution.py:76
  504.8 9.5 %collective-permute-done.84 = bf16[128,2048]{1,0:T(8,128)(2,1)S(1)} collective-permute-done((bf16[128,2048]{1,0:T(8,128)(2,1)S(1)}, bf16[128,2048]{1,0:T(8,128)(2,1)S(1)}, u32[]{:S(2)}, u32[]{:S(2)}) %collective-permute-start.84) | collective-permute-done | bytes 524320 | tf_op jit(solution)/shard_map/ppermute | solution.py:76
  525.2 6.4 %collective-permute-done.69 = bf16[3,256,512]{1,2,0:T(8,128)(2,1)S(1)} collective-permute-done((bf16[3,256,512]{1,2,0:T(8,128)(2,1)S(1)}, bf16[3,256,512]{1,2,0:T(8,128)(2,1)S(1)}, u32[]{:S(2)}, u32[]{:S(2)}) %collective-permute-start.69) | collective-permute-done | bytes 786464 | tf_op jit(solution)/shard_map/ppermute | solution.py:76
  533.5 23.0 %collective-permute-done.90 = bf16[2048,256]{0,1:T(8,128)(2,1)} collective-permute-done((bf16[2048,256]{0,1:T(8,128)(2,1)S(1)}, bf16[2048,256]{0,1:T(8,128)(2,1)}, u32[]{:S(2)}, u32[]{:S(2)}) %collective-permute-start.90) | collective-permute-done | bytes 1048608 | tf_op jit(solution)/shard_map/ppermute | solution.py:76
  556.6 20.1 %collective-permute-done.88 = bf16[2048,256]{0,1:T(8,128)(2,1)} collective-permute-done((bf16[2048,256]{0,1:T(8,128)(2,1)}, bf16[2048,256]{0,1:T(8,128)(2,1)}, u32[]{:S(2)}, u32[]{:S(2)}) %collective-permute-start.88) | collective-permute-done | bytes 1048608 | tf_op jit(solution)/shard_map/ppermute | solution.py:76
  581.1 18.2 %collective-permute-done.85 = bf16[256,2048]{1,0:T(8,128)(2,1)} collective-permute-done((bf16[256,2048]{1,0:T(8,128)(2,1)}, bf16[256,2048]{1,0:T(8,128)(2,1)}, u32[]{:S(2)}, u32[]{:S(2)}) %collective-permute-start.85) | collective-permute-done | bytes 1048608 | tf_op jit(solution)/shard_map/ppermute | solution.py:76
  599.2 20.6 %collective-permute-done.83 = bf16[256,2048]{1,0:T(8,128)(2,1)} collective-permute-done((bf16[256,2048]{1,0:T(8,128)(2,1)}, bf16[256,2048]{1,0:T(8,128)(2,1)}, u32[]{:S(2)}, u32[]{:S(2)}) %collective-permute-start.83) | collective-permute-done | bytes 1048608 | tf_op jit(solution)/shard_map/ppermute | solution.py:76
  619.8 4.0 fusion.8
  (517 shorter events, 246.9 us)
Async XLA Ops:
  0.6 29.4 %collective-permute-start.9 = (bf16[512,256]{1,0:T(8,128)(2,1)}, bf16[512,256]{1,0:T(8,128)(2,1)}, u32[]{:S(2)}, u32[]{:S(2)}) collective-permute-start(bf16[512,256]{1,0:T(8,128)(2,1)} %param.23), channel_id=1, source_target_pairs={{0,24},{4,28},{8,0},{12,4},{16,8},{20,12},{24,16},{28,20},{1,25},{... | collective-permute-start | bytes 786440 | tf_op jit(solution)/shard_map/ppermute | solution.py:76
  2.7 39.3 %collective-permute-start.13 = (bf16[512,256]{1,0:T(8,128)(2,1)}, bf16[512,256]{1,0:T(8,128)(2,1)}, u32[]{:S(2)}, u32[]{:S(2)}) collective-permute-start(bf16[512,256]{1,0:T(8,128)(2,1)} %param.23), channel_id=1, source_target_pairs={{0,4},{4,0},{8,12},{12,8},{16,20},{20,16},{24,28},{28,24},{1,5},{5... | collective-permute-start | bytes 786440 | tf_op jit(solution)/shard_map/ppermute | solution.py:76
  2.7 48.9 %collective-permute-start.1 = (bf16[3,256,512]{2,1,0:T(8,128)(2,1)}, bf16[3,256,512]{2,1,0:T(8,128)(2,1)}, u32[]{:S(2)}, u32[]{:S(2)}) collective-permute-start(bf16[3,256,512]{2,1,0:T(8,128)(2,1)} %param.20), channel_id=1, source_target_pairs={{0,8},{4,12},{8,16},{12,20},{16,24},{20,28},{24,0},{28,4},{1,9},{5... | collective-permute-start | bytes 2359304 | tf_op jit(solution)/shard_map/ppermute | solution.py:76
  43.6 66.6 %collective-permute-start.24 = (bf16[256,2048]{1,0:T(8,128)(2,1)}, bf16[256,2048]{1,0:T(8,128)(2,1)}, u32[]{:S(2)}, u32[]{:S(2)}) collective-permute-start(bf16[256,2048]{1,0:T(8,128)(2,1)} %param.27), channel_id=1, source_target_pairs={{0,24},{4,28},{8,0},{12,4},{16,8},{20,12},{24,16},{28,20},{1,25},{... | collective-permute-start | bytes 3145736 | tf_op jit(solution)/shard_map/ppermute | solution.py:76
  44.1 66.1 %collective-permute-start.25 = (bf16[256,2048]{1,0:T(8,128)(2,1)}, bf16[256,2048]{1,0:T(8,128)(2,1)S(1)}, u32[]{:S(2)}, u32[]{:S(2)}) collective-permute-start(bf16[256,2048]{1,0:T(8,128)(2,1)} %param.27), channel_id=1, source_target_pairs={{0,8},{4,12},{8,16},{12,20},{16,24},{20,28},{24,0},{28,4},{1,9},{5... | collective-permute-start | bytes 3145736 | tf_op jit(solution)/shard_map/ppermute | solution.py:76
  46.7 62.6 %collective-permute-start = (bf16[3,256,512]{2,1,0:T(8,128)(2,1)}, bf16[3,256,512]{2,1,0:T(8,128)(2,1)S(1)}, u32[]{:S(2)}, u32[]{:S(2)}) collective-permute-start(bf16[3,256,512]{2,1,0:T(8,128)(2,1)} %param.20), channel_id=1, source_target_pairs={{0,24},{4,28},{8,0},{12,4},{16,8},{20,12},{24,16},{28,20},{1,25},{... | collective-permute-start | bytes 2359304 | tf_op jit(solution)/shard_map/ppermute | solution.py:76
  48.1 114.5 %collective-permute-start.33 = (bf16[2048,256]{1,0:T(8,128)(2,1)}, bf16[2048,256]{1,0:T(8,128)(2,1)S(1)}, u32[]{:S(2)}, u32[]{:S(2)}) collective-permute-start(bf16[2048,256]{1,0:T(8,128)(2,1)} %param.29), channel_id=1, source_target_pairs={{0,24},{4,28},{8,0},{12,4},{16,8},{20,12},{24,16},{28,20},{1,25},{... | collective-permute-start | bytes 3145736 | tf_op jit(solution)/shard_map/ppermute | solution.py:76
  51.6 113.3 %collective-permute-start.34 = (bf16[2048,256]{1,0:T(8,128)(2,1)}, bf16[2048,256]{1,0:T(8,128)(2,1)S(1)}, u32[]{:S(2)}, u32[]{:S(2)}) collective-permute-start(bf16[2048,256]{1,0:T(8,128)(2,1)} %param.29), channel_id=1, source_target_pairs={{0,8},{4,12},{8,16},{12,20},{16,24},{20,28},{24,0},{28,4},{1,9},{5... | collective-permute-start | bytes 3145736 | tf_op jit(solution)/shard_map/ppermute | solution.py:76
  109.3 74.1 %collective-permute-start.4 = (bf16[3,256,512]{2,1,0:T(8,128)(2,1)S(1)}, bf16[3,256,512]{2,1,0:T(8,128)(2,1)S(1)}, u32[]{:S(2)}, u32[]{:S(2)}) collective-permute-start(bf16[3,256,512]{2,1,0:T(8,128)(2,1)S(1)} %copy-done.31), channel_id=1, source_target_pairs={{0,4},{4,0},{8,12},{12,8},{16,20},{20,16},{24,28},{28,24},{1,5},{5... | collective-permute-start | bytes 2359304 | tf_op jit(solution)/shard_map/ppermute | solution.py:76
  110.2 54.9 %collective-permute-start.2 = (bf16[3,128,512]{2,1,0:T(8,128)(2,1)S(1)}, bf16[3,128,512]{2,1,0:T(8,128)(2,1)S(1)}, u32[]{:S(2)}, u32[]{:S(2)}) collective-permute-start(bf16[3,128,512]{2,1,0:T(8,128)(2,1)S(1)} %slice.392), channel_id=1, source_target_pairs={{0,8},{4,12},{8,16},{12,20},{16,24},{20,28},{24,0},{28,4},{1,9},{5... | collective-permute-start | bytes 1179656 | tf_op jit(solution)/shard_map/ppermute | solution.py:76
  110.3 71.5 %collective-permute-start.3 = (bf16[3,128,512]{2,1,0:T(8,128)(2,1)S(1)}, bf16[3,128,512]{2,1,0:T(8,128)(2,1)S(1)}, u32[]{:S(2)}, u32[]{:S(2)}) collective-permute-start(bf16[3,128,512]{2,1,0:T(8,128)(2,1)S(1)} %slice.393), channel_id=1, source_target_pairs={{0,24},{4,28},{8,0},{12,4},{16,8},{20,12},{24,16},{28,20},{1,25},{... | collective-permute-start | bytes 1179656 | tf_op jit(solution)/shard_map/ppermute | solution.py:76
  165.0 70.9 %collective-permute-start.28 = (bf16[256,2048]{1,0:T(8,128)(2,1)}, bf16[256,2048]{1,0:T(8,128)(2,1)}, u32[]{:S(2)}, u32[]{:S(2)}) collective-permute-start(bf16[256,2048]{1,0:T(8,128)(2,1)} %param.27), channel_id=1, source_target_pairs={{0,4},{4,0},{8,12},{12,8},{16,20},{20,16},{24,28},{28,24},{1,5},{5... | collective-permute-start | bytes 3145736 | tf_op jit(solution)/shard_map/ppermute | solution.py:76
  165.1 54.6 %collective-permute-start.5 = (bf16[3,256,512]{2,1,0:T(8,128)(2,1)S(1)}, bf16[3,256,512]{2,1,0:T(8,128)(2,1)S(1)}, u32[]{:S(2)}, u32[]{:S(2)}) collective-permute-start(bf16[3,256,512]{2,1,0:T(8,128)(2,1)S(1)} %collective-permute-done), channel_id=1, source_target_pairs={{0,4},{4,0},{8,12},{12,8},{16,20},{20,16},{24,28},{28,24},{1,5},{5... | collective-permute-start | bytes 2359304 | tf_op jit(solution)/shard_map/ppermute | solution.py:76
  181.8 25.6 %collective-permute-start.27 = (bf16[128,2048]{1,0:T(8,128)(2,1)S(1)}, bf16[128,2048]{1,0:T(8,128)(2,1)S(1)}, u32[]{:S(2)}, u32[]{:S(2)}) collective-permute-start(bf16[128,2048]{1,0:T(8,128)(2,1)S(1)} %slice.407), channel_id=1, source_target_pairs={{0,24},{4,28},{8,0},{12,4},{16,8},{20,12},{24,16},{28,20},{1,25},{... | collective-permute-start | bytes 1572872 | tf_op jit(solution)/shard_map/ppermute | solution.py:76
  185.2 35.3 %collective-permute-start.8 = (bf16[3,256,512]{2,1,0:T(8,128)(2,1)}, bf16[3,256,512]{2,1,0:T(8,128)(2,1)S(1)}, u32[]{:S(2)}, u32[]{:S(2)}) collective-permute-start(bf16[3,256,512]{2,1,0:T(8,128)(2,1)} %collective-permute-done.1), channel_id=1, source_target_pairs={{0,4},{4,0},{8,12},{12,8},{16,20},{20,16},{24,28},{28,24},{1,5},{5... | collective-permute-start | bytes 2359304 | tf_op jit(solution)/shard_map/ppermute | solution.py:76
  220.2 29.6 %collective-permute-start.29 = (bf16[256,2048]{1,0:T(8,128)(2,1)}, bf16[256,2048]{1,0:T(8,128)(2,1)}, u32[]{:S(2)}, u32[]{:S(2)}) collective-permute-start(bf16[256,2048]{1,0:T(8,128)(2,1)} %collective-permute-done.24), channel_id=1, source_target_pairs={{0,4},{4,0},{8,12},{12,8},{16,20},{20,16},{24,28},{28,24},{1,5},{5... | collective-permute-start | bytes 3145736 | tf_op jit(solution)/shard_map/ppermute | solution.py:76
  307.7 138.1 %collective-permute-start.86 = (bf16[2048,1024]{0,1:T(8,128)(2,1)}, bf16[2048,1024]{0,1:T(8,128)(2,1)}, u32[]{:S(2)}, u32[]{:S(2)}) collective-permute-start(bf16[2048,1024]{0,1:T(8,128)(2,1)} %convolution_convert_fusion), channel_id=1, source_target_pairs={{0,4},{4,0},{8,12},{12,8},{16,20},{20,16},{24,28},{28,24},{1,5},{5... | collective-permute-start | bytes 12582920 | tf_op jit(solution)/shard_map/ppermute | solution.py:76
  323.9 33.4 %collective-permute-start.45 = (bf16[64,2048]{1,0:T(8,128)(2,1)}, bf16[64,2048]{1,0:T(8,128)(2,1)}, u32[]{:S(2)}, u32[]{:S(2)}) collective-permute-start(bf16[64,2048]{1,0:T(8,128)(2,1)} %constant_dynamic-update-slice_fusion.56), channel_id=1, source_target_pairs={{0,1},{1,0},{2,3},{3,2},{4,5},{5,4},{6,7},{7,6},{8,9},{9,8},{10,11... | collective-permute-start | bytes 786440 | tf_op jit(solution)/shard_map/ppermute | solution.py:79
  327.8 32.9 %collective-permute-start.46 = (bf16[64,2048]{1,0:T(8,128)(2,1)}, bf16[64,2048]{1,0:T(8,128)(2,1)}, u32[]{:S(2)}, u32[]{:S(2)}) collective-permute-start(bf16[64,2048]{1,0:T(8,128)(2,1)} %constant_dynamic-update-slice_fusion.56), channel_id=1, source_target_pairs={{0,2},{1,3},{2,0},{3,1},{4,6},{5,7},{6,4},{7,5},{8,10},{9,11},{10,... | collective-permute-start | bytes 786440 | tf_op jit(solution)/shard_map/ppermute | solution.py:79
  330.0 33.6 %collective-permute-start.47 = (bf16[64,2048]{1,0:T(8,128)(2,1)}, bf16[64,2048]{1,0:T(8,128)(2,1)}, u32[]{:S(2)}, u32[]{:S(2)}) collective-permute-start(bf16[64,2048]{1,0:T(8,128)(2,1)} %constant_dynamic-update-slice_fusion.56), channel_id=1, source_target_pairs={{0,3},{1,2},{2,1},{3,0},{4,7},{5,6},{6,5},{7,4},{8,11},{9,10},{10,... | collective-permute-start | bytes 786440 | tf_op jit(solution)/shard_map/ppermute | solution.py:79
  370.4 45.6 %collective-permute-start.67 = (bf16[3,1024,512]{1,2,0:T(8,128)(2,1)}, bf16[3,1024,512]{1,2,0:T(8,128)(2,1)}, u32[]{:S(2)}, u32[]{:S(2)}) collective-permute-start(bf16[3,1024,512]{1,2,0:T(8,128)(2,1)} %convert_bitcast_fusion), channel_id=1, source_target_pairs={{0,4},{4,0},{8,12},{12,8},{16,20},{20,16},{24,28},{28,24},{1,5},{5... | collective-permute-start | bytes 9437192 | tf_op jit(solution)/shard_map/ppermute | solution.py:76
  402.2 49.2 %collective-permute-start.81 = (bf16[1024,2048]{1,0:T(8,128)(2,1)S(1)}, bf16[1024,2048]{1,0:T(8,128)(2,1)S(1)}, u32[]{:S(2)}, u32[]{:S(2)}) collective-permute-start(bf16[1024,2048]{1,0:T(8,128)(2,1)S(1)} %copy-done.2), channel_id=1, source_target_pairs={{0,4},{4,0},{8,12},{12,8},{16,20},{20,16},{24,28},{28,24},{1,5},{5... | collective-permute-start | bytes 12582920 | tf_op jit(solution)/shard_map/ppermute | solution.py:76
  424.9 91.8 %collective-permute-start.80 = (bf16[512,256]{1,0:T(8,128)(2,1)}, bf16[512,256]{1,0:T(8,128)(2,1)}, u32[]{:S(2)}, u32[]{:S(2)}) collective-permute-start(bf16[512,256]{1,0:T(8,128)(2,1)} %pad_maximum_fusion.14), channel_id=1, source_target_pairs={{0,24},{4,28},{8,0},{12,4},{16,8},{20,12},{24,16},{28,20},{1,25},{... | collective-permute-start | bytes 786440 | tf_op jit(solution)/shard_map/ppermute | solution.py:76
  433.1 88.0 %collective-permute-start.78 = (bf16[512,256]{1,0:T(8,128)(2,1)}, bf16[512,256]{1,0:T(8,128)(2,1)}, u32[]{:S(2)}, u32[]{:S(2)}) collective-permute-start(bf16[512,256]{1,0:T(8,128)(2,1)} %pad_maximum_fusion.13), channel_id=1, source_target_pairs={{0,8},{4,12},{8,16},{12,20},{16,24},{20,28},{24,0},{28,4},{1,9},{5... | collective-permute-start | bytes 786440 | tf_op jit(solution)/shard_map/ppermute | solution.py:76
  442.0 80.0 %collective-permute-start.71 = (bf16[3,256,512]{1,2,0:T(8,128)(2,1)}, bf16[3,256,512]{1,2,0:T(8,128)(2,1)S(1)}, u32[]{:S(2)}, u32[]{:S(2)}) collective-permute-start(bf16[3,256,512]{1,2,0:T(8,128)(2,1)} %pad_maximum_fusion.10), channel_id=1, source_target_pairs={{0,24},{4,28},{8,0},{12,4},{16,8},{20,12},{24,16},{28,20},{1,25},{... | collective-permute-start | bytes 2359304 | tf_op jit(solution)/shard_map/ppermute | solution.py:76
  450.3 30.6 %collective-permute-start.87 = (bf16[2048,128]{0,1:T(8,128)(2,1)}, bf16[2048,128]{0,1:T(8,128)(2,1)S(1)}, u32[]{:S(2)}, u32[]{:S(2)}) collective-permute-start(bf16[2048,128]{0,1:T(8,128)(2,1)} %get-tuple-element.71), channel_id=1, source_target_pairs={{0,8},{4,12},{8,16},{12,20},{16,24},{20,28},{24,0},{28,4},{1,9},{5... | collective-permute-start | bytes 1572872 | tf_op jit(solution)/shard_map/ppermute | solution.py:76
  454.2 35.5 %collective-permute-start.89 = (bf16[2048,128]{0,1:T(8,128)(2,1)S(1)}, bf16[2048,128]{0,1:T(8,128)(2,1)S(1)}, u32[]{:S(2)}, u32[]{:S(2)}) collective-permute-start(bf16[2048,128]{0,1:T(8,128)(2,1)S(1)} %get-tuple-element.72), channel_id=1, source_target_pairs={{0,24},{4,28},{8,0},{12,4},{16,8},{20,12},{24,16},{28,20},{1,25},{... | collective-permute-start | bytes 1572872 | tf_op jit(solution)/shard_map/ppermute | solution.py:76
  503.4 28.1 %collective-permute-start.69 = (bf16[3,256,512]{1,2,0:T(8,128)(2,1)S(1)}, bf16[3,256,512]{1,2,0:T(8,128)(2,1)S(1)}, u32[]{:S(2)}, u32[]{:S(2)}) collective-permute-start(bf16[3,256,512]{1,2,0:T(8,128)(2,1)S(1)} %copy-done.32), channel_id=1, source_target_pairs={{0,8},{4,12},{8,16},{12,20},{16,24},{20,28},{24,0},{28,4},{1,9},{5... | collective-permute-start | bytes 2359304 | tf_op jit(solution)/shard_map/ppermute | solution.py:76
  514.3 42.2 %collective-permute-start.90 = (bf16[2048,256]{0,1:T(8,128)(2,1)S(1)}, bf16[2048,256]{0,1:T(8,128)(2,1)}, u32[]{:S(2)}, u32[]{:S(2)}) collective-permute-start(bf16[2048,256]{0,1:T(8,128)(2,1)S(1)} %pad_maximum_fusion.7), channel_id=1, source_target_pairs={{0,24},{4,28},{8,0},{12,4},{16,8},{20,12},{24,16},{28,20},{1,25},{... | collective-permute-start | bytes 3145736 | tf_op jit(solution)/shard_map/ppermute | solution.py:76
  516.7 59.9 %collective-permute-start.88 = (bf16[2048,256]{0,1:T(8,128)(2,1)}, bf16[2048,256]{0,1:T(8,128)(2,1)}, u32[]{:S(2)}, u32[]{:S(2)}) collective-permute-start(bf16[2048,256]{0,1:T(8,128)(2,1)} %pad_maximum_fusion.6), channel_id=1, source_target_pairs={{0,8},{4,12},{8,16},{12,20},{16,24},{20,28},{24,0},{28,4},{1,9},{5... | collective-permute-start | bytes 3145736 | tf_op jit(solution)/shard_map/ppermute | solution.py:76
  521.0 78.2 %collective-permute-start.85 = (bf16[256,2048]{1,0:T(8,128)(2,1)}, bf16[256,2048]{1,0:T(8,128)(2,1)}, u32[]{:S(2)}, u32[]{:S(2)}) collective-permute-start(bf16[256,2048]{1,0:T(8,128)(2,1)} %pad_maximum_fusion.5), channel_id=1, source_target_pairs={{0,24},{4,28},{8,0},{12,4},{16,8},{20,12},{24,16},{28,20},{1,25},{... | collective-permute-start | bytes 3145736 | tf_op jit(solution)/shard_map/ppermute | solution.py:76
  522.0 97.8 %collective-permute-start.83 = (bf16[256,2048]{1,0:T(8,128)(2,1)}, bf16[256,2048]{1,0:T(8,128)(2,1)}, u32[]{:S(2)}, u32[]{:S(2)}) collective-permute-start(bf16[256,2048]{1,0:T(8,128)(2,1)} %pad_maximum_fusion.4), channel_id=1, source_target_pairs={{0,8},{4,12},{8,16},{12,20},{16,24},{20,28},{24,0},{28,4},{1,9},{5... | collective-permute-start | bytes 3145736 | tf_op jit(solution)/shard_map/ppermute | solution.py:76
  (132 other events, 1692.6 us)

commit v2 on v1

v2 whole, which is shorter than its diff:
```python
import functools

import jax
import jax.numpy as jnp
from jax import lax
from jax.experimental import pallas as pl
from jax.experimental.pallas import tpu as pltpu
from jax.sharding import PartitionSpec as P

DH = 128
EPSILON = 1e-05
NEGATIVE = -1e30
SCALE = DH ** (-0.5)
F32 = jnp.float32
BF16 = jnp.bfloat16
TILE = 256
ANY = pl.BlockSpec(memory_space=pl.ANY)
VMEM = pl.BlockSpec(memory_space=pltpu.VMEM)
SMEM = pl.BlockSpec(memory_space=pltpu.SMEM)


def nn(left, right):
    return lax.dot_general(left, right, (((1,), (0,)), ((), ())), preferred_element_type=F32)


def nt(left, right):
    return lax.dot_general(left, right, (((1,), (1,)), ((), ())), preferred_element_type=F32)


def tn(left, right):
    return lax.dot_general(left, right, (((0,), (0,)), ((), ())), preferred_element_type=F32)


def split_rows(values, parts):
    rows = values.shape[0] // parts
    return [values[i * rows : (i + 1) * rows] for i in range(parts)]


def shape(dims, dtype):
    return jax.ShapeDtypeStruct(tuple(dims), dtype)


def call(body, name, in_specs, outs, scratch, flops, args):
    moved = sum(a.size * a.dtype.itemsize for a in args)
    moved += sum(o.size * o.dtype.itemsize for o in outs)
    return pl.pallas_call(
        body,
        name=name,
        out_shape=outs,
        in_specs=in_specs,
        out_specs=[VMEM] * len(outs),
        scratch_shapes=scratch,
        cost_estimate=pl.CostEstimate(flops=flops, bytes_accessed=moved, transcendentals=0),
    )(*args)


class Places:
    def __init__(self, dp, tensor):
        self.dp, self.tensor, self.chips = dp, tensor, dp // 2
        self.rank = lax.axis_index("dp")
        self.part = lax.axis_index("tensor")
        self.chip, self.core = self.rank // 2, self.rank % 2
        chips = self.chips
        self.plus = [(i, (i // 2 + 1) % chips * 2 + i % 2) for i in range(dp)]
        self.minus = [(i, (i // 2 - 1) % chips * 2 + i % 2) for i in range(dp)]
        self.swap = [(i, i ^ 1) for i in range(dp)]

    def owner(self, place):
        other, hops = place // self.chips, place % self.chips
        return (self.chip + hops) % self.chips * 2 + (self.core ^ other)

    def table(self):
        blocks = self.owner(jnp.arange(self.dp, dtype=jnp.int32))
        chunks = self.part ^ jnp.arange(self.tensor, dtype=jnp.int32)
        return jnp.concatenate([blocks, chunks]).astype(jnp.int32)

    def tokens_in(self, values):
        size = values.shape[0] // self.tensor
        return jnp.take(
            values.reshape(self.tensor, size),
            self.part ^ jnp.arange(self.tensor, dtype=jnp.int32),
            axis=0,
        ).reshape(-1)

    def send(self, values, pairs):
        return lax.ppermute(values, "dp", pairs)

    def to_peer(self, values, k):
        return lax.ppermute(values, "tensor", [(i, i ^ k) for i in range(self.tensor)])

    def to_peers(self, values):
        many = isinstance(values, (list, tuple))
        return [
            self.to_peer(values[k - 1] if many else values, k)
            for k in range(self.tensor - 1, 0, -1)
        ][::-1]

    def first_hop(self, block):
        return self.send(block, self.plus), self.send(block, self.minus)

    def later_hops(self, block, hop):
        half = self.chips // 2
        pieces = {0: [block]}
        behind, ahead = hop
        for step in range(1, half):
            if step > 1:
                behind, ahead = self.send(behind, self.plus), self.send(ahead, self.minus)
            pieces[self.chips - step], pieces[step] = [behind], [ahead]
        axis = block.ndim - 2
        rows = block.shape[axis] // 2
        low = lax.slice_in_dim(behind, 0, rows, axis=axis)
        high = lax.slice_in_dim(ahead, rows, 2 * rows, axis=axis)
        pieces[half] = [self.send(low, self.plus), self.send(high, self.minus)]
        return [piece for hops in range(self.chips) for piece in pieces[hops]]

    def both_cores(self, pieces):
        return pieces + [self.send(piece, self.swap) for piece in pieces]

    def sum_small(self, values, over_tensor):
        if over_tensor:
            values = values + sum(self.to_peer(values, k) for k in range(1, self.tensor))
        values = values + self.send(values, self.swap)
        total = values
        for hops in range(1, self.chips):
            total = total + self.send(
                values, [(i, (i // 2 + hops) % self.chips * 2 + i % 2) for i in range(self.dp)]
            )
        return total


def piece_places(chips, size, parts):
    places = []
    rows = size // parts
    for part in range(parts):
        mine = []
        for hops in range(chips):
            start = part * rows
            if hops == chips // 2:
                mine += [(hops, start, rows // 2), (hops, start + rows // 2, rows // 2)]
            else:
                mine += [(hops, start, rows)]
        places += mine + [(chips + block, start, height) for block, start, height in mine]
    return places


def by_block(places):
    return [
        [p for p, place in enumerate(places) if place[0] == block]
        for block in range(1 + max(place[0] for place in places))
    ]


def after(values, *events):
    values, _ = lax.optimization_barrier((values, events))
    return values


def center_of(values):
    center = values - jnp.mean(values, axis=-1, keepdims=True)
    inverse = lax.rsqrt(jnp.mean(center * center, axis=-1, keepdims=True) + EPSILON)
    return center * inverse, inverse


def norm_back(norm_grad, normed, inverse, gain):
    scaled = norm_grad * gain
    return inverse * (
        scaled
        - jnp.mean(scaled, axis=-1, keepdims=True)
        - normed * jnp.mean(scaled * normed, axis=-1, keepdims=True)
    )


def prologue_body(dp, tensor, table, x, g, vec, x_rel, g_rel, low, vec_rel):
    width, rows = x.shape[1] // dp, x.shape[0] // tensor
    for j in range(dp):
        cols = pl.ds(pl.multiple_of(table[j] * width, width), width)
        here = slice(j * width, (j + 1) * width)
        vec_rel[:, here] = vec[:, cols]
        for k in range(tensor):
            start = pl.ds(pl.multiple_of(table[dp + k] * rows, rows), rows)
            there = slice(k * rows, (k + 1) * rows)
            x_rel[there, here] = x[start, cols]
            g_rel[there, here] = g[start, cols]
    for k in range(tensor):
        there = slice(k * rows, (k + 1) * rows)
        normed, _ = center_of(x_rel[there, :].astype(F32))
        low[there, :] = (normed * vec_rel[0:1, :] + vec_rel[1:2, :]).astype(BF16)


def attend_body(places, x, q_bias, v_bias, allowed, *refs):
    count = len(places)
    pieces, (q, k, v, probs, mixed), (weight, sems) = refs[:count], refs[count:-2], refs[-2:]
    size = block_rows(places)

    def copy(j, p):
        block, start, rows = places[p]
        return pltpu.make_async_copy(
            pieces[p].at[j], weight.at[j, pl.ds(block * size + start, rows)], sems.at[j, p]
        )

    for j in range(3):
        for p in range(count):
            copy(j, p).start()
    columns = q.shape[1]
    tile = min(TILE, columns)
    for j, out in enumerate((q, k, v)):
        for p in range(count):
            copy(j, p).wait()
        for start in range(0, columns, tile):
            cols = slice(start, start + tile)
            total = nn(x[...], weight[j, :, cols])
            if j == 0:
                total = total + q_bias[:, cols].astype(F32)
            if j == 2:
                total = total + v_bias[:, cols].astype(F32)
            out[:, cols] = total.astype(BF16)
    for h in range(columns // DH):
        cols = slice(h * DH, (h + 1) * DH)
        scores = jnp.where(allowed[...] > 0, nt(q[:, cols], k[:, cols]) * SCALE, NEGATIVE)
        weights = jnp.exp(scores - jnp.max(scores, axis=-1, keepdims=True))
        prob = weights / jnp.sum(weights, axis=-1, keepdims=True)
        probs[h] = prob
        mixed[:, cols] = nn(prob.astype(BF16), v[:, cols]).astype(BF16)


def put_chunks(total, cols, own, sends):
    rows = own.shape[0]
    own[:, cols] = total[:rows]
    for k, ref in enumerate(sends):
        ref[:, cols] = total[(k + 1) * rows : (k + 2) * rows].astype(BF16)


def block_rows(places):
    return max(start + rows for _, start, rows in places)


def column_copies(places, pieces, weight, sems):
    width = pieces[0].shape[1]
    return [
        pltpu.make_async_copy(
            pieces[p],
            weight.at[pl.ds(start, rows), pl.ds(block * width, width)],
            sems.at[p],
        )
        for p, (block, start, rows) in enumerate(places)
    ]


def row_copies(places, pieces, weight, sems):
    size = block_rows(places)
    return [
        pltpu.make_async_copy(
            pieces[p], weight.at[pl.ds(block * size + start, rows)], sems.at[p]
        )
        for p, (block, start, rows) in enumerate(places)
    ]


def start_all(places, copies):
    for group in by_block(places):
        for p in group:
            copies[p].start()


def project_body(places, left, *refs):
    count = len(places)
    pieces, (own, *sends), (weight, sems) = refs[:count], refs[count:-2], refs[-2:]
    copies = column_copies(places, pieces, weight, sems)
    start_all(places, copies)
    width = pieces[0].shape[1]
    for block, group in enumerate(by_block(places)):
        for p in group:
            copies[p].wait()
        cols = slice(block * width, (block + 1) * width)
        put_chunks(nn(left[...], weight[:, cols]), cols, own, sends)


def second_body(tensor, own, x_rel, vec, *refs):
    received, (hidden, normed_out, inverse_out, low) = refs[: tensor - 1], refs[tensor - 1 :]
    rows = own.shape[0]
    total = own[...]
    for ref in received:
        total = total + ref[...].astype(F32)
    value = x_rel[0:rows, :].astype(F32) + total + vec[2:3, :]
    hidden[...] = value
    normed, inverse = center_of(value)
    normed_out[...] = normed
    inverse_out[...] = jnp.broadcast_to(inverse, inverse_out.shape)
    low[...] = (normed * vec[3:4, :] + vec[4:5, :]).astype(BF16)


def upper_body(places, tensor, bias, *refs):
    chunks, refs = refs[:tensor], refs[tensor:]
    count = len(places)
    pieces, (low, activated, slope), (weight, sems) = refs[:count], refs[count:-2], refs[-2:]
    copies = row_copies(places, pieces, weight, sems)
    for copy in copies:
        copy.start()
    rows = chunks[0].shape[0]
    for k, chunk in enumerate(chunks):
        low[k * rows : (k + 1) * rows, :] = chunk[...]
    for copy in copies:
        copy.wait()
    columns = weight.shape[1]
    tile = min(TILE, columns)

    @pl.loop(0, columns // tile)
    def _(i):
        cols = pl.ds(pl.multiple_of(i * tile, tile), tile)
        value = nn(low[...], weight[:, cols]) + bias[:, cols].astype(F32)
        below = 0.5 * (1.0 + lax.erf(value * (0.5**0.5)))
        activated[:, cols] = (value * below).astype(BF16)
        density = jnp.exp(-0.5 * value * value) * 0.3989422804014327
        slope[:, cols] = below + value * density


def upper_grad_body(places, g, slope, *refs):
    count = len(places)
    pieces, (low, bias_grad), (weight, sems) = refs[:count], refs[count:-2], refs[-2:]
    copies = column_copies(places, pieces, weight, sems)
    for copy in copies:
        copy.start()
    for copy in copies:
        copy.wait()
    hidden = weight.shape[0]
    tile = min(TILE, hidden)

    @pl.loop(0, hidden // tile)
    def _(i):
        cols = pl.ds(pl.multiple_of(i * tile, tile), tile)
        grad = nt(g[...], weight[cols, :]) * slope[:, cols]
        low[:, cols] = grad.astype(BF16)
        bias_grad[:, cols] = jnp.sum(grad, axis=0, keepdims=True)


def second_part_body(places, left, *refs):
    count = len(places)
    pieces, (own, *sends), (weight, sems) = refs[:count], refs[count:-2], refs[-2:]
    copies = row_copies(places, pieces, weight, sems)
    start_all(places, copies)
    size = block_rows(places)
    for block, group in enumerate(by_block(places)):
        for p in group:
            copies[p].wait()
        cols = slice(block * size, (block + 1) * size)
        put_chunks(nt(left[...], weight[cols, :]), cols, own, sends)


def put_features(table, dp, out, rows, values):
    width = out.shape[1] // dp
    for j in range(dp):
        cols = pl.ds(pl.multiple_of(table[j] * width, width), width)
        out[rows, cols] = values[:, j * width : (j + 1) * width]


def second_back_body(dp, tensor, table, own, g_rel, vec, normed, inverse, *refs):
    received, (hidden_grad, low, sums) = refs[: tensor - 1], refs[tensor - 1 :]
    rows = own.shape[0]
    total = own[...]
    for ref in received:
        total = total + ref[...].astype(F32)
    upstream = g_rel[0:rows, :].astype(F32)
    grad = upstream + norm_back(total, normed[...], inverse[:, 0:1], vec[3:4, :])
    hidden_grad[...] = grad
    low[...] = grad.astype(BF16)
    for i, values in enumerate((grad, total * normed[...], total, upstream)):
        put_features(
            table, dp, sums, slice(i, i + 1), jnp.sum(values, axis=0, keepdims=True)
        )


def attend_back_body(in_places, out_places, tensor, q, k, v, probs, *refs):
    chunks, refs = refs[:tensor], refs[tensor:]
    outs_p, refs = refs[: len(out_places)], refs[len(out_places) :]
    ins_p, refs = refs[: len(in_places)], refs[len(in_places) :]
    (low, q_low, k_low, v_low, bias_grad, own, *sends) = refs[:-5]
    out_weight, in_weight, mixed_grad, out_sems, in_sems = refs[-5:]
    copies = column_copies(out_places, outs_p, out_weight, out_sems)
    for copy in copies:
        copy.start()
    size = block_rows(in_places)
    ins = [
        pltpu.make_async_copy(
            ins_p[p], in_weight.at[:, pl.ds(block * size + start, rows)], in_sems.at[p]
        )
        for p, (block, start, rows) in enumerate(in_places)
    ]
    start_all(in_places, ins)
    rows = chunks[0].shape[0]
    for j, chunk in enumerate(chunks):
        low[j * rows : (j + 1) * rows, :] = chunk[...]
    for copy in copies:
        copy.wait()
    columns = q.shape[1]
    tile = min(TILE, columns)
    for start in range(0, columns, tile):
        cols = slice(start, start + tile)
        mixed_grad[:, cols] = nt(low[...], out_weight[cols, :]).astype(BF16)
    for h in range(columns // DH):
        cols = slice(h * DH, (h + 1) * DH)
        there = slice(columns + h * DH, columns + (h + 1) * DH)
        prob, down = probs[h], mixed_grad[:, cols]
        prob_grad = nt(down, v[:, cols])
        inner = jnp.sum(prob * prob_grad, axis=-1, keepdims=True)
        score_low = (prob * (prob_grad - inner) * SCALE).astype(BF16)
        query_grad = nn(score_low, k[:, cols])
        q_low[:, cols] = query_grad.astype(BF16)
        bias_grad[:, cols] = jnp.sum(query_grad, axis=0, keepdims=True)
        k_low[:, cols] = tn(score_low, q[:, cols]).astype(BF16)
        value_grad = tn(prob.astype(BF16), down)
        v_low[:, cols] = value_grad.astype(BF16)
        bias_grad[:, there] = jnp.sum(value_grad, axis=0, keepdims=True)
    for block, group in enumerate(by_block(in_places)):
        for p in group:
            ins[p].wait()
        cols = slice(block * size, (block + 1) * size)
        total = nt(q_low[...], in_weight[0, cols, :])
        total = total + nt(k_low[...], in_weight[1, cols, :])
        total = total + nt(v_low[...], in_weight[2, cols, :])
        put_chunks(total, cols, own, sends)


def first_back_body(dp, tensor, table, own, x_rel, vec, hidden_grad, *refs):
    received, (result, sums) = refs[: tensor - 1], refs[tensor - 1 :]
    rows = own.shape[0]
    total = own[...]
    for ref in received:
        total = total + ref[...].astype(F32)
    normed, inverse = center_of(x_rel[0:rows, :].astype(F32))
    grad = hidden_grad[...] + norm_back(total, normed, inverse, vec[0:1, :])
    put_features(table, dp, result, slice(0, rows), grad.astype(BF16))
    for i, values in enumerate((total * normed, total)):
        put_features(
            table, dp, sums, slice(i, i + 1), jnp.sum(values, axis=0, keepdims=True)
        )


def output_body(dp, tensor, table, own, hidden, vec, *refs):
    received, (result,) = refs[: tensor - 1], refs[tensor - 1 :]
    total = own[...]
    for ref in received:
        total = total + ref[...].astype(F32)
    value = hidden[...] + total + vec[5:6, :]
    put_features(table, dp, result, slice(0, own.shape[0]), value.astype(BF16))


def assemble_body(dp, tensor, table, *refs):
    chunks, (result,) = refs[:tensor], refs[tensor:]
    rows = chunks[0].shape[0]
    for k, chunk in enumerate(chunks):
        result[pl.ds(pl.multiple_of(table[dp + k] * rows, rows), rows), :] = chunk[...]


def grad_blocks(left, right, by_rows, first, chips, size, put):
    if by_rows:
        columns = sum(r.shape[1] for r in right)
        width = right[0].shape[1]
        tile = min(TILE, width)
        for block in range(chips):
            start = (first + block) * size
            turned = left[:, start : start + size].T
            for j, ref in enumerate(right):
                for c in range(0, width, tile):
                    put(block, 0, size, j * width + c, nn(turned, ref[:, c : c + tile]))
        del columns
    else:
        hidden = left.shape[1]
        step = min(512, hidden // 2)
        for r in range(0, hidden, step):
            turned = left[:, r : r + step].T
            for block in range(chips):
                start = (first + block) * size
                put(block, r, r + step, 0, nn(turned, right[0][:, start : start + size]))


def grad_far_body(by_rows, chips, size, count, left, *refs):
    right, out = refs[:count], refs[count]
    height = out.shape[0] // chips

    def put(block, low, high, column, value):
        out[block * height + low : block * height + high, column : column + value.shape[1]] = (
            value.astype(BF16)
        )

    grad_blocks(left, right, by_rows, chips, chips, size, put)


def half_plan(chips):
    h = chips // 2
    plan, keeps = {(0, 0): ("own", 0), (0, 1): ("own", 1)}, []
    plan[(h, 0)], plan[(h, 1)] = ("plus", 0), ("minus", 0)
    if h > 1:
        plan[(h - 1, 1)], plan[(chips - h + 1, 0)] = ("plus", 1), ("minus", 1)
    for key in [(b, s) for b in range(chips) for s in range(2)]:
        if key not in plan:
            plan[key] = (len(keeps), None)
            keeps.append(key)
    return plan, keeps


def grad_near_body(by_rows, chips, size, count, left, theirs, *refs):
    right, (own, plus, minus, *keeps) = refs[:count], refs[count:]
    plan, _ = half_plan(chips)
    height = own.shape[0]
    middle = height // 2

    def put(block, low, high, column, value):
        cols = slice(column, column + value.shape[1])
        value = value + theirs[block * height + low : block * height + high, cols].astype(F32)
        for half in range(2):
            start, stop = max(low, half * middle), min(high, (half + 1) * middle)
            if start >= stop:
                continue
            part = value[start - low : stop - low]
            name, place = plan[(block, half)]
            ref = {"own": own, "plus": plus, "minus": minus}.get(name)
            ref = keeps[name] if ref is None else ref
            base = (place or 0) * middle - half * middle
            ref[start + base : stop + base, cols] = part.astype(ref.dtype)

    grad_blocks(left, right, by_rows, 0, chips, size, put)


def finish_body(planes, own, low_a, low_b, high_a, high_b, out):
    half = own.shape[0] // 2
    for s, parts in enumerate(((low_a, low_b), (high_a, high_b))):
        rows = slice(s * half, (s + 1) * half)
        total = own[rows, :]
        for ref, start in parts:
            total = total + ref[start : start + half, :].astype(F32)
        if planes == 1:
            out[rows, :] = total
        else:
            width = own.shape[1] // planes
            for j in range(planes):
                out[j, rows, :] = total[:, j * width : (j + 1) * width]


def sems(*dims):
    return pltpu.SemaphoreType.DMA(tuple(dims))


class Layer:
    def __init__(self, at, length, features):
        self.at = at
        self.length, self.features = length, features
        self.own = length // at.tensor

    def chunk_outs(self):
        return [shape((self.own, self.features), F32)] + [
            shape((self.own, self.features), BF16)
        ] * (self.at.tensor - 1)

    def project(self, name, left, pieces, places, by_rows):
        inner = left.shape[1]
        weight = (self.features, inner) if by_rows else (inner, self.features)
        body = second_part_body if by_rows else project_body
        return call(
            functools.partial(body, places),
            name,
            [VMEM] + [ANY] * len(places),
            self.chunk_outs(),
            [pltpu.VMEM(weight, BF16), sems(len(places))],
            2 * self.length * inner * self.features,
            [left] + list(pieces),
        )

    def swapped(self, far):
        return self.at.send(far, self.at.swap)

    def grad_far(self, name, left, right, by_rows):
        at = self.at
        size = self.features // at.dp
        height = size if by_rows else left.shape[1]
        width = sum(r.shape[1] for r in right) if by_rows else size
        return call(
            functools.partial(grad_far_body, by_rows, at.chips, size, len(right)),
            name + "_far",
            [VMEM] * (1 + len(right)),
            [shape((at.chips * height, width), BF16)],
            [],
            2 * self.length * at.chips * height * width,
            [left] + list(right),
        )[0]

    def grad_near(self, name, left, right, by_rows, theirs):
        at = self.at
        size = self.features // at.dp
        height = size if by_rows else left.shape[1]
        width = sum(r.shape[1] for r in right) if by_rows else size
        _, keeps = half_plan(at.chips)
        return call(
            functools.partial(grad_near_body, by_rows, at.chips, size, len(right)),
            name + "_near",
            [VMEM] * (2 + len(right)),
            [shape((height, width), F32)]
            + [shape((height, width), BF16)] * 2
            + [shape((height // 2, width), F32)] * len(keeps),
            [],
            2 * self.length * at.chips * height * width,
            [left, theirs] + list(right),
        )

    def ring_start(self, blocks):
        own, plus, minus, *keeps = blocks
        at = self.at
        return blocks, (at.send(plus, at.plus), at.send(minus, at.minus))

    def ring_rest(self, ring):
        at = self.at
        (own, _, _, *keeps), (from_behind, from_ahead) = ring
        _, order = half_plan(at.chips)
        kept = dict(zip(order, keeps))
        h, n = at.chips // 2, at.chips
        middle = own.shape[0] // 2
        last_b = (from_behind, middle), (from_ahead, middle)
        for step in range(2, h + 1):
            d, e = h - step + 1, h - step
            up = [kept[(d, 0)] + from_behind[:middle].astype(F32)]
            down = [kept[(n - d, 1)] + from_ahead[:middle].astype(F32)]
            if e >= 1:
                up.append(kept[(e, 1)] + from_behind[middle:].astype(F32))
                down.append(kept[(n - e, 0)] + from_ahead[middle:].astype(F32))
            up = up[0] if len(up) == 1 else jnp.concatenate(up, 0)
            down = down[0] if len(down) == 1 else jnp.concatenate(down, 0)
            if e == 0:
                last_b = (from_behind, middle), (from_ahead, middle)
            from_behind = at.send(up.astype(BF16), at.plus)
            from_ahead = at.send(down.astype(BF16), at.minus)
        return own, (from_behind, last_b[1][0]), (last_b[0][0], from_ahead)

    def grad_finish(self, name, ring, planes):
        own, low, high = ring
        out = own.shape if planes == 1 else (planes, own.shape[0], own.shape[1] // planes)
        middle = own.shape[0] // 2
        refs = [low[0], low[1], high[0], high[1]]
        starts = [0, middle, middle, 0]

        def body(own_ref, a, b, c, d, out_ref):
            finish_body(
                planes,
                own_ref,
                (a, starts[0]),
                (b, starts[1]),
                (c, starts[2]),
                (d, starts[3]),
                out_ref,
            )

        return call(
            body,
            name + "_finish",
            [VMEM] * 5,
            [shape(out, F32)],
            [],
            4 * own.size,
            [own] + refs,
        )[0]


def shards(
    dp,
    tensor,
    inputs,
    segment_ids,
    first_gain,
    first_shift,
    project_in,
    query_bias,
    value_bias,
    project_out,
    out_bias,
    second_gain,
    second_shift,
    up_weight,
    up_bias,
    down_weight,
    down_bias,
    cotangent,
):
    at = Places(dp, tensor)
    length, features = inputs.shape
    heads = query_bias.shape[0]
    hidden_units = up_bias.shape[0]
    layer = Layer(at, length, features)
    own = layer.own
    table = at.table()
    chunk32, chunk16 = shape((own, features), F32), shape((own, features), BF16)
    tokens16 = shape((length, features), BF16)
    size = features // dp
    in_places = piece_places(at.chips, size, 1)
    out_places = piece_places(at.chips, heads, 1)
    up_places = piece_places(at.chips, size, 2)
    down_places = piece_places(at.chips, hidden_units, 2)

    hop_in = at.first_hop(project_in)
    vectors = jnp.stack(
        [
            first_gain,
            first_shift,
            out_bias,
            second_gain,
            second_shift,
            down_bias,
            down_bias,
            down_bias,
        ]
    ).astype(F32)
    x_rel, g_rel, first_low, vec = call(
        functools.partial(prologue_body, dp, tensor),
        "prologue",
        [SMEM] + [VMEM] * 3,
        [tokens16] * 3 + [shape(vectors.shape, F32)],
        [],
        20 * length * features,
        [table, inputs, cotangent, vectors],
    )
    ids = at.tokens_in(segment_ids)
    order = at.tokens_in(jnp.arange(length, dtype=jnp.int32))
    allowed = (
        (ids[:, None] == ids[None, :])
        & (ids[:, None] != 0)
        & (order[None, :] <= order[:, None])
    )
    allowed = (allowed | (order[None, :] == order[:, None])).astype(F32)
    biases = (query_bias[None], value_bias[None], up_bias[None])

    hop_in = after(hop_in, first_low, allowed, biases)
    mine_in = at.later_hops(project_in, hop_in)
    hop_out = at.first_hop(after(project_out, hop_in))
    up_parts, down_parts = split_rows(up_weight, 2), split_rows(down_weight, 2)
    hop_up = [at.first_hop(after(up_parts[0], mine_in))]
    mine_out = at.later_hops(project_out, hop_out)
    all_in = at.both_cores(mine_in)

    low_heads = shape((length, heads), BF16)
    query, key, value, probs, mixed = call(
        functools.partial(attend_body, in_places),
        "attend",
        [VMEM] * 4 + [ANY] * len(in_places),
        [low_heads] * 3 + [shape((heads // DH, length, length), F32), low_heads],
        [pltpu.VMEM((3, features, heads), BF16), sems(3, len(in_places))],
        6 * length * heads * features,
        [after(first_low, hop_out), biases[0], biases[1], allowed] + all_in,
    )
    all_out = at.both_cores(mine_out)
    mixed = after(mixed, hop_up[0])
    mine_up = [at.later_hops(up_parts[0], hop_up[0])]
    hop_up += [at.first_hop(after(up_parts[1], hop_up[0]))]
    part = layer.project("project_out", mixed, all_out, out_places, False)
    received = at.to_peers(part[1:])
    hidden, normed_two, inverse_two, second_own = call(
        functools.partial(second_body, tensor),
        "second_norm",
        [VMEM] * (2 + tensor),
        [chunk32, chunk32, shape((own, 128), F32), chunk16],
        [],
        20 * own * features,
        [after(part[0], mine_up[0], hop_up[1]), x_rel, vec] + received,
    )
    mine_up += [at.later_hops(up_parts[1], hop_up[1])]
    hop_down = [at.first_hop(after(down_parts[0], hop_up[1]))]
    all_up = at.both_cores(mine_up[0]) + at.both_cores(mine_up[1])
    second_low, activated, slope = call(
        functools.partial(upper_body, up_places, tensor),
        "upper",
        [VMEM] * (1 + tensor) + [ANY] * len(up_places),
        [
            tokens16,
            shape((length, hidden_units), BF16),
            shape((length, hidden_units), F32),
        ],
        [pltpu.VMEM((features, hidden_units), BF16), sems(len(up_places))],
        2 * length * features * hidden_units,
        [after(biases[2], hop_down[0]), second_own] + at.to_peers(second_own) + all_up,
    )
    mine_down = [at.later_hops(down_parts[0], hop_down[0])]
    hop_down += [at.first_hop(after(down_parts[1], hop_down[0]))]
    far_down = layer.grad_far(
        "grad_down", after(activated, mine_down[0], hop_down[1]), [g_rel], False
    )
    mine_down += [at.later_hops(down_parts[1], hop_down[1])]
    all_down = at.both_cores(mine_down[0]) + at.both_cores(mine_down[1])
    near_down = layer.grad_near(
        "grad_down", after(activated, far_down), [g_rel], False, layer.swapped(far_down)
    )
    upper_low, up_bias_grad = call(
        functools.partial(upper_grad_body, down_places),
        "upper_grad",
        [VMEM] * 2 + [ANY] * len(down_places),
        [shape((length, hidden_units), BF16), shape((1, hidden_units), F32)],
        [pltpu.VMEM((hidden_units, features), BF16), sems(len(down_places))],
        2 * length * features * hidden_units,
        [after(g_rel, near_down), slope] + all_down,
    )
    ring_down = layer.ring_start(near_down)
    part = layer.project("second_part", upper_low, all_up, up_places, True)
    received = at.to_peers(part[1:])
    far_up = layer.grad_far("grad_up", second_low, after([upper_low], part), True)
    feed = layer.project("feed", after(activated, far_up), all_down, down_places, False)
    hidden_grad, hidden_low_own, sums_two = call(
        functools.partial(second_back_body, dp, tensor),
        "second_back",
        [SMEM] + [VMEM] * (4 + tensor),
        [chunk32, chunk16, shape((8, features), F32)],
        [],
        20 * own * features,
        [table, after(part[0], ring_down[1], feed), g_rel, vec, normed_two, inverse_two] + received,
    )
    ring_down = layer.ring_rest(ring_down)
    hidden_pieces = at.to_peers(hidden_low_own)
    near_up = layer.grad_near(
        "grad_up", second_low, after([upper_low], hidden_low_own), True, layer.swapped(far_up)
    )
    back = call(
        functools.partial(attend_back_body, in_places, out_places, tensor),
        "attend_back",
        [VMEM] * (4 + tensor) + [ANY] * (len(out_places) + len(in_places)),
        [tokens16, low_heads, low_heads, low_heads, shape((1, 2 * heads), F32)]
        + layer.chunk_outs(),
        [
            pltpu.VMEM((heads, features), BF16),
            pltpu.VMEM((3, features, heads), BF16),
            pltpu.VMEM((length, heads), BF16),
            sems(len(out_places)),
            sems(len(in_places)),
        ],
        8 * length * heads * features,
        [after(query, ring_down[1:], near_up), key, value, probs, hidden_low_own]
        + hidden_pieces
        + all_out
        + all_in,
    )
    hidden_low, q_low, k_low, v_low, heads_grad, *part = back
    ring_up = layer.ring_start(after(near_up, ring_down[1:]))
    feed_received = at.to_peers(after(feed[1:], hidden_pieces))
    outputs_own = call(
        functools.partial(output_body, dp, tensor),
        "outputs_own",
        [SMEM] + [VMEM] * (2 + tensor),
        [chunk16],
        [],
        4 * own * features,
        [table, after(feed[0], part), hidden, vec] + feed_received,
    )[0]
    received = at.to_peers(after(part[1:], feed_received))
    lows = [q_low, k_low, v_low]
    far_in = layer.grad_far("grad_in", first_low, after(lows, part), True)
    far_out = layer.grad_far("grad_out", mixed, after([hidden_low], far_in), False)
    near_in = layer.grad_near(
        "grad_in", first_low, after(lows, far_out), True, layer.swapped(far_in)
    )
    near_out = layer.grad_near(
        "grad_out", mixed, after([hidden_low], near_in), False, layer.swapped(far_out)
    )
    input_own, sums_one = call(
        functools.partial(first_back_body, dp, tensor),
        "first_back",
        [SMEM] + [VMEM] * (3 + tensor),
        [chunk16, shape((8, features), F32)],
        [],
        20 * own * features,
        [table, after(part[0], ring_up[1], near_out), x_rel, vec, hidden_grad] + received,
    )
    ring_in = layer.ring_start(after(near_in, ring_up[1]))
    ring_out = layer.ring_start(after(near_out, ring_up[1]))
    ring_up = layer.ring_rest(ring_up)

    def assemble(name, chunk, others):
        return call(
            functools.partial(assemble_body, dp, tensor),
            name,
            [SMEM] + [VMEM] * tensor,
            [tokens16],
            [],
            length * features,
            [table, chunk] + others,
        )[0]

    input_others = at.to_peers(input_own)
    output_others = at.to_peers(after(outputs_own, input_others))
    input_gradient = assemble("input_gradient", input_own, input_others)
    outputs = assemble("outputs", outputs_own, output_others)
    ring_in = layer.ring_rest(ring_in)
    ring_out = layer.ring_rest(ring_out)
    grad_down = layer.grad_finish("grad_down", ring_down, 1)
    grad_up = layer.grad_finish("grad_up", ring_up, 1)
    grad_out = layer.grad_finish("grad_out", ring_out, 1)
    grad_in = layer.grad_finish("grad_in", ring_in, 3)

    wide = at.sum_small(jnp.concatenate([sums_one[:2], sums_two[:4]]), True)
    narrow = at.sum_small(jnp.concatenate([heads_grad[0], up_bias_grad[0]]), False)
    return (
        outputs,
        input_gradient,
        wide[0],
        wide[1],
        grad_in,
        narrow[:heads],
        narrow[heads : 2 * heads],
        grad_out,
        wide[2],
        wide[3],
        wide[4],
        grad_up,
        narrow[2 * heads :],
        grad_down,
        wide[5],
    )


def solution(mesh):
    dp, tensor = mesh.shape["dp"], mesh.shape["tensor"]

    def program(*arguments):
        return shards(dp, tensor, *arguments)

    in_specs = (
        P("dp", None),
        P("dp"),
        P(),
        P(),
        P(None, "dp", "tensor"),
        P("tensor"),
        P("tensor"),
        P("tensor", "dp"),
        P(),
        P(),
        P(),
        P("dp", "tensor"),
        P("tensor"),
        P("tensor", "dp"),
        P(),
        P("dp", None),
    )
    out_specs = (
        P("dp", None),
        P("dp", None),
        P(),
        P(),
        P(None, "dp", "tensor"),
        P("tensor"),
        P("tensor"),
        P("tensor", "dp"),
        P(),
        P(),
        P(),
        P("dp", "tensor"),
        P("tensor"),
        P("tensor", "dp"),
        P(),
    )
    return jax.shard_map(program, mesh=mesh, in_specs=in_specs, out_specs=out_specs, check_vma=False)
```

time: 635 us -> 566 us (0.89)
  Pallas kernels: 0 us -> 136 us
  matrix products: 73.3 us -> 0 us
  waiting for transfers between devices: 341 us -> 281 us
  local copies, waits for them, and re-layouts: 88.4 us -> 28.5 us
  other arithmetic: 31.2 us -> 8.91 us
  starting transfers between devices: 87.6 us -> 98.4 us
    pallas_call x0 -> x26, Pallas kernels: none -> 136 us  [call(): pl.pallas_call(body, name=name, out_shape=outs, in_specs=in_specs, out_sp...]
    dot_general x25 -> x0, matrix products: 70.2 us -> none  [the longest x18 52.1 us: dot(): lax.dot_general(left, right, (dims, ((), ())), preferred_element_type=F32)]
    ppermute x64 -> x82, waiting for transfers between devices: 303 us -> 255 us  [send(): return lax.ppermute(values, 'dp', pairs)]
    unnamed x224 -> x172, local copies, waits for them, and re-layouts: 55 us -> 8.74 us
    ppermute x27, waiting for transfers between devices: 38.2 us -> 26 us  [to_peer(): lax.ppermute(values, 'tensor', [(i, i ^ k) for i in range(self.tensor)])]
    dynamic_update_slice x8 -> x0, local copies, waits for them, and re-layouts: 9.76 us -> none  [tokens_out(): lax.dynamic_update_slice_in_dim(result, piece, (self.part ^ k) * size, 0)]
    add x4 -> x1, other arithmetic: 8.95 us -> 0.01 us  [owner(): return (self.chip + hops) % self.chips * 2 + (self.core ^ other)]
    concatenate x14 -> x3, other arithmetic: 7.1 us -> 0.62 us  [the longest x1 0.6 us: table(): return jnp.concatenate([blocks, chunks]).astype(jnp.int32)]
  transfers between devices with their start and end apart: 91 -> 109, of which waited for: 34 -> 40; matrix products, arithmetic and copies ran while one was open for 27% -> 5% of each run, Pallas kernels for 0% -> 15%
where the time goes in v2:
time: 566 us; the launch traced here: 555 us
  waiting for transfers between devices  281 us (50%)
  Pallas kernels  136 us (24%)
  starting transfers between devices  98.4 us (17%)
  local copies, waits for them, and re-layouts  28.5 us (5%)
  other arithmetic  8.91 us (2%)
    ppermute x82, waiting for transfers between devices, send(): return lax.ppermute(values, 'dp', pairs)  255 us
    pallas_call x26, Pallas kernels, call(): pl.pallas_call(body, name=name, out_shape=outs, in_specs=in_specs, out_sp...  136 us
    ppermute x82, starting transfers between devices, send(): return lax.ppermute(values, 'dp', pairs)  60 us
    ppermute x27, starting transfers between devices, to_peer(): lax.ppermute(values, 'tensor', [(i, i ^ k) for i in range(self.tensor)])  38.4 us
    ppermute x27, waiting for transfers between devices, to_peer(): lax.ppermute(values, 'tensor', [(i, i ^ k) for i in range(self.tensor)])  26 us
  transfers between devices with their start and end apart: 109, of which 40 were waited for; matrix products, arithmetic and copies ran while one was open for 5% of the time, Pallas kernels for 15%

profile of v2, /device:TPU:8, one launch (start us, length us, event | category | flops | bytes accessed | tf_op | source)
XLA Modules:
  0.0 554.5 jit_solution(2029868415798459652)
XLA Ops:
  21.3 16.6 %collective-permute-done.1.refs_1_.refs_15_ = bf16[3,256,512]{2,1,0:T(8,128)(2,1)S(1)} collective-permute-done((bf16[3,256,512]{2,1,0:T(8,128)(2,1)}, bf16[3,256,512]{2,1,0:T(8,128)(2,1)S(1)}, u32[]{:S(2)}, u32[]{:S(2)}) %collective-permute-start.1) | collective-permute-done | bytes 786464 | tf_op jit(solution)/shard_map/ppermute | solution.py:86
  47.1 6.9 %collective-permute-done.11.refs_1_.refs_5_ = bf16[512,256]{1,0:T(8,128)(2,1)S(1)} collective-permute-done((bf16[512,256]{1,0:T(8,128)(2,1)S(1)}, bf16[512,256]{1,0:T(8,128)(2,1)S(1)}, u32[]{:S(2)}, u32[]{:S(2)}) %collective-permute-start.11) | collective-permute-done | bytes 262176 | tf_op jit(solution)/shard_map/ppermute | solution.py:86
  56.1 16.3 %collective-permute-done.17.refs_2_.refs_6_ = bf16[256,256]{1,0:T(8,128)(2,1)S(1)} collective-permute-done((bf16[256,256]{1,0:T(8,128)(2,1)S(1)}, bf16[256,256]{1,0:T(8,128)(2,1)S(1)}, u32[]{:S(2)}, u32[]{:S(2)}) %collective-permute-start.17) | collective-permute-done | bytes 131104 | tf_op jit(solution)/shard_map/ppermute | solution.py:86
  79.6 10.3 %collective-permute-done.4.refs_8_.refs_4_ = bf16[128,2048]{1,0:T(8,128)(2,1)S(1)} collective-permute-done((bf16[128,2048]{1,0:T(8,128)(2,1)S(1)}, bf16[128,2048]{1,0:T(8,128)(2,1)S(1)}, u32[]{:S(2)}, u32[]{:S(2)}) %collective-permute-start.4) | collective-permute-done | bytes 524320 | tf_op jit(solution)/shard_map/ppermute | solution.py:86
  89.9 11.8 %collective-permute-done.5.refs_5_.refs_1_ = bf16[128,2048]{1,0:T(8,128)(2,1)} collective-permute-done((bf16[128,2048]{1,0:T(8,128)(2,1)S(1)}, bf16[128,2048]{1,0:T(8,128)(2,1)}, u32[]{:S(2)}, u32[]{:S(2)}) %collective-permute-start.5) | collective-permute-done | bytes 524320 | tf_op jit(solution)/shard_map/ppermute | solution.py:86
  107.1 6.9 %attend.1 = (bf16[256,512]{1,0:T(8,128)(2,1)}, bf16[256,512]{1,0:T(8,128)(2,1)}, bf16[256,512]{1,0:T(8,128)(2,1)}, f32[4,256,256]{2,1,0:T(8,128)}, bf16[256,512]{1,0:T(8,128)(2,1)}) custom-call(bf16[256,2048]{1,0:T(8,128)(2,1)} %get-tuple-element.139.x.left, bf16[1,512]{1,0:T(2,128)(2,1)} %broadcast_in_dim.19.q_bias, ...), custom_call_target="tpu_custom_call" | custom-call | flops 1610612736 | bytes 9701376 | tf_op jit(solution)/shard_map/attend/pallas_call | solution.py:46
  115.8 5.3 project_out.1
  126.5 14.7 %collective-permute-done.25.refs_7_.refs_3_ = bf16[64,2048]{1,0:T(8,128)(2,1)S(1)} collective-permute-done((bf16[64,2048]{1,0:T(8,128)(2,1)}, bf16[64,2048]{1,0:T(8,128)(2,1)S(1)}, u32[]{:S(2)}, u32[]{:S(2)}) %collective-permute-start.25) | collective-permute-done | bytes 262176 | tf_op jit(solution)/shard_map/ppermute | solution.py:86
  144.9 5.6 %collective-permute-done.28.refs_2_ = bf16[64,2048]{1,0:T(8,128)(2,1)S(1)} collective-permute-done((bf16[64,2048]{1,0:T(8,128)(2,1)}, bf16[64,2048]{1,0:T(8,128)(2,1)S(1)}, u32[]{:S(2)}, u32[]{:S(2)}) %collective-permute-start.28) | collective-permute-done | bytes 262176 | tf_op jit(solution)/shard_map/ppermute | solution.py:89
  170.0 12.2 %collective-permute-done.37.refs_16_.refs_12_ = bf16[64,2048]{1,0:T(8,128)(2,1)S(1)} collective-permute-done((bf16[64,2048]{1,0:T(8,128)(2,1)}, bf16[64,2048]{1,0:T(8,128)(2,1)S(1)}, u32[]{:S(2)}, u32[]{:S(2)}) %collective-permute-start.37) | collective-permute-done | bytes 262176 | tf_op jit(solution)/shard_map/ppermute | solution.py:86
  195.1 10.6 %upper.1 = (bf16[256,2048]{1,0:T(8,128)(2,1)}, bf16[256,2048]{1,0:T(8,128)(2,1)}, f32[256,2048]{1,0:T(8,128)}) custom-call(bf16[1,2048]{1,0:T(2,128)(2,1)} %broadcast_in_dim.18.bias, bf16[64,2048]{1,0:T(8,128)(2,1)} %get-tuple-element.149.refs_0_, bf16[64,2048]{1,0:T(8,128)(2,1)} %collective-permute-done.29.refs_1_, bf16[64,2048]{1,0:T(8,128)(2,1)} %copy-done.65, ...), custom_call_target="tpu_custom_call" | custom-call | flops 2147483648 | bytes 13635584 | tf_op jit(solution)/shard_map/upper/pallas_call | solution.py:46
  205.7 12.9 %collective-permute-done.44.refs_2_ = bf16[512,256]{1,0:T(8,128)(2,1)} collective-permute-done((bf16[512,256]{1,0:T(8,128)(2,1)}, bf16[512,256]{1,0:T(8,128)(2,1)}, u32[]{:S(2)}, u32[]{:S(2)}) %collective-permute-start.44) | collective-permute-done | bytes 262176 | tf_op jit(solution)/shard_map/ppermute | solution.py:86
  218.5 6.8 %collective-permute-done.45.refs_3_ = bf16[512,256]{1,0:T(8,128)(2,1)} collective-permute-done((bf16[512,256]{1,0:T(8,128)(2,1)}, bf16[512,256]{1,0:T(8,128)(2,1)}, u32[]{:S(2)}, u32[]{:S(2)}) %collective-permute-start.45) | collective-permute-done | bytes 262176 | tf_op jit(solution)/shard_map/ppermute | solution.py:86
  225.4 5.2 grad_down_far.1
  231.6 7.0 %collective-permute-done.49.refs_5_ = bf16[1024,256]{1,0:T(8,128)(2,1)S(1)} collective-permute-done((bf16[1024,256]{1,0:T(8,128)(2,1)S(1)}, bf16[1024,256]{1,0:T(8,128)(2,1)S(1)}, u32[]{:S(2)}, u32[]{:S(2)}) %collective-permute-start.49) | collective-permute-done | bytes 524320 | tf_op jit(solution)/shard_map/ppermute | solution.py:86
  242.1 6.8 %collective-permute-done.54.refs_12_ = bf16[512,256]{1,0:T(8,128)(2,1)} collective-permute-done((bf16[512,256]{1,0:T(8,128)(2,1)S(1)}, bf16[512,256]{1,0:T(8,128)(2,1)}, u32[]{:S(2)}, u32[]{:S(2)}) %collective-permute-start.54) | collective-permute-done | bytes 262176 | tf_op jit(solution)/shard_map/ppermute | solution.py:86
  249.0 6.1 %collective-permute-done.55.refs_13_ = bf16[512,256]{1,0:T(8,128)(2,1)} collective-permute-done((bf16[512,256]{1,0:T(8,128)(2,1)S(1)}, bf16[512,256]{1,0:T(8,128)(2,1)}, u32[]{:S(2)}, u32[]{:S(2)}) %collective-permute-start.55) | collective-permute-done | bytes 262176 | tf_op jit(solution)/shard_map/ppermute | solution.py:86
  255.6 6.3 %grad_down_near.1 = (f32[2048,256]{1,0:T(8,128)}, bf16[2048,256]{1,0:T(8,128)(2,1)}, bf16[2048,256]{1,0:T(8,128)(2,1)}, f32[1024,256]{1,0:T(8,128)}, f32[1024,256]{1,0:T(8,128)}) custom-call(bf16[256,2048]{1,0:T(8,128)(2,1)} %get-tuple-element.169.left, bf16[8192,256]{1,0:T(8,128)(2,1)} %collective-permute-done.48.theirs, ...), custom_call_target="tpu_custom_call" | custom-call | flops 1073741824 | bytes 12582912 | tf_op jit(solution)/shard_map/grad_down_near/pallas_call | solution.py:46
  263.1 10.3 %upper_grad.1 = (bf16[256,2048]{1,0:T(8,128)(2,1)}, f32[1,2048]{1,0:T(1,128)}) custom-call(bf16[256,2048]{1,0:T(8,128)(2,1)} %get-tuple-element.161.refs_0_.g.g_rel, f32[256,2048]{1,0:T(8,128)} %get-tuple-element.162.slope, bf16[1024,256]{1,0:T(8,128)(2,1)} %copy-done.3, bf16[1024,256]{1,0:T(8,128)(2,1)} %copy-done.7, ...), custom_call_target="tpu_custom_call" | custom-call | flops 2147483648 | bytes 12591104 | tf_op jit(solution)/shard_map/upper_grad/pallas_call | solution.py:46
  273.4 9.4 %second_part.1 = (f32[64,2048]{1,0:T(8,128)}, bf16[64,2048]{1,0:T(8,128)(2,1)}, bf16[64,2048]{1,0:T(8,128)(2,1)}, bf16[64,2048]{1,0:T(8,128)(2,1)}) custom-call(bf16[256,2048]{1,0:T(8,128)(2,1)} %get-tuple-element.179.left.refs_0_, bf16[128,2048]{1,0:T(8,128)(2,1)} %copy-done.4, bf16[128,2048]{1,0:T(8,128)(2,1)} %collective-permute-done.5.refs_5_.refs_1_, ...), custom_call_target="tpu_custom_call" | custom-call | flops 2147483648 | bytes 10747904 | tf_op jit(solution)/shard_map/second_part/pallas_call | solution.py:46
  292.9 20.9 %collective-permute-done.63.b = bf16[2048,256]{1,0:T(8,128)(2,1)S(1)} collective-permute-done((bf16[2048,256]{1,0:T(8,128)(2,1)S(1)}, bf16[2048,256]{1,0:T(8,128)(2,1)S(1)}, u32[]{:S(2)}, u32[]{:S(2)}) %collective-permute-start.63) | collective-permute-done | bytes 1048608 | tf_op jit(solution)/shard_map/ppermute | solution.py:86
  316.4 20.2 %collective-permute-done.61.c = bf16[2048,256]{1,0:T(8,128)(2,1)S(1)} collective-permute-done((bf16[2048,256]{1,0:T(8,128)(2,1)}, bf16[2048,256]{1,0:T(8,128)(2,1)S(1)}, u32[]{:S(2)}, u32[]{:S(2)}) %collective-permute-start.61) | collective-permute-done | bytes 1048608 | tf_op jit(solution)/shard_map/ppermute | solution.py:86
  339.1 9.1 %feed.1 = (f32[64,2048]{1,0:T(8,128)}, bf16[64,2048]{1,0:T(8,128)(2,1)}, bf16[64,2048]{1,0:T(8,128)(2,1)}, bf16[64,2048]{1,0:T(8,128)(2,1)}) custom-call(bf16[256,2048]{1,0:T(8,128)(2,1)} %get-tuple-element.169.left, bf16[1024,256]{1,0:T(8,128)(2,1)} %copy-done.3, bf16[1024,256]{1,0:T(8,128)(2,1)} %copy-done.7, ...), custom_call_target="tpu_custom_call" | custom-call | flops 2147483648 | bytes 10747904 | tf_op jit(solution)/shard_map/feed/pallas_call | solution.py:46
  355.7 6.1 %grad_up_near.1 = (f32[256,2048]{1,0:T(8,128)}, bf16[256,2048]{1,0:T(8,128)(2,1)}, bf16[256,2048]{1,0:T(8,128)(2,1)}, f32[128,2048]{1,0:T(8,128)}, f32[128,2048]{1,0:T(8,128)}) custom-call(bf16[256,2048]{1,0:T(8,128)(2,1)} %get-tuple-element.151.left, bf16[1024,2048]{1,0:T(8,128)(2,1)} %collective-permute-done.65.theirs, ...), custom_call_target="tpu_custom_call" | custom-call | flops 1073741824 | bytes 12582912 | tf_op jit(solution)/shard_map/grad_up_near/pallas_call | solution.py:46
  361.9 5.0 collective-permute-done.70.refs_2_
  367.7 13.2 %attend_back.1 = (bf16[256,2048]{1,0:T(8,128)(2,1)}, bf16[256,512]{1,0:T(8,128)(2,1)}, bf16[256,512]{1,0:T(8,128)(2,1)}, bf16[256,512]{1,0:T(8,128)(2,1)}, f32[1...) custom-call(bf16[256,512]{1,0:T(8,128)(2,1)} %get-tuple-element.185., ...), custom_call_target="tpu_custom_call" | custom-call | flops 2147483648 | bytes 14422016 | tf_op jit(solution)/shard_map/attend_back/pallas_call | solution.py:46
  415.9 5.2 grad_in_near.1
  425.6 9.8 %collective-permute-done.75.c = bf16[256,2048]{1,0:T(8,128)(2,1)} collective-permute-done((bf16[256,2048]{1,0:T(8,128)(2,1)}, bf16[256,2048]{1,0:T(8,128)(2,1)}, u32[]{:S(2)}, u32[]{:S(2)}) %collective-permute-start.75) | collective-permute-done | bytes 1048608 | tf_op jit(solution)/shard_map/ppermute | solution.py:86
  457.1 18.8 %collective-permute-done.108.d = bf16[128,2048]{1,0:T(8,128)(2,1)S(1)} collective-permute-done((bf16[128,2048]{1,0:T(8,128)(2,1)S(1)}, bf16[128,2048]{1,0:T(8,128)(2,1)S(1)}, u32[]{:S(2)}, u32[]{:S(2)}) %collective-permute-start.108) | collective-permute-done | bytes 524320 | tf_op jit(solution)/shard_map/ppermute | solution.py:86
  497.0 12.1 %collective-permute-done.103.c = bf16[512,256]{1,0:T(8,128)(2,1)S(1)} collective-permute-done((bf16[512,256]{1,0:T(8,128)(2,1)}, bf16[512,256]{1,0:T(8,128)(2,1)S(1)}, u32[]{:S(2)}, u32[]{:S(2)}) %collective-permute-start.103) | collective-permute-done | bytes 262176 | tf_op jit(solution)/shard_map/ppermute | solution.py:86
  511.4 11.5 %collective-permute-done.97.b = bf16[256,1536]{1,0:T(8,128)(2,1)S(1)} collective-permute-done((bf16[256,1536]{1,0:T(8,128)(2,1)}, bf16[256,1536]{1,0:T(8,128)(2,1)S(1)}, u32[]{:S(2)}, u32[]{:S(2)}) %collective-permute-start.97) | collective-permute-done | bytes 786464 | tf_op jit(solution)/shard_map/ppermute | solution.py:86
  523.0 8.0 %collective-permute-done.95.c = bf16[256,1536]{1,0:T(8,128)(2,1)S(1)} collective-permute-done((bf16[256,1536]{1,0:T(8,128)(2,1)}, bf16[256,1536]{1,0:T(8,128)(2,1)S(1)}, u32[]{:S(2)}, u32[]{:S(2)}) %collective-permute-start.95) | collective-permute-done | bytes 786464 | tf_op jit(solution)/shard_map/ppermute | solution.py:86
  (444 shorter events, 224.6 us)
Async XLA Ops:
  2.3 35.6 %collective-permute-start.1 = (bf16[3,256,512]{2,1,0:T(8,128)(2,1)}, bf16[3,256,512]{2,1,0:T(8,128)(2,1)S(1)}, u32[]{:S(2)}, u32[]{:S(2)}) collective-permute-start(bf16[3,256,512]{2,1,0:T(8,128)(2,1)} %refs_14_.1), channel_id=1, source_target_pairs={{0,24},{4,28},{8,0},{12,4},{16,8},{20,12},{24,16},{28,20},{1,25},{... | collective-permute-start | bytes 2359304 | tf_op jit(solution)/shard_map/ppermute | solution.py:86
  40.0 34.3 %collective-permute-start.2 = (bf16[3,128,512]{2,1,0:T(8,128)(2,1)S(1)}, bf16[3,128,512]{2,1,0:T(8,128)(2,1)S(1)}, u32[]{:S(2)}, u32[]{:S(2)}) collective-permute-start(bf16[3,128,512]{2,1,0:T(8,128)(2,1)S(1)} %slice.108), channel_id=1, source_target_pairs={{0,8},{4,12},{8,16},{12,20},{16,24},{20,28},{24,0},{28,4},{1,9},{5... | collective-permute-start | bytes 1179656 | tf_op jit(solution)/shard_map/ppermute | solution.py:86
  40.8 34.0 %collective-permute-start.3 = (bf16[3,128,512]{2,1,0:T(8,128)(2,1)S(1)}, bf16[3,128,512]{2,1,0:T(8,128)(2,1)S(1)}, u32[]{:S(2)}, u32[]{:S(2)}) collective-permute-start(bf16[3,128,512]{2,1,0:T(8,128)(2,1)S(1)} %slice.109), channel_id=1, source_target_pairs={{0,24},{4,28},{8,0},{12,4},{16,8},{20,12},{24,16},{28,20},{1,25},{... | collective-permute-start | bytes 1179656 | tf_op jit(solution)/shard_map/ppermute | solution.py:86
  47.1 27.9 %collective-permute-start.12 = (bf16[3,256,512]{2,1,0:T(8,128)(2,1)}, bf16[3,256,512]{2,1,0:T(8,128)(2,1)S(1)}, u32[]{:S(2)}, u32[]{:S(2)}) collective-permute-start(bf16[3,256,512]{2,1,0:T(8,128)(2,1)} %refs_14_.1), channel_id=1, source_target_pairs={{0,4},{4,0},{8,12},{12,8},{16,20},{20,16},{24,28},{28,24},{1,5},{5... | collective-permute-start | bytes 2359304 | tf_op jit(solution)/shard_map/ppermute | solution.py:86
  89.9 31.2 %collective-permute-start.32 = (bf16[128,2048]{1,0:T(8,128)(2,1)S(1)}, bf16[128,2048]{1,0:T(8,128)(2,1)}, u32[]{:S(2)}, u32[]{:S(2)}) collective-permute-start(bf16[128,2048]{1,0:T(8,128)(2,1)S(1)} %get-tuple-element.134.refs_4_.refs_0_), channel_id=1, source_target_pairs={{0,4},{4,0},{8,12},{12,8},{16,20},{20,16},{24,28},{28,24},{1,5},{5... | collective-permute-start | bytes 1572872 | tf_op jit(solution)/shard_map/ppermute | solution.py:86
  104.1 40.1 %collective-permute-start.6 = (bf16[128,2048]{1,0:T(8,128)(2,1)S(1)}, bf16[128,2048]{1,0:T(8,128)(2,1)}, u32[]{:S(2)}, u32[]{:S(2)}) collective-permute-start(bf16[128,2048]{1,0:T(8,128)(2,1)S(1)} %get-tuple-element.135.refs_14_.refs_10_), channel_id=1, source_target_pairs={{0,8},{4,12},{8,16},{12,20},{16,24},{20,28},{24,0},{28,4},{1,9},{5... | collective-permute-start | bytes 1572872 | tf_op jit(solution)/shard_map/ppermute | solution.py:86
  105.9 38.4 %collective-permute-start.7 = (bf16[128,2048]{1,0:T(8,128)(2,1)S(1)}, bf16[128,2048]{1,0:T(8,128)(2,1)}, u32[]{:S(2)}, u32[]{:S(2)}) collective-permute-start(bf16[128,2048]{1,0:T(8,128)(2,1)S(1)} %get-tuple-element.135.refs_14_.refs_10_), channel_id=1, source_target_pairs={{0,24},{4,28},{8,0},{12,4},{16,8},{20,12},{24,16},{28,20},{1,25},{... | collective-permute-start | bytes 1572872 | tf_op jit(solution)/shard_map/ppermute | solution.py:86
  150.5 31.7 %collective-permute-start.8 = (bf16[1024,256]{1,0:T(8,128)(2,1)S(1)}, bf16[1024,256]{1,0:T(8,128)(2,1)S(1)}, u32[]{:S(2)}, u32[]{:S(2)}) collective-permute-start(bf16[1024,256]{1,0:T(8,128)(2,1)S(1)} %get-tuple-element.136.refs_0_), channel_id=1, source_target_pairs={{0,8},{4,12},{8,16},{12,20},{16,24},{20,28},{24,0},{28,4},{1,9},{5... | collective-permute-start | bytes 1572872 | tf_op jit(solution)/shard_map/ppermute | solution.py:86
  151.2 31.5 %collective-permute-start.9 = (bf16[1024,256]{1,0:T(8,128)(2,1)S(1)}, bf16[1024,256]{1,0:T(8,128)(2,1)S(1)}, u32[]{:S(2)}, u32[]{:S(2)}) collective-permute-start(bf16[1024,256]{1,0:T(8,128)(2,1)S(1)} %get-tuple-element.136.refs_0_), channel_id=1, source_target_pairs={{0,24},{4,28},{8,0},{12,4},{16,8},{20,12},{24,16},{28,20},{1,25},{... | collective-permute-start | bytes 1572872 | tf_op jit(solution)/shard_map/ppermute | solution.py:86
  186.7 38.7 %collective-permute-start.46 = (bf16[1024,256]{1,0:T(8,128)(2,1)S(1)}, bf16[1024,256]{1,0:T(8,128)(2,1)S(1)}, u32[]{:S(2)}, u32[]{:S(2)}) collective-permute-start(bf16[1024,256]{1,0:T(8,128)(2,1)S(1)} %get-tuple-element.153.refs_10_), channel_id=1, source_target_pairs={{0,8},{4,12},{8,16},{12,20},{16,24},{20,28},{24,0},{28,4},{1,9},{5... | collective-permute-start | bytes 1572872 | tf_op jit(solution)/shard_map/ppermute | solution.py:86
  189.2 36.2 %collective-permute-start.47 = (bf16[1024,256]{1,0:T(8,128)(2,1)S(1)}, bf16[1024,256]{1,0:T(8,128)(2,1)S(1)}, u32[]{:S(2)}, u32[]{:S(2)}) collective-permute-start(bf16[1024,256]{1,0:T(8,128)(2,1)S(1)} %get-tuple-element.153.refs_10_), channel_id=1, source_target_pairs={{0,24},{4,28},{8,0},{12,4},{16,8},{20,12},{24,16},{28,20},{1,25},{... | collective-permute-start | bytes 1572872 | tf_op jit(solution)/shard_map/ppermute | solution.py:86
  191.7 26.9 %collective-permute-start.44 = (bf16[512,256]{1,0:T(8,128)(2,1)}, bf16[512,256]{1,0:T(8,128)(2,1)}, u32[]{:S(2)}, u32[]{:S(2)}) collective-permute-start(bf16[512,256]{1,0:T(8,128)(2,1)} %slice.150), channel_id=1, source_target_pairs={{0,8},{4,12},{8,16},{12,20},{16,24},{20,28},{24,0},{28,4},{1,9},{5... | collective-permute-start | bytes 786440 | tf_op jit(solution)/shard_map/ppermute | solution.py:86
  193.4 32.0 %collective-permute-start.45 = (bf16[512,256]{1,0:T(8,128)(2,1)}, bf16[512,256]{1,0:T(8,128)(2,1)}, u32[]{:S(2)}, u32[]{:S(2)}) collective-permute-start(bf16[512,256]{1,0:T(8,128)(2,1)} %slice.151), channel_id=1, source_target_pairs={{0,24},{4,28},{8,0},{12,4},{16,8},{20,12},{24,16},{28,20},{1,25},{... | collective-permute-start | bytes 786440 | tf_op jit(solution)/shard_map/ppermute | solution.py:86
  287.8 67.4 %collective-permute-start.65 = (bf16[1024,2048]{1,0:T(8,128)(2,1)}, bf16[1024,2048]{1,0:T(8,128)(2,1)}, u32[]{:S(2)}, u32[]{:S(2)}) collective-permute-start(bf16[1024,2048]{1,0:T(8,128)(2,1)} %grad_up_far.1), channel_id=1, source_target_pairs={{0,4},{4,0},{8,12},{12,8},{16,20},{20,16},{24,28},{28,24},{1,5},{5... | collective-permute-start | bytes 12582920 | tf_op jit(solution)/shard_map/ppermute | solution.py:86
  289.1 47.5 %collective-permute-start.61 = (bf16[2048,256]{1,0:T(8,128)(2,1)}, bf16[2048,256]{1,0:T(8,128)(2,1)S(1)}, u32[]{:S(2)}, u32[]{:S(2)}) collective-permute-start(bf16[2048,256]{1,0:T(8,128)(2,1)} %get-tuple-element.157), channel_id=1, source_target_pairs={{0,8},{4,12},{8,16},{12,20},{16,24},{20,28},{24,0},{28,4},{1,9},{5... | collective-permute-start | bytes 3145736 | tf_op jit(solution)/shard_map/ppermute | solution.py:86
  289.9 47.6 %collective-permute-start.66 = (bf16[64,2048]{1,0:T(8,128)(2,1)}, bf16[64,2048]{1,0:T(8,128)(2,1)S(1)}, u32[]{:S(2)}, u32[]{:S(2)}) collective-permute-start(bf16[64,2048]{1,0:T(8,128)(2,1)} %get-tuple-element.165), channel_id=1, source_target_pairs={{0,1},{1,0},{2,3},{3,2},{4,5},{5,4},{6,7},{7,6},{8,9},{9,8},{10,11... | collective-permute-start | bytes 786440 | tf_op jit(solution)/shard_map/ppermute | solution.py:89
  291.4 56.8 %collective-permute-start.67 = (bf16[64,2048]{1,0:T(8,128)(2,1)S(1)}, bf16[64,2048]{1,0:T(8,128)(2,1)S(1)}, u32[]{:S(2)}, u32[]{:S(2)}) collective-permute-start(bf16[64,2048]{1,0:T(8,128)(2,1)S(1)} %copy-done.85), channel_id=1, source_target_pairs={{0,2},{1,3},{2,0},{3,1},{4,6},{5,7},{6,4},{7,5},{8,10},{9,11},{10,... | collective-permute-start | bytes 786440 | tf_op jit(solution)/shard_map/ppermute | solution.py:89
  313.9 34.4 %collective-permute-start.68 = (bf16[64,2048]{1,0:T(8,128)(2,1)S(1)}, bf16[64,2048]{1,0:T(8,128)(2,1)S(1)}, u32[]{:S(2)}, u32[]{:S(2)}) collective-permute-start(bf16[64,2048]{1,0:T(8,128)(2,1)S(1)} %copy-done.84), channel_id=1, source_target_pairs={{0,3},{1,2},{2,1},{3,0},{4,7},{5,6},{6,5},{7,4},{8,11},{9,10},{10,... | collective-permute-start | bytes 786440 | tf_op jit(solution)/shard_map/ppermute | solution.py:89
  385.0 27.5 %collective-permute-start.78 = (bf16[1024,1536]{1,0:T(8,128)(2,1)}, bf16[1024,1536]{1,0:T(8,128)(2,1)S(1)}, u32[]{:S(2)}, u32[]{:S(2)}) collective-permute-start(bf16[1024,1536]{1,0:T(8,128)(2,1)} %grad_in_far.1), channel_id=1, source_target_pairs={{0,4},{4,0},{8,12},{12,8},{16,20},{20,16},{24,28},{28,24},{1,5},{5... | collective-permute-start | bytes 9437192 | tf_op jit(solution)/shard_map/ppermute | solution.py:86
  399.4 36.0 %collective-permute-start.75 = (bf16[256,2048]{1,0:T(8,128)(2,1)}, bf16[256,2048]{1,0:T(8,128)(2,1)}, u32[]{:S(2)}, u32[]{:S(2)}) collective-permute-start(bf16[256,2048]{1,0:T(8,128)(2,1)} %get-tuple-element.198), channel_id=1, source_target_pairs={{0,8},{4,12},{8,16},{12,20},{16,24},{20,28},{24,0},{28,4},{1,9},{5... | collective-permute-start | bytes 3145736 | tf_op jit(solution)/shard_map/ppermute | solution.py:86
  407.6 30.1 %collective-permute-start.79 = (bf16[64,2048]{1,0:T(8,128)(2,1)}, bf16[64,2048]{1,0:T(8,128)(2,1)S(1)}, u32[]{:S(2)}, u32[]{:S(2)}) collective-permute-start(bf16[64,2048]{1,0:T(8,128)(2,1)} %get-tuple-element.224), channel_id=1, source_target_pairs={{0,1},{1,0},{2,3},{3,2},{4,5},{5,4},{6,7},{7,6},{8,9},{9,8},{10,11... | collective-permute-start | bytes 786440 | tf_op jit(solution)/shard_map/ppermute | solution.py:89
  421.0 29.7 %collective-permute-start.100 = (f32[3072]{0:T(1024)S(1)}, f32[3072]{0:T(1024)S(1)}, u32[]{:S(2)}, u32[]{:S(2)}) collective-permute-start(f32[3072]{0:T(1024)S(1)} %fusion.5), channel_id=1, source_target_pairs={{0,8},{4,12},{8,16},{12,20},{16,24},{20,28},{24,0},{28,4},{1,9},{5... | collective-permute-start | bytes 36872 | tf_op jit(solution)/shard_map/ppermute | solution.py:86
  448.6 27.3 %collective-permute-start.108 = (bf16[128,2048]{1,0:T(8,128)(2,1)S(1)}, bf16[128,2048]{1,0:T(8,128)(2,1)S(1)}, u32[]{:S(2)}, u32[]{:S(2)}) collective-permute-start(bf16[128,2048]{1,0:T(8,128)(2,1)S(1)} %copy-done.61), channel_id=1, source_target_pairs={{0,24},{4,28},{8,0},{12,4},{16,8},{20,12},{24,16},{28,20},{1,25},{... | collective-permute-start | bytes 1572872 | tf_op jit(solution)/shard_map/ppermute | solution.py:86
  449.8 27.4 %collective-permute-start.107 = (bf16[128,2048]{1,0:T(8,128)(2,1)S(1)}, bf16[128,2048]{1,0:T(8,128)(2,1)S(1)}, u32[]{:S(2)}, u32[]{:S(2)}) collective-permute-start(bf16[128,2048]{1,0:T(8,128)(2,1)S(1)} %add_convert_fusion.1), channel_id=1, source_target_pairs={{0,8},{4,12},{8,16},{12,20},{16,24},{20,28},{24,0},{28,4},{1,9},{5... | collective-permute-start | bytes 1572872 | tf_op jit(solution)/shard_map/ppermute | solution.py:86
  450.7 35.3 %collective-permute-start.82 = (bf16[64,2048]{1,0:T(8,128)(2,1)S(1)}, bf16[64,2048]{1,0:T(8,128)(2,1)}, u32[]{:S(2)}, u32[]{:S(2)}) collective-permute-start(bf16[64,2048]{1,0:T(8,128)(2,1)S(1)} %copy-done.63), channel_id=1, source_target_pairs={{0,1},{1,0},{2,3},{3,2},{4,5},{5,4},{6,7},{7,6},{8,9},{9,8},{10,11... | collective-permute-start | bytes 786440 | tf_op jit(solution)/shard_map/ppermute | solution.py:89
  453.0 29.0 %collective-permute-start.92 = (f32[6,2048]{1,0:T(8,128)S(1)}, f32[6,2048]{1,0:T(8,128)S(1)}, u32[]{:S(2)}, u32[]{:S(2)}) collective-permute-start(f32[6,2048]{1,0:T(8,128)S(1)} %add.97), channel_id=1, source_target_pairs={{0,8},{4,12},{8,16},{12,20},{16,24},{20,28},{24,0},{28,4},{1,9},{5... | collective-permute-start | bytes 147464 | tf_op jit(solution)/shard_map/ppermute | solution.py:86
  453.9 30.0 %collective-permute-start.93 = (f32[6,2048]{1,0:T(8,128)S(1)}, f32[6,2048]{1,0:T(8,128)}, u32[]{:S(2)}, u32[]{:S(2)}) collective-permute-start(f32[6,2048]{1,0:T(8,128)S(1)} %add.97), channel_id=1, source_target_pairs={{0,16},{4,20},{8,24},{12,28},{16,0},{20,4},{24,8},{28,12},{1,17},{... | collective-permute-start | bytes 147464 | tf_op jit(solution)/shard_map/ppermute | solution.py:86
  486.0 36.9 %collective-permute-start.97 = (bf16[256,1536]{1,0:T(8,128)(2,1)}, bf16[256,1536]{1,0:T(8,128)(2,1)S(1)}, u32[]{:S(2)}, u32[]{:S(2)}) collective-permute-start(bf16[256,1536]{1,0:T(8,128)(2,1)} %get-tuple-element.234), channel_id=1, source_target_pairs={{0,24},{4,28},{8,0},{12,4},{16,8},{20,12},{24,16},{28,20},{1,25},{... | collective-permute-start | bytes 2359304 | tf_op jit(solution)/shard_map/ppermute | solution.py:86
  491.3 39.6 %collective-permute-start.95 = (bf16[256,1536]{1,0:T(8,128)(2,1)}, bf16[256,1536]{1,0:T(8,128)(2,1)S(1)}, u32[]{:S(2)}, u32[]{:S(2)}) collective-permute-start(bf16[256,1536]{1,0:T(8,128)(2,1)} %get-tuple-element.233), channel_id=1, source_target_pairs={{0,8},{4,12},{8,16},{12,20},{16,24},{20,28},{24,0},{28,4},{1,9},{5... | collective-permute-start | bytes 2359304 | tf_op jit(solution)/shard_map/ppermute | solution.py:86
  493.3 53.3 %collective-permute-start.85 = (bf16[64,2048]{1,0:T(8,128)(2,1)S(1)}, bf16[64,2048]{1,0:T(8,128)(2,1)}, u32[]{:S(2)}, u32[]{:S(2)}) collective-permute-start(bf16[64,2048]{1,0:T(8,128)(2,1)S(1)} %copy-done.36), channel_id=1, source_target_pairs={{0,1},{1,0},{2,3},{3,2},{4,5},{5,4},{6,7},{7,6},{8,9},{9,8},{10,11... | collective-permute-start | bytes 786440 | tf_op jit(solution)/shard_map/ppermute | solution.py:89
  494.6 51.9 %collective-permute-start.86 = (bf16[64,2048]{1,0:T(8,128)(2,1)S(1)}, bf16[64,2048]{1,0:T(8,128)(2,1)}, u32[]{:S(2)}, u32[]{:S(2)}) collective-permute-start(bf16[64,2048]{1,0:T(8,128)(2,1)S(1)} %copy-done.36), channel_id=1, source_target_pairs={{0,2},{1,3},{2,0},{3,1},{4,6},{5,7},{6,4},{7,5},{8,10},{9,11},{10,... | collective-permute-start | bytes 786440 | tf_op jit(solution)/shard_map/ppermute | solution.py:89
  509.1 37.5 %collective-permute-start.87 = (bf16[64,2048]{1,0:T(8,128)(2,1)S(1)}, bf16[64,2048]{1,0:T(8,128)(2,1)}, u32[]{:S(2)}, u32[]{:S(2)}) collective-permute-start(bf16[64,2048]{1,0:T(8,128)(2,1)S(1)} %copy-done.36), channel_id=1, source_target_pairs={{0,3},{1,2},{2,1},{3,0},{4,7},{5,6},{6,5},{7,4},{8,11},{9,10},{10,... | collective-permute-start | bytes 786440 | tf_op jit(solution)/shard_map/ppermute | solution.py:89
  (163 other events, 2876.4 us)

commit v3 on v0

v3 whole, which is shorter than its diff:
```python
import functools

import jax
import jax.numpy as jnp
from jax import lax
from jax.experimental import pallas as pl
from jax.experimental.pallas import tpu as pltpu
from jax.sharding import PartitionSpec as P

DH = 128
EPSILON = 1e-05
NEGATIVE = -1e30
SCALE = DH ** (-0.5)
F32 = jnp.float32
BF16 = jnp.bfloat16
TILE = 256
ANY = pl.BlockSpec(memory_space=pl.ANY)
VMEM = pl.BlockSpec(memory_space=pltpu.VMEM)
SMEM = pl.BlockSpec(memory_space=pltpu.SMEM)


def nn(left, right):
    return lax.dot_general(left, right, (((1,), (0,)), ((), ())), preferred_element_type=F32)


def nt(left, right):
    return lax.dot_general(left, right, (((1,), (1,)), ((), ())), preferred_element_type=F32)


def tn(left, right):
    return lax.dot_general(left, right, (((0,), (0,)), ((), ())), preferred_element_type=F32)


def shape(dims, dtype):
    return jax.ShapeDtypeStruct(tuple(dims), dtype)


def call(body, name, in_specs, outs, scratch, flops, args):
    moved = sum(a.size * a.dtype.itemsize for a in args)
    moved += sum(o.size * o.dtype.itemsize for o in outs)
    return pl.pallas_call(
        body,
        name=name,
        out_shape=outs,
        in_specs=in_specs,
        out_specs=[VMEM] * len(outs),
        scratch_shapes=scratch,
        cost_estimate=pl.CostEstimate(flops=flops, bytes_accessed=moved, transcendentals=0),
    )(*args)


class Places:
    def __init__(self, dp, tensor):
        self.dp, self.tensor, self.chips = dp, tensor, dp // 2
        self.rank = lax.axis_index("dp")
        self.part = lax.axis_index("tensor")
        self.chip, self.core = self.rank // 2, self.rank % 2
        self.side = self.chip % 2
        self.swap = [(i, i ^ 1) for i in range(dp)]

    def table(self):
        owners = jnp.arange(self.chips, dtype=jnp.int32) * 2
        chunks = self.part ^ jnp.arange(self.tensor, dtype=jnp.int32)
        return jnp.concatenate(
            [owners + self.core, owners + (1 - self.core), chunks, self.side[None]]
        ).astype(jnp.int32)

    def tokens_in(self, values):
        size = values.shape[0] // self.tensor
        return jnp.take(
            values.reshape(self.tensor, size),
            self.part ^ jnp.arange(self.tensor, dtype=jnp.int32),
            axis=0,
        ).reshape(-1)

    def chunk_of(self, values):
        size = values.shape[0] // self.tensor
        return lax.dynamic_slice_in_dim(values, self.part * size, size, 0)

    def half_of(self, values):
        size = values.shape[0] // 2
        return lax.dynamic_slice_in_dim(values, self.side * size, size, 0)

    def to_core(self, values):
        return lax.ppermute(values, "dp", self.swap)

    def to_chip(self, values, k):
        return lax.ppermute(values, "dp", [(i, i ^ (2 * k)) for i in range(self.dp)])

    def to_mate(self, values):
        return self.to_chip(values, 1)

    def to_peer(self, values, k):
        return lax.ppermute(values, "tensor", [(i, i ^ k) for i in range(self.tensor)])

    def to_peers(self, values):
        many = isinstance(values, (list, tuple))
        return [
            self.to_peer(values[k - 1] if many else values, k)
            for k in range(self.tensor - 1, 0, -1)
        ][::-1]

    def exchange(self, blocks):
        groups = [[2 * j + core for j in range(self.chips)] for core in range(2)]
        return lax.all_to_all(blocks, "dp", 0, 0, axis_index_groups=groups, tiled=True)

    def halves(self, block, axis):
        halves = jnp.split(block, 2, axis)
        return jnp.stack([halves[j % 2] for j in range(self.chips)])

    def both_cores(self, blocks):
        return [blocks, self.to_core(blocks)]

    def spread(self, chunk):
        own = self.to_peers(chunk)
        mate = after(self.to_mate(chunk), own)
        return [chunk] + own + [mate] + self.to_peers(mate)

    def sum_small(self, wide, narrow):
        step = 1
        while step < self.tensor:
            wide = wide + self.to_peer(wide, step)
            step *= 2
        values = jnp.concatenate([wide, narrow])
        values = values + self.to_core(values)
        step = 1
        while step < self.chips:
            values = values + self.to_chip(values, step)
            step *= 2
        return values


def after(values, *events):
    values, _ = lax.optimization_barrier((values, events))
    return values


def center_of(values):
    center = values - jnp.mean(values, axis=-1, keepdims=True)
    inverse = lax.rsqrt(jnp.mean(center * center, axis=-1, keepdims=True) + EPSILON)
    return center * inverse, inverse


def norm_back(norm_grad, normed, inverse, gain):
    scaled = norm_grad * gain
    return inverse * (
        scaled
        - jnp.mean(scaled, axis=-1, keepdims=True)
        - normed * jnp.mean(scaled * normed, axis=-1, keepdims=True)
    )


def place(table, p, size):
    return pl.ds(pl.multiple_of(table[p] * size, size), size)


def collect_body(dp, tensor, norm, table, own, vec, *refs):
    chunks, (out,) = refs[:tensor], refs[tensor:]
    rows = chunks[0].shape[0] // 2
    first = 0 if norm else rows
    for s in range(2):
        for k in range(tensor):
            value = own[place(table, dp + k, rows), :] if s == 0 else chunks[k][first : first + rows, :]
            if norm:
                normed, _ = center_of(value.astype(F32))
                value = (normed * vec[0:1, :] + vec[1:2, :]).astype(BF16)
            start = (s * tensor + k) * rows
            out[start : start + rows, :] = value


def blocks_of(arrays):
    return [ref.at[j] for ref in arrays for j in range(ref.shape[0])]


def attend_body(table, x, q_bias, v_bias, allowed, *refs):
    pieces, (q, k, v, probs, mixed), (weight, sems) = blocks_of(refs[:2]), refs[2:-2], refs[-2:]
    count, size = len(pieces), refs[0].shape[2]

    def copy(j, p):
        return pltpu.make_async_copy(
            pieces[p].at[j], weight.at[j, place(table, p, size)], sems.at[j, p]
        )

    for j in range(3):
        for p in range(count):
            copy(j, p).start()
    columns = q.shape[1]
    tile = min(TILE, columns)
    for j, out in enumerate((q, k, v)):
        for p in range(count):
            copy(j, p).wait()
        for start in range(0, columns, tile):
            cols = slice(start, start + tile)
            total = nn(x[...], weight[j, :, cols])
            if j == 0:
                total = total + q_bias[:, cols].astype(F32)
            if j == 2:
                total = total + v_bias[:, cols].astype(F32)
            out[:, cols] = total.astype(BF16)
    heads = columns // DH
    length = allowed.shape[1]
    for s in range(2):
        rows = slice(s * length, (s + 1) * length)
        for h in range(heads):
            cols = slice(h * DH, (h + 1) * DH)
            scores = nt(q[rows, cols], k[rows, cols]) * SCALE
            scores = jnp.where(allowed[s] > 0, scores, NEGATIVE)
            weights = jnp.exp(scores - jnp.max(scores, axis=-1, keepdims=True))
            prob = weights / jnp.sum(weights, axis=-1, keepdims=True)
            probs[s * heads + h] = prob
            mixed[rows, cols] = nn(prob.astype(BF16), v[rows, cols]).astype(BF16)


def put_chunks(total, cols, own, mate, sends):
    rows = own.shape[0]
    length = total.shape[0] // 2
    chunks = length // rows
    own[:, cols] = total[:rows]
    mate[:, cols] = total[length : length + rows]
    for k in range(1, chunks):
        for s in range(2):
            part = total[s * length + k * rows : s * length + (k + 1) * rows].astype(BF16)
            if len(sends) == chunks - 1:
                sends[k - 1][s * rows : (s + 1) * rows, cols] = part
            else:
                sends[s * (chunks - 1) + k - 1][:, cols] = part


def column_copies(table, arrays, weight, sems):
    width = arrays[0].shape[2]
    return [
        pltpu.make_async_copy(piece, weight.at[:, place(table, p, width)], sems.at[p])
        for p, piece in enumerate(blocks_of(arrays))
    ]


def row_copies(table, arrays, weight, sems):
    size = arrays[0].shape[1]
    return [
        pltpu.make_async_copy(piece, weight.at[place(table, p, size)], sems.at[p])
        for p, piece in enumerate(blocks_of(arrays))
    ]


def project_body(by_rows, table, left, *refs):
    pieces, (own, mate, *sends), (weight, sems) = refs[:2], refs[2:-2], refs[-2:]
    copies = (row_copies if by_rows else column_copies)(table, pieces, weight, sems)
    for copy in copies:
        copy.start()
    size = pieces[0].shape[1 if by_rows else 2]
    for p, copy in enumerate(copies):
        copy.wait()
        cols = place(table, p, size)
        if by_rows:
            total = nt(left[...], weight[cols, :])
        else:
            total = nn(left[...], weight[:, cols])
        put_chunks(total, cols, own, mate, sends)


def fold_body(mate, *refs):
    received, (out,) = refs[:-1], refs[-1:]
    total = mate[...]
    rows = mate.shape[0]
    for ref in received:
        total = total + ref[ref.shape[0] - rows :, :].astype(F32)
    out[...] = total.astype(BF16)


def summed(own, received):
    total = own[...]
    rows = own.shape[0]
    for ref in received:
        total = total + ref[:rows, :].astype(F32)
    return total


def second_body(count, own, x, vec, *refs):
    received, (hidden, normed_out, inverse_out, low) = refs[:count], refs[count:]
    value = x[...].astype(F32) + summed(own, received) + vec[2:3, :]
    hidden[...] = value
    normed, inverse = center_of(value)
    normed_out[...] = normed
    inverse_out[...] = jnp.broadcast_to(inverse, inverse_out.shape)
    low[...] = (normed * vec[3:4, :] + vec[4:5, :]).astype(BF16)


def upper_body(chunk_count, table, bias, *refs):
    chunks, refs = refs[:chunk_count], refs[chunk_count:]
    pieces, (low, activated, slope), (weight, sems) = refs[:2], refs[2:-2], refs[-2:]
    copies = row_copies(table, pieces, weight, sems)
    for copy in copies:
        copy.start()
    rows = chunks[0].shape[0]
    for k, chunk in enumerate(chunks):
        low[k * rows : (k + 1) * rows, :] = chunk[...]
    for copy in copies:
        copy.wait()
    columns = weight.shape[1]
    tile = min(TILE, columns)

    @pl.loop(0, columns // tile)
    def _(i):
        cols = pl.ds(pl.multiple_of(i * tile, tile), tile)
        value = nn(low[...], weight[:, cols]) + bias[:, cols].astype(F32)
        below = 0.5 * (1.0 + lax.erf(value * (0.5**0.5)))
        activated[:, cols] = (value * below).astype(BF16)
        density = jnp.exp(-0.5 * value * value) * 0.3989422804014327
        slope[:, cols] = below + value * density


def upper_grad_body(side_at, table, g, slope, *refs):
    pieces, (low, bias_grad), (weight, sems) = refs[:2], refs[2:-2], refs[-2:]
    copies = column_copies(table, pieces, weight, sems)
    for copy in copies:
        copy.start()
    bias_grad[...] = jnp.zeros(bias_grad.shape, F32)
    for copy in copies:
        copy.wait()
    hidden = weight.shape[0]
    tile = min(TILE, hidden)
    first = table[side_at] * hidden

    @pl.loop(0, hidden // tile)
    def _(i):
        cols = pl.ds(pl.multiple_of(i * tile, tile), tile)
        grad = nt(g[...], weight[cols, :]) * slope[:, cols]
        low[:, cols] = grad.astype(BF16)
        there = pl.ds(pl.multiple_of(first + i * tile, tile), tile)
        bias_grad[:, there] = jnp.sum(grad, axis=0, keepdims=True)


def second_back_body(count, own, g, vec, normed, inverse, *refs):
    received, (hidden_grad, low, sums) = refs[:count], refs[count:]
    total = summed(own, received)
    upstream = g[...].astype(F32)
    grad = upstream + norm_back(total, normed[...], inverse[:, 0:1], vec[3:4, :])
    hidden_grad[...] = grad
    low[...] = grad.astype(BF16)
    for i, values in enumerate((grad, total * normed[...], total, upstream)):
        sums[i : i + 1, :] = jnp.sum(values, axis=0, keepdims=True)


def attend_back_body(side_at, chunk_count, table, q, k, v, probs, *refs):
    chunks, refs = refs[:chunk_count], refs[chunk_count:]
    outs_p, ins_p, refs = refs[:2], refs[2:4], refs[4:]
    (low, q_low, k_low, v_low, bias_grad, own, mate, *sends) = refs[:-5]
    out_weight, in_weight, mixed_grad, out_sems, in_sems = refs[-5:]
    copies = column_copies(table, outs_p, out_weight, out_sems)
    for copy in copies:
        copy.start()
    size = ins_p[0].shape[2]
    ins = [
        pltpu.make_async_copy(piece, in_weight.at[:, place(table, p, size)], in_sems.at[p])
        for p, piece in enumerate(blocks_of(ins_p))
    ]
    for copy in ins:
        copy.start()
    rows = chunks[0].shape[0]
    for j, chunk in enumerate(chunks):
        low[j * rows : (j + 1) * rows, :] = chunk[...]
    bias_grad[...] = jnp.zeros(bias_grad.shape, F32)
    for copy in copies:
        copy.wait()
    columns = q.shape[1]
    tile = min(TILE, columns)
    for start in range(0, columns, tile):
        cols = slice(start, start + tile)
        mixed_grad[:, cols] = nt(low[...], out_weight[cols, :]).astype(BF16)
    heads = columns // DH
    length = probs.shape[1]
    first = table[side_at] * columns
    for h in range(heads):
        cols = slice(h * DH, (h + 1) * DH)
        q_sum = v_sum = 0.0
        for s in range(2):
            rows = slice(s * length, (s + 1) * length)
            prob, down = probs[s * heads + h], mixed_grad[rows, cols]
            prob_grad = nt(down, v[rows, cols])
            inner = jnp.sum(prob * prob_grad, axis=-1, keepdims=True)
            score_low = (prob * (prob_grad - inner) * SCALE).astype(BF16)
            query_grad = nn(score_low, k[rows, cols])
            q_low[rows, cols] = query_grad.astype(BF16)
            q_sum = q_sum + jnp.sum(query_grad, axis=0, keepdims=True)
            k_low[rows, cols] = tn(score_low, q[rows, cols]).astype(BF16)
            value_grad = tn(prob.astype(BF16), down)
            v_low[rows, cols] = value_grad.astype(BF16)
            v_sum = v_sum + jnp.sum(value_grad, axis=0, keepdims=True)
        there = pl.multiple_of(first + h * DH, DH)
        bias_grad[:, pl.ds(there, DH)] = q_sum
        bias_grad[:, pl.ds(pl.multiple_of(there + 2 * columns, DH), DH)] = v_sum
    for p, copy in enumerate(ins):
        copy.wait()
        cols = place(table, p, size)
        total = nt(q_low[...], in_weight[0, cols, :])
        total = total + nt(k_low[...], in_weight[1, cols, :])
        total = total + nt(v_low[...], in_weight[2, cols, :])
        put_chunks(total, cols, own, mate, sends)


def first_back_body(count, own, x, vec, hidden_grad, *refs):
    received, (result, sums) = refs[:count], refs[count:]
    total = summed(own, received)
    normed, inverse = center_of(x[...].astype(F32))
    grad = hidden_grad[...] + norm_back(total, normed, inverse, vec[0:1, :])
    result[...] = grad.astype(BF16)
    for i, values in enumerate((total * normed, total)):
        sums[i : i + 1, :] = jnp.sum(values, axis=0, keepdims=True)


def output_body(count, own, hidden, vec, *refs):
    received, (result,) = refs[:count], refs[count:]
    result[...] = (hidden[...] + summed(own, received) + vec[5:6, :]).astype(BF16)


def assemble_body(dp, tensor, table, *refs):
    chunks, (result,) = refs[:tensor], refs[tensor:]
    rows = chunks[0].shape[0]
    for k, chunk in enumerate(chunks):
        result[place(table, dp + k, rows), :] = chunk[...]


def grad_blocks(table, left, right, by_rows, first, chips, size, put):
    if by_rows:
        width = right[0].shape[1]
        tile = min(TILE, width)
        for block in range(chips):
            turned = left[:, place(table, first + block, size)].T
            for j, ref in enumerate(right):
                for c in range(0, width, tile):
                    put(block, 0, j * width + c, nn(turned, ref[:, c : c + tile]))
    else:
        hidden = left.shape[1]
        step = min(512, hidden)
        for r in range(0, hidden, step):
            turned = left[:, r : r + step].T
            for block in range(chips):
                put(block, r, 0, nn(turned, right[0][:, place(table, first + block, size)]))


def grad_body(by_rows, first, chips, size, count, table, left, *refs):
    right, theirs, out = refs[:count], refs[count:-1], refs[-1]

    def put(block, low, column, value):
        rows, cols = slice(low, low + value.shape[0]), slice(column, column + value.shape[1])
        for ref in theirs:
            value = value + ref[block, rows, cols].astype(F32)
        out[block, rows, cols] = value.astype(BF16)

    grad_blocks(table, left, right, by_rows, first, chips, size, put)


def finish_body(by_rows, planes, first, cols, blocks, out):
    chips, rows, _ = blocks.shape
    here = slice(first, first + cols)
    for half in range(2):
        total = blocks[half, :, here].astype(F32)
        for j in range(half + 2, chips, 2):
            total = total + blocks[j, :, here].astype(F32)
        if not by_rows:
            out[half * rows : (half + 1) * rows, :] = total
        elif planes == 1:
            out[:, half * cols : (half + 1) * cols] = total
        else:
            width = cols // planes
            for j in range(planes):
                out[j, :, half * width : (half + 1) * width] = total[:, j * width : (j + 1) * width]


def sems(*dims):
    return pltpu.SemaphoreType.DMA(tuple(dims))


class Layer:
    def __init__(self, at, length, features):
        self.at, self.table = at, at.table()
        self.length, self.features = length, features
        self.own = length // at.tensor
        self.side_at = at.dp + at.tensor

    def chunk_outs(self, split):
        count = self.at.tensor - 1
        sends = [shape((self.own, self.features), BF16)] * (2 * count)
        if not split:
            sends = [shape((2 * self.own, self.features), BF16)] * count
        return [shape((self.own, self.features), F32)] * 2 + sends

    def collect(self, name, own, vec, chunks, norm):
        at = self.at
        return call(
            functools.partial(collect_body, at.dp, at.tensor, norm),
            name,
            [SMEM] + [VMEM] * (2 + at.tensor),
            [shape((2 * self.length, self.features), BF16)],
            [],
            20 * self.length * self.features,
            [self.table, own, vec] + chunks,
        )[0]

    def project(self, name, left, blocks, by_rows, split):
        inner = left.shape[1]
        weight = (self.features, inner) if by_rows else (inner, self.features)
        return call(
            functools.partial(project_body, by_rows),
            name,
            [SMEM, VMEM] + [ANY] * 2,
            self.chunk_outs(split),
            [pltpu.VMEM(weight, BF16), sems(self.at.dp)],
            4 * self.length * inner * self.features,
            [self.table, left] + blocks,
        )

    def fold(self, name, mate, received):
        return call(
            fold_body,
            name,
            [VMEM] * (1 + len(received)),
            [shape(mate.shape, BF16)],
            [],
            mate.size * 4,
            [mate] + received,
        )[0]

    def trade(self, part, split):
        count = self.at.tensor - 1
        if not split:
            received = self.at.to_peers(part[2:])
            return received, received
        return self.at.to_peers(part[2 + count :]), self.at.to_peers(part[2 : 2 + count])

    def reduce(self, name, part, traded):
        for_mate, others = traded
        folded = self.fold(name + "_fold", part[1], for_mate)
        return others + [self.at.to_mate(folded)], folded

    def block_shape(self, left, right, by_rows):
        size = self.features // self.at.dp
        if by_rows:
            return size, (size, sum(r.shape[1] for r in right))
        return size, (left.shape[1], size)

    def grad(self, name, left, right, by_rows, *theirs):
        chips = self.at.chips
        size, block = self.block_shape(left, right, by_rows)
        return call(
            functools.partial(grad_body, by_rows, 0 if theirs else chips, chips, size, len(right)),
            name + ("_near" if theirs else "_far"),
            [SMEM] + [VMEM] * (1 + len(right) + len(theirs)),
            [shape((chips,) + block, BF16)],
            [],
            4 * self.length * chips * block[0] * block[1],
            [self.table, left] + list(right) + list(theirs),
        )[0]

    def grad_far(self, name, left, right, by_rows):
        return self.grad(name, left, right, by_rows)

    def grad_near(self, name, left, right, by_rows, theirs):
        return self.grad(name, left, right, by_rows, theirs)

    def grad_finish(self, name, blocks, by_rows, where, planes=1):
        _, rows, width = blocks.shape
        first, cols = where[0] % width, where[1]
        out = (rows, 2 * cols) if by_rows else (2 * rows, cols)
        if planes > 1:
            out = (planes, rows, 2 * cols // planes)
        return call(
            functools.partial(finish_body, by_rows, planes, first, cols),
            name + "_finish",
            [VMEM],
            [shape(out, F32)],
            [],
            blocks.size,
            [blocks],
        )[0]


def shards(
    dp,
    tensor,
    inputs,
    segment_ids,
    first_gain,
    first_shift,
    project_in,
    query_bias,
    value_bias,
    project_out,
    out_bias,
    second_gain,
    second_shift,
    up_weight,
    up_bias,
    down_weight,
    down_bias,
    cotangent,
):
    at = Places(dp, tensor)
    length, features = inputs.shape
    layer = Layer(at, length, features)
    own, table, side_at = layer.own, layer.table, layer.side_at
    heads, hidden_units = query_bias.shape[0] // 2, up_bias.shape[0] // 2
    both = 2 * length
    chunk_count, size = 2 * tensor, features // dp
    chunk32, chunk16 = shape((own, features), F32), shape((own, features), BF16)
    tokens16 = shape((both, features), BF16)

    x_own, g_own = at.chunk_of(inputs), at.chunk_of(cotangent)
    mate = at.to_mate(jnp.concatenate([x_own, g_own]))
    ids = at.tokens_in(segment_ids)
    mate_ids = at.to_mate(ids)
    mine_in = at.exchange(after(at.halves(project_in, 2), mate, mate_ids))
    mate_chunks = [mate] + at.to_peers(mate)
    out_blocks, up_blocks = at.halves(project_out, 0), at.halves(up_weight, 1)
    down_blocks = at.halves(down_weight, 0)
    mate_chunks = after(mate_chunks, out_blocks, up_blocks, down_blocks)
    vec = jnp.stack(
        [
            first_gain,
            first_shift,
            out_bias,
            second_gain,
            second_shift,
            down_bias,
            down_bias,
            down_bias,
        ]
    ).astype(F32)
    biases = [at.half_of(b)[None] for b in (query_bias, value_bias, up_bias)]
    order = at.tokens_in(jnp.arange(length, dtype=jnp.int32))
    ids = jnp.stack([ids, mate_ids])
    allowed = (
        (ids[:, :, None] == ids[:, None, :])
        & (ids[:, :, None] != 0)
        & (order[None, None, :] <= order[None, :, None])
    )
    allowed = (allowed | (order[None, None, :] == order[None, :, None])).astype(F32)
    first_low = layer.collect("first_norm", inputs, vec, mate_chunks, True)
    g = layer.collect("upstream", cotangent, vec, mate_chunks, False)
    mine_in = after(mine_in, first_low, allowed, biases, g)
    mine_out = at.exchange(after(out_blocks, mine_in))

    all_in = at.both_cores(mine_in)
    low_heads = shape((both, heads), BF16)
    query, key, value, probs, mixed = call(
        attend_body,
        "attend",
        [SMEM] + [VMEM] * 4 + [ANY] * 2,
        [low_heads] * 3 + [shape((2 * heads // DH, length, length), F32), low_heads],
        [pltpu.VMEM((3, features, heads), BF16), sems(3, dp)],
        12 * length * heads * features,
        [table, first_low, biases[0], biases[1], allowed] + all_in,
    )
    mine_out = after(mine_out, mixed)
    mine_up = at.exchange(after(up_blocks, mine_out))
    all_out = at.both_cores(mine_out)
    part = layer.project("project_out", mixed, all_out, False, True)
    received, _ = layer.reduce("project_out", part, layer.trade(part, True))
    hidden, normed_two, inverse_two, second_own = call(
        functools.partial(second_body, len(received)),
        "second_norm",
        [VMEM] * (3 + len(received)),
        [chunk32, chunk32, shape((own, 128), F32), chunk16],
        [],
        20 * own * features,
        [part[0], x_own, vec] + received,
    )
    second_chunks = at.spread(second_own)
    mine_up = after(mine_up, second_own)
    mine_down = at.exchange(after(down_blocks, mine_up, second_chunks[tensor]))
    all_up = at.both_cores(mine_up)
    second_low, activated, slope = call(
        functools.partial(upper_body, chunk_count),
        "upper",
        [SMEM] + [VMEM] * (1 + chunk_count) + [ANY] * 2,
        [tokens16, shape((both, hidden_units), BF16), shape((both, hidden_units), F32)],
        [pltpu.VMEM((features, hidden_units), BF16), sems(dp)],
        4 * length * features * hidden_units,
        [table, biases[2]] + second_chunks + all_up,
    )
    far_down = layer.grad_far("grad_down", activated, [g], False)
    near_down = layer.grad_near("grad_down", activated, [g], False, at.to_core(far_down))
    mine_down = after(mine_down, near_down)
    ring_down = at.exchange(after(near_down, mine_down))
    all_down = at.both_cores(mine_down)
    upper_low, up_bias_grad = call(
        functools.partial(upper_grad_body, side_at),
        "upper_grad",
        [SMEM] + [VMEM] * 2 + [ANY] * 2,
        [shape((both, hidden_units), BF16), shape((1, 2 * hidden_units), F32)],
        [pltpu.VMEM((hidden_units, features), BF16), sems(dp)],
        4 * length * features * hidden_units,
        [table, g, slope] + all_down,
    )
    part = layer.project("second_part", upper_low, all_up, True, True)
    traded = layer.trade(part, True)
    far_up = layer.grad_far("grad_up", second_low, after([upper_low], traded[0][0]), True)
    received, folded = layer.reduce("second_part", part, traded)
    near_up = layer.grad_near(
        "grad_up", second_low, after([upper_low], folded), True, at.to_core(far_up)
    )
    hidden_grad, hidden_low_own, sums_two = call(
        functools.partial(second_back_body, len(received)),
        "second_back",
        [VMEM] * (5 + len(received)),
        [chunk32, chunk16, shape((8, features), F32)],
        [],
        20 * own * features,
        [after(part[0], near_up), g_own, vec, normed_two, inverse_two] + received,
    )
    hidden_chunks = at.spread(hidden_low_own)
    ring_up = at.exchange(after(near_up, ring_down, hidden_chunks[tensor]))
    feed = layer.project("feed", after(activated, hidden_low_own), all_down, False, False)
    feed_traded = layer.trade(after(feed, hidden_chunks), False)
    back = call(
        functools.partial(attend_back_body, side_at, chunk_count),
        "attend_back",
        [SMEM] + [VMEM] * (4 + chunk_count) + [ANY] * 4,
        [tokens16, low_heads, low_heads, low_heads, shape((1, 4 * heads), F32)]
        + layer.chunk_outs(True),
        [
            pltpu.VMEM((heads, features), BF16),
            pltpu.VMEM((3, features, heads), BF16),
            pltpu.VMEM((both, heads), BF16),
            sems(dp),
            sems(dp),
        ],
        16 * length * heads * features,
        [table, after(query, feed, ring_down), key, value, probs]
        + hidden_chunks
        + all_out
        + all_in,
    )
    hidden_low, q_low, k_low, v_low, heads_grad, *part = back
    lows = [q_low, k_low, v_low]
    part, feed_traded = after(part, feed_traded), after(feed_traded, part)
    traded = layer.trade(part, True)
    feed_received, feed_folded = layer.reduce("feed", feed, feed_traded)
    far_in = layer.grad_far("grad_in", first_low, after(lows, feed_folded, traded[0][0]), True)
    far_out = layer.grad_far("grad_out", mixed, after([hidden_low], far_in), False)
    received, folded = layer.reduce("first_part", part, traded)
    near_in = layer.grad_near(
        "grad_in", first_low, after(lows, far_out, folded, traded[1][0]), True, at.to_core(far_in)
    )
    near_out = layer.grad_near(
        "grad_out", mixed, after([hidden_low], near_in), False, at.to_core(far_out)
    )
    width = near_in.shape[2]
    if near_in.shape[1] == near_out.shape[1]:
        blocks = jnp.concatenate([near_in, near_out], 2)
        ring_in = ring_out = at.exchange(after(blocks, ring_up, received[-1]))
    else:
        ring_in = at.exchange(after(near_in, ring_up, received[-1]))
        ring_out = at.exchange(after(near_out, ring_in))
    input_own, sums_one = call(
        functools.partial(first_back_body, len(received)),
        "first_back",
        [VMEM] * (4 + len(received)),
        [chunk16, shape((8, features), F32)],
        [],
        20 * own * features,
        [part[0], x_own, vec, hidden_grad] + received,
    )
    outputs_own = call(
        functools.partial(output_body, len(feed_received)),
        "outputs_own",
        [VMEM] * (3 + len(feed_received)),
        [chunk16],
        [],
        4 * own * features,
        [feed[0], hidden, vec] + feed_received,
    )[0]

    def assemble(name, chunk):
        return call(
            functools.partial(assemble_body, dp, tensor),
            name,
            [SMEM] + [VMEM] * tensor,
            [shape((length, features), BF16)],
            [],
            length * features,
            [table, chunk] + at.to_peers(chunk),
        )[0]

    input_gradient = assemble("input_gradient", input_own)
    outputs = assemble("outputs", outputs_own)
    grad_down = layer.grad_finish("grad_down", ring_down, False, (0, size))
    grad_up = layer.grad_finish("grad_up", ring_up, True, (0, hidden_units))
    grad_out = layer.grad_finish("grad_out", ring_out, False, (-size, size))
    grad_in = layer.grad_finish("grad_in", ring_in, True, (0, width), 3)

    narrow = jnp.concatenate([heads_grad[0], up_bias_grad[0]])
    rows = -(-narrow.shape[0] // features)
    narrow = jnp.pad(narrow, (0, rows * features - narrow.shape[0])).reshape(rows, features)
    sums = at.sum_small(jnp.concatenate([sums_one[:2], sums_two[:4]]), narrow)
    narrow = sums[6:].reshape(-1)
    heads, hidden_units = 2 * heads, 2 * hidden_units
    return (
        outputs,
        input_gradient,
        sums[0],
        sums[1],
        grad_in,
        narrow[:heads],
        narrow[heads : 2 * heads],
        grad_out,
        sums[2],
        sums[3],
        sums[4],
        grad_up,
        narrow[2 * heads : 2 * heads + hidden_units],
        grad_down,
        sums[5],
    )


def solution(mesh):
    dp, tensor = mesh.shape["dp"], mesh.shape["tensor"]

    def program(*arguments):
        return shards(dp, tensor, *arguments)

    in_specs = (
        P("dp", None),
        P("dp"),
        P(),
        P(),
        P(None, "dp", "tensor"),
        P("tensor"),
        P("tensor"),
        P("tensor", "dp"),
        P(),
        P(),
        P(),
        P("dp", "tensor"),
        P("tensor"),
        P("tensor", "dp"),
        P(),
        P("dp", None),
    )
    out_specs = (
        P("dp", None),
        P("dp", None),
        P(),
        P(),
        P(None, "dp", "tensor"),
        P("tensor"),
        P("tensor"),
        P("tensor", "dp"),
        P(),
        P(),
        P(),
        P("dp", "tensor"),
        P("tensor"),
        P("tensor", "dp"),
        P(),
    )
    return jax.shard_map(program, mesh=mesh, in_specs=in_specs, out_specs=out_specs, check_vma=False)
```

time: 1120 us -> 474 us (0.42)
  waiting for transfers between devices: 941 us -> 174 us
  Pallas kernels: 0 us -> 143 us
  starting transfers between devices: 1.15 us -> 110 us
  matrix products: 89.2 us -> 0 us
  blocking collectives: 27.4 us -> 0 us
  between operations: 14.6 us -> 1.91 us
  other arithmetic: 23.1 us -> 11.7 us
    reduce_scatter x4 -> x0, waiting for transfers between devices: 483 us -> none  [the longest x1 170 us: shards(): lax.psum_scatter(grad_up, 'dp', scatter_dimension=0, tiled=True)]
    all_gather x4 -> x0, waiting for transfers between devices: 239 us -> none  [the longest x1 78.5 us: shards(): lax.all_gather(up_weight, 'dp', axis=0, tiled=True)]
    psum x4 -> x0, waiting for transfers between devices: 216 us -> none  [the longest x1 65.4 us: shards(): attention = lax.psum(attention_part, 'tensor')]
    ppermute x0 -> x63, waiting for transfers between devices: none -> 163 us  [the longest x44 129 us: to_peer(): lax.ppermute(values, 'tensor', [(i, i ^ k) for i in range(self.tensor)])]
    pallas_call x0 -> x31, Pallas kernels: none -> 143 us  [call(): pl.pallas_call(body, name=name, out_shape=outs, in_specs=in_specs, out_sp...]
    dot_general x20 -> x0, matrix products: 89.2 us -> none  [the longest x1 11.1 us: shards(): jnp.einsum('rd,fd->rf', cotangent, full_down, preferred_element_type=jnp....]
    ppermute x0 -> x63, starting transfers between devices: none -> 66.3 us  [the longest x44 49.1 us: to_peer(): lax.ppermute(values, 'tensor', [(i, i ^ k) for i in range(self.tensor)])]
    all_to_all x0 -> x7, starting transfers between devices: none -> 43.5 us  [exchange(): lax.all_to_all(blocks, 'dp', 0, 0, axis_index_groups=groups, tiled=True)]
  transfers between devices with their start and end apart: 12 -> 70, of which waited for: 12 -> 36; matrix products, arithmetic and copies ran while one was open for 7% -> 4% of each run, Pallas kernels for 0% -> 30%
where the time goes in v3:
time: 474 us; the launch traced here: 464 us
  waiting for transfers between devices  174 us (37%)
  Pallas kernels  143 us (30%)
  starting transfers between devices  110 us (23%)
  local copies, waits for them, and re-layouts  24.1 us (5%)
  other arithmetic  11.7 us (2%)
    pallas_call x31, Pallas kernels, call(): pl.pallas_call(body, name=name, out_shape=outs, in_specs=in_specs, out_sp...  143 us
    ppermute x44, waiting for transfers between devices, to_peer(): lax.ppermute(values, 'tensor', [(i, i ^ k) for i in range(self.tensor)])  129 us
    ppermute x44, starting transfers between devices, to_peer(): lax.ppermute(values, 'tensor', [(i, i ^ k) for i in range(self.tensor)])  49.1 us
    all_to_all x7, starting transfers between devices, exchange(): lax.all_to_all(blocks, 'dp', 0, 0, axis_index_groups=groups, tiled=True)  43.5 us
    ppermute x10, waiting for transfers between devices, to_chip(): return lax.ppermute(values, 'dp', [(i, i ^ 2 * k) for i in range(self.dp)])  28 us
    unnamed x158, local copies, waits for them, and re-layouts  16.6 us
    ppermute x10, starting transfers between devices, to_chip(): return lax.ppermute(values, 'dp', [(i, i ^ 2 * k) for i in range(self.dp)])  16.5 us
    all_to_all x7, waiting for transfers between devices, exchange(): lax.all_to_all(blocks, 'dp', 0, 0, axis_index_groups=groups, tiled=True)  10.6 us
  transfers between devices with their start and end apart: 70, of which 36 were waited for; matrix products, arithmetic and copies ran while one was open for 4% of the time, Pallas kernels for 30%

profile of v3, /device:TPU:8, one launch (start us, length us, event | category | flops | bytes accessed | tf_op | source)
XLA Modules:
  0.0 464.3 jit_solution(16454140516679209224)
XLA Ops:
  7.7 9.0 %collective-permute-done.4 = s32[256]{0:T(256)S(1)} collective-permute-done((s32[256]{0:T(256)S(1)}, s32[256]{0:T(256)S(1)}, u32[]{:S(2)}, u32[]{:S(2)}) %collective-permute-start.4) | collective-permute-done | bytes 1056 | tf_op jit(solution)/shard_map/ppermute | solution.py:88
  16.7 5.3 %all-to-all-start = ((bf16[4,3,256,256]{3,2,1,0:T(8,128)(2,1)}), bf16[4,3,256,256]{3,2,1,0:T(8,128)(2,1)S(1)}, u32[]{:S(2)}, u32[]{:S(2)}) async-start(bf16[4,3,256,256]{3,2,1,0:T(8,128)(2,1)} %pad_maximum_fusion.3), calls=%async_computation | async-start | bytes 3145728 | tf_op jit(solution)/shard_map/all_to_all | solution.py:105
  34.6 9.7 %collective-permute-done.1.refs_1_ = bf16[128,2048]{1,0:T(8,128)(2,1)S(1)} collective-permute-done((bf16[128,2048]{1,0:T(8,128)(2,1)S(1)}, bf16[128,2048]{1,0:T(8,128)(2,1)S(1)}, u32[]{:S(2)}, u32[]{:S(2)}) %collective-permute-start.1) | collective-permute-done | bytes 524320 | tf_op jit(solution)/shard_map/ppermute | solution.py:94
  44.2 9.9 %collective-permute-done.2.refs_2_ = bf16[128,2048]{1,0:T(8,128)(2,1)S(1)} collective-permute-done((bf16[128,2048]{1,0:T(8,128)(2,1)S(1)}, bf16[128,2048]{1,0:T(8,128)(2,1)S(1)}, u32[]{:S(2)}, u32[]{:S(2)}) %collective-permute-start.2) | collective-permute-done | bytes 524320 | tf_op jit(solution)/shard_map/ppermute | solution.py:94
  58.3 4.8 %first_norm.1.x.left = bf16[512,2048]{1,0:T(8,128)(2,1)} custom-call(s32[13]{0:T(128)} %pad_add_fusion.1.table, bf16[256,2048]{1,0:T(8,128)(2,1)} %own.2, f32[8,2048]{1,0:T(8,128)} %convert_element_type.8.vec, bf16[128,2048]{1,0:T(8,128)(2,1)} %copy-done.12, bf16[128,2048]{1,0:T(8,128)(2,1)} %copy-done.13, bf16[128,2048]{1,0:T(8,128)(2,1)} %copy-done.14, ...), custom_call_target="tpu_custom_call" | custom-call | flops 10485760 | bytes 5308468 | tf_op jit(solution)/shard_map/first_norm/pallas_call | solution.py:41
  63.1 5.1 %all-to-all-start.1 = ((bf16[4,256,256]{2,1,0:T(8,128)(2,1)}), bf16[4,256,256]{2,1,0:T(8,128)(2,1)S(1)}, u32[]{:S(2)}, u32[]{:S(2)}) async-start(bf16[4,256,256]{2,1,0:T(8,128)(2,1)} %pad_maximum_fusion.5), calls=%async_computation.1 | async-start | bytes 1048576 | tf_op jit(solution)/shard_map/all_to_all | solution.py:105
  68.2 8.9 %attend.1 = (bf16[512,256]{1,0:T(8,128)(2,1)}, bf16[512,256]{1,0:T(8,128)(2,1)}, bf16[512,256]{1,0:T(8,128)(2,1)}, f32[4,256,256]{2,1,0:T(8,128)}, bf16[512,256]{1,0:T(8,128)(2,1)}) custom-call(s32[13]{0:T(128)} %pad_add_fusion.1.table, bf16[512,2048]{1,0:T(8,128)(2,1)} %first_norm.1.x.left, bf16[1,256]{1,0:T(2,128)(2,1)} %broadcast_in_dim.26.q_bias, ...), custom_call_target="tpu_custom_call" | custom-call | flops 1610612736 | bytes 7865396 | tf_op jit(solution)/shard_map/attend/pallas_call | solution.py:41
  80.1 6.8 %all-to-all-start.2 = ((bf16[4,256,1024]{2,1,0:T(8,128)(2,1)}), bf16[4,256,1024]{2,1,0:T(8,128)(2,1)S(1)}, u32[]{:S(2)}, u32[]{:S(2)}) async-start(bf16[4,256,1024]{2,1,0:T(8,128)(2,1)} %pad_maximum_fusion), calls=%async_computation.2 | async-start | bytes 4194304 | tf_op jit(solution)/shard_map/all_to_all | solution.py:105
  89.7 5.7 %project_out.1 = (f32[64,2048]{1,0:T(8,128)}, f32[64,2048]{1,0:T(8,128)}, bf16[64,2048]{1,0:T(8,128)(2,1)}, bf16[64,2048]{1,0:T(8,128)(2,1)}, bf16[64,2048]{1,0:...) custom-call(s32[13]{0:T(128)} %pad_add_fusion.1.table, ...), custom_call_target="tpu_custom_call" | custom-call | flops 536870912 | bytes 3932212 | tf_op jit(solution)/shard_map/project_out/pallas_call | solution.py:41
  116.1 5.8 %collective-permute-done.9.refs_2_ = bf16[64,2048]{1,0:T(8,128)(2,1)} collective-permute-done((bf16[64,2048]{1,0:T(8,128)(2,1)}, bf16[64,2048]{1,0:T(8,128)(2,1)}, u32[]{:S(2)}, u32[]{:S(2)}) %collective-permute-start.9) | collective-permute-done | bytes 262176 | tf_op jit(solution)/shard_map/ppermute | solution.py:94
  121.9 4.8 %collective-permute-done.13.refs_3_ = bf16[64,2048]{1,0:T(8,128)(2,1)S(1)} collective-permute-done((bf16[64,2048]{1,0:T(8,128)(2,1)}, bf16[64,2048]{1,0:T(8,128)(2,1)S(1)}, u32[]{:S(2)}, u32[]{:S(2)}) %collective-permute-start.13) | collective-permute-done | bytes 262176 | tf_op jit(solution)/shard_map/ppermute | solution.py:88
  147.9 7.9 %all-to-all-start.3 = ((bf16[4,1024,256]{2,1,0:T(8,128)(2,1)}), bf16[4,1024,256]{2,1,0:T(8,128)(2,1)}, u32[]{:S(2)}, u32[]{:S(2)}) async-start(bf16[4,1024,256]{2,1,0:T(8,128)(2,1)} %pad_maximum_fusion.1), calls=%async_computation.3 | async-start | bytes 4194304 | tf_op jit(solution)/shard_map/all_to_all | solution.py:105
  159.3 5.7 %collective-permute-done.18.refs_5_ = bf16[64,2048]{1,0:T(8,128)(2,1)S(1)} collective-permute-done((bf16[64,2048]{1,0:T(8,128)(2,1)S(1)}, bf16[64,2048]{1,0:T(8,128)(2,1)S(1)}, u32[]{:S(2)}, u32[]{:S(2)}) %collective-permute-start.18) | collective-permute-done | bytes 262176 | tf_op jit(solution)/shard_map/ppermute | solution.py:94
  170.1 8.8 %upper.1 = (bf16[512,2048]{1,0:T(8,128)(2,1)}, bf16[512,1024]{1,0:T(8,128)(2,1)}, f32[512,1024]{1,0:T(8,128)}) custom-call(s32[13]{0:T(128)} %pad_add_fusion.1.table, bf16[1,1024]{1,0:T(2,128)(2,1)} %broadcast_in_dim.25.bias, bf16[64,2048]{1,0:T(8,128)(2,1)} %get-tuple-element.133.refs_0_, bf16[64,2048]{1,0:T(8,128)(2,1)} %copy-done.68, ...), custom_call_target="tpu_custom_call" | custom-call | flops 2147483648 | bytes 11536436 | tf_op jit(solution)/shard_map/upper/pallas_call | solution.py:41
  189.3 5.2 %grad_down_near.1 = bf16[4,1024,256]{2,1,0:T(8,128)(2,1)} custom-call(s32[13]{0:T(128)} %pad_add_fusion.1.table, bf16[512,1024]{1,0:T(8,128)(2,1)} %get-tuple-element.157.left, bf16[512,2048]{1,0:T(8,128)(2,1)} %upstream.1.refs_0_.g, bf16[4,1024,256]{2,1,0:T(8,128)(2,1)} %copy-done.11), custom_call_target="tpu_custom_call" | custom-call | flops 1073741824 | bytes 7340084 | tf_op jit(solution)/shard_map/grad_down_near/pallas_call | solution.py:41
  194.5 6.3 %all-to-all-done.3.refs_0_ = bf16[4,1024,256]{2,1,0:T(8,128)(2,1)} async-done(((bf16[4,1024,256]{2,1,0:T(8,128)(2,1)}), bf16[4,1024,256]{2,1,0:T(8,128)(2,1)}, u32[]{:S(2)}, u32[]{:S(2)}) %all-to-all-start.3) | async-done | bytes 2097184 | tf_op jit(solution)/shard_map/all_to_all | solution.py:105
  200.8 7.0 %all-to-all-start.4 = ((bf16[4,1024,256]{2,1,0:T(8,128)(2,1)}), bf16[4,1024,256]{2,1,0:T(8,128)(2,1)S(1)}, u32[]{:S(2)}, u32[]{:S(2)}) async-start(bf16[4,1024,256]{2,1,0:T(8,128)(2,1)} %grad_down_near.1), calls=%async_computation.4 | async-start | bytes 4194304 | tf_op jit(solution)/shard_map/all_to_all | solution.py:105
  207.7 8.5 %upper_grad.1 = (bf16[512,1024]{1,0:T(8,128)(2,1)}, f32[1,2048]{1,0:T(1,128)}) custom-call(s32[13]{0:T(128)} %pad_add_fusion.1.table, bf16[512,2048]{1,0:T(8,128)(2,1)} %upstream.1.refs_0_.g, f32[512,1024]{1,0:T(8,128)} %get-tuple-element.138.slope, bf16[4,1024,256]{2,1,0:T(8,128)(2,1)} %all-to-all-done.3.refs_0_, ...), custom_call_target="tpu_custom_call" | custom-call | flops 2147483648 | bytes 9445428 | tf_op jit(solution)/shard_map/upper_grad/pallas_call | solution.py:41
  216.2 9.6 %second_part.1 = (f32[64,2048]{1,0:T(8,128)}, f32[64,2048]{1,0:T(8,128)}, bf16[64,2048]{1,0:T(8,128)(2,1)}, bf16[64,2048]{1,0:T(8,128)(2,1)}, bf16[64,2048]{1,0:...) custom-call(s32[13]{0:T(128)} %pad_add_fusion.1.table, ...), custom_call_target="tpu_custom_call" | custom-call | flops 2147483648 | bytes 7864372 | tf_op jit(solution)/shard_map/second_part/pallas_call | solution.py:41
  226.5 8.1 %collective-permute-done.24.refs_0_ = bf16[64,2048]{1,0:T(8,128)(2,1)S(1)} collective-permute-done((bf16[64,2048]{1,0:T(8,128)(2,1)}, bf16[64,2048]{1,0:T(8,128)(2,1)S(1)}, u32[]{:S(2)}, u32[]{:S(2)}) %collective-permute-start.24) | collective-permute-done | bytes 262176 | tf_op jit(solution)/shard_map/ppermute | solution.py:94
  243.3 10.8 %collective-permute-done.25.refs_1_ = bf16[64,2048]{1,0:T(8,128)(2,1)S(1)} collective-permute-done((bf16[64,2048]{1,0:T(8,128)(2,1)S(1)}, bf16[64,2048]{1,0:T(8,128)(2,1)S(1)}, u32[]{:S(2)}, u32[]{:S(2)}) %collective-permute-start.25) | collective-permute-done | bytes 262176 | tf_op jit(solution)/shard_map/ppermute | solution.py:94
  259.2 5.2 %grad_up_near.1 = bf16[4,256,1024]{2,1,0:T(8,128)(2,1)} custom-call(s32[13]{0:T(128)} %pad_add_fusion.1.table, bf16[512,2048]{1,0:T(8,128)(2,1)} %get-tuple-element.143.left, bf16[512,1024]{1,0:T(8,128)(2,1)} %get-tuple-element.149.left.refs_0_, bf16[4,256,1024]{2,1,0:T(8,128)(2,1)} %collective-permute-done.27.refs_1_), custom_call_target="tpu_custom_call" | custom-call | flops 1073741824 | bytes 7340084 | tf_op jit(solution)/shard_map/grad_up_near/pallas_call | solution.py:41
  273.6 5.1 %collective-permute-done.32.refs_1_ = bf16[64,2048]{1,0:T(8,128)(2,1)S(1)} collective-permute-done((bf16[64,2048]{1,0:T(8,128)(2,1)}, bf16[64,2048]{1,0:T(8,128)(2,1)S(1)}, u32[]{:S(2)}, u32[]{:S(2)}) %collective-permute-start.32) | collective-permute-done | bytes 262176 | tf_op jit(solution)/shard_map/ppermute | solution.py:94
  282.6 5.5 %all-to-all-start.5 = ((bf16[4,256,1024]{2,1,0:T(8,128)(2,1)}), bf16[4,256,1024]{2,1,0:T(8,128)(2,1)}, u32[]{:S(2)}, u32[]{:S(2)}) async-start(bf16[4,256,1024]{2,1,0:T(8,128)(2,1)} %grad_up_near.1), calls=%async_computation.5 | async-start | bytes 4194304 | tf_op jit(solution)/shard_map/all_to_all | solution.py:105
  291.6 9.3 %feed.1 = (f32[64,2048]{1,0:T(8,128)}, f32[64,2048]{1,0:T(8,128)}, bf16[128,2048]{1,0:T(8,128)(2,1)}, bf16[128,2048]{1,0:T(8,128)(2,1)}, bf16[128,2048]{1,0:T(8,128)(2,1)}) custom-call(s32[13]{0:T(128)} %pad_add_fusion.1.table, bf16[512,1024]{1,0:T(8,128)(2,1)} %get-tuple-element.157.left, bf16[4,1024,256]{2,1,0:T(8,128)(2,1)} %all-to-all-done.3.refs_0_, ...), custom_call_target="tpu_custom_call" | custom-call | flops 2147483648 | bytes 7864372 | tf_op jit(solution)/shard_map/feed/pallas_call | solution.py:41
  305.2 14.1 %attend_back.1 = (bf16[512,2048]{1,0:T(8,128)(2,1)}, bf16[512,256]{1,0:T(8,128)(2,1)}, bf16[512,256]{1,0:T(8,128)(2,1)}, bf16[512,256]{1,0:T(8,128)(2,1)}, f32[1...) custom-call(s32[13]{0:T(128)} %pad_add_fusion.1.table, ...), custom_call_target="tpu_custom_call" | custom-call | flops 2147483648 | bytes 13635636 | tf_op jit(solution)/shard_map/attend_back/pallas_call | solution.py:41
  319.3 5.3 %collective-permute-done.40.refs_1_ = bf16[128,2048]{1,0:T(8,128)(2,1)S(1)} collective-permute-done((bf16[128,2048]{1,0:T(8,128)(2,1)}, bf16[128,2048]{1,0:T(8,128)(2,1)S(1)}, u32[]{:S(2)}, u32[]{:S(2)}) %collective-permute-start.40) | collective-permute-done | bytes 524320 | tf_op jit(solution)/shard_map/ppermute | solution.py:94
  343.2 10.6 %collective-permute-done.50.refs_1_ = bf16[64,2048]{1,0:T(8,128)(2,1)S(1)} collective-permute-done((bf16[64,2048]{1,0:T(8,128)(2,1)}, bf16[64,2048]{1,0:T(8,128)(2,1)S(1)}, u32[]{:S(2)}, u32[]{:S(2)}) %collective-permute-start.50) | collective-permute-done | bytes 262176 | tf_op jit(solution)/shard_map/ppermute | solution.py:94
  370.3 6.0 %all-to-all-start.6 = ((bf16[4,256,1024]{2,1,0:T(8,128)(2,1)}), bf16[4,256,1024]{2,1,0:T(8,128)(2,1)S(1)}, u32[]{:S(2)}, u32[]{:S(2)}) async-start(bf16[4,256,1024]{2,1,0:T(8,128)(2,1)} %pad_maximum_fusion.2), calls=%async_computation.6 | async-start | bytes 4194304 | tf_op jit(solution)/shard_map/all_to_all | solution.py:105
  378.6 10.0 %collective-permute-done.47.refs_1_ = bf16[64,2048]{1,0:T(8,128)(2,1)S(1)} collective-permute-done((bf16[64,2048]{1,0:T(8,128)(2,1)S(1)}, bf16[64,2048]{1,0:T(8,128)(2,1)S(1)}, u32[]{:S(2)}, u32[]{:S(2)}) %collective-permute-start.47) | collective-permute-done | bytes 262176 | tf_op jit(solution)/shard_map/ppermute | solution.py:94
  402.0 13.3 %collective-permute-done.42.refs_3_ = bf16[64,2048]{1,0:T(8,128)(2,1)S(1)} collective-permute-done((bf16[64,2048]{1,0:T(8,128)(2,1)S(1)}, bf16[64,2048]{1,0:T(8,128)(2,1)S(1)}, u32[]{:S(2)}, u32[]{:S(2)}) %collective-permute-start.42) | collective-permute-done | bytes 262176 | tf_op jit(solution)/shard_map/ppermute | solution.py:88
  434.9 8.9 %collective-permute-start.60 = (f32[8,2048]{1,0:T(8,128)S(1)}, f32[8,2048]{1,0:T(8,128)S(1)}, u32[]{:S(2)}, u32[]{:S(2)}) collective-permute-start(f32[8,2048]{1,0:T(8,128)S(1)} %add.64), channel_id=1, source_target_pairs={{0,16},{4,20},{8,24},{12,28},{16,0},{20,4},{24,8},{28,12},{1,17},{... | collective-permute-start | bytes 196616 | tf_op jit(solution)/shard_map/ppermute | solution.py:88
  (354 shorter events, 215.8 us)
Async XLA Ops:
  16.7 46.3 %all-to-all-start = ((bf16[4,3,256,256]{3,2,1,0:T(8,128)(2,1)}), bf16[4,3,256,256]{3,2,1,0:T(8,128)(2,1)S(1)}, u32[]{:S(2)}, u32[]{:S(2)}) async-start(bf16[4,3,256,256]{3,2,1,0:T(8,128)(2,1)} %pad_maximum_fusion.3), calls=%async_computation | async-start | bytes 3145728 | tf_op jit(solution)/shard_map/all_to_all | solution.py:105
  29.4 14.9 %collective-permute-start.1 = (bf16[128,2048]{1,0:T(8,128)(2,1)S(1)}, bf16[128,2048]{1,0:T(8,128)(2,1)S(1)}, u32[]{:S(2)}, u32[]{:S(2)}) collective-permute-start(bf16[128,2048]{1,0:T(8,128)(2,1)S(1)} %collective-permute-done.refs_0_), channel_id=1, source_target_pairs={{0,1},{1,0},{2,3},{3,2},{4,5},{5,4},{6,7},{7,6},{8,9},{9,8},{10,11... | collective-permute-start | bytes 1572872 | tf_op jit(solution)/shard_map/ppermute | solution.py:94
  30.9 23.2 %collective-permute-start.2 = (bf16[128,2048]{1,0:T(8,128)(2,1)S(1)}, bf16[128,2048]{1,0:T(8,128)(2,1)S(1)}, u32[]{:S(2)}, u32[]{:S(2)}) collective-permute-start(bf16[128,2048]{1,0:T(8,128)(2,1)S(1)} %collective-permute-done.refs_0_), channel_id=1, source_target_pairs={{0,2},{1,3},{2,0},{3,1},{4,6},{5,7},{6,4},{7,5},{8,10},{9,11},{10,... | collective-permute-start | bytes 1572872 | tf_op jit(solution)/shard_map/ppermute | solution.py:94
  32.5 21.6 %collective-permute-start.3 = (bf16[128,2048]{1,0:T(8,128)(2,1)S(1)}, bf16[128,2048]{1,0:T(8,128)(2,1)}, u32[]{:S(2)}, u32[]{:S(2)}) collective-permute-start(bf16[128,2048]{1,0:T(8,128)(2,1)S(1)} %collective-permute-done.refs_0_), channel_id=1, source_target_pairs={{0,3},{1,2},{2,1},{3,0},{4,7},{5,6},{6,5},{7,4},{8,11},{9,10},{10,... | collective-permute-start | bytes 1572872 | tf_op jit(solution)/shard_map/ppermute | solution.py:94
  63.1 17.0 %all-to-all-start.1 = ((bf16[4,256,256]{2,1,0:T(8,128)(2,1)}), bf16[4,256,256]{2,1,0:T(8,128)(2,1)S(1)}, u32[]{:S(2)}, u32[]{:S(2)}) async-start(bf16[4,256,256]{2,1,0:T(8,128)(2,1)} %pad_maximum_fusion.5), calls=%async_computation.1 | async-start | bytes 1048576 | tf_op jit(solution)/shard_map/all_to_all | solution.py:105
  80.1 51.5 %all-to-all-start.2 = ((bf16[4,256,1024]{2,1,0:T(8,128)(2,1)}), bf16[4,256,1024]{2,1,0:T(8,128)(2,1)S(1)}, u32[]{:S(2)}, u32[]{:S(2)}) async-start(bf16[4,256,1024]{2,1,0:T(8,128)(2,1)} %pad_maximum_fusion), calls=%async_computation.2 | async-start | bytes 4194304 | tf_op jit(solution)/shard_map/all_to_all | solution.py:105
  98.9 17.2 %collective-permute-start.7 = (bf16[64,2048]{1,0:T(8,128)(2,1)}, bf16[64,2048]{1,0:T(8,128)(2,1)S(1)}, u32[]{:S(2)}, u32[]{:S(2)}) collective-permute-start(bf16[64,2048]{1,0:T(8,128)(2,1)} %get-tuple-element.126), channel_id=1, source_target_pairs={{0,1},{1,0},{2,3},{3,2},{4,5},{5,4},{6,7},{7,6},{8,9},{9,8},{10,11... | collective-permute-start | bytes 786440 | tf_op jit(solution)/shard_map/ppermute | solution.py:94
  99.5 16.6 %collective-permute-start.8 = (bf16[64,2048]{1,0:T(8,128)(2,1)}, bf16[64,2048]{1,0:T(8,128)(2,1)S(1)}, u32[]{:S(2)}, u32[]{:S(2)}) collective-permute-start(bf16[64,2048]{1,0:T(8,128)(2,1)} %get-tuple-element.127), channel_id=1, source_target_pairs={{0,2},{1,3},{2,0},{3,1},{4,6},{5,7},{6,4},{7,5},{8,10},{9,11},{10,... | collective-permute-start | bytes 786440 | tf_op jit(solution)/shard_map/ppermute | solution.py:94
  104.8 17.1 %collective-permute-start.9 = (bf16[64,2048]{1,0:T(8,128)(2,1)}, bf16[64,2048]{1,0:T(8,128)(2,1)}, u32[]{:S(2)}, u32[]{:S(2)}) collective-permute-start(bf16[64,2048]{1,0:T(8,128)(2,1)} %get-tuple-element.128), channel_id=1, source_target_pairs={{0,3},{1,2},{2,1},{3,0},{4,7},{5,6},{6,5},{7,4},{8,11},{9,10},{10,... | collective-permute-start | bytes 786440 | tf_op jit(solution)/shard_map/ppermute | solution.py:94
  131.7 37.7 %collective-permute-start.21 = (bf16[4,256,1024]{2,1,0:T(8,128)(2,1)S(1)}, bf16[4,256,1024]{2,1,0:T(8,128)(2,1)}, u32[]{:S(2)}, u32[]{:S(2)}) collective-permute-start(bf16[4,256,1024]{2,1,0:T(8,128)(2,1)S(1)} %all-to-all-done.2.refs_8_.refs_0_), channel_id=1, source_target_pairs={{0,4},{4,0},{8,12},{12,8},{16,20},{20,16},{24,28},{28,24},{1,5},{5... | collective-permute-start | bytes 6291464 | tf_op jit(solution)/shard_map/ppermute | solution.py:85
  147.9 52.9 %all-to-all-start.3 = ((bf16[4,1024,256]{2,1,0:T(8,128)(2,1)}), bf16[4,1024,256]{2,1,0:T(8,128)(2,1)}, u32[]{:S(2)}, u32[]{:S(2)}) async-start(bf16[4,1024,256]{2,1,0:T(8,128)(2,1)} %pad_maximum_fusion.1), calls=%async_computation.3 | async-start | bytes 4194304 | tf_op jit(solution)/shard_map/all_to_all | solution.py:105
  200.8 81.8 %all-to-all-start.4 = ((bf16[4,1024,256]{2,1,0:T(8,128)(2,1)}), bf16[4,1024,256]{2,1,0:T(8,128)(2,1)S(1)}, u32[]{:S(2)}, u32[]{:S(2)}) async-start(bf16[4,1024,256]{2,1,0:T(8,128)(2,1)} %grad_down_near.1), calls=%async_computation.4 | async-start | bytes 4194304 | tf_op jit(solution)/shard_map/all_to_all | solution.py:105
  239.1 20.1 %collective-permute-start.27 = (bf16[4,256,1024]{2,1,0:T(8,128)(2,1)}, bf16[4,256,1024]{2,1,0:T(8,128)(2,1)}, u32[]{:S(2)}, u32[]{:S(2)}) collective-permute-start(bf16[4,256,1024]{2,1,0:T(8,128)(2,1)} %grad_up_far.1), channel_id=1, source_target_pairs={{0,4},{4,0},{8,12},{12,8},{16,20},{20,16},{24,28},{28,24},{1,5},{5... | collective-permute-start | bytes 6291464 | tf_op jit(solution)/shard_map/ppermute | solution.py:85
  239.8 15.8 %collective-permute-start.26 = (bf16[64,2048]{1,0:T(8,128)(2,1)}, bf16[64,2048]{1,0:T(8,128)(2,1)S(1)}, u32[]{:S(2)}, u32[]{:S(2)}) collective-permute-start(bf16[64,2048]{1,0:T(8,128)(2,1)} %get-tuple-element.147), channel_id=1, source_target_pairs={{0,3},{1,2},{2,1},{3,0},{4,7},{5,6},{6,5},{7,4},{8,11},{9,10},{10,... | collective-permute-start | bytes 786440 | tf_op jit(solution)/shard_map/ppermute | solution.py:94
  241.3 23.1 %collective-permute-start.28 = (bf16[64,2048]{1,0:T(8,128)(2,1)}, bf16[64,2048]{1,0:T(8,128)(2,1)S(1)}, u32[]{:S(2)}, u32[]{:S(2)}) collective-permute-start(bf16[64,2048]{1,0:T(8,128)(2,1)} %get-tuple-element.153), channel_id=1, source_target_pairs={{0,1},{1,0},{2,3},{3,2},{4,5},{5,4},{6,7},{7,6},{8,9},{9,8},{10,11... | collective-permute-start | bytes 786440 | tf_op jit(solution)/shard_map/ppermute | solution.py:94
  242.7 22.0 %collective-permute-start.29 = (bf16[64,2048]{1,0:T(8,128)(2,1)}, bf16[64,2048]{1,0:T(8,128)(2,1)S(1)}, u32[]{:S(2)}, u32[]{:S(2)}) collective-permute-start(bf16[64,2048]{1,0:T(8,128)(2,1)} %get-tuple-element.154), channel_id=1, source_target_pairs={{0,2},{1,3},{2,0},{3,1},{4,6},{5,7},{6,4},{7,5},{8,10},{9,11},{10,... | collective-permute-start | bytes 786440 | tf_op jit(solution)/shard_map/ppermute | solution.py:94
  282.6 87.0 %all-to-all-start.5 = ((bf16[4,256,1024]{2,1,0:T(8,128)(2,1)}), bf16[4,256,1024]{2,1,0:T(8,128)(2,1)}, u32[]{:S(2)}, u32[]{:S(2)}) async-start(bf16[4,256,1024]{2,1,0:T(8,128)(2,1)} %grad_up_near.1), calls=%async_computation.5 | async-start | bytes 4194304 | tf_op jit(solution)/shard_map/all_to_all | solution.py:105
  301.7 17.6 %collective-permute-start.39 = (bf16[128,2048]{1,0:T(8,128)(2,1)}, bf16[128,2048]{1,0:T(8,128)(2,1)S(1)}, u32[]{:S(2)}, u32[]{:S(2)}) collective-permute-start(bf16[128,2048]{1,0:T(8,128)(2,1)} %get-tuple-element.165), channel_id=1, source_target_pairs={{0,1},{1,0},{2,3},{3,2},{4,5},{5,4},{6,7},{7,6},{8,9},{9,8},{10,11... | collective-permute-start | bytes 1572872 | tf_op jit(solution)/shard_map/ppermute | solution.py:94
  303.1 21.5 %collective-permute-start.40 = (bf16[128,2048]{1,0:T(8,128)(2,1)}, bf16[128,2048]{1,0:T(8,128)(2,1)S(1)}, u32[]{:S(2)}, u32[]{:S(2)}) collective-permute-start(bf16[128,2048]{1,0:T(8,128)(2,1)} %get-tuple-element.166), channel_id=1, source_target_pairs={{0,2},{1,3},{2,0},{3,1},{4,6},{5,7},{6,4},{7,5},{8,10},{9,11},{10,... | collective-permute-start | bytes 1572872 | tf_op jit(solution)/shard_map/ppermute | solution.py:94
  303.7 21.9 %collective-permute-start.41 = (bf16[128,2048]{1,0:T(8,128)(2,1)}, bf16[128,2048]{1,0:T(8,128)(2,1)S(1)}, u32[]{:S(2)}, u32[]{:S(2)}) collective-permute-start(bf16[128,2048]{1,0:T(8,128)(2,1)} %get-tuple-element.167), channel_id=1, source_target_pairs={{0,3},{1,2},{2,1},{3,0},{4,7},{5,6},{6,5},{7,4},{8,11},{9,10},{10,... | collective-permute-start | bytes 1572872 | tf_op jit(solution)/shard_map/ppermute | solution.py:94
  336.1 21.1 %collective-permute-start.61 = (bf16[4,256,768]{2,1,0:T(8,128)(2,1)}, bf16[4,256,768]{2,1,0:T(8,128)(2,1)S(1)}, u32[]{:S(2)}, u32[]{:S(2)}) collective-permute-start(bf16[4,256,768]{2,1,0:T(8,128)(2,1)} %grad_in_far.1), channel_id=1, source_target_pairs={{0,4},{4,0},{8,12},{12,8},{16,20},{20,16},{24,28},{28,24},{1,5},{5... | collective-permute-start | bytes 4718600 | tf_op jit(solution)/shard_map/ppermute | solution.py:85
  339.2 23.8 %collective-permute-start.62 = (bf16[4,256,256]{2,1,0:T(8,128)(2,1)}, bf16[4,256,256]{2,1,0:T(8,128)(2,1)S(1)}, u32[]{:S(2)}, u32[]{:S(2)}) collective-permute-start(bf16[4,256,256]{2,1,0:T(8,128)(2,1)} %grad_out_far.1), channel_id=1, source_target_pairs={{0,4},{4,0},{8,12},{12,8},{16,20},{20,16},{24,28},{28,24},{1,5},{5... | collective-permute-start | bytes 1572872 | tf_op jit(solution)/shard_map/ppermute | solution.py:85
  341.6 15.7 %collective-permute-start.46 = (bf16[64,2048]{1,0:T(8,128)(2,1)S(1)}, bf16[64,2048]{1,0:T(8,128)(2,1)S(1)}, u32[]{:S(2)}, u32[]{:S(2)}) collective-permute-start(bf16[64,2048]{1,0:T(8,128)(2,1)S(1)} %copy-done.67), channel_id=1, source_target_pairs={{0,1},{1,0},{2,3},{3,2},{4,5},{5,4},{6,7},{7,6},{8,9},{9,8},{10,11... | collective-permute-start | bytes 786440 | tf_op jit(solution)/shard_map/ppermute | solution.py:94
  370.3 87.0 %all-to-all-start.6 = ((bf16[4,256,1024]{2,1,0:T(8,128)(2,1)}), bf16[4,256,1024]{2,1,0:T(8,128)(2,1)S(1)}, u32[]{:S(2)}, u32[]{:S(2)}) async-start(bf16[4,256,1024]{2,1,0:T(8,128)(2,1)} %pad_maximum_fusion.2), calls=%async_computation.6 | async-start | bytes 4194304 | tf_op jit(solution)/shard_map/all_to_all | solution.py:105
  398.2 17.2 %collective-permute-start.42 = (bf16[64,2048]{1,0:T(8,128)(2,1)S(1)}, bf16[64,2048]{1,0:T(8,128)(2,1)S(1)}, u32[]{:S(2)}, u32[]{:S(2)}) collective-permute-start(bf16[64,2048]{1,0:T(8,128)(2,1)S(1)} %copy-done.21), channel_id=1, source_target_pairs={{0,8},{4,12},{8,0},{12,4},{16,24},{20,28},{24,16},{28,20},{1,9},{5... | collective-permute-start | bytes 786440 | tf_op jit(solution)/shard_map/ppermute | solution.py:88
  402.0 17.8 %collective-permute-start.58 = (f32[8,2048]{1,0:T(8,128)S(1)}, f32[8,2048]{1,0:T(8,128)S(1)}, u32[]{:S(2)}, u32[]{:S(2)}) collective-permute-start(f32[8,2048]{1,0:T(8,128)S(1)} %pad_maximum_fusion.7), channel_id=1, source_target_pairs={{0,4},{4,0},{8,12},{12,8},{16,20},{20,16},{24,28},{28,24},{1,5},{5... | collective-permute-start | bytes 196616 | tf_op jit(solution)/shard_map/ppermute | solution.py:85
  419.9 15.1 %collective-permute-start.44 = (bf16[64,2048]{1,0:T(8,128)(2,1)}, bf16[64,2048]{1,0:T(8,128)(2,1)S(1)}, u32[]{:S(2)}, u32[]{:S(2)}) collective-permute-start(bf16[64,2048]{1,0:T(8,128)(2,1)} %outputs_own.1.refs_0_), channel_id=1, source_target_pairs={{0,2},{1,3},{2,0},{3,1},{4,6},{5,7},{6,4},{7,5},{8,10},{9,11},{10,... | collective-permute-start | bytes 786440 | tf_op jit(solution)/shard_map/ppermute | solution.py:94
  421.4 25.5 %collective-permute-start.45 = (bf16[64,2048]{1,0:T(8,128)(2,1)}, bf16[64,2048]{1,0:T(8,128)(2,1)}, u32[]{:S(2)}, u32[]{:S(2)}) collective-permute-start(bf16[64,2048]{1,0:T(8,128)(2,1)} %outputs_own.1.refs_0_), channel_id=1, source_target_pairs={{0,3},{1,2},{2,1},{3,0},{4,7},{5,6},{6,5},{7,4},{8,11},{9,10},{10,... | collective-permute-start | bytes 786440 | tf_op jit(solution)/shard_map/ppermute | solution.py:94
  422.4 26.8 %collective-permute-start.53 = (bf16[64,2048]{1,0:T(8,128)(2,1)S(1)}, bf16[64,2048]{1,0:T(8,128)(2,1)S(1)}, u32[]{:S(2)}, u32[]{:S(2)}) collective-permute-start(bf16[64,2048]{1,0:T(8,128)(2,1)S(1)} %copy-done.22), channel_id=1, source_target_pairs={{0,1},{1,0},{2,3},{3,2},{4,5},{5,4},{6,7},{7,6},{8,9},{9,8},{10,11... | collective-permute-start | bytes 786440 | tf_op jit(solution)/shard_map/ppermute | solution.py:94
  428.1 21.1 %collective-permute-start.54 = (bf16[64,2048]{1,0:T(8,128)(2,1)S(1)}, bf16[64,2048]{1,0:T(8,128)(2,1)S(1)}, u32[]{:S(2)}, u32[]{:S(2)}) collective-permute-start(bf16[64,2048]{1,0:T(8,128)(2,1)S(1)} %copy-done.22), channel_id=1, source_target_pairs={{0,2},{1,3},{2,0},{3,1},{4,6},{5,7},{6,4},{7,5},{8,10},{9,11},{10,... | collective-permute-start | bytes 786440 | tf_op jit(solution)/shard_map/ppermute | solution.py:94
  428.6 20.6 %collective-permute-start.55 = (bf16[64,2048]{1,0:T(8,128)(2,1)S(1)}, bf16[64,2048]{1,0:T(8,128)(2,1)}, u32[]{:S(2)}, u32[]{:S(2)}) collective-permute-start(bf16[64,2048]{1,0:T(8,128)(2,1)S(1)} %copy-done.22), channel_id=1, source_target_pairs={{0,3},{1,2},{2,1},{3,0},{4,7},{5,6},{6,5},{7,4},{8,11},{9,10},{10,... | collective-permute-start | bytes 786440 | tf_op jit(solution)/shard_map/ppermute | solution.py:94
  434.9 17.3 %collective-permute-start.60 = (f32[8,2048]{1,0:T(8,128)S(1)}, f32[8,2048]{1,0:T(8,128)S(1)}, u32[]{:S(2)}, u32[]{:S(2)}) collective-permute-start(f32[8,2048]{1,0:T(8,128)S(1)} %add.64), channel_id=1, source_target_pairs={{0,16},{4,20},{8,24},{12,28},{16,0},{20,4},{24,8},{28,12},{1,17},{... | collective-permute-start | bytes 196616 | tf_op jit(solution)/shard_map/ppermute | solution.py:88
  (116 other events, 1001.3 us)

commit v4 on v3

--- a/solution.py
+++ b/solution.py
@@ -13,7 +13,7 @@
 SCALE = DH ** (-0.5)
 F32 = jnp.float32
 BF16 = jnp.bfloat16
-TILE = 256
+TILE = 512
 ANY = pl.BlockSpec(memory_space=pl.ANY)
 VMEM = pl.BlockSpec(memory_space=pltpu.VMEM)
 SMEM = pl.BlockSpec(memory_space=pltpu.SMEM)
@@ -113,7 +113,7 @@
 
     def spread(self, chunk):
         own = self.to_peers(chunk)
-        mate = after(self.to_mate(chunk), own)
+        mate = after(self.to_mate(chunk), own[:-1])
         return [chunk] + own + [mate] + self.to_peers(mate)
 
     def sum_small(self, wide, narrow):
@@ -220,17 +220,17 @@
     for k in range(1, chunks):
         for s in range(2):
             part = total[s * length + k * rows : s * length + (k + 1) * rows].astype(BF16)
-            if len(sends) == chunks - 1:
-                sends[k - 1][s * rows : (s + 1) * rows, cols] = part
-            else:
-                sends[s * (chunks - 1) + k - 1][:, cols] = part
+            sends[s * (chunks - 1) + k - 1][:, cols] = part
 
 
 def column_copies(table, arrays, weight, sems):
-    width = arrays[0].shape[2]
+    width = arrays[0].shape[-1]
+    blocks = blocks_of(arrays)
+    if len(arrays[0].shape) == 4:
+        blocks = [block.at[3] for block in blocks]
     return [
-        pltpu.make_async_copy(piece, weight.at[:, place(table, p, width)], sems.at[p])
-        for p, piece in enumerate(blocks_of(arrays))
+        pltpu.make_async_copy(block, weight.at[:, place(table, p, width)], sems.at[p])
+        for p, block in enumerate(blocks)
     ]
 
 
@@ -247,10 +247,12 @@
     copies = (row_copies if by_rows else column_copies)(table, pieces, weight, sems)
     for copy in copies:
         copy.start()
-    size = pieces[0].shape[1 if by_rows else 2]
-    for p, copy in enumerate(copies):
-        copy.wait()
-        cols = place(table, p, size)
+    size = pieces[0].shape[1 if by_rows else -1]
+    chips = pieces[0].shape[0]
+    for j in range(chips):
+        copies[j].wait()
+        copies[chips + j].wait()
+        cols = slice(2 * j * size, 2 * (j + 1) * size)
         if by_rows:
             total = nt(left[...], weight[cols, :])
         else:
@@ -259,19 +261,13 @@
 
 
 def fold_body(mate, *refs):
-    received, (out,) = refs[:-1], refs[-1:]
-    total = mate[...]
-    rows = mate.shape[0]
-    for ref in received:
-        total = total + ref[ref.shape[0] - rows :, :].astype(F32)
-    out[...] = total.astype(BF16)
+    refs[-1][...] = summed(mate, refs[:-1]).astype(BF16)
 
 
 def summed(own, received):
     total = own[...]
-    rows = own.shape[0]
     for ref in received:
-        total = total + ref[:rows, :].astype(F32)
+        total = total + ref[...].astype(F32)
     return total
 
 
@@ -343,16 +339,18 @@
 
 def attend_back_body(side_at, chunk_count, table, q, k, v, probs, *refs):
     chunks, refs = refs[:chunk_count], refs[chunk_count:]
-    outs_p, ins_p, refs = refs[:2], refs[2:4], refs[4:]
+    pieces, refs = refs[:2], refs[2:]
     (low, q_low, k_low, v_low, bias_grad, own, mate, *sends) = refs[:-5]
     out_weight, in_weight, mixed_grad, out_sems, in_sems = refs[-5:]
-    copies = column_copies(table, outs_p, out_weight, out_sems)
+    copies = column_copies(table, pieces, out_weight, out_sems)
     for copy in copies:
         copy.start()
-    size = ins_p[0].shape[2]
+    size = pieces[0].shape[2]
     ins = [
-        pltpu.make_async_copy(piece, in_weight.at[:, place(table, p, size)], in_sems.at[p])
-        for p, piece in enumerate(blocks_of(ins_p))
+        pltpu.make_async_copy(
+            piece.at[pl.ds(0, 3)], in_weight.at[:, place(table, p, size)], in_sems.at[p]
+        )
+        for p, piece in enumerate(blocks_of(pieces))
     ]
     for copy in ins:
         copy.start()
@@ -389,9 +387,11 @@
         there = pl.multiple_of(first + h * DH, DH)
         bias_grad[:, pl.ds(there, DH)] = q_sum
         bias_grad[:, pl.ds(pl.multiple_of(there + 2 * columns, DH), DH)] = v_sum
-    for p, copy in enumerate(ins):
-        copy.wait()
-        cols = place(table, p, size)
+    chips = pieces[0].shape[0]
+    for j in range(chips):
+        ins[j].wait()
+        ins[chips + j].wait()
+        cols = slice(2 * j * size, 2 * (j + 1) * size)
         total = nt(q_low[...], in_weight[0, cols, :])
         total = total + nt(k_low[...], in_weight[1, cols, :])
         total = total + nt(v_low[...], in_weight[2, cols, :])
@@ -410,7 +410,8 @@
 
 def output_body(count, own, hidden, vec, *refs):
     received, (result,) = refs[:count], refs[count:]
-    result[...] = (hidden[...] + summed(own, received) + vec[5:6, :]).astype(BF16)
+    total = summed(own, received)
+    result[...] = (hidden[...] + total + vec[5:6, :]).astype(BF16)
 
 
 def assemble_body(dp, tensor, table, *refs):
@@ -478,11 +479,8 @@
         self.own = length // at.tensor
         self.side_at = at.dp + at.tensor
 
-    def chunk_outs(self, split):
-        count = self.at.tensor - 1
-        sends = [shape((self.own, self.features), BF16)] * (2 * count)
-        if not split:
-            sends = [shape((2 * self.own, self.features), BF16)] * count
+    def chunk_outs(self):
+        sends = [shape((self.own, self.features), BF16)] * (2 * self.at.tensor - 2)
         return [shape((self.own, self.features), F32)] * 2 + sends
 
     def collect(self, name, own, vec, chunks, norm):
@@ -497,14 +495,14 @@
             [self.table, own, vec] + chunks,
         )[0]
 
-    def project(self, name, left, blocks, by_rows, split):
+    def project(self, name, left, blocks, by_rows):
         inner = left.shape[1]
         weight = (self.features, inner) if by_rows else (inner, self.features)
         return call(
             functools.partial(project_body, by_rows),
             name,
             [SMEM, VMEM] + [ANY] * 2,
-            self.chunk_outs(split),
+            self.chunk_outs(),
             [pltpu.VMEM(weight, BF16), sems(self.at.dp)],
             4 * self.length * inner * self.features,
             [self.table, left] + blocks,
@@ -521,17 +519,16 @@
             [mate] + received,
         )[0]
 
-    def trade(self, part, split):
-        count = self.at.tensor - 1
-        if not split:
-            received = self.at.to_peers(part[2:])
-            return received, received
-        return self.at.to_peers(part[2 + count :]), self.at.to_peers(part[2 : 2 + count])
-
-    def reduce(self, name, part, traded):
-        for_mate, others = traded
+    def trade_mate(self, part):
+        return self.at.to_peers(part[1 + self.at.tensor :])
+
+    def trade_own(self, part):
+        return self.at.to_peers(part[2 : 1 + self.at.tensor])
+
+    def reduce(self, name, part):
+        for_mate, own = self.trade_mate(part), self.trade_own(part)
         folded = self.fold(name + "_fold", part[1], for_mate)
-        return others + [self.at.to_mate(folded)], folded
+        return own + [self.at.to_mate(folded)], folded
 
     def block_shape(self, left, right, by_rows):
         size = self.features // self.at.dp
@@ -558,21 +555,66 @@
     def grad_near(self, name, left, right, by_rows, theirs):
         return self.grad(name, left, right, by_rows, theirs)
 
-    def grad_finish(self, name, blocks, by_rows, where, planes=1):
-        _, rows, width = blocks.shape
-        first, cols = where[0] % width, where[1]
-        out = (rows, 2 * cols) if by_rows else (2 * rows, cols)
-        if planes > 1:
-            out = (planes, rows, 2 * cols // planes)
+    def grad_attention(self, first_low, mixed, lows, hidden_low, *theirs):
+        chips, size = self.at.chips, self.features // self.at.dp
+        width, heads = len(lows) * lows[0].shape[1], mixed.shape[1]
+        first = 0 if theirs else chips
+
+        def body(table, left, other, *refs):
+            right, low, got, out = refs[:3], refs[3], refs[4:-1], refs[-1]
+
+            def put_at(start):
+                def put(block, row, column, value):
+                    rows = slice(row, row + value.shape[0])
+                    cols = slice(start + column, start + column + value.shape[1])
+                    for ref in got:
+                        value = value + ref[block, rows, cols].astype(F32)
+                    out[block, rows, cols] = value.astype(BF16)
+
+                return put
+
+            grad_blocks(table, left, right, True, first, chips, size, put_at(0))
+            grad_blocks(table, other, [low], False, first, chips, size, put_at(width))
+
+        args = [self.table, first_low, mixed] + list(lows) + [hidden_low] + list(theirs)
         return call(
-            functools.partial(finish_body, by_rows, planes, first, cols),
+            body,
+            "grad_attention_near" if theirs else "grad_attention_far",
+            [SMEM] + [VMEM] * (len(args) - 1),
+            [shape((chips, heads, width + size), BF16)],
+            [],
+            4 * self.length * chips * size * (width + heads),
+            args,
+        )[0]
+
+    def grad_finish(self, name, blocks, by_rows):
+        _, rows, cols = blocks.shape
+        return call(
+            functools.partial(finish_body, by_rows, 1, 0, cols),
             name + "_finish",
             [VMEM],
-            [shape(out, F32)],
+            [shape((rows, 2 * cols) if by_rows else (2 * rows, cols), F32)],
             [],
             blocks.size,
             [blocks],
         )[0]
+
+    def attention_finish(self, blocks, width, planes):
+        _, rows, cols = blocks.shape
+
+        def body(ref, grad_in, grad_out):
+            finish_body(True, planes, 0, width, ref, grad_in)
+            finish_body(False, 1, width, cols - width, ref, grad_out)
+
+        return call(
+            body,
+            "attention_finish",
+            [VMEM],
+            [shape((planes, rows, 2 * width // planes), F32), shape((2 * rows, cols - width), F32)],
+            [],
+            blocks.size,
+            [blocks],
+        )
 
 
 def shards(
@@ -601,7 +643,7 @@
     own, table, side_at = layer.own, layer.table, layer.side_at
     heads, hidden_units = query_bias.shape[0] // 2, up_bias.shape[0] // 2
     both = 2 * length
-    chunk_count, size = 2 * tensor, features // dp
+    chunk_count = 2 * tensor
     chunk32, chunk16 = shape((own, features), F32), shape((own, features), BF16)
     tokens16 = shape((both, features), BF16)
 
@@ -609,11 +651,11 @@
     mate = at.to_mate(jnp.concatenate([x_own, g_own]))
     ids = at.tokens_in(segment_ids)
     mate_ids = at.to_mate(ids)
-    mine_in = at.exchange(after(at.halves(project_in, 2), mate, mate_ids))
+    blocks = [at.halves(project_in, 2), at.halves(project_out, 0)[:, None]]
+    mine_in = at.exchange(after(jnp.concatenate(blocks, 1), mate, mate_ids))
     mate_chunks = [mate] + at.to_peers(mate)
-    out_blocks, up_blocks = at.halves(project_out, 0), at.halves(up_weight, 1)
-    down_blocks = at.halves(down_weight, 0)
-    mate_chunks = after(mate_chunks, out_blocks, up_blocks, down_blocks)
+    up_blocks, down_blocks = at.halves(up_weight, 1), at.halves(down_weight, 0)
+    mate_chunks = after(mate_chunks, up_blocks, down_blocks)
     vec = jnp.stack(
         [
             first_gain,
@@ -638,7 +680,7 @@
     first_low = layer.collect("first_norm", inputs, vec, mate_chunks, True)
     g = layer.collect("upstream", cotangent, vec, mate_chunks, False)
     mine_in = after(mine_in, first_low, allowed, biases, g)
-    mine_out = at.exchange(after(out_blocks, mine_in))
+    mine_up = at.exchange(after(up_blocks, mine_in))
 
     all_in = at.both_cores(mine_in)
     low_heads = shape((both, heads), BF16)
@@ -651,11 +693,8 @@
         12 * length * heads * features,
         [table, first_low, biases[0], biases[1], allowed] + all_in,
     )
-    mine_out = after(mine_out, mixed)
-    mine_up = at.exchange(after(up_blocks, mine_out))
-    all_out = at.both_cores(mine_out)
-    part = layer.project("project_out", mixed, all_out, False, True)
-    received, _ = layer.reduce("project_out", part, layer.trade(part, True))
+    part = layer.project("project_out", mixed, all_in, False)
+    received, _ = layer.reduce("project_out", part)
     hidden, normed_two, inverse_two, second_own = call(
         functools.partial(second_body, len(received)),
         "second_norm",
@@ -666,8 +705,8 @@
         [part[0], x_own, vec] + received,
     )
     second_chunks = at.spread(second_own)
-    mine_up = after(mine_up, second_own)
-    mine_down = at.exchange(after(down_blocks, mine_up, second_chunks[tensor]))
+    mine_up = after(mine_up, second_chunks[tensor])
+    mine_down = at.exchange(after(down_blocks, mine_up))
     all_up = at.both_cores(mine_up)
     second_low, activated, slope = call(
         functools.partial(upper_body, chunk_count),
@@ -692,13 +731,14 @@
         4 * length * features * hidden_units,
         [table, g, slope] + all_down,
     )
-    part = layer.project("second_part", upper_low, all_up, True, True)
-    traded = layer.trade(part, True)
-    far_up = layer.grad_far("grad_up", second_low, after([upper_low], traded[0][0]), True)
-    received, folded = layer.reduce("second_part", part, traded)
+    far_up = layer.grad_far("grad_up", second_low, [upper_low], True)
+    part = layer.project("second_part", after(upper_low, far_up), all_up, True)
+    for_mate = layer.trade_mate(part)
     near_up = layer.grad_near(
-        "grad_up", second_low, after([upper_low], folded), True, at.to_core(far_up)
-    )
+        "grad_up", second_low, after([upper_low], part), True, at.to_core(far_up)
+    )
+    folded = layer.fold("second_part_fold", part[1], for_mate)
+    received = layer.trade_own(after(part, near_up)) + [at.to_mate(folded)]
     hidden_grad, hidden_low_own, sums_two = call(
         functools.partial(second_back_body, len(received)),
         "second_back",
@@ -706,18 +746,17 @@
         [chunk32, chunk16, shape((8, features), F32)],
         [],
         20 * own * features,
-        [after(part[0], near_up), g_own, vec, normed_two, inverse_two] + received,
+        [after(part[0], ring_down), g_own, vec, normed_two, inverse_two] + received,
     )
     hidden_chunks = at.spread(hidden_low_own)
-    ring_up = at.exchange(after(near_up, ring_down, hidden_chunks[tensor]))
-    feed = layer.project("feed", after(activated, hidden_low_own), all_down, False, False)
-    feed_traded = layer.trade(after(feed, hidden_chunks), False)
+    ring_up = at.exchange(after(near_up, hidden_chunks[tensor]))
+    feed = layer.project("feed", after(activated, hidden_low_own), all_down, False)
     back = call(
         functools.partial(attend_back_body, side_at, chunk_count),
         "attend_back",
-        [SMEM] + [VMEM] * (4 + chunk_count) + [ANY] * 4,
+        [SMEM] + [VMEM] * (4 + chunk_count) + [ANY] * 2,
         [tokens16, low_heads, low_heads, low_heads, shape((1, 4 * heads), F32)]
-        + layer.chunk_outs(True),
+        + layer.chunk_outs(),
         [
             pltpu.VMEM((heads, features), BF16),
             pltpu.VMEM((3, features, heads), BF16),
@@ -726,32 +765,24 @@
             sems(dp),
         ],
         16 * length * heads * features,
-        [table, after(query, feed, ring_down), key, value, probs]
+        [table, after(query, feed), key, value, probs]
         + hidden_chunks
-        + all_out
         + all_in,
     )
     hidden_low, q_low, k_low, v_low, heads_grad, *part = back
     lows = [q_low, k_low, v_low]
-    part, feed_traded = after(part, feed_traded), after(feed_traded, part)
-    traded = layer.trade(part, True)
-    feed_received, feed_folded = layer.reduce("feed", feed, feed_traded)
-    far_in = layer.grad_far("grad_in", first_low, after(lows, feed_folded, traded[0][0]), True)
-    far_out = layer.grad_far("grad_out", mixed, after([hidden_low], far_in), False)
-    received, folded = layer.reduce("first_part", part, traded)
-    near_in = layer.grad_near(
-        "grad_in", first_low, after(lows, far_out, folded, traded[1][0]), True, at.to_core(far_in)
-    )
-    near_out = layer.grad_near(
-        "grad_out", mixed, after([hidden_low], near_in), False, at.to_core(far_out)
-    )
-    width = near_in.shape[2]
-    if near_in.shape[1] == near_out.shape[1]:
-        blocks = jnp.concatenate([near_in, near_out], 2)
-        ring_in = ring_out = at.exchange(after(blocks, ring_up, received[-1]))
-    else:
-        ring_in = at.exchange(after(near_in, ring_up, received[-1]))
-        ring_out = at.exchange(after(near_out, ring_in))
+    for_mate = layer.trade_mate(part)
+    far = layer.grad_attention(first_low, mixed, lows, hidden_low)
+    feed_for_mate = layer.trade_mate(after(feed, far))
+    folded = layer.fold("first_part_fold", part[1], for_mate)
+    from_mate = at.to_mate(folded)
+    near = layer.grad_attention(first_low, mixed, after(lows, folded), hidden_low, at.to_core(far))
+    received = layer.trade_own(after(part, feed_for_mate[0])) + [from_mate]
+    feed_folded = layer.fold("feed_fold", after(feed[1], near), feed_for_mate)
+    feed_from_mate = at.to_mate(feed_folded)
+    ring_in = at.exchange(after(near, ring_up, from_mate, feed_from_mate))
+    grad_down = layer.grad_finish("grad_down", ring_down, False)
+    grad_up = layer.grad_finish("grad_up", ring_up, True)
     input_own, sums_one = call(
         functools.partial(first_back_body, len(received)),
         "first_back",
@@ -759,8 +790,22 @@
         [chunk16, shape((8, features), F32)],
         [],
         20 * own * features,
-        [part[0], x_own, vec, hidden_grad] + received,
-    )
+        [after(part[0], grad_up, grad_down), x_own, vec, hidden_grad] + received,
+    )
+    def assemble(name, chunk, others):
+        return call(
+            functools.partial(assemble_body, dp, tensor),
+            name,
+            [SMEM] + [VMEM] * tensor,
+            [shape((length, features), BF16)],
+            [],
+            length * features,
+            [table, chunk] + others,
+        )[0]
+
+    input_others = at.to_peers(input_own)
+    input_gradient = assemble("input_gradient", input_own, input_others)
+    feed_received = layer.trade_own(after(feed, received[0])) + [feed_from_mate]
     outputs_own = call(
         functools.partial(output_body, len(feed_received)),
         "outputs_own",
@@ -768,31 +813,16 @@
         [chunk16],
         [],
         4 * own * features,
-        [feed[0], hidden, vec] + feed_received,
+        [after(feed[0], input_others), hidden, vec] + feed_received,
     )[0]
-
-    def assemble(name, chunk):
-        return call(
-            functools.partial(assemble_body, dp, tensor),
-            name,
-            [SMEM] + [VMEM] * tensor,
-            [shape((length, features), BF16)],
-            [],
-            length * features,
-            [table, chunk] + at.to_peers(chunk),
-        )[0]
-
-    input_gradient = assemble("input_gradient", input_own)
-    outputs = assemble("outputs", outputs_own)
-    grad_down = layer.grad_finish("grad_down", ring_down, False, (0, size))
-    grad_up = layer.grad_finish("grad_up", ring_up, True, (0, hidden_units))
-    grad_out = layer.grad_finish("grad_out", ring_out, False, (-size, size))
-    grad_in = layer.grad_finish("grad_in", ring_in, True, (0, width), 3)
+    output_others = at.to_peers(outputs_own)
+    outputs = assemble("outputs", outputs_own, output_others)
+    grad_in, grad_out = layer.attention_finish(ring_in, 3 * heads, 3)
 
     narrow = jnp.concatenate([heads_grad[0], up_bias_grad[0]])
     rows = -(-narrow.shape[0] // features)
     narrow = jnp.pad(narrow, (0, rows * features - narrow.shape[0])).reshape(rows, features)
-    sums = at.sum_small(jnp.concatenate([sums_one[:2], sums_two[:4]]), narrow)
+    sums = at.sum_small(after(jnp.concatenate([sums_one[:2], sums_two[:4]]), input_others), narrow)
     narrow = sums[6:].reshape(-1)
     heads, hidden_units = 2 * heads, 2 * hidden_units
     return (

time: 474 us -> 420 us (0.89); the launches traced: 464 us -> 417 us
  waiting for transfers between devices: 174 us -> 143 us
  Pallas kernels: 143 us -> 129 us
    ppermute x44 -> x47, waiting for transfers between devices: 129 us -> 100 us  [to_peer(): lax.ppermute(values, 'tensor', [(i, i ^ k) for i in range(self.tensor)])]
    pallas_call x31 -> x28, Pallas kernels: 143 us -> 129 us  [call(): pl.pallas_call(body, name=name, out_shape=outs, in_specs=in_specs, out_sp...]
    ppermute x44 -> x47, starting transfers between devices: 49.1 us -> 62.3 us  [to_peer(): lax.ppermute(values, 'tensor', [(i, i ^ k) for i in range(self.tensor)])]
    all_to_all x7 -> x6, waiting for transfers between devices: 10.6 us -> 2.65 us  [exchange(): lax.all_to_all(blocks, 'dp', 0, 0, axis_index_groups=groups, tiled=True)]
    all_to_all x7 -> x6, starting transfers between devices: 43.5 us -> 35.6 us  [exchange(): lax.all_to_all(blocks, 'dp', 0, 0, axis_index_groups=groups, tiled=True)]
    ppermute x9 -> x7, waiting for transfers between devices: 6.29 us -> 9.91 us  [to_core(): return lax.ppermute(values, 'dp', self.swap)]
    unnamed x158 -> x160, local copies, waits for them, and re-layouts: 16.6 us -> 15.8 us
  transfers between devices with their start and end apart: 70 -> 70, of which waited for: 36 -> 36; matrix products, arithmetic and copies ran while one was open for 4% -> 4% of each run, Pallas kernels for 30% -> 29%
where the time goes in v4:
time: 420 us; the launch traced here: 417 us
  waiting for transfers between devices  143 us (34%)
  Pallas kernels  129 us (31%)
  starting transfers between devices  110 us (26%)
  local copies, waits for them, and re-layouts  25.3 us (6%)
  other arithmetic  8.15 us (2%)
    pallas_call x28, Pallas kernels, call(): pl.pallas_call(body, name=name, out_shape=outs, in_specs=in_specs, out_sp...  129 us
    ppermute x47, waiting for transfers between devices, to_peer(): lax.ppermute(values, 'tensor', [(i, i ^ k) for i in range(self.tensor)])  100 us
    ppermute x47, starting transfers between devices, to_peer(): lax.ppermute(values, 'tensor', [(i, i ^ k) for i in range(self.tensor)])  62.3 us
    all_to_all x6, starting transfers between devices, exchange(): lax.all_to_all(blocks, 'dp', 0, 0, axis_index_groups=groups, tiled=True)  35.6 us
    ppermute x10, waiting for transfers between devices, to_chip(): return lax.ppermute(values, 'dp', [(i, i ^ 2 * k) for i in range(self.dp)])  30.2 us
    unnamed x160, local copies, waits for them, and re-layouts  15.8 us
    ppermute x10, starting transfers between devices, to_chip(): return lax.ppermute(values, 'dp', [(i, i ^ 2 * k) for i in range(self.dp)])  11.7 us
    ppermute x7, waiting for transfers between devices, to_core(): return lax.ppermute(values, 'dp', self.swap)  9.91 us
  transfers between devices with their start and end apart: 70, of which 36 were waited for; matrix products, arithmetic and copies ran while one was open for 4% of the time, Pallas kernels for 29%

profile of v4, /device:TPU:8, one launch (start us, length us, event | category | flops | bytes accessed | tf_op | source)
XLA Modules:
  0.0 416.5 jit_solution(3391454455001260695)
XLA Ops:
  7.3 8.4 %collective-permute-done.4 = s32[256]{0:T(256)S(1)} collective-permute-done((s32[256]{0:T(256)S(1)}, s32[256]{0:T(256)S(1)}, u32[]{:S(2)}, u32[]{:S(2)}) %collective-permute-start.4) | collective-permute-done | bytes 1056 | tf_op jit(solution)/shard_map/ppermute | solution.py:88
  15.7 5.3 %all-to-all-start = ((bf16[4,4,256,256]{3,2,1,0:T(8,128)(2,1)}), bf16[4,4,256,256]{3,2,1,0:T(8,128)(2,1)S(1)}, u32[]{:S(2)}, u32[]{:S(2)}) async-start(bf16[4,4,256,256]{3,2,1,0:T(8,128)(2,1)} %pad_maximum_fusion.2), calls=%async_computation | async-start | bytes 4194304 | tf_op jit(solution)/shard_map/all_to_all | solution.py:105
  33.9 9.7 %collective-permute-done.1.refs_1_ = bf16[128,2048]{1,0:T(8,128)(2,1)S(1)} collective-permute-done((bf16[128,2048]{1,0:T(8,128)(2,1)S(1)}, bf16[128,2048]{1,0:T(8,128)(2,1)S(1)}, u32[]{:S(2)}, u32[]{:S(2)}) %collective-permute-start.1) | collective-permute-done | bytes 524320 | tf_op jit(solution)/shard_map/ppermute | solution.py:94
  43.6 9.9 %collective-permute-done.2.refs_2_ = bf16[128,2048]{1,0:T(8,128)(2,1)S(1)} collective-permute-done((bf16[128,2048]{1,0:T(8,128)(2,1)S(1)}, bf16[128,2048]{1,0:T(8,128)(2,1)S(1)}, u32[]{:S(2)}, u32[]{:S(2)}) %collective-permute-start.2) | collective-permute-done | bytes 524320 | tf_op jit(solution)/shard_map/ppermute | solution.py:94
  57.7 4.8 %first_norm.1.x.left = bf16[512,2048]{1,0:T(8,128)(2,1)} custom-call(s32[13]{0:T(128)} %pad_add_fusion.1.table, bf16[256,2048]{1,0:T(8,128)(2,1)} %own.2, f32[8,2048]{1,0:T(8,128)} %convert_element_type.8.vec, bf16[128,2048]{1,0:T(8,128)(2,1)} %copy-done.7, bf16[128,2048]{1,0:T(8,128)(2,1)} %copy-done.8, bf16[128,2048]{1,0:T(8,128)(2,1)} %copy-done.9, ...), custom_call_target="tpu_custom_call" | custom-call | flops 10485760 | bytes 5308468 | tf_op jit(solution)/shard_map/first_norm/pallas_call | solution.py:41
  65.1 7.7 %all-to-all-start.1 = ((bf16[4,256,1024]{2,1,0:T(8,128)(2,1)}), bf16[4,256,1024]{2,1,0:T(8,128)(2,1)}, u32[]{:S(2)}, u32[]{:S(2)}) async-start(bf16[4,256,1024]{2,1,0:T(8,128)(2,1)} %pad_maximum_fusion), calls=%async_computation.1 | async-start | bytes 4194304 | tf_op jit(solution)/shard_map/all_to_all | solution.py:105
  77.0 8.9 %attend.1 = (bf16[512,256]{1,0:T(8,128)(2,1)}, bf16[512,256]{1,0:T(8,128)(2,1)}, bf16[512,256]{1,0:T(8,128)(2,1)}, f32[4,256,256]{2,1,0:T(8,128)}, bf16[512,256]{1,0:T(8,128)(2,1)}) custom-call(s32[13]{0:T(128)} %pad_add_fusion.1.table, bf16[512,2048]{1,0:T(8,128)(2,1)} %first_norm.1.x.left, bf16[1,256]{1,0:T(2,128)(2,1)} %broadcast_in_dim.29.q_bias, ...), custom_call_target="tpu_custom_call" | custom-call | flops 1610612736 | bytes 8913972 | tf_op jit(solution)/shard_map/attend/pallas_call | solution.py:41
  97.3 8.5 %collective-permute-done.10.refs_1_ = bf16[64,2048]{1,0:T(8,128)(2,1)S(1)} collective-permute-done((bf16[64,2048]{1,0:T(8,128)(2,1)}, bf16[64,2048]{1,0:T(8,128)(2,1)S(1)}, u32[]{:S(2)}, u32[]{:S(2)}) %collective-permute-start.10) | collective-permute-done | bytes 262176 | tf_op jit(solution)/shard_map/ppermute | solution.py:94
  112.9 5.5 %collective-permute-done.8.refs_2_ = bf16[64,2048]{1,0:T(8,128)(2,1)S(1)} collective-permute-done((bf16[64,2048]{1,0:T(8,128)(2,1)}, bf16[64,2048]{1,0:T(8,128)(2,1)S(1)}, u32[]{:S(2)}, u32[]{:S(2)}) %collective-permute-start.8) | collective-permute-done | bytes 262176 | tf_op jit(solution)/shard_map/ppermute | solution.py:94
  118.4 5.4 %collective-permute-done.12.refs_3_ = bf16[64,2048]{1,0:T(8,128)(2,1)S(1)} collective-permute-done((bf16[64,2048]{1,0:T(8,128)(2,1)}, bf16[64,2048]{1,0:T(8,128)(2,1)S(1)}, u32[]{:S(2)}, u32[]{:S(2)}) %collective-permute-start.12) | collective-permute-done | bytes 262176 | tf_op jit(solution)/shard_map/ppermute | solution.py:88
  138.8 6.1 %all-to-all-start.2 = ((bf16[4,1024,256]{2,1,0:T(8,128)(2,1)}), bf16[4,1024,256]{2,1,0:T(8,128)(2,1)}, u32[]{:S(2)}, u32[]{:S(2)}) async-start(bf16[4,1024,256]{2,1,0:T(8,128)(2,1)} %pad_maximum_fusion.1), calls=%async_computation.2 | async-start | bytes 4194304 | tf_op jit(solution)/shard_map/all_to_all | solution.py:105
  148.9 6.2 %collective-permute-done.15.refs_3_ = bf16[64,2048]{1,0:T(8,128)(2,1)S(1)} collective-permute-done((bf16[64,2048]{1,0:T(8,128)(2,1)S(1)}, bf16[64,2048]{1,0:T(8,128)(2,1)S(1)}, u32[]{:S(2)}, u32[]{:S(2)}) %collective-permute-start.15) | collective-permute-done | bytes 262176 | tf_op jit(solution)/shard_map/ppermute | solution.py:94
  160.6 5.0 %collective-permute-done.19.refs_7_ = bf16[64,2048]{1,0:T(8,128)(2,1)S(1)} collective-permute-done((bf16[64,2048]{1,0:T(8,128)(2,1)S(1)}, bf16[64,2048]{1,0:T(8,128)(2,1)S(1)}, u32[]{:S(2)}, u32[]{:S(2)}) %collective-permute-start.19) | collective-permute-done | bytes 262176 | tf_op jit(solution)/shard_map/ppermute | solution.py:94
  167.6 8.6 %upper.1 = (bf16[512,2048]{1,0:T(8,128)(2,1)}, bf16[512,1024]{1,0:T(8,128)(2,1)}, f32[512,1024]{1,0:T(8,128)}) custom-call(s32[13]{0:T(128)} %pad_add_fusion.1.table, bf16[1,1024]{1,0:T(2,128)(2,1)} %broadcast_in_dim.28.bias, bf16[64,2048]{1,0:T(8,128)(2,1)} %get-tuple-element.128.refs_0_, bf16[64,2048]{1,0:T(8,128)(2,1)} %copy-done.68, ...), custom_call_target="tpu_custom_call" | custom-call | flops 2147483648 | bytes 11536436 | tf_op jit(solution)/shard_map/upper/pallas_call | solution.py:41
  186.5 5.2 %grad_down_near.1 = bf16[4,1024,256]{2,1,0:T(8,128)(2,1)} custom-call(s32[13]{0:T(128)} %pad_add_fusion.1.table, bf16[512,1024]{1,0:T(8,128)(2,1)} %get-tuple-element.156.left, bf16[512,2048]{1,0:T(8,128)(2,1)} %upstream.1.refs_0_.g, bf16[4,1024,256]{2,1,0:T(8,128)(2,1)} %copy-done.6), custom_call_target="tpu_custom_call" | custom-call | flops 1073741824 | bytes 7340084 | tf_op jit(solution)/shard_map/grad_down_near/pallas_call | solution.py:41
  191.8 5.9 %all-to-all-start.3 = ((bf16[4,1024,256]{2,1,0:T(8,128)(2,1)}), bf16[4,1024,256]{2,1,0:T(8,128)(2,1)S(1)}, u32[]{:S(2)}, u32[]{:S(2)}) async-start(bf16[4,1024,256]{2,1,0:T(8,128)(2,1)} %grad_down_near.1), calls=%async_computation.3 | async-start | bytes 4194304 | tf_op jit(solution)/shard_map/all_to_all | solution.py:105
  197.8 8.0 %upper_grad.1 = (bf16[512,1024]{1,0:T(8,128)(2,1)}, f32[1,2048]{1,0:T(1,128)}) custom-call(s32[13]{0:T(128)} %pad_add_fusion.1.table, bf16[512,2048]{1,0:T(8,128)(2,1)} %upstream.1.refs_0_.g, f32[512,1024]{1,0:T(8,128)} %get-tuple-element.133.slope, bf16[4,1024,256]{2,1,0:T(8,128)(2,1)} %all-to-all-done.2.refs_0_, ...), custom_call_target="tpu_custom_call" | custom-call | flops 2147483648 | bytes 9445428 | tf_op jit(solution)/shard_map/upper_grad/pallas_call | solution.py:41
  210.6 7.3 %second_part.1 = (f32[64,2048]{1,0:T(8,128)}, f32[64,2048]{1,0:T(8,128)}, bf16[64,2048]{1,0:T(8,128)(2,1)}, bf16[64,2048]{1,0:T(8,128)(2,1)}, bf16[64,2048]{1,0:...) custom-call(s32[13]{0:T(128)} %pad_add_fusion.1.table, ...), custom_call_target="tpu_custom_call" | custom-call | flops 2147483648 | bytes 7864372 | tf_op jit(solution)/shard_map/second_part/pallas_call | solution.py:41
  221.5 5.9 %collective-permute-done.27.refs_0_ = bf16[64,2048]{1,0:T(8,128)(2,1)S(1)} collective-permute-done((bf16[64,2048]{1,0:T(8,128)(2,1)}, bf16[64,2048]{1,0:T(8,128)(2,1)S(1)}, u32[]{:S(2)}, u32[]{:S(2)}) %collective-permute-start.27) | collective-permute-done | bytes 262176 | tf_op jit(solution)/shard_map/ppermute | solution.py:94
  227.4 5.2 %collective-permute-done.28.refs_1_ = bf16[64,2048]{1,0:T(8,128)(2,1)S(1)} collective-permute-done((bf16[64,2048]{1,0:T(8,128)(2,1)}, bf16[64,2048]{1,0:T(8,128)(2,1)S(1)}, u32[]{:S(2)}, u32[]{:S(2)}) %collective-permute-start.28) | collective-permute-done | bytes 262176 | tf_op jit(solution)/shard_map/ppermute | solution.py:94
  237.0 5.2 %grad_up_near.1 = bf16[4,256,1024]{2,1,0:T(8,128)(2,1)} custom-call(s32[13]{0:T(128)} %pad_add_fusion.1.table, bf16[512,2048]{1,0:T(8,128)(2,1)} %get-tuple-element.137.left, bf16[512,1024]{1,0:T(8,128)(2,1)} %get-tuple-element.151.refs_0_.left, bf16[4,256,1024]{2,1,0:T(8,128)(2,1)} %collective-permute-done.23.refs_1_), custom_call_target="tpu_custom_call" | custom-call | flops 1073741824 | bytes 7340084 | tf_op jit(solution)/shard_map/grad_up_near/pallas_call | solution.py:41
  251.6 4.9 %collective-permute-done.25.refs_1_ = bf16[64,2048]{1,0:T(8,128)(2,1)S(1)} collective-permute-done((bf16[64,2048]{1,0:T(8,128)(2,1)}, bf16[64,2048]{1,0:T(8,128)(2,1)S(1)}, u32[]{:S(2)}, u32[]{:S(2)}) %collective-permute-start.25) | collective-permute-done | bytes 262176 | tf_op jit(solution)/shard_map/ppermute | solution.py:94
  268.5 5.4 %all-to-all-start.4 = ((bf16[4,256,1024]{2,1,0:T(8,128)(2,1)}), bf16[4,256,1024]{2,1,0:T(8,128)(2,1)}, u32[]{:S(2)}, u32[]{:S(2)}) async-start(bf16[4,256,1024]{2,1,0:T(8,128)(2,1)} %grad_up_near.1), calls=%async_computation.4 | async-start | bytes 4194304 | tf_op jit(solution)/shard_map/all_to_all | solution.py:105
  279.3 7.2 %feed.1 = (f32[64,2048]{1,0:T(8,128)}, f32[64,2048]{1,0:T(8,128)}, bf16[64,2048]{1,0:T(8,128)(2,1)}, bf16[64,2048]{1,0:T(8,128)(2,1)}, bf16[64,2048]{1,0:T(8,128...) custom-call(s32[13]{0:T(128)} %pad_add_fusion.1.table, ...), custom_call_target="tpu_custom_call" | custom-call | flops 2147483648 | bytes 7864372 | tf_op jit(solution)/shard_map/feed/pallas_call | solution.py:41
  291.5 11.8 %attend_back.1 = (bf16[512,2048]{1,0:T(8,128)(2,1)}, bf16[512,256]{1,0:T(8,128)(2,1)}, bf16[512,256]{1,0:T(8,128)(2,1)}, bf16[512,256]{1,0:T(8,128)(2,1)}, f32[1...) custom-call(s32[13]{0:T(128)} %pad_add_fusion.1.table, ...), custom_call_target="tpu_custom_call" | custom-call | flops 2147483648 | bytes 13635636 | tf_op jit(solution)/shard_map/attend_back/pallas_call | solution.py:41
  303.2 5.2 %grad_attention_far.1 = bf16[4,256,1024]{2,1,0:T(8,128)(2,1)} custom-call(s32[13]{0:T(128)} %pad_add_fusion.1.table, bf16[512,2048]{1,0:T(8,128)(2,1)} %first_norm.1.x.left, bf16[512,256]{1,0:T(8,128)(2,1)} %get-tuple-element.119.left.other, bf16[512,256]{1,0:T(8,128)(2,1)} %get-tuple-element.196.refs_0_, bf16[512,256]{1,0:T(8,128)(2,1)} %get-tuple-element.197.refs_1_, ...), custom_call_target="tpu_custom_call" | custom-call | flops 1073741824 | bytes 7340084 | tf_op jit(solution)/shard_map/grad_attention_far/pallas_call | solution.py:41
  312.6 5.1 %collective-permute-done.42.refs_0_ = bf16[64,2048]{1,0:T(8,128)(2,1)S(1)} collective-permute-done((bf16[64,2048]{1,0:T(8,128)(2,1)S(1)}, bf16[64,2048]{1,0:T(8,128)(2,1)S(1)}, u32[]{:S(2)}, u32[]{:S(2)}) %collective-permute-start.42) | collective-permute-done | bytes 262176 | tf_op jit(solution)/shard_map/ppermute | solution.py:94
  318.7 6.8 %collective-permute-start.54 = (bf16[64,2048]{1,0:T(8,128)(2,1)}, bf16[64,2048]{1,0:T(8,128)(2,1)S(1)}, u32[]{:S(2)}, u32[]{:S(2)}) collective-permute-start(bf16[64,2048]{1,0:T(8,128)(2,1)} %get-tuple-element.201), channel_id=1, source_target_pairs={{0,3},{1,2},{2,1},{3,0},{4,7},{5,6},{6,5},{7,4},{8,11},{9,10},{10,... | collective-permute-start | bytes 786440 | tf_op jit(solution)/shard_map/ppermute | solution.py:94
  329.6 5.9 %grad_attention_near.1 = bf16[4,256,1024]{2,1,0:T(8,128)(2,1)} custom-call(s32[13]{0:T(128)} %pad_add_fusion.1.table, bf16[512,2048]{1,0:T(8,128)(2,1)} %first_norm.1.x.left, bf16[512,256]{1,0:T(8,128)(2,1)} %get-tuple-element.119.left.other, bf16[512,256]{1,0:T(8,128)(2,1)} %get-tuple-element.196.refs_0_, bf16[512,256]{1,0:T(8,128)(2,1)} %get-tuple-element.197.refs_1_, ...), custom_call_target="tpu_custom_call" | custom-call | flops 1073741824 | bytes 9437236 | tf_op jit(solution)/shard_map/grad_attention_near/pallas_call | solution.py:41
  340.4 5.2 %collective-permute-done.55.refs_3_ = bf16[64,2048]{1,0:T(8,128)(2,1)S(1)} collective-permute-done((bf16[64,2048]{1,0:T(8,128)(2,1)}, bf16[64,2048]{1,0:T(8,128)(2,1)S(1)}, u32[]{:S(2)}, u32[]{:S(2)}) %collective-permute-start.55) | collective-permute-done | bytes 262176 | tf_op jit(solution)/shard_map/ppermute | solution.py:88
  346.3 5.1 %all-to-all-start.5 = ((bf16[4,256,1024]{2,1,0:T(8,128)(2,1)}), bf16[4,256,1024]{2,1,0:T(8,128)(2,1)S(1)}, u32[]{:S(2)}, u32[]{:S(2)}) async-start(bf16[4,256,1024]{2,1,0:T(8,128)(2,1)} %grad_attention_near.1), calls=%async_computation.5 | async-start | bytes 4194304 | tf_op jit(solution)/shard_map/all_to_all | solution.py:105
  382.9 4.8 %collective-permute-done.59 = f32[6,2048]{1,0:T(8,128)S(1)} collective-permute-done((f32[6,2048]{1,0:T(8,128)S(1)}, f32[6,2048]{1,0:T(8,128)S(1)}, u32[]{:S(2)}, u32[]{:S(2)}) %collective-permute-start.59) | collective-permute-done | bytes 49184 | tf_op jit(solution)/shard_map/ppermute | solution.py:94
  (352 shorter events, 205.1 us)
Async XLA Ops:
  1.9 13.8 %collective-permute-start = (bf16[128,2048]{1,0:T(8,128)(2,1)S(1)}, bf16[128,2048]{1,0:T(8,128)(2,1)S(1)}, u32[]{:S(2)}, u32[]{:S(2)}) collective-permute-start(bf16[128,2048]{1,0:T(8,128)(2,1)S(1)} %pad_maximum_fusion.3), channel_id=1, source_target_pairs={{0,8},{4,12},{8,0},{12,4},{16,24},{20,28},{24,16},{28,20},{1,9},{5... | collective-permute-start | bytes 1572872 | tf_op jit(solution)/shard_map/ppermute | solution.py:88
  15.7 49.3 %all-to-all-start = ((bf16[4,4,256,256]{3,2,1,0:T(8,128)(2,1)}), bf16[4,4,256,256]{3,2,1,0:T(8,128)(2,1)S(1)}, u32[]{:S(2)}, u32[]{:S(2)}) async-start(bf16[4,4,256,256]{3,2,1,0:T(8,128)(2,1)} %pad_maximum_fusion.2), calls=%async_computation | async-start | bytes 4194304 | tf_op jit(solution)/shard_map/all_to_all | solution.py:105
  28.7 14.9 %collective-permute-start.1 = (bf16[128,2048]{1,0:T(8,128)(2,1)S(1)}, bf16[128,2048]{1,0:T(8,128)(2,1)S(1)}, u32[]{:S(2)}, u32[]{:S(2)}) collective-permute-start(bf16[128,2048]{1,0:T(8,128)(2,1)S(1)} %collective-permute-done.refs_0_), channel_id=1, source_target_pairs={{0,1},{1,0},{2,3},{3,2},{4,5},{5,4},{6,7},{7,6},{8,9},{9,8},{10,11... | collective-permute-start | bytes 1572872 | tf_op jit(solution)/shard_map/ppermute | solution.py:94
  30.3 23.2 %collective-permute-start.2 = (bf16[128,2048]{1,0:T(8,128)(2,1)S(1)}, bf16[128,2048]{1,0:T(8,128)(2,1)S(1)}, u32[]{:S(2)}, u32[]{:S(2)}) collective-permute-start(bf16[128,2048]{1,0:T(8,128)(2,1)S(1)} %collective-permute-done.refs_0_), channel_id=1, source_target_pairs={{0,2},{1,3},{2,0},{3,1},{4,6},{5,7},{6,4},{7,5},{8,10},{9,11},{10,... | collective-permute-start | bytes 1572872 | tf_op jit(solution)/shard_map/ppermute | solution.py:94
  31.8 22.4 %collective-permute-start.3 = (bf16[128,2048]{1,0:T(8,128)(2,1)S(1)}, bf16[128,2048]{1,0:T(8,128)(2,1)}, u32[]{:S(2)}, u32[]{:S(2)}) collective-permute-start(bf16[128,2048]{1,0:T(8,128)(2,1)S(1)} %collective-permute-done.refs_0_), channel_id=1, source_target_pairs={{0,3},{1,2},{2,1},{3,0},{4,7},{5,6},{6,5},{7,4},{8,11},{9,10},{10,... | collective-permute-start | bytes 1572872 | tf_op jit(solution)/shard_map/ppermute | solution.py:94
  65.1 73.7 %all-to-all-start.1 = ((bf16[4,256,1024]{2,1,0:T(8,128)(2,1)}), bf16[4,256,1024]{2,1,0:T(8,128)(2,1)}, u32[]{:S(2)}, u32[]{:S(2)}) async-start(bf16[4,256,1024]{2,1,0:T(8,128)(2,1)} %pad_maximum_fusion), calls=%async_computation.1 | async-start | bytes 4194304 | tf_op jit(solution)/shard_map/all_to_all | solution.py:105
  90.7 15.1 %collective-permute-start.10 = (bf16[64,2048]{1,0:T(8,128)(2,1)}, bf16[64,2048]{1,0:T(8,128)(2,1)S(1)}, u32[]{:S(2)}, u32[]{:S(2)}) collective-permute-start(bf16[64,2048]{1,0:T(8,128)(2,1)} %get-tuple-element.126), channel_id=1, source_target_pairs={{0,2},{1,3},{2,0},{3,1},{4,6},{5,7},{6,4},{7,5},{8,10},{9,11},{10,... | collective-permute-start | bytes 786440 | tf_op jit(solution)/shard_map/ppermute | solution.py:94
  92.3 15.9 %collective-permute-start.11 = (bf16[64,2048]{1,0:T(8,128)(2,1)}, bf16[64,2048]{1,0:T(8,128)(2,1)S(1)}, u32[]{:S(2)}, u32[]{:S(2)}) collective-permute-start(bf16[64,2048]{1,0:T(8,128)(2,1)} %get-tuple-element.127), channel_id=1, source_target_pairs={{0,3},{1,2},{2,1},{3,0},{4,7},{5,6},{6,5},{7,4},{8,11},{9,10},{10,... | collective-permute-start | bytes 786440 | tf_op jit(solution)/shard_map/ppermute | solution.py:94
  93.7 14.5 %collective-permute-start.9 = (bf16[64,2048]{1,0:T(8,128)(2,1)}, bf16[64,2048]{1,0:T(8,128)(2,1)S(1)}, u32[]{:S(2)}, u32[]{:S(2)}) collective-permute-start(bf16[64,2048]{1,0:T(8,128)(2,1)} %get-tuple-element.125), channel_id=1, source_target_pairs={{0,1},{1,0},{2,3},{3,2},{4,5},{5,4},{6,7},{7,6},{8,9},{9,8},{10,11... | collective-permute-start | bytes 786440 | tf_op jit(solution)/shard_map/ppermute | solution.py:94
  94.3 18.6 %collective-permute-start.6 = (bf16[64,2048]{1,0:T(8,128)(2,1)}, bf16[64,2048]{1,0:T(8,128)(2,1)S(1)}, u32[]{:S(2)}, u32[]{:S(2)}) collective-permute-start(bf16[64,2048]{1,0:T(8,128)(2,1)} %get-tuple-element.121), channel_id=1, source_target_pairs={{0,1},{1,0},{2,3},{3,2},{4,5},{5,4},{6,7},{7,6},{8,9},{9,8},{10,11... | collective-permute-start | bytes 786440 | tf_op jit(solution)/shard_map/ppermute | solution.py:94
  95.7 17.1 %collective-permute-start.7 = (bf16[64,2048]{1,0:T(8,128)(2,1)}, bf16[64,2048]{1,0:T(8,128)(2,1)S(1)}, u32[]{:S(2)}, u32[]{:S(2)}) collective-permute-start(bf16[64,2048]{1,0:T(8,128)(2,1)} %get-tuple-element.122), channel_id=1, source_target_pairs={{0,2},{1,3},{2,0},{3,1},{4,6},{5,7},{6,4},{7,5},{8,10},{9,11},{10,... | collective-permute-start | bytes 786440 | tf_op jit(solution)/shard_map/ppermute | solution.py:94
  138.8 27.5 %collective-permute-start.20 = (bf16[4,256,1024]{2,1,0:T(8,128)(2,1)}, bf16[4,256,1024]{2,1,0:T(8,128)(2,1)S(1)}, u32[]{:S(2)}, u32[]{:S(2)}) collective-permute-start(bf16[4,256,1024]{2,1,0:T(8,128)(2,1)} %all-to-all-done.1.refs_8_.refs_0_), channel_id=1, source_target_pairs={{0,4},{4,0},{8,12},{12,8},{16,20},{20,16},{24,28},{28,24},{1,5},{5... | collective-permute-start | bytes 6291464 | tf_op jit(solution)/shard_map/ppermute | solution.py:85
  138.8 52.9 %all-to-all-start.2 = ((bf16[4,1024,256]{2,1,0:T(8,128)(2,1)}), bf16[4,1024,256]{2,1,0:T(8,128)(2,1)}, u32[]{:S(2)}, u32[]{:S(2)}) async-start(bf16[4,1024,256]{2,1,0:T(8,128)(2,1)} %pad_maximum_fusion.1), calls=%async_computation.2 | async-start | bytes 4194304 | tf_op jit(solution)/shard_map/all_to_all | solution.py:105
  145.4 14.3 %collective-permute-start.17 = (bf16[64,2048]{1,0:T(8,128)(2,1)S(1)}, bf16[64,2048]{1,0:T(8,128)(2,1)S(1)}, u32[]{:S(2)}, u32[]{:S(2)}) collective-permute-start(bf16[64,2048]{1,0:T(8,128)(2,1)S(1)} %collective-permute-done.16.refs_4_), channel_id=1, source_target_pairs={{0,1},{1,0},{2,3},{3,2},{4,5},{5,4},{6,7},{7,6},{8,9},{9,8},{10,11... | collective-permute-start | bytes 786440 | tf_op jit(solution)/shard_map/ppermute | solution.py:94
  146.9 13.7 %collective-permute-start.18 = (bf16[64,2048]{1,0:T(8,128)(2,1)S(1)}, bf16[64,2048]{1,0:T(8,128)(2,1)S(1)}, u32[]{:S(2)}, u32[]{:S(2)}) collective-permute-start(bf16[64,2048]{1,0:T(8,128)(2,1)S(1)} %collective-permute-done.16.refs_4_), channel_id=1, source_target_pairs={{0,2},{1,3},{2,0},{3,1},{4,6},{5,7},{6,4},{7,5},{8,10},{9,11},{10,... | collective-permute-start | bytes 786440 | tf_op jit(solution)/shard_map/ppermute | solution.py:94
  148.4 17.1 %collective-permute-start.19 = (bf16[64,2048]{1,0:T(8,128)(2,1)S(1)}, bf16[64,2048]{1,0:T(8,128)(2,1)S(1)}, u32[]{:S(2)}, u32[]{:S(2)}) collective-permute-start(bf16[64,2048]{1,0:T(8,128)(2,1)S(1)} %collective-permute-done.16.refs_4_), channel_id=1, source_target_pairs={{0,3},{1,2},{2,1},{3,0},{4,7},{5,6},{6,5},{7,4},{8,11},{9,10},{10,... | collective-permute-start | bytes 786440 | tf_op jit(solution)/shard_map/ppermute | solution.py:94
  191.8 53.9 %all-to-all-start.3 = ((bf16[4,1024,256]{2,1,0:T(8,128)(2,1)}), bf16[4,1024,256]{2,1,0:T(8,128)(2,1)S(1)}, u32[]{:S(2)}, u32[]{:S(2)}) async-start(bf16[4,1024,256]{2,1,0:T(8,128)(2,1)} %grad_down_near.1), calls=%async_computation.3 | async-start | bytes 4194304 | tf_op jit(solution)/shard_map/all_to_all | solution.py:105
  210.4 26.6 %collective-permute-start.23 = (bf16[4,256,1024]{2,1,0:T(8,128)(2,1)}, bf16[4,256,1024]{2,1,0:T(8,128)(2,1)}, u32[]{:S(2)}, u32[]{:S(2)}) collective-permute-start(bf16[4,256,1024]{2,1,0:T(8,128)(2,1)} %grad_up_far.1), channel_id=1, source_target_pairs={{0,4},{4,0},{8,12},{12,8},{16,20},{20,16},{24,28},{28,24},{1,5},{5... | collective-permute-start | bytes 6291464 | tf_op jit(solution)/shard_map/ppermute | solution.py:85
  218.5 14.0 %collective-permute-start.28 = (bf16[64,2048]{1,0:T(8,128)(2,1)}, bf16[64,2048]{1,0:T(8,128)(2,1)S(1)}, u32[]{:S(2)}, u32[]{:S(2)}) collective-permute-start(bf16[64,2048]{1,0:T(8,128)(2,1)} %get-tuple-element.149), channel_id=1, source_target_pairs={{0,2},{1,3},{2,0},{3,1},{4,6},{5,7},{6,4},{7,5},{8,10},{9,11},{10,... | collective-permute-start | bytes 786440 | tf_op jit(solution)/shard_map/ppermute | solution.py:94
  236.1 14.1 %collective-permute-start.30 = (bf16[64,2048]{1,0:T(8,128)(2,1)}, bf16[64,2048]{1,0:T(8,128)(2,1)S(1)}, u32[]{:S(2)}, u32[]{:S(2)}) collective-permute-start(bf16[64,2048]{1,0:T(8,128)(2,1)} %second_part_fold.1), channel_id=1, source_target_pairs={{0,8},{4,12},{8,0},{12,4},{16,24},{20,28},{24,16},{28,20},{1,9},{5... | collective-permute-start | bytes 786440 | tf_op jit(solution)/shard_map/ppermute | solution.py:88
  268.5 77.0 %all-to-all-start.4 = ((bf16[4,256,1024]{2,1,0:T(8,128)(2,1)}), bf16[4,256,1024]{2,1,0:T(8,128)(2,1)}, u32[]{:S(2)}, u32[]{:S(2)}) async-start(bf16[4,256,1024]{2,1,0:T(8,128)(2,1)} %grad_up_near.1), calls=%async_computation.4 | async-start | bytes 4194304 | tf_op jit(solution)/shard_map/all_to_all | solution.py:105
  308.5 19.8 %collective-permute-start.52 = (bf16[4,256,1024]{2,1,0:T(8,128)(2,1)}, bf16[4,256,1024]{2,1,0:T(8,128)(2,1)S(1)}, u32[]{:S(2)}, u32[]{:S(2)}) collective-permute-start(bf16[4,256,1024]{2,1,0:T(8,128)(2,1)} %grad_attention_far.1), channel_id=1, source_target_pairs={{0,4},{4,0},{8,12},{12,8},{16,20},{20,16},{24,28},{28,24},{1,5},{5... | collective-permute-start | bytes 6291464 | tf_op jit(solution)/shard_map/ppermute | solution.py:85
  310.2 15.3 %collective-permute-start.44 = (bf16[64,2048]{1,0:T(8,128)(2,1)}, bf16[64,2048]{1,0:T(8,128)(2,1)}, u32[]{:S(2)}, u32[]{:S(2)}) collective-permute-start(bf16[64,2048]{1,0:T(8,128)(2,1)} %get-tuple-element.181), channel_id=1, source_target_pairs={{0,3},{1,2},{2,1},{3,0},{4,7},{5,6},{6,5},{7,4},{8,11},{9,10},{10,... | collective-permute-start | bytes 786440 | tf_op jit(solution)/shard_map/ppermute | solution.py:94
  312.0 23.4 %collective-permute-start.38 = (bf16[64,2048]{1,0:T(8,128)(2,1)}, bf16[64,2048]{1,0:T(8,128)(2,1)S(1)}, u32[]{:S(2)}, u32[]{:S(2)}) collective-permute-start(bf16[64,2048]{1,0:T(8,128)(2,1)} %get-tuple-element.186), channel_id=1, source_target_pairs={{0,1},{1,0},{2,3},{3,2},{4,5},{5,4},{6,7},{7,6},{8,9},{9,8},{10,11... | collective-permute-start | bytes 786440 | tf_op jit(solution)/shard_map/ppermute | solution.py:94
  317.7 17.7 %collective-permute-start.53 = (bf16[64,2048]{1,0:T(8,128)(2,1)}, bf16[64,2048]{1,0:T(8,128)(2,1)S(1)}, u32[]{:S(2)}, u32[]{:S(2)}) collective-permute-start(bf16[64,2048]{1,0:T(8,128)(2,1)} %get-tuple-element.200), channel_id=1, source_target_pairs={{0,2},{1,3},{2,0},{3,1},{4,6},{5,7},{6,4},{7,5},{8,10},{9,11},{10,... | collective-permute-start | bytes 786440 | tf_op jit(solution)/shard_map/ppermute | solution.py:94
  318.7 16.8 %collective-permute-start.54 = (bf16[64,2048]{1,0:T(8,128)(2,1)}, bf16[64,2048]{1,0:T(8,128)(2,1)S(1)}, u32[]{:S(2)}, u32[]{:S(2)}) collective-permute-start(bf16[64,2048]{1,0:T(8,128)(2,1)} %get-tuple-element.201), channel_id=1, source_target_pairs={{0,3},{1,2},{2,1},{3,0},{4,7},{5,6},{6,5},{7,4},{8,11},{9,10},{10,... | collective-permute-start | bytes 786440 | tf_op jit(solution)/shard_map/ppermute | solution.py:94
  346.3 65.8 %all-to-all-start.5 = ((bf16[4,256,1024]{2,1,0:T(8,128)(2,1)}), bf16[4,256,1024]{2,1,0:T(8,128)(2,1)S(1)}, u32[]{:S(2)}, u32[]{:S(2)}) async-start(bf16[4,256,1024]{2,1,0:T(8,128)(2,1)} %grad_attention_near.1), calls=%async_computation.5 | async-start | bytes 4194304 | tf_op jit(solution)/shard_map/all_to_all | solution.py:105
  367.3 14.5 %collective-permute-start.47 = (bf16[64,2048]{1,0:T(8,128)(2,1)}, bf16[64,2048]{1,0:T(8,128)(2,1)S(1)}, u32[]{:S(2)}, u32[]{:S(2)}) collective-permute-start(bf16[64,2048]{1,0:T(8,128)(2,1)} %get-tuple-element.190.refs_0_), channel_id=1, source_target_pairs={{0,2},{1,3},{2,0},{3,1},{4,6},{5,7},{6,4},{7,5},{8,10},{9,11},{10,... | collective-permute-start | bytes 786440 | tf_op jit(solution)/shard_map/ppermute | solution.py:94
  369.5 20.6 %collective-permute-start.49 = (bf16[64,2048]{1,0:T(8,128)(2,1)}, bf16[64,2048]{1,0:T(8,128)(2,1)S(1)}, u32[]{:S(2)}, u32[]{:S(2)}) collective-permute-start(bf16[64,2048]{1,0:T(8,128)(2,1)} %get-tuple-element.193), channel_id=1, source_target_pairs={{0,1},{1,0},{2,3},{3,2},{4,5},{5,4},{6,7},{7,6},{8,9},{9,8},{10,11... | collective-permute-start | bytes 786440 | tf_op jit(solution)/shard_map/ppermute | solution.py:94
  370.9 19.2 %collective-permute-start.50 = (bf16[64,2048]{1,0:T(8,128)(2,1)}, bf16[64,2048]{1,0:T(8,128)(2,1)S(1)}, u32[]{:S(2)}, u32[]{:S(2)}) collective-permute-start(bf16[64,2048]{1,0:T(8,128)(2,1)} %get-tuple-element.194), channel_id=1, source_target_pairs={{0,2},{1,3},{2,0},{3,1},{4,6},{5,7},{6,4},{7,5},{8,10},{9,11},{10,... | collective-permute-start | bytes 786440 | tf_op jit(solution)/shard_map/ppermute | solution.py:94
  375.4 14.8 %collective-permute-start.51 = (bf16[64,2048]{1,0:T(8,128)(2,1)}, bf16[64,2048]{1,0:T(8,128)(2,1)}, u32[]{:S(2)}, u32[]{:S(2)}) collective-permute-start(bf16[64,2048]{1,0:T(8,128)(2,1)} %get-tuple-element.195), channel_id=1, source_target_pairs={{0,3},{1,2},{2,1},{3,0},{4,7},{5,6},{6,5},{7,4},{8,11},{9,10},{10,... | collective-permute-start | bytes 786440 | tf_op jit(solution)/shard_map/ppermute | solution.py:94
  393.3 13.9 %collective-permute-start.56 = (bf16[64,2048]{1,0:T(8,128)(2,1)}, bf16[64,2048]{1,0:T(8,128)(2,1)S(1)}, u32[]{:S(2)}, u32[]{:S(2)}) collective-permute-start(bf16[64,2048]{1,0:T(8,128)(2,1)} %outputs_own.1.refs_0_), channel_id=1, source_target_pairs={{0,1},{1,0},{2,3},{3,2},{4,5},{5,4},{6,7},{7,6},{8,9},{9,8},{10,11... | collective-permute-start | bytes 786440 | tf_op jit(solution)/shard_map/ppermute | solution.py:94
  (117 other events, 1002.5 us)

commit v5 on v4

--- a/solution.py
+++ b/solution.py
@@ -733,12 +733,10 @@
     )
     far_up = layer.grad_far("grad_up", second_low, [upper_low], True)
     part = layer.project("second_part", after(upper_low, far_up), all_up, True)
-    for_mate = layer.trade_mate(part)
+    received, folded = layer.reduce("second_part", part)
     near_up = layer.grad_near(
-        "grad_up", second_low, after([upper_low], part), True, at.to_core(far_up)
-    )
-    folded = layer.fold("second_part_fold", part[1], for_mate)
-    received = layer.trade_own(after(part, near_up)) + [at.to_mate(folded)]
+        "grad_up", second_low, after([upper_low], folded, received[:-1]), True, at.to_core(far_up)
+    )
     hidden_grad, hidden_low_own, sums_two = call(
         functools.partial(second_back_body, len(received)),
         "second_back",
@@ -746,7 +744,7 @@
         [chunk32, chunk16, shape((8, features), F32)],
         [],
         20 * own * features,
-        [after(part[0], ring_down), g_own, vec, normed_two, inverse_two] + received,
+        [after(part[0], ring_down, near_up), g_own, vec, normed_two, inverse_two] + received,
     )
     hidden_chunks = at.spread(hidden_low_own)
     ring_up = at.exchange(after(near_up, hidden_chunks[tensor]))
@@ -780,7 +778,7 @@
     received = layer.trade_own(after(part, feed_for_mate[0])) + [from_mate]
     feed_folded = layer.fold("feed_fold", after(feed[1], near), feed_for_mate)
     feed_from_mate = at.to_mate(feed_folded)
-    ring_in = at.exchange(after(near, ring_up, from_mate, feed_from_mate))
+    ring_in = at.exchange(after(near, ring_up, received, feed_from_mate))
     grad_down = layer.grad_finish("grad_down", ring_down, False)
     grad_up = layer.grad_finish("grad_up", ring_up, True)
     input_own, sums_one = call(
@@ -790,7 +788,7 @@
         [chunk16, shape((8, features), F32)],
         [],
         20 * own * features,
-        [after(part[0], grad_up, grad_down), x_own, vec, hidden_grad] + received,
+        [part[0], x_own, vec, hidden_grad] + received,
     )
     def assemble(name, chunk, others):
         return call(
@@ -822,7 +820,7 @@
     narrow = jnp.concatenate([heads_grad[0], up_bias_grad[0]])
     rows = -(-narrow.shape[0] // features)
     narrow = jnp.pad(narrow, (0, rows * features - narrow.shape[0])).reshape(rows, features)
-    sums = at.sum_small(after(jnp.concatenate([sums_one[:2], sums_two[:4]]), input_others), narrow)
+    sums = at.sum_small(after(jnp.concatenate([sums_one[:2], sums_two[:4]]), input_others, grad_down, grad_up), narrow)
     narrow = sums[6:].reshape(-1)
     heads, hidden_units = 2 * heads, 2 * hidden_units
     return (

time: 420 us -> 414 us (0.986)
  starting transfers between devices: 110 us -> 105 us
  waiting for transfers between devices: 143 us -> 148 us
    ppermute x47, waiting for transfers between devices: 100 us -> 109 us  [to_peer(): lax.ppermute(values, 'tensor', [(i, i ^ k) for i in range(self.tensor)])]
    ppermute x47, starting transfers between devices: 62.3 us -> 55.2 us  [to_peer(): lax.ppermute(values, 'tensor', [(i, i ^ k) for i in range(self.tensor)])]
    unnamed x160 -> x150, local copies, waits for them, and re-layouts: 15.8 us -> 12.3 us
  transfers between devices with their start and end apart: 70 -> 70, of which waited for: 36 -> 37; matrix products, arithmetic and copies ran while one was open for 4% -> 4% of each run, Pallas kernels for 29% -> 30%
where the time goes in v5:
time: 414 us; the launch traced here: 412 us
  waiting for transfers between devices  148 us (36%)
  Pallas kernels  129 us (31%)
  starting transfers between devices  105 us (25%)
  local copies, waits for them, and re-layouts  21.1 us (5%)
  other arithmetic  7.6 us (2%)
    pallas_call x28, Pallas kernels, call(): pl.pallas_call(body, name=name, out_shape=outs, in_specs=in_specs, out_sp...  129 us
    ppermute x47, waiting for transfers between devices, to_peer(): lax.ppermute(values, 'tensor', [(i, i ^ k) for i in range(self.tensor)])  109 us
    ppermute x47, starting transfers between devices, to_peer(): lax.ppermute(values, 'tensor', [(i, i ^ k) for i in range(self.tensor)])  55.2 us
    all_to_all x6, starting transfers between devices, exchange(): lax.all_to_all(blocks, 'dp', 0, 0, axis_index_groups=groups, tiled=True)  36.7 us
    ppermute x10, waiting for transfers between devices, to_chip(): return lax.ppermute(values, 'dp', [(i, i ^ 2 * k) for i in range(self.dp)])  26.7 us
    ppermute x10, starting transfers between devices, to_chip(): return lax.ppermute(values, 'dp', [(i, i ^ 2 * k) for i in range(self.dp)])  12.4 us
    unnamed x150, local copies, waits for them, and re-layouts  12.3 us
    ppermute x7, waiting for transfers between devices, to_core(): return lax.ppermute(values, 'dp', self.swap)  9.91 us
  transfers between devices with their start and end apart: 70, of which 37 were waited for; matrix products, arithmetic and copies ran while one was open for 4% of the time, Pallas kernels for 30%

profile of v5, /device:TPU:8, one launch (start us, length us, event | category | flops | bytes accessed | tf_op | source)
XLA Modules:
  0.0 411.8 jit_solution(13718638403221222600)
XLA Ops:
  7.3 8.4 %collective-permute-done.4 = s32[256]{0:T(256)S(1)} collective-permute-done((s32[256]{0:T(256)S(1)}, s32[256]{0:T(256)S(1)}, u32[]{:S(2)}, u32[]{:S(2)}) %collective-permute-start.4) | collective-permute-done | bytes 1056 | tf_op jit(solution)/shard_map/ppermute | solution.py:88
  15.7 5.3 %all-to-all-start = ((bf16[4,4,256,256]{3,2,1,0:T(8,128)(2,1)}), bf16[4,4,256,256]{3,2,1,0:T(8,128)(2,1)S(1)}, u32[]{:S(2)}, u32[]{:S(2)}) async-start(bf16[4,4,256,256]{3,2,1,0:T(8,128)(2,1)} %pad_maximum_fusion.2), calls=%async_computation | async-start | bytes 4194304 | tf_op jit(solution)/shard_map/all_to_all | solution.py:105
  34.0 9.7 %collective-permute-done.1.refs_1_ = bf16[128,2048]{1,0:T(8,128)(2,1)S(1)} collective-permute-done((bf16[128,2048]{1,0:T(8,128)(2,1)S(1)}, bf16[128,2048]{1,0:T(8,128)(2,1)S(1)}, u32[]{:S(2)}, u32[]{:S(2)}) %collective-permute-start.1) | collective-permute-done | bytes 524320 | tf_op jit(solution)/shard_map/ppermute | solution.py:94
  43.6 9.9 %collective-permute-done.2.refs_2_ = bf16[128,2048]{1,0:T(8,128)(2,1)S(1)} collective-permute-done((bf16[128,2048]{1,0:T(8,128)(2,1)S(1)}, bf16[128,2048]{1,0:T(8,128)(2,1)S(1)}, u32[]{:S(2)}, u32[]{:S(2)}) %collective-permute-start.2) | collective-permute-done | bytes 524320 | tf_op jit(solution)/shard_map/ppermute | solution.py:94
  57.7 4.8 %first_norm.1.x.left = bf16[512,2048]{1,0:T(8,128)(2,1)} custom-call(s32[13]{0:T(128)} %pad_add_fusion.1.table, bf16[256,2048]{1,0:T(8,128)(2,1)} %own.2, f32[8,2048]{1,0:T(8,128)} %convert_element_type.8.vec, bf16[128,2048]{1,0:T(8,128)(2,1)} %copy-done.7, bf16[128,2048]{1,0:T(8,128)(2,1)} %copy-done.8, bf16[128,2048]{1,0:T(8,128)(2,1)} %copy-done.9, ...), custom_call_target="tpu_custom_call" | custom-call | flops 10485760 | bytes 5308468 | tf_op jit(solution)/shard_map/first_norm/pallas_call | solution.py:41
  65.1 7.7 %all-to-all-start.1 = ((bf16[4,256,1024]{2,1,0:T(8,128)(2,1)}), bf16[4,256,1024]{2,1,0:T(8,128)(2,1)}, u32[]{:S(2)}, u32[]{:S(2)}) async-start(bf16[4,256,1024]{2,1,0:T(8,128)(2,1)} %pad_maximum_fusion), calls=%async_computation.1 | async-start | bytes 4194304 | tf_op jit(solution)/shard_map/all_to_all | solution.py:105
  77.0 8.9 %attend.1 = (bf16[512,256]{1,0:T(8,128)(2,1)}, bf16[512,256]{1,0:T(8,128)(2,1)}, bf16[512,256]{1,0:T(8,128)(2,1)}, f32[4,256,256]{2,1,0:T(8,128)}, bf16[512,256]{1,0:T(8,128)(2,1)}) custom-call(s32[13]{0:T(128)} %pad_add_fusion.1.table, bf16[512,2048]{1,0:T(8,128)(2,1)} %first_norm.1.x.left, bf16[1,256]{1,0:T(2,128)(2,1)} %broadcast_in_dim.29.q_bias, ...), custom_call_target="tpu_custom_call" | custom-call | flops 1610612736 | bytes 8913972 | tf_op jit(solution)/shard_map/attend/pallas_call | solution.py:41
  86.0 4.8 %project_out.1 = (f32[64,2048]{1,0:T(8,128)}, f32[64,2048]{1,0:T(8,128)}, bf16[64,2048]{1,0:T(8,128)(2,1)}, bf16[64,2048]{1,0:T(8,128)(2,1)}, bf16[64,2048]{1,0:...) custom-call(s32[13]{0:T(128)} %pad_add_fusion.1.table, ...), custom_call_target="tpu_custom_call" | custom-call | flops 536870912 | bytes 7077940 | tf_op jit(solution)/shard_map/project_out/pallas_call | solution.py:41
  97.3 8.5 %collective-permute-done.10.refs_1_ = bf16[64,2048]{1,0:T(8,128)(2,1)S(1)} collective-permute-done((bf16[64,2048]{1,0:T(8,128)(2,1)}, bf16[64,2048]{1,0:T(8,128)(2,1)S(1)}, u32[]{:S(2)}, u32[]{:S(2)}) %collective-permute-start.10) | collective-permute-done | bytes 262176 | tf_op jit(solution)/shard_map/ppermute | solution.py:94
  112.9 5.5 %collective-permute-done.8.refs_2_ = bf16[64,2048]{1,0:T(8,128)(2,1)S(1)} collective-permute-done((bf16[64,2048]{1,0:T(8,128)(2,1)}, bf16[64,2048]{1,0:T(8,128)(2,1)S(1)}, u32[]{:S(2)}, u32[]{:S(2)}) %collective-permute-start.8) | collective-permute-done | bytes 262176 | tf_op jit(solution)/shard_map/ppermute | solution.py:94
  118.4 5.3 %collective-permute-done.12.refs_3_ = bf16[64,2048]{1,0:T(8,128)(2,1)S(1)} collective-permute-done((bf16[64,2048]{1,0:T(8,128)(2,1)}, bf16[64,2048]{1,0:T(8,128)(2,1)S(1)}, u32[]{:S(2)}, u32[]{:S(2)}) %collective-permute-start.12) | collective-permute-done | bytes 262176 | tf_op jit(solution)/shard_map/ppermute | solution.py:88
  138.9 6.2 %all-to-all-start.2 = ((bf16[4,1024,256]{2,1,0:T(8,128)(2,1)}), bf16[4,1024,256]{2,1,0:T(8,128)(2,1)}, u32[]{:S(2)}, u32[]{:S(2)}) async-start(bf16[4,1024,256]{2,1,0:T(8,128)(2,1)} %pad_maximum_fusion.1), calls=%async_computation.2 | async-start | bytes 4194304 | tf_op jit(solution)/shard_map/all_to_all | solution.py:105
  149.0 6.2 %collective-permute-done.15.refs_3_ = bf16[64,2048]{1,0:T(8,128)(2,1)S(1)} collective-permute-done((bf16[64,2048]{1,0:T(8,128)(2,1)S(1)}, bf16[64,2048]{1,0:T(8,128)(2,1)S(1)}, u32[]{:S(2)}, u32[]{:S(2)}) %collective-permute-start.15) | collective-permute-done | bytes 262176 | tf_op jit(solution)/shard_map/ppermute | solution.py:94
  160.7 5.0 %collective-permute-done.19.refs_7_ = bf16[64,2048]{1,0:T(8,128)(2,1)S(1)} collective-permute-done((bf16[64,2048]{1,0:T(8,128)(2,1)S(1)}, bf16[64,2048]{1,0:T(8,128)(2,1)S(1)}, u32[]{:S(2)}, u32[]{:S(2)}) %collective-permute-start.19) | collective-permute-done | bytes 262176 | tf_op jit(solution)/shard_map/ppermute | solution.py:94
  167.7 8.6 %upper.1 = (bf16[512,2048]{1,0:T(8,128)(2,1)}, bf16[512,1024]{1,0:T(8,128)(2,1)}, f32[512,1024]{1,0:T(8,128)}) custom-call(s32[13]{0:T(128)} %pad_add_fusion.1.table, bf16[1,1024]{1,0:T(2,128)(2,1)} %broadcast_in_dim.28.bias, bf16[64,2048]{1,0:T(8,128)(2,1)} %get-tuple-element.124.refs_0_, bf16[64,2048]{1,0:T(8,128)(2,1)} %copy-done.65, ...), custom_call_target="tpu_custom_call" | custom-call | flops 2147483648 | bytes 11536436 | tf_op jit(solution)/shard_map/upper/pallas_call | solution.py:41
  186.6 5.2 %grad_down_near.1 = bf16[4,1024,256]{2,1,0:T(8,128)(2,1)} custom-call(s32[13]{0:T(128)} %pad_add_fusion.1.table, bf16[512,1024]{1,0:T(8,128)(2,1)} %get-tuple-element.149.left, bf16[512,2048]{1,0:T(8,128)(2,1)} %upstream.1.refs_0_.g, bf16[4,1024,256]{2,1,0:T(8,128)(2,1)} %copy-done.6), custom_call_target="tpu_custom_call" | custom-call | flops 1073741824 | bytes 7340084 | tf_op jit(solution)/shard_map/grad_down_near/pallas_call | solution.py:41
  192.0 5.9 %all-to-all-start.3 = ((bf16[4,1024,256]{2,1,0:T(8,128)(2,1)}), bf16[4,1024,256]{2,1,0:T(8,128)(2,1)S(1)}, u32[]{:S(2)}, u32[]{:S(2)}) async-start(bf16[4,1024,256]{2,1,0:T(8,128)(2,1)} %grad_down_near.1), calls=%async_computation.3 | async-start | bytes 4194304 | tf_op jit(solution)/shard_map/all_to_all | solution.py:105
  197.9 8.0 %upper_grad.1 = (bf16[512,1024]{1,0:T(8,128)(2,1)}, f32[1,2048]{1,0:T(1,128)}) custom-call(s32[13]{0:T(128)} %pad_add_fusion.1.table, bf16[512,2048]{1,0:T(8,128)(2,1)} %upstream.1.refs_0_.g, f32[512,1024]{1,0:T(8,128)} %get-tuple-element.129.slope, bf16[4,1024,256]{2,1,0:T(8,128)(2,1)} %all-to-all-done.2.refs_0_, ...), custom_call_target="tpu_custom_call" | custom-call | flops 2147483648 | bytes 9445428 | tf_op jit(solution)/shard_map/upper_grad/pallas_call | solution.py:41
  210.7 7.3 %second_part.1 = (f32[64,2048]{1,0:T(8,128)}, f32[64,2048]{1,0:T(8,128)}, bf16[64,2048]{1,0:T(8,128)(2,1)}, bf16[64,2048]{1,0:T(8,128)(2,1)}, bf16[64,2048]{1,0:...) custom-call(s32[13]{0:T(128)} %pad_add_fusion.1.table, ...), custom_call_target="tpu_custom_call" | custom-call | flops 2147483648 | bytes 7864372 | tf_op jit(solution)/shard_map/second_part/pallas_call | solution.py:41
  222.1 5.4 %collective-permute-done.23.refs_0_ = bf16[64,2048]{1,0:T(8,128)(2,1)S(1)} collective-permute-done((bf16[64,2048]{1,0:T(8,128)(2,1)}, bf16[64,2048]{1,0:T(8,128)(2,1)S(1)}, u32[]{:S(2)}, u32[]{:S(2)}) %collective-permute-start.23) | collective-permute-done | bytes 262176 | tf_op jit(solution)/shard_map/ppermute | solution.py:94
  238.8 5.2 %collective-permute-done.27.refs_1_ = bf16[64,2048]{1,0:T(8,128)(2,1)S(1)} collective-permute-done((bf16[64,2048]{1,0:T(8,128)(2,1)}, bf16[64,2048]{1,0:T(8,128)(2,1)S(1)}, u32[]{:S(2)}, u32[]{:S(2)}) %collective-permute-start.27) | collective-permute-done | bytes 262176 | tf_op jit(solution)/shard_map/ppermute | solution.py:94
  243.9 5.4 %grad_up_near.1 = bf16[4,256,1024]{2,1,0:T(8,128)(2,1)} custom-call(s32[13]{0:T(128)} %pad_add_fusion.1.table, bf16[512,2048]{1,0:T(8,128)(2,1)} %get-tuple-element.133.left, bf16[512,1024]{1,0:T(8,128)(2,1)} %get-tuple-element.144.refs_0_.left, bf16[4,256,1024]{2,1,0:T(8,128)(2,1)} %collective-permute-done.29.refs_1_), custom_call_target="tpu_custom_call" | custom-call | flops 1073741824 | bytes 7340084 | tf_op jit(solution)/shard_map/grad_up_near/pallas_call | solution.py:41
  257.3 5.0 %collective-permute-done.31.refs_1_ = bf16[64,2048]{1,0:T(8,128)(2,1)S(1)} collective-permute-done((bf16[64,2048]{1,0:T(8,128)(2,1)}, bf16[64,2048]{1,0:T(8,128)(2,1)S(1)}, u32[]{:S(2)}, u32[]{:S(2)}) %collective-permute-start.31) | collective-permute-done | bytes 262176 | tf_op jit(solution)/shard_map/ppermute | solution.py:94
  263.5 6.6 %all-to-all-start.4 = ((bf16[4,256,1024]{2,1,0:T(8,128)(2,1)}), bf16[4,256,1024]{2,1,0:T(8,128)(2,1)}, u32[]{:S(2)}, u32[]{:S(2)}) async-start(bf16[4,256,1024]{2,1,0:T(8,128)(2,1)} %grad_up_near.1), calls=%async_computation.4 | async-start | bytes 4194304 | tf_op jit(solution)/shard_map/all_to_all | solution.py:105
  275.6 7.2 %feed.1 = (f32[64,2048]{1,0:T(8,128)}, f32[64,2048]{1,0:T(8,128)}, bf16[64,2048]{1,0:T(8,128)(2,1)}, bf16[64,2048]{1,0:T(8,128)(2,1)}, bf16[64,2048]{1,0:T(8,128...) custom-call(s32[13]{0:T(128)} %pad_add_fusion.1.table, ...), custom_call_target="tpu_custom_call" | custom-call | flops 2147483648 | bytes 7864372 | tf_op jit(solution)/shard_map/feed/pallas_call | solution.py:41
  289.9 11.8 %attend_back.1 = (bf16[512,2048]{1,0:T(8,128)(2,1)}, bf16[512,256]{1,0:T(8,128)(2,1)}, bf16[512,256]{1,0:T(8,128)(2,1)}, bf16[512,256]{1,0:T(8,128)(2,1)}, f32[1...) custom-call(s32[13]{0:T(128)} %pad_add_fusion.1.table, ...), custom_call_target="tpu_custom_call" | custom-call | flops 2147483648 | bytes 13635636 | tf_op jit(solution)/shard_map/attend_back/pallas_call | solution.py:41
  301.7 5.2 %grad_attention_far.1 = bf16[4,256,1024]{2,1,0:T(8,128)(2,1)} custom-call(s32[13]{0:T(128)} %pad_add_fusion.1.table, bf16[512,2048]{1,0:T(8,128)(2,1)} %first_norm.1.x.left, bf16[512,256]{1,0:T(8,128)(2,1)} %get-tuple-element.115.left.other, bf16[512,256]{1,0:T(8,128)(2,1)} %get-tuple-element.187.refs_0_, bf16[512,256]{1,0:T(8,128)(2,1)} %get-tuple-element.188.refs_1_, ...), custom_call_target="tpu_custom_call" | custom-call | flops 1073741824 | bytes 7340084 | tf_op jit(solution)/shard_map/grad_attention_far/pallas_call | solution.py:41
  317.0 6.3 %collective-permute-done.43.refs_1_ = bf16[64,2048]{1,0:T(8,128)(2,1)S(1)} collective-permute-done((bf16[64,2048]{1,0:T(8,128)(2,1)}, bf16[64,2048]{1,0:T(8,128)(2,1)S(1)}, u32[]{:S(2)}, u32[]{:S(2)}) %collective-permute-start.43) | collective-permute-done | bytes 262176 | tf_op jit(solution)/shard_map/ppermute | solution.py:94
  330.3 5.9 %grad_attention_near.1 = bf16[4,256,1024]{2,1,0:T(8,128)(2,1)} custom-call(s32[13]{0:T(128)} %pad_add_fusion.1.table, bf16[512,2048]{1,0:T(8,128)(2,1)} %first_norm.1.x.left, bf16[512,256]{1,0:T(8,128)(2,1)} %get-tuple-element.115.left.other, bf16[512,256]{1,0:T(8,128)(2,1)} %get-tuple-element.187.refs_0_, bf16[512,256]{1,0:T(8,128)(2,1)} %get-tuple-element.188.refs_1_, ...), custom_call_target="tpu_custom_call" | custom-call | flops 1073741824 | bytes 9437236 | tf_op jit(solution)/shard_map/grad_attention_near/pallas_call | solution.py:41
  346.8 5.1 %all-to-all-start.5 = ((bf16[4,256,1024]{2,1,0:T(8,128)(2,1)}), bf16[4,256,1024]{2,1,0:T(8,128)(2,1)S(1)}, u32[]{:S(2)}, u32[]{:S(2)}) async-start(bf16[4,256,1024]{2,1,0:T(8,128)(2,1)} %grad_attention_near.1), calls=%async_computation.5 | async-start | bytes 4194304 | tf_op jit(solution)/shard_map/all_to_all | solution.py:105
  372.2 6.7 %collective-permute-done.59 = f32[6,2048]{1,0:T(8,128)S(1)} collective-permute-done((f32[6,2048]{1,0:T(8,128)S(1)}, f32[6,2048]{1,0:T(8,128)S(1)}, u32[]{:S(2)}, u32[]{:S(2)}) %collective-permute-start.59) | collective-permute-done | bytes 49184 | tf_op jit(solution)/shard_map/ppermute | solution.py:94
  388.9 8.2 %collective-permute-done.62 = f32[8,2048]{1,0:T(8,128)S(1)} collective-permute-done((f32[8,2048]{1,0:T(8,128)S(1)}, f32[8,2048]{1,0:T(8,128)S(1)}, u32[]{:S(2)}, u32[]{:S(2)}) %collective-permute-start.62) | collective-permute-done | bytes 65568 | tf_op jit(solution)/shard_map/ppermute | solution.py:88
  (342 shorter events, 195.3 us)
Async XLA Ops:
  15.7 49.3 %all-to-all-start = ((bf16[4,4,256,256]{3,2,1,0:T(8,128)(2,1)}), bf16[4,4,256,256]{3,2,1,0:T(8,128)(2,1)S(1)}, u32[]{:S(2)}, u32[]{:S(2)}) async-start(bf16[4,4,256,256]{3,2,1,0:T(8,128)(2,1)} %pad_maximum_fusion.2), calls=%async_computation | async-start | bytes 4194304 | tf_op jit(solution)/shard_map/all_to_all | solution.py:105
  28.8 14.9 %collective-permute-start.1 = (bf16[128,2048]{1,0:T(8,128)(2,1)S(1)}, bf16[128,2048]{1,0:T(8,128)(2,1)S(1)}, u32[]{:S(2)}, u32[]{:S(2)}) collective-permute-start(bf16[128,2048]{1,0:T(8,128)(2,1)S(1)} %collective-permute-done.refs_0_), channel_id=1, source_target_pairs={{0,1},{1,0},{2,3},{3,2},{4,5},{5,4},{6,7},{7,6},{8,9},{9,8},{10,11... | collective-permute-start | bytes 1572872 | tf_op jit(solution)/shard_map/ppermute | solution.py:94
  30.3 23.2 %collective-permute-start.2 = (bf16[128,2048]{1,0:T(8,128)(2,1)S(1)}, bf16[128,2048]{1,0:T(8,128)(2,1)S(1)}, u32[]{:S(2)}, u32[]{:S(2)}) collective-permute-start(bf16[128,2048]{1,0:T(8,128)(2,1)S(1)} %collective-permute-done.refs_0_), channel_id=1, source_target_pairs={{0,2},{1,3},{2,0},{3,1},{4,6},{5,7},{6,4},{7,5},{8,10},{9,11},{10,... | collective-permute-start | bytes 1572872 | tf_op jit(solution)/shard_map/ppermute | solution.py:94
  31.9 22.4 %collective-permute-start.3 = (bf16[128,2048]{1,0:T(8,128)(2,1)S(1)}, bf16[128,2048]{1,0:T(8,128)(2,1)}, u32[]{:S(2)}, u32[]{:S(2)}) collective-permute-start(bf16[128,2048]{1,0:T(8,128)(2,1)S(1)} %collective-permute-done.refs_0_), channel_id=1, source_target_pairs={{0,3},{1,2},{2,1},{3,0},{4,7},{5,6},{6,5},{7,4},{8,11},{9,10},{10,... | collective-permute-start | bytes 1572872 | tf_op jit(solution)/shard_map/ppermute | solution.py:94
  65.1 73.8 %all-to-all-start.1 = ((bf16[4,256,1024]{2,1,0:T(8,128)(2,1)}), bf16[4,256,1024]{2,1,0:T(8,128)(2,1)}, u32[]{:S(2)}, u32[]{:S(2)}) async-start(bf16[4,256,1024]{2,1,0:T(8,128)(2,1)} %pad_maximum_fusion), calls=%async_computation.1 | async-start | bytes 4194304 | tf_op jit(solution)/shard_map/all_to_all | solution.py:105
  90.8 15.1 %collective-permute-start.10 = (bf16[64,2048]{1,0:T(8,128)(2,1)}, bf16[64,2048]{1,0:T(8,128)(2,1)S(1)}, u32[]{:S(2)}, u32[]{:S(2)}) collective-permute-start(bf16[64,2048]{1,0:T(8,128)(2,1)} %get-tuple-element.122), channel_id=1, source_target_pairs={{0,2},{1,3},{2,0},{3,1},{4,6},{5,7},{6,4},{7,5},{8,10},{9,11},{10,... | collective-permute-start | bytes 786440 | tf_op jit(solution)/shard_map/ppermute | solution.py:94
  92.3 15.9 %collective-permute-start.11 = (bf16[64,2048]{1,0:T(8,128)(2,1)}, bf16[64,2048]{1,0:T(8,128)(2,1)S(1)}, u32[]{:S(2)}, u32[]{:S(2)}) collective-permute-start(bf16[64,2048]{1,0:T(8,128)(2,1)} %get-tuple-element.123), channel_id=1, source_target_pairs={{0,3},{1,2},{2,1},{3,0},{4,7},{5,6},{6,5},{7,4},{8,11},{9,10},{10,... | collective-permute-start | bytes 786440 | tf_op jit(solution)/shard_map/ppermute | solution.py:94
  93.8 14.5 %collective-permute-start.9 = (bf16[64,2048]{1,0:T(8,128)(2,1)}, bf16[64,2048]{1,0:T(8,128)(2,1)S(1)}, u32[]{:S(2)}, u32[]{:S(2)}) collective-permute-start(bf16[64,2048]{1,0:T(8,128)(2,1)} %get-tuple-element.121), channel_id=1, source_target_pairs={{0,1},{1,0},{2,3},{3,2},{4,5},{5,4},{6,7},{7,6},{8,9},{9,8},{10,11... | collective-permute-start | bytes 786440 | tf_op jit(solution)/shard_map/ppermute | solution.py:94
  94.3 18.6 %collective-permute-start.6 = (bf16[64,2048]{1,0:T(8,128)(2,1)}, bf16[64,2048]{1,0:T(8,128)(2,1)S(1)}, u32[]{:S(2)}, u32[]{:S(2)}) collective-permute-start(bf16[64,2048]{1,0:T(8,128)(2,1)} %get-tuple-element.117), channel_id=1, source_target_pairs={{0,1},{1,0},{2,3},{3,2},{4,5},{5,4},{6,7},{7,6},{8,9},{9,8},{10,11... | collective-permute-start | bytes 786440 | tf_op jit(solution)/shard_map/ppermute | solution.py:94
  95.8 17.1 %collective-permute-start.7 = (bf16[64,2048]{1,0:T(8,128)(2,1)}, bf16[64,2048]{1,0:T(8,128)(2,1)S(1)}, u32[]{:S(2)}, u32[]{:S(2)}) collective-permute-start(bf16[64,2048]{1,0:T(8,128)(2,1)} %get-tuple-element.118), channel_id=1, source_target_pairs={{0,2},{1,3},{2,0},{3,1},{4,6},{5,7},{6,4},{7,5},{8,10},{9,11},{10,... | collective-permute-start | bytes 786440 | tf_op jit(solution)/shard_map/ppermute | solution.py:94
  138.9 27.5 %collective-permute-start.20 = (bf16[4,256,1024]{2,1,0:T(8,128)(2,1)}, bf16[4,256,1024]{2,1,0:T(8,128)(2,1)S(1)}, u32[]{:S(2)}, u32[]{:S(2)}) collective-permute-start(bf16[4,256,1024]{2,1,0:T(8,128)(2,1)} %all-to-all-done.1.refs_8_.refs_0_), channel_id=1, source_target_pairs={{0,4},{4,0},{8,12},{12,8},{16,20},{20,16},{24,28},{28,24},{1,5},{5... | collective-permute-start | bytes 6291464 | tf_op jit(solution)/shard_map/ppermute | solution.py:85
  138.9 53.0 %all-to-all-start.2 = ((bf16[4,1024,256]{2,1,0:T(8,128)(2,1)}), bf16[4,1024,256]{2,1,0:T(8,128)(2,1)}, u32[]{:S(2)}, u32[]{:S(2)}) async-start(bf16[4,1024,256]{2,1,0:T(8,128)(2,1)} %pad_maximum_fusion.1), calls=%async_computation.2 | async-start | bytes 4194304 | tf_op jit(solution)/shard_map/all_to_all | solution.py:105
  148.5 17.1 %collective-permute-start.19 = (bf16[64,2048]{1,0:T(8,128)(2,1)S(1)}, bf16[64,2048]{1,0:T(8,128)(2,1)S(1)}, u32[]{:S(2)}, u32[]{:S(2)}) collective-permute-start(bf16[64,2048]{1,0:T(8,128)(2,1)S(1)} %collective-permute-done.16.refs_4_), channel_id=1, source_target_pairs={{0,3},{1,2},{2,1},{3,0},{4,7},{5,6},{6,5},{7,4},{8,11},{9,10},{10,... | collective-permute-start | bytes 786440 | tf_op jit(solution)/shard_map/ppermute | solution.py:94
  192.0 57.4 %all-to-all-start.3 = ((bf16[4,1024,256]{2,1,0:T(8,128)(2,1)}), bf16[4,1024,256]{2,1,0:T(8,128)(2,1)S(1)}, u32[]{:S(2)}, u32[]{:S(2)}) async-start(bf16[4,1024,256]{2,1,0:T(8,128)(2,1)} %grad_down_near.1), calls=%async_computation.3 | async-start | bytes 4194304 | tf_op jit(solution)/shard_map/all_to_all | solution.py:105
  210.5 33.4 %collective-permute-start.29 = (bf16[4,256,1024]{2,1,0:T(8,128)(2,1)}, bf16[4,256,1024]{2,1,0:T(8,128)(2,1)}, u32[]{:S(2)}, u32[]{:S(2)}) collective-permute-start(bf16[4,256,1024]{2,1,0:T(8,128)(2,1)} %grad_up_far.1), channel_id=1, source_target_pairs={{0,4},{4,0},{8,12},{12,8},{16,20},{20,16},{24,28},{28,24},{1,5},{5... | collective-permute-start | bytes 6291464 | tf_op jit(solution)/shard_map/ppermute | solution.py:85
  219.1 15.1 %collective-permute-start.25 = (bf16[64,2048]{1,0:T(8,128)(2,1)}, bf16[64,2048]{1,0:T(8,128)(2,1)}, u32[]{:S(2)}, u32[]{:S(2)}) collective-permute-start(bf16[64,2048]{1,0:T(8,128)(2,1)} %get-tuple-element.140), channel_id=1, source_target_pairs={{0,3},{1,2},{2,1},{3,0},{4,7},{5,6},{6,5},{7,4},{8,11},{9,10},{10,... | collective-permute-start | bytes 786440 | tf_op jit(solution)/shard_map/ppermute | solution.py:94
  221.6 17.2 %collective-permute-start.26 = (bf16[64,2048]{1,0:T(8,128)(2,1)}, bf16[64,2048]{1,0:T(8,128)(2,1)S(1)}, u32[]{:S(2)}, u32[]{:S(2)}) collective-permute-start(bf16[64,2048]{1,0:T(8,128)(2,1)} %get-tuple-element.141), channel_id=1, source_target_pairs={{0,1},{1,0},{2,3},{3,2},{4,5},{5,4},{6,7},{7,6},{8,9},{9,8},{10,11... | collective-permute-start | bytes 786440 | tf_op jit(solution)/shard_map/ppermute | solution.py:94
  227.5 16.4 %collective-permute-start.27 = (bf16[64,2048]{1,0:T(8,128)(2,1)}, bf16[64,2048]{1,0:T(8,128)(2,1)S(1)}, u32[]{:S(2)}, u32[]{:S(2)}) collective-permute-start(bf16[64,2048]{1,0:T(8,128)(2,1)} %get-tuple-element.142), channel_id=1, source_target_pairs={{0,2},{1,3},{2,0},{3,1},{4,6},{5,7},{6,4},{7,5},{8,10},{9,11},{10,... | collective-permute-start | bytes 786440 | tf_op jit(solution)/shard_map/ppermute | solution.py:94
  263.5 82.6 %all-to-all-start.4 = ((bf16[4,256,1024]{2,1,0:T(8,128)(2,1)}), bf16[4,256,1024]{2,1,0:T(8,128)(2,1)}, u32[]{:S(2)}, u32[]{:S(2)}) async-start(bf16[4,256,1024]{2,1,0:T(8,128)(2,1)} %grad_up_near.1), calls=%async_computation.4 | async-start | bytes 4194304 | tf_op jit(solution)/shard_map/all_to_all | solution.py:105
  273.6 15.6 %collective-permute-start.37 = (bf16[64,2048]{1,0:T(8,128)(2,1)S(1)}, bf16[64,2048]{1,0:T(8,128)(2,1)S(1)}, u32[]{:S(2)}, u32[]{:S(2)}) collective-permute-start(bf16[64,2048]{1,0:T(8,128)(2,1)S(1)} %collective-permute-done.34.refs_4_), channel_id=1, source_target_pairs={{0,3},{1,2},{2,1},{3,0},{4,7},{5,6},{6,5},{7,4},{8,11},{9,10},{10,... | collective-permute-start | bytes 786440 | tf_op jit(solution)/shard_map/ppermute | solution.py:94
  306.9 22.0 %collective-permute-start.52 = (bf16[4,256,1024]{2,1,0:T(8,128)(2,1)}, bf16[4,256,1024]{2,1,0:T(8,128)(2,1)S(1)}, u32[]{:S(2)}, u32[]{:S(2)}) collective-permute-start(bf16[4,256,1024]{2,1,0:T(8,128)(2,1)} %grad_attention_far.1), channel_id=1, source_target_pairs={{0,4},{4,0},{8,12},{12,8},{16,20},{20,16},{24,28},{28,24},{1,5},{5... | collective-permute-start | bytes 6291464 | tf_op jit(solution)/shard_map/ppermute | solution.py:85
  308.3 15.0 %collective-permute-start.43 = (bf16[64,2048]{1,0:T(8,128)(2,1)}, bf16[64,2048]{1,0:T(8,128)(2,1)S(1)}, u32[]{:S(2)}, u32[]{:S(2)}) collective-permute-start(bf16[64,2048]{1,0:T(8,128)(2,1)} %get-tuple-element.171), channel_id=1, source_target_pairs={{0,2},{1,3},{2,0},{3,1},{4,6},{5,7},{6,4},{7,5},{8,10},{9,11},{10,... | collective-permute-start | bytes 786440 | tf_op jit(solution)/shard_map/ppermute | solution.py:94
  310.4 17.2 %collective-permute-start.38 = (bf16[64,2048]{1,0:T(8,128)(2,1)}, bf16[64,2048]{1,0:T(8,128)(2,1)S(1)}, u32[]{:S(2)}, u32[]{:S(2)}) collective-permute-start(bf16[64,2048]{1,0:T(8,128)(2,1)} %get-tuple-element.177), channel_id=1, source_target_pairs={{0,1},{1,0},{2,3},{3,2},{4,5},{5,4},{6,7},{7,6},{8,9},{9,8},{10,11... | collective-permute-start | bytes 786440 | tf_op jit(solution)/shard_map/ppermute | solution.py:94
  316.3 19.8 %collective-permute-start.53 = (bf16[64,2048]{1,0:T(8,128)(2,1)S(1)}, bf16[64,2048]{1,0:T(8,128)(2,1)}, u32[]{:S(2)}, u32[]{:S(2)}) collective-permute-start(bf16[64,2048]{1,0:T(8,128)(2,1)S(1)} %copy-done.63), channel_id=1, source_target_pairs={{0,2},{1,3},{2,0},{3,1},{4,6},{5,7},{6,4},{7,5},{8,10},{9,11},{10,... | collective-permute-start | bytes 786440 | tf_op jit(solution)/shard_map/ppermute | solution.py:94
  329.0 16.1 %collective-permute-start.40 = (bf16[64,2048]{1,0:T(8,128)(2,1)}, bf16[64,2048]{1,0:T(8,128)(2,1)S(1)}, u32[]{:S(2)}, u32[]{:S(2)}) collective-permute-start(bf16[64,2048]{1,0:T(8,128)(2,1)} %get-tuple-element.179), channel_id=1, source_target_pairs={{0,2},{1,3},{2,0},{3,1},{4,6},{5,7},{6,4},{7,5},{8,10},{9,11},{10,... | collective-permute-start | bytes 786440 | tf_op jit(solution)/shard_map/ppermute | solution.py:94
  346.8 60.6 %all-to-all-start.5 = ((bf16[4,256,1024]{2,1,0:T(8,128)(2,1)}), bf16[4,256,1024]{2,1,0:T(8,128)(2,1)S(1)}, u32[]{:S(2)}, u32[]{:S(2)}) async-start(bf16[4,256,1024]{2,1,0:T(8,128)(2,1)} %grad_attention_near.1), calls=%async_computation.5 | async-start | bytes 4194304 | tf_op jit(solution)/shard_map/all_to_all | solution.py:105
  362.4 18.1 %collective-permute-start.49 = (bf16[64,2048]{1,0:T(8,128)(2,1)}, bf16[64,2048]{1,0:T(8,128)(2,1)S(1)}, u32[]{:S(2)}, u32[]{:S(2)}) collective-permute-start(bf16[64,2048]{1,0:T(8,128)(2,1)} %get-tuple-element.184), channel_id=1, source_target_pairs={{0,1},{1,0},{2,3},{3,2},{4,5},{5,4},{6,7},{7,6},{8,9},{9,8},{10,11... | collective-permute-start | bytes 786440 | tf_op jit(solution)/shard_map/ppermute | solution.py:94
  363.9 16.6 %collective-permute-start.50 = (bf16[64,2048]{1,0:T(8,128)(2,1)}, bf16[64,2048]{1,0:T(8,128)(2,1)S(1)}, u32[]{:S(2)}, u32[]{:S(2)}) collective-permute-start(bf16[64,2048]{1,0:T(8,128)(2,1)} %get-tuple-element.185), channel_id=1, source_target_pairs={{0,2},{1,3},{2,0},{3,1},{4,6},{5,7},{6,4},{7,5},{8,10},{9,11},{10,... | collective-permute-start | bytes 786440 | tf_op jit(solution)/shard_map/ppermute | solution.py:94
  365.1 15.4 %collective-permute-start.51 = (bf16[64,2048]{1,0:T(8,128)(2,1)}, bf16[64,2048]{1,0:T(8,128)(2,1)}, u32[]{:S(2)}, u32[]{:S(2)}) collective-permute-start(bf16[64,2048]{1,0:T(8,128)(2,1)} %get-tuple-element.186), channel_id=1, source_target_pairs={{0,3},{1,2},{2,1},{3,0},{4,7},{5,6},{6,5},{7,4},{8,11},{9,10},{10,... | collective-permute-start | bytes 786440 | tf_op jit(solution)/shard_map/ppermute | solution.py:94
  383.6 18.2 %collective-permute-start.56 = (bf16[64,2048]{1,0:T(8,128)(2,1)}, bf16[64,2048]{1,0:T(8,128)(2,1)S(1)}, u32[]{:S(2)}, u32[]{:S(2)}) collective-permute-start(bf16[64,2048]{1,0:T(8,128)(2,1)} %outputs_own.1.refs_0_), channel_id=1, source_target_pairs={{0,1},{1,0},{2,3},{3,2},{4,5},{5,4},{6,7},{7,6},{8,9},{9,8},{10,11... | collective-permute-start | bytes 786440 | tf_op jit(solution)/shard_map/ppermute | solution.py:94
  385.0 16.8 %collective-permute-start.57 = (bf16[64,2048]{1,0:T(8,128)(2,1)}, bf16[64,2048]{1,0:T(8,128)(2,1)S(1)}, u32[]{:S(2)}, u32[]{:S(2)}) collective-permute-start(bf16[64,2048]{1,0:T(8,128)(2,1)} %outputs_own.1.refs_0_), channel_id=1, source_target_pairs={{0,2},{1,3},{2,0},{3,1},{4,6},{5,7},{6,4},{7,5},{8,10},{9,11},{10,... | collective-permute-start | bytes 786440 | tf_op jit(solution)/shard_map/ppermute | solution.py:94
  385.4 16.4 %collective-permute-start.58 = (bf16[64,2048]{1,0:T(8,128)(2,1)}, bf16[64,2048]{1,0:T(8,128)(2,1)S(1)}, u32[]{:S(2)}, u32[]{:S(2)}) collective-permute-start(bf16[64,2048]{1,0:T(8,128)(2,1)} %outputs_own.1.refs_0_), channel_id=1, source_target_pairs={{0,3},{1,2},{2,1},{3,0},{4,7},{5,6},{6,5},{7,4},{8,11},{9,10},{10,... | collective-permute-start | bytes 786440 | tf_op jit(solution)/shard_map/ppermute | solution.py:94
  (112 other events, 982.4 us)

commit v6 on v5

--- a/solution.py
+++ b/solution.py
@@ -747,8 +747,8 @@
         [after(part[0], ring_down, near_up), g_own, vec, normed_two, inverse_two] + received,
     )
     hidden_chunks = at.spread(hidden_low_own)
-    ring_up = at.exchange(after(near_up, hidden_chunks[tensor]))
     feed = layer.project("feed", after(activated, hidden_low_own), all_down, False)
+    ring_up = at.exchange(after(near_up, hidden_chunks[tensor], feed[0]))
     back = call(
         functools.partial(attend_back_body, side_at, chunk_count),
         "attend_back",

time: 414 us -> 413 us (level)
    unnamed x150 -> x156, local copies, waits for them, and re-layouts: 12.3 us -> 12.4 us
  transfers between devices with their start and end apart: 70 -> 70, of which waited for: 37 -> 34; matrix products, arithmetic and copies ran while one was open for 4% -> 4% of each run, Pallas kernels for 30% -> 30%
where the time goes in v6:
time: 413 us; the launch traced here: 410 us
  waiting for transfers between devices  146 us (35%)
  Pallas kernels  129 us (31%)
  starting transfers between devices  106 us (26%)
  local copies, waits for them, and re-layouts  21.1 us (5%)
  other arithmetic  7.54 us (2%)
    pallas_call x28, Pallas kernels, call(): pl.pallas_call(body, name=name, out_shape=outs, in_specs=in_specs, out_sp...  129 us
    ppermute x47, waiting for transfers between devices, to_peer(): lax.ppermute(values, 'tensor', [(i, i ^ k) for i in range(self.tensor)])  108 us
    ppermute x47, starting transfers between devices, to_peer(): lax.ppermute(values, 'tensor', [(i, i ^ k) for i in range(self.tensor)])  58.5 us
    all_to_all x6, starting transfers between devices, exchange(): lax.all_to_all(blocks, 'dp', 0, 0, axis_index_groups=groups, tiled=True)  34.8 us
    ppermute x10, waiting for transfers between devices, to_chip(): return lax.ppermute(values, 'dp', [(i, i ^ 2 * k) for i in range(self.dp)])  24.7 us
    unnamed x156, local copies, waits for them, and re-layouts  12.4 us
    ppermute x10, starting transfers between devices, to_chip(): return lax.ppermute(values, 'dp', [(i, i ^ 2 * k) for i in range(self.dp)])  12.2 us
    ppermute x7, waiting for transfers between devices, to_core(): return lax.ppermute(values, 'dp', self.swap)  9.91 us
  transfers between devices with their start and end apart: 70, of which 34 were waited for; matrix products, arithmetic and copies ran while one was open for 4% of the time, Pallas kernels for 30%

profile of v6, /device:TPU:8, one launch (start us, length us, event | category | flops | bytes accessed | tf_op | source)
XLA Modules:
  0.0 410.5 jit_solution(15033703354893011286)
XLA Ops:
  7.3 8.4 %collective-permute-done.4 = s32[256]{0:T(256)S(1)} collective-permute-done((s32[256]{0:T(256)S(1)}, s32[256]{0:T(256)S(1)}, u32[]{:S(2)}, u32[]{:S(2)}) %collective-permute-start.4) | collective-permute-done | bytes 1056 | tf_op jit(solution)/shard_map/ppermute | solution.py:88
  15.7 5.3 %all-to-all-start = ((bf16[4,4,256,256]{3,2,1,0:T(8,128)(2,1)}), bf16[4,4,256,256]{3,2,1,0:T(8,128)(2,1)S(1)}, u32[]{:S(2)}, u32[]{:S(2)}) async-start(bf16[4,4,256,256]{3,2,1,0:T(8,128)(2,1)} %pad_maximum_fusion.2), calls=%async_computation | async-start | bytes 4194304 | tf_op jit(solution)/shard_map/all_to_all | solution.py:105
  33.9 9.7 %collective-permute-done.1.refs_1_ = bf16[128,2048]{1,0:T(8,128)(2,1)S(1)} collective-permute-done((bf16[128,2048]{1,0:T(8,128)(2,1)S(1)}, bf16[128,2048]{1,0:T(8,128)(2,1)S(1)}, u32[]{:S(2)}, u32[]{:S(2)}) %collective-permute-start.1) | collective-permute-done | bytes 524320 | tf_op jit(solution)/shard_map/ppermute | solution.py:94
  43.6 9.9 %collective-permute-done.2.refs_2_ = bf16[128,2048]{1,0:T(8,128)(2,1)S(1)} collective-permute-done((bf16[128,2048]{1,0:T(8,128)(2,1)S(1)}, bf16[128,2048]{1,0:T(8,128)(2,1)S(1)}, u32[]{:S(2)}, u32[]{:S(2)}) %collective-permute-start.2) | collective-permute-done | bytes 524320 | tf_op jit(solution)/shard_map/ppermute | solution.py:94
  57.7 4.8 %first_norm.1.x.left = bf16[512,2048]{1,0:T(8,128)(2,1)} custom-call(s32[13]{0:T(128)} %pad_add_fusion.1.table, bf16[256,2048]{1,0:T(8,128)(2,1)} %own.2, f32[8,2048]{1,0:T(8,128)} %convert_element_type.8.vec, bf16[128,2048]{1,0:T(8,128)(2,1)} %copy-done.6, bf16[128,2048]{1,0:T(8,128)(2,1)} %copy-done.7, bf16[128,2048]{1,0:T(8,128)(2,1)} %copy-done.8, ...), custom_call_target="tpu_custom_call" | custom-call | flops 10485760 | bytes 5308468 | tf_op jit(solution)/shard_map/first_norm/pallas_call | solution.py:41
  65.1 7.7 %all-to-all-start.1 = ((bf16[4,256,1024]{2,1,0:T(8,128)(2,1)}), bf16[4,256,1024]{2,1,0:T(8,128)(2,1)}, u32[]{:S(2)}, u32[]{:S(2)}) async-start(bf16[4,256,1024]{2,1,0:T(8,128)(2,1)} %pad_maximum_fusion), calls=%async_computation.1 | async-start | bytes 4194304 | tf_op jit(solution)/shard_map/all_to_all | solution.py:105
  77.0 8.9 %attend.1 = (bf16[512,256]{1,0:T(8,128)(2,1)}, bf16[512,256]{1,0:T(8,128)(2,1)}, bf16[512,256]{1,0:T(8,128)(2,1)}, f32[4,256,256]{2,1,0:T(8,128)}, bf16[512,256]{1,0:T(8,128)(2,1)}) custom-call(s32[13]{0:T(128)} %pad_add_fusion.1.table, bf16[512,2048]{1,0:T(8,128)(2,1)} %first_norm.1.x.left, bf16[1,256]{1,0:T(2,128)(2,1)} %broadcast_in_dim.29.q_bias, ...), custom_call_target="tpu_custom_call" | custom-call | flops 1610612736 | bytes 8913972 | tf_op jit(solution)/shard_map/attend/pallas_call | solution.py:41
  85.9 4.7 %project_out.1 = (f32[64,2048]{1,0:T(8,128)}, f32[64,2048]{1,0:T(8,128)}, bf16[64,2048]{1,0:T(8,128)(2,1)}, bf16[64,2048]{1,0:T(8,128)(2,1)}, bf16[64,2048]{1,0:...) custom-call(s32[13]{0:T(128)} %pad_add_fusion.1.table, ...), custom_call_target="tpu_custom_call" | custom-call | flops 536870912 | bytes 7077940 | tf_op jit(solution)/shard_map/project_out/pallas_call | solution.py:41
  97.3 8.5 %collective-permute-done.10.refs_1_ = bf16[64,2048]{1,0:T(8,128)(2,1)S(1)} collective-permute-done((bf16[64,2048]{1,0:T(8,128)(2,1)}, bf16[64,2048]{1,0:T(8,128)(2,1)S(1)}, u32[]{:S(2)}, u32[]{:S(2)}) %collective-permute-start.10) | collective-permute-done | bytes 262176 | tf_op jit(solution)/shard_map/ppermute | solution.py:94
  112.9 5.5 %collective-permute-done.8.refs_2_ = bf16[64,2048]{1,0:T(8,128)(2,1)S(1)} collective-permute-done((bf16[64,2048]{1,0:T(8,128)(2,1)}, bf16[64,2048]{1,0:T(8,128)(2,1)S(1)}, u32[]{:S(2)}, u32[]{:S(2)}) %collective-permute-start.8) | collective-permute-done | bytes 262176 | tf_op jit(solution)/shard_map/ppermute | solution.py:94
  118.4 5.4 %collective-permute-done.12.refs_3_ = bf16[64,2048]{1,0:T(8,128)(2,1)S(1)} collective-permute-done((bf16[64,2048]{1,0:T(8,128)(2,1)}, bf16[64,2048]{1,0:T(8,128)(2,1)S(1)}, u32[]{:S(2)}, u32[]{:S(2)}) %collective-permute-start.12) | collective-permute-done | bytes 262176 | tf_op jit(solution)/shard_map/ppermute | solution.py:88
  138.8 6.2 %all-to-all-start.2 = ((bf16[4,1024,256]{2,1,0:T(8,128)(2,1)}), bf16[4,1024,256]{2,1,0:T(8,128)(2,1)}, u32[]{:S(2)}, u32[]{:S(2)}) async-start(bf16[4,1024,256]{2,1,0:T(8,128)(2,1)} %pad_maximum_fusion.1), calls=%async_computation.2 | async-start | bytes 4194304 | tf_op jit(solution)/shard_map/all_to_all | solution.py:105
  148.9 6.2 %collective-permute-done.15.refs_3_ = bf16[64,2048]{1,0:T(8,128)(2,1)S(1)} collective-permute-done((bf16[64,2048]{1,0:T(8,128)(2,1)S(1)}, bf16[64,2048]{1,0:T(8,128)(2,1)S(1)}, u32[]{:S(2)}, u32[]{:S(2)}) %collective-permute-start.15) | collective-permute-done | bytes 262176 | tf_op jit(solution)/shard_map/ppermute | solution.py:94
  160.6 5.0 %collective-permute-done.19.refs_7_ = bf16[64,2048]{1,0:T(8,128)(2,1)S(1)} collective-permute-done((bf16[64,2048]{1,0:T(8,128)(2,1)S(1)}, bf16[64,2048]{1,0:T(8,128)(2,1)S(1)}, u32[]{:S(2)}, u32[]{:S(2)}) %collective-permute-start.19) | collective-permute-done | bytes 262176 | tf_op jit(solution)/shard_map/ppermute | solution.py:94
  167.6 8.7 %upper.1 = (bf16[512,2048]{1,0:T(8,128)(2,1)}, bf16[512,1024]{1,0:T(8,128)(2,1)}, f32[512,1024]{1,0:T(8,128)}) custom-call(s32[13]{0:T(128)} %pad_add_fusion.1.table, bf16[1,1024]{1,0:T(2,128)(2,1)} %broadcast_in_dim.28.bias, bf16[64,2048]{1,0:T(8,128)(2,1)} %get-tuple-element.124.refs_0_, bf16[64,2048]{1,0:T(8,128)(2,1)} %copy-done.68, ...), custom_call_target="tpu_custom_call" | custom-call | flops 2147483648 | bytes 11536436 | tf_op jit(solution)/shard_map/upper/pallas_call | solution.py:41
  186.5 5.2 %grad_down_near.1 = bf16[4,1024,256]{2,1,0:T(8,128)(2,1)} custom-call(s32[13]{0:T(128)} %pad_add_fusion.1.table, bf16[512,1024]{1,0:T(8,128)(2,1)} %get-tuple-element.149.left, bf16[512,2048]{1,0:T(8,128)(2,1)} %upstream.1.refs_0_.g, bf16[4,1024,256]{2,1,0:T(8,128)(2,1)} %copy-done.5), custom_call_target="tpu_custom_call" | custom-call | flops 1073741824 | bytes 7340084 | tf_op jit(solution)/shard_map/grad_down_near/pallas_call | solution.py:41
  191.8 5.9 %all-to-all-start.3 = ((bf16[4,1024,256]{2,1,0:T(8,128)(2,1)}), bf16[4,1024,256]{2,1,0:T(8,128)(2,1)S(1)}, u32[]{:S(2)}, u32[]{:S(2)}) async-start(bf16[4,1024,256]{2,1,0:T(8,128)(2,1)} %grad_down_near.1), calls=%async_computation.3 | async-start | bytes 4194304 | tf_op jit(solution)/shard_map/all_to_all | solution.py:105
  197.8 8.0 %upper_grad.1 = (bf16[512,1024]{1,0:T(8,128)(2,1)}, f32[1,2048]{1,0:T(1,128)}) custom-call(s32[13]{0:T(128)} %pad_add_fusion.1.table, bf16[512,2048]{1,0:T(8,128)(2,1)} %upstream.1.refs_0_.g, f32[512,1024]{1,0:T(8,128)} %get-tuple-element.129.slope, bf16[4,1024,256]{2,1,0:T(8,128)(2,1)} %all-to-all-done.2.refs_0_, ...), custom_call_target="tpu_custom_call" | custom-call | flops 2147483648 | bytes 9445428 | tf_op jit(solution)/shard_map/upper_grad/pallas_call | solution.py:41
  210.6 7.3 %second_part.1 = (f32[64,2048]{1,0:T(8,128)}, f32[64,2048]{1,0:T(8,128)}, bf16[64,2048]{1,0:T(8,128)(2,1)}, bf16[64,2048]{1,0:T(8,128)(2,1)}, bf16[64,2048]{1,0:...) custom-call(s32[13]{0:T(128)} %pad_add_fusion.1.table, ...), custom_call_target="tpu_custom_call" | custom-call | flops 2147483648 | bytes 7864372 | tf_op jit(solution)/shard_map/second_part/pallas_call | solution.py:41
  222.0 5.3 %collective-permute-done.23.refs_0_ = bf16[64,2048]{1,0:T(8,128)(2,1)S(1)} collective-permute-done((bf16[64,2048]{1,0:T(8,128)(2,1)}, bf16[64,2048]{1,0:T(8,128)(2,1)S(1)}, u32[]{:S(2)}, u32[]{:S(2)}) %collective-permute-start.23) | collective-permute-done | bytes 262176 | tf_op jit(solution)/shard_map/ppermute | solution.py:94
  227.9 4.7 %collective-permute-done.24.refs_1_ = bf16[64,2048]{1,0:T(8,128)(2,1)S(1)} collective-permute-done((bf16[64,2048]{1,0:T(8,128)(2,1)}, bf16[64,2048]{1,0:T(8,128)(2,1)S(1)}, u32[]{:S(2)}, u32[]{:S(2)}) %collective-permute-start.24) | collective-permute-done | bytes 262176 | tf_op jit(solution)/shard_map/ppermute | solution.py:94
  238.6 5.2 %collective-permute-done.27.refs_1_ = bf16[64,2048]{1,0:T(8,128)(2,1)S(1)} collective-permute-done((bf16[64,2048]{1,0:T(8,128)(2,1)}, bf16[64,2048]{1,0:T(8,128)(2,1)S(1)}, u32[]{:S(2)}, u32[]{:S(2)}) %collective-permute-start.27) | collective-permute-done | bytes 262176 | tf_op jit(solution)/shard_map/ppermute | solution.py:94
  243.8 5.4 %grad_up_near.1 = bf16[4,256,1024]{2,1,0:T(8,128)(2,1)} custom-call(s32[13]{0:T(128)} %pad_add_fusion.1.table, bf16[512,2048]{1,0:T(8,128)(2,1)} %get-tuple-element.133.left, bf16[512,1024]{1,0:T(8,128)(2,1)} %get-tuple-element.144.refs_0_.left, bf16[4,256,1024]{2,1,0:T(8,128)(2,1)} %collective-permute-done.29.refs_1_), custom_call_target="tpu_custom_call" | custom-call | flops 1073741824 | bytes 7340084 | tf_op jit(solution)/shard_map/grad_up_near/pallas_call | solution.py:41
  257.3 7.2 %feed.1 = (f32[64,2048]{1,0:T(8,128)}, f32[64,2048]{1,0:T(8,128)}, bf16[64,2048]{1,0:T(8,128)(2,1)}, bf16[64,2048]{1,0:T(8,128)(2,1)}, bf16[64,2048]{1,0:T(8,128...) custom-call(s32[13]{0:T(128)} %pad_add_fusion.1.table, ...), custom_call_target="tpu_custom_call" | custom-call | flops 2147483648 | bytes 7864372 | tf_op jit(solution)/shard_map/feed/pallas_call | solution.py:41
  279.3 5.7 %collective-permute-done.35.refs_5_ = bf16[64,2048]{1,0:T(8,128)(2,1)S(1)} collective-permute-done((bf16[64,2048]{1,0:T(8,128)(2,1)S(1)}, bf16[64,2048]{1,0:T(8,128)(2,1)S(1)}, u32[]{:S(2)}, u32[]{:S(2)}) %collective-permute-start.35) | collective-permute-done | bytes 262176 | tf_op jit(solution)/shard_map/ppermute | solution.py:94
  289.5 11.8 %attend_back.1 = (bf16[512,2048]{1,0:T(8,128)(2,1)}, bf16[512,256]{1,0:T(8,128)(2,1)}, bf16[512,256]{1,0:T(8,128)(2,1)}, bf16[512,256]{1,0:T(8,128)(2,1)}, f32[1...) custom-call(s32[13]{0:T(128)} %pad_add_fusion.1.table, ...), custom_call_target="tpu_custom_call" | custom-call | flops 2147483648 | bytes 13635636 | tf_op jit(solution)/shard_map/attend_back/pallas_call | solution.py:41
  301.3 5.2 %grad_attention_far.1 = bf16[4,256,1024]{2,1,0:T(8,128)(2,1)} custom-call(s32[13]{0:T(128)} %pad_add_fusion.1.table, bf16[512,2048]{1,0:T(8,128)(2,1)} %first_norm.1.x.left, bf16[512,256]{1,0:T(8,128)(2,1)} %get-tuple-element.115.left.other, bf16[512,256]{1,0:T(8,128)(2,1)} %get-tuple-element.187.refs_0_, bf16[512,256]{1,0:T(8,128)(2,1)} %get-tuple-element.188.refs_1_, ...), custom_call_target="tpu_custom_call" | custom-call | flops 1073741824 | bytes 7340084 | tf_op jit(solution)/shard_map/grad_attention_far/pallas_call | solution.py:41
  317.4 4.9 %collective-permute-done.43.refs_1_ = bf16[64,2048]{1,0:T(8,128)(2,1)S(1)} collective-permute-done((bf16[64,2048]{1,0:T(8,128)(2,1)}, bf16[64,2048]{1,0:T(8,128)(2,1)S(1)}, u32[]{:S(2)}, u32[]{:S(2)}) %collective-permute-start.43) | collective-permute-done | bytes 262176 | tf_op jit(solution)/shard_map/ppermute | solution.py:94
  330.2 5.9 %grad_attention_near.1 = bf16[4,256,1024]{2,1,0:T(8,128)(2,1)} custom-call(s32[13]{0:T(128)} %pad_add_fusion.1.table, bf16[512,2048]{1,0:T(8,128)(2,1)} %first_norm.1.x.left, bf16[512,256]{1,0:T(8,128)(2,1)} %get-tuple-element.115.left.other, bf16[512,256]{1,0:T(8,128)(2,1)} %get-tuple-element.187.refs_0_, bf16[512,256]{1,0:T(8,128)(2,1)} %get-tuple-element.188.refs_1_, ...), custom_call_target="tpu_custom_call" | custom-call | flops 1073741824 | bytes 9437236 | tf_op jit(solution)/shard_map/grad_attention_near/pallas_call | solution.py:41
  347.0 5.8 %all-to-all-start.5 = ((bf16[4,256,1024]{2,1,0:T(8,128)(2,1)}), bf16[4,256,1024]{2,1,0:T(8,128)(2,1)}, u32[]{:S(2)}, u32[]{:S(2)}) async-start(bf16[4,256,1024]{2,1,0:T(8,128)(2,1)} %grad_attention_near.1), calls=%async_computation.5 | async-start | bytes 4194304 | tf_op jit(solution)/shard_map/all_to_all | solution.py:105
  372.3 6.9 %collective-permute-done.59 = f32[6,2048]{1,0:T(8,128)S(1)} collective-permute-done((f32[6,2048]{1,0:T(8,128)S(1)}, f32[6,2048]{1,0:T(8,128)S(1)}, u32[]{:S(2)}, u32[]{:S(2)}) %collective-permute-start.59) | collective-permute-done | bytes 49184 | tf_op jit(solution)/shard_map/ppermute | solution.py:94
  389.7 7.3 %collective-permute-done.62 = f32[8,2048]{1,0:T(8,128)S(1)} collective-permute-done((f32[8,2048]{1,0:T(8,128)S(1)}, f32[8,2048]{1,0:T(8,128)S(1)}, u32[]{:S(2)}, u32[]{:S(2)}) %collective-permute-start.62) | collective-permute-done | bytes 65568 | tf_op jit(solution)/shard_map/ppermute | solution.py:88
  (348 shorter events, 196.6 us)
Async XLA Ops:
  15.7 49.3 %all-to-all-start = ((bf16[4,4,256,256]{3,2,1,0:T(8,128)(2,1)}), bf16[4,4,256,256]{3,2,1,0:T(8,128)(2,1)S(1)}, u32[]{:S(2)}, u32[]{:S(2)}) async-start(bf16[4,4,256,256]{3,2,1,0:T(8,128)(2,1)} %pad_maximum_fusion.2), calls=%async_computation | async-start | bytes 4194304 | tf_op jit(solution)/shard_map/all_to_all | solution.py:105
  28.7 14.9 %collective-permute-start.1 = (bf16[128,2048]{1,0:T(8,128)(2,1)S(1)}, bf16[128,2048]{1,0:T(8,128)(2,1)S(1)}, u32[]{:S(2)}, u32[]{:S(2)}) collective-permute-start(bf16[128,2048]{1,0:T(8,128)(2,1)S(1)} %collective-permute-done.refs_0_), channel_id=1, source_target_pairs={{0,1},{1,0},{2,3},{3,2},{4,5},{5,4},{6,7},{7,6},{8,9},{9,8},{10,11... | collective-permute-start | bytes 1572872 | tf_op jit(solution)/shard_map/ppermute | solution.py:94
  30.3 23.2 %collective-permute-start.2 = (bf16[128,2048]{1,0:T(8,128)(2,1)S(1)}, bf16[128,2048]{1,0:T(8,128)(2,1)S(1)}, u32[]{:S(2)}, u32[]{:S(2)}) collective-permute-start(bf16[128,2048]{1,0:T(8,128)(2,1)S(1)} %collective-permute-done.refs_0_), channel_id=1, source_target_pairs={{0,2},{1,3},{2,0},{3,1},{4,6},{5,7},{6,4},{7,5},{8,10},{9,11},{10,... | collective-permute-start | bytes 1572872 | tf_op jit(solution)/shard_map/ppermute | solution.py:94
  31.8 22.4 %collective-permute-start.3 = (bf16[128,2048]{1,0:T(8,128)(2,1)S(1)}, bf16[128,2048]{1,0:T(8,128)(2,1)}, u32[]{:S(2)}, u32[]{:S(2)}) collective-permute-start(bf16[128,2048]{1,0:T(8,128)(2,1)S(1)} %collective-permute-done.refs_0_), channel_id=1, source_target_pairs={{0,3},{1,2},{2,1},{3,0},{4,7},{5,6},{6,5},{7,4},{8,11},{9,10},{10,... | collective-permute-start | bytes 1572872 | tf_op jit(solution)/shard_map/ppermute | solution.py:94
  65.1 73.7 %all-to-all-start.1 = ((bf16[4,256,1024]{2,1,0:T(8,128)(2,1)}), bf16[4,256,1024]{2,1,0:T(8,128)(2,1)}, u32[]{:S(2)}, u32[]{:S(2)}) async-start(bf16[4,256,1024]{2,1,0:T(8,128)(2,1)} %pad_maximum_fusion), calls=%async_computation.1 | async-start | bytes 4194304 | tf_op jit(solution)/shard_map/all_to_all | solution.py:105
  90.7 15.1 %collective-permute-start.10 = (bf16[64,2048]{1,0:T(8,128)(2,1)}, bf16[64,2048]{1,0:T(8,128)(2,1)S(1)}, u32[]{:S(2)}, u32[]{:S(2)}) collective-permute-start(bf16[64,2048]{1,0:T(8,128)(2,1)} %get-tuple-element.122), channel_id=1, source_target_pairs={{0,2},{1,3},{2,0},{3,1},{4,6},{5,7},{6,4},{7,5},{8,10},{9,11},{10,... | collective-permute-start | bytes 786440 | tf_op jit(solution)/shard_map/ppermute | solution.py:94
  92.3 15.9 %collective-permute-start.11 = (bf16[64,2048]{1,0:T(8,128)(2,1)}, bf16[64,2048]{1,0:T(8,128)(2,1)S(1)}, u32[]{:S(2)}, u32[]{:S(2)}) collective-permute-start(bf16[64,2048]{1,0:T(8,128)(2,1)} %get-tuple-element.123), channel_id=1, source_target_pairs={{0,3},{1,2},{2,1},{3,0},{4,7},{5,6},{6,5},{7,4},{8,11},{9,10},{10,... | collective-permute-start | bytes 786440 | tf_op jit(solution)/shard_map/ppermute | solution.py:94
  93.7 14.5 %collective-permute-start.9 = (bf16[64,2048]{1,0:T(8,128)(2,1)}, bf16[64,2048]{1,0:T(8,128)(2,1)S(1)}, u32[]{:S(2)}, u32[]{:S(2)}) collective-permute-start(bf16[64,2048]{1,0:T(8,128)(2,1)} %get-tuple-element.121), channel_id=1, source_target_pairs={{0,1},{1,0},{2,3},{3,2},{4,5},{5,4},{6,7},{7,6},{8,9},{9,8},{10,11... | collective-permute-start | bytes 786440 | tf_op jit(solution)/shard_map/ppermute | solution.py:94
  94.3 18.6 %collective-permute-start.6 = (bf16[64,2048]{1,0:T(8,128)(2,1)}, bf16[64,2048]{1,0:T(8,128)(2,1)S(1)}, u32[]{:S(2)}, u32[]{:S(2)}) collective-permute-start(bf16[64,2048]{1,0:T(8,128)(2,1)} %get-tuple-element.117), channel_id=1, source_target_pairs={{0,1},{1,0},{2,3},{3,2},{4,5},{5,4},{6,7},{7,6},{8,9},{9,8},{10,11... | collective-permute-start | bytes 786440 | tf_op jit(solution)/shard_map/ppermute | solution.py:94
  95.8 17.1 %collective-permute-start.7 = (bf16[64,2048]{1,0:T(8,128)(2,1)}, bf16[64,2048]{1,0:T(8,128)(2,1)S(1)}, u32[]{:S(2)}, u32[]{:S(2)}) collective-permute-start(bf16[64,2048]{1,0:T(8,128)(2,1)} %get-tuple-element.118), channel_id=1, source_target_pairs={{0,2},{1,3},{2,0},{3,1},{4,6},{5,7},{6,4},{7,5},{8,10},{9,11},{10,... | collective-permute-start | bytes 786440 | tf_op jit(solution)/shard_map/ppermute | solution.py:94
  138.8 27.5 %collective-permute-start.20 = (bf16[4,256,1024]{2,1,0:T(8,128)(2,1)}, bf16[4,256,1024]{2,1,0:T(8,128)(2,1)S(1)}, u32[]{:S(2)}, u32[]{:S(2)}) collective-permute-start(bf16[4,256,1024]{2,1,0:T(8,128)(2,1)} %all-to-all-done.1.refs_8_.refs_0_), channel_id=1, source_target_pairs={{0,4},{4,0},{8,12},{12,8},{16,20},{20,16},{24,28},{28,24},{1,5},{5... | collective-permute-start | bytes 6291464 | tf_op jit(solution)/shard_map/ppermute | solution.py:85
  138.8 52.9 %all-to-all-start.2 = ((bf16[4,1024,256]{2,1,0:T(8,128)(2,1)}), bf16[4,1024,256]{2,1,0:T(8,128)(2,1)}, u32[]{:S(2)}, u32[]{:S(2)}) async-start(bf16[4,1024,256]{2,1,0:T(8,128)(2,1)} %pad_maximum_fusion.1), calls=%async_computation.2 | async-start | bytes 4194304 | tf_op jit(solution)/shard_map/all_to_all | solution.py:105
  148.4 17.1 %collective-permute-start.19 = (bf16[64,2048]{1,0:T(8,128)(2,1)S(1)}, bf16[64,2048]{1,0:T(8,128)(2,1)S(1)}, u32[]{:S(2)}, u32[]{:S(2)}) collective-permute-start(bf16[64,2048]{1,0:T(8,128)(2,1)S(1)} %collective-permute-done.16.refs_4_), channel_id=1, source_target_pairs={{0,3},{1,2},{2,1},{3,0},{4,7},{5,6},{6,5},{7,4},{8,11},{9,10},{10,... | collective-permute-start | bytes 786440 | tf_op jit(solution)/shard_map/ppermute | solution.py:94
  191.8 57.4 %all-to-all-start.3 = ((bf16[4,1024,256]{2,1,0:T(8,128)(2,1)}), bf16[4,1024,256]{2,1,0:T(8,128)(2,1)S(1)}, u32[]{:S(2)}, u32[]{:S(2)}) async-start(bf16[4,1024,256]{2,1,0:T(8,128)(2,1)} %grad_down_near.1), calls=%async_computation.3 | async-start | bytes 4194304 | tf_op jit(solution)/shard_map/all_to_all | solution.py:105
  210.4 33.5 %collective-permute-start.29 = (bf16[4,256,1024]{2,1,0:T(8,128)(2,1)}, bf16[4,256,1024]{2,1,0:T(8,128)(2,1)}, u32[]{:S(2)}, u32[]{:S(2)}) collective-permute-start(bf16[4,256,1024]{2,1,0:T(8,128)(2,1)} %grad_up_far.1), channel_id=1, source_target_pairs={{0,4},{4,0},{8,12},{12,8},{16,20},{20,16},{24,28},{28,24},{1,5},{5... | collective-permute-start | bytes 6291464 | tf_op jit(solution)/shard_map/ppermute | solution.py:85
  219.0 15.1 %collective-permute-start.25 = (bf16[64,2048]{1,0:T(8,128)(2,1)}, bf16[64,2048]{1,0:T(8,128)(2,1)}, u32[]{:S(2)}, u32[]{:S(2)}) collective-permute-start(bf16[64,2048]{1,0:T(8,128)(2,1)} %get-tuple-element.140), channel_id=1, source_target_pairs={{0,3},{1,2},{2,1},{3,0},{4,7},{5,6},{6,5},{7,4},{8,11},{9,10},{10,... | collective-permute-start | bytes 786440 | tf_op jit(solution)/shard_map/ppermute | solution.py:94
  221.5 17.2 %collective-permute-start.26 = (bf16[64,2048]{1,0:T(8,128)(2,1)}, bf16[64,2048]{1,0:T(8,128)(2,1)S(1)}, u32[]{:S(2)}, u32[]{:S(2)}) collective-permute-start(bf16[64,2048]{1,0:T(8,128)(2,1)} %get-tuple-element.141), channel_id=1, source_target_pairs={{0,1},{1,0},{2,3},{3,2},{4,5},{5,4},{6,7},{7,6},{8,9},{9,8},{10,11... | collective-permute-start | bytes 786440 | tf_op jit(solution)/shard_map/ppermute | solution.py:94
  227.4 16.5 %collective-permute-start.27 = (bf16[64,2048]{1,0:T(8,128)(2,1)}, bf16[64,2048]{1,0:T(8,128)(2,1)S(1)}, u32[]{:S(2)}, u32[]{:S(2)}) collective-permute-start(bf16[64,2048]{1,0:T(8,128)(2,1)} %get-tuple-element.142), channel_id=1, source_target_pairs={{0,2},{1,3},{2,0},{3,1},{4,6},{5,7},{6,4},{7,5},{8,10},{9,11},{10,... | collective-permute-start | bytes 786440 | tf_op jit(solution)/shard_map/ppermute | solution.py:94
  265.3 80.3 %all-to-all-start.4 = ((bf16[4,256,1024]{2,1,0:T(8,128)(2,1)}), bf16[4,256,1024]{2,1,0:T(8,128)(2,1)S(1)}, u32[]{:S(2)}, u32[]{:S(2)}) async-start(bf16[4,256,1024]{2,1,0:T(8,128)(2,1)} %grad_up_near.1), calls=%async_computation.4 | async-start | bytes 4194304 | tf_op jit(solution)/shard_map/all_to_all | solution.py:105
  272.7 16.1 %collective-permute-start.37 = (bf16[64,2048]{1,0:T(8,128)(2,1)S(1)}, bf16[64,2048]{1,0:T(8,128)(2,1)S(1)}, u32[]{:S(2)}, u32[]{:S(2)}) collective-permute-start(bf16[64,2048]{1,0:T(8,128)(2,1)S(1)} %collective-permute-done.34.refs_4_), channel_id=1, source_target_pairs={{0,3},{1,2},{2,1},{3,0},{4,7},{5,6},{6,5},{7,4},{8,11},{9,10},{10,... | collective-permute-start | bytes 786440 | tf_op jit(solution)/shard_map/ppermute | solution.py:94
  306.5 22.6 %collective-permute-start.52 = (bf16[4,256,1024]{2,1,0:T(8,128)(2,1)}, bf16[4,256,1024]{2,1,0:T(8,128)(2,1)}, u32[]{:S(2)}, u32[]{:S(2)}) collective-permute-start(bf16[4,256,1024]{2,1,0:T(8,128)(2,1)} %grad_attention_far.1), channel_id=1, source_target_pairs={{0,4},{4,0},{8,12},{12,8},{16,20},{20,16},{24,28},{28,24},{1,5},{5... | collective-permute-start | bytes 6291464 | tf_op jit(solution)/shard_map/ppermute | solution.py:85
  309.5 14.5 %collective-permute-start.44 = (bf16[64,2048]{1,0:T(8,128)(2,1)}, bf16[64,2048]{1,0:T(8,128)(2,1)S(1)}, u32[]{:S(2)}, u32[]{:S(2)}) collective-permute-start(bf16[64,2048]{1,0:T(8,128)(2,1)} %get-tuple-element.172), channel_id=1, source_target_pairs={{0,3},{1,2},{2,1},{3,0},{4,7},{5,6},{6,5},{7,4},{8,11},{9,10},{10,... | collective-permute-start | bytes 786440 | tf_op jit(solution)/shard_map/ppermute | solution.py:94
  310.0 17.2 %collective-permute-start.38 = (bf16[64,2048]{1,0:T(8,128)(2,1)}, bf16[64,2048]{1,0:T(8,128)(2,1)S(1)}, u32[]{:S(2)}, u32[]{:S(2)}) collective-permute-start(bf16[64,2048]{1,0:T(8,128)(2,1)} %get-tuple-element.177), channel_id=1, source_target_pairs={{0,1},{1,0},{2,3},{3,2},{4,5},{5,4},{6,7},{7,6},{8,9},{9,8},{10,11... | collective-permute-start | bytes 786440 | tf_op jit(solution)/shard_map/ppermute | solution.py:94
  315.9 20.1 %collective-permute-start.53 = (bf16[64,2048]{1,0:T(8,128)(2,1)S(1)}, bf16[64,2048]{1,0:T(8,128)(2,1)}, u32[]{:S(2)}, u32[]{:S(2)}) collective-permute-start(bf16[64,2048]{1,0:T(8,128)(2,1)S(1)} %copy-done.66), channel_id=1, source_target_pairs={{0,2},{1,3},{2,0},{3,1},{4,6},{5,7},{6,4},{7,5},{8,10},{9,11},{10,... | collective-permute-start | bytes 786440 | tf_op jit(solution)/shard_map/ppermute | solution.py:94
  329.1 15.6 %collective-permute-start.40 = (bf16[64,2048]{1,0:T(8,128)(2,1)}, bf16[64,2048]{1,0:T(8,128)(2,1)S(1)}, u32[]{:S(2)}, u32[]{:S(2)}) collective-permute-start(bf16[64,2048]{1,0:T(8,128)(2,1)} %get-tuple-element.179), channel_id=1, source_target_pairs={{0,2},{1,3},{2,0},{3,1},{4,6},{5,7},{6,4},{7,5},{8,10},{9,11},{10,... | collective-permute-start | bytes 786440 | tf_op jit(solution)/shard_map/ppermute | solution.py:94
  347.0 60.4 %all-to-all-start.5 = ((bf16[4,256,1024]{2,1,0:T(8,128)(2,1)}), bf16[4,256,1024]{2,1,0:T(8,128)(2,1)}, u32[]{:S(2)}, u32[]{:S(2)}) async-start(bf16[4,256,1024]{2,1,0:T(8,128)(2,1)} %grad_attention_near.1), calls=%async_computation.5 | async-start | bytes 4194304 | tf_op jit(solution)/shard_map/all_to_all | solution.py:105
  363.3 18.2 %collective-permute-start.49 = (bf16[64,2048]{1,0:T(8,128)(2,1)S(1)}, bf16[64,2048]{1,0:T(8,128)(2,1)S(1)}, u32[]{:S(2)}, u32[]{:S(2)}) collective-permute-start(bf16[64,2048]{1,0:T(8,128)(2,1)S(1)} %copy-done.65), channel_id=1, source_target_pairs={{0,1},{1,0},{2,3},{3,2},{4,5},{5,4},{6,7},{7,6},{8,9},{9,8},{10,11... | collective-permute-start | bytes 786440 | tf_op jit(solution)/shard_map/ppermute | solution.py:94
  365.2 16.3 %collective-permute-start.50 = (bf16[64,2048]{1,0:T(8,128)(2,1)S(1)}, bf16[64,2048]{1,0:T(8,128)(2,1)S(1)}, u32[]{:S(2)}, u32[]{:S(2)}) collective-permute-start(bf16[64,2048]{1,0:T(8,128)(2,1)S(1)} %copy-done.64), channel_id=1, source_target_pairs={{0,2},{1,3},{2,0},{3,1},{4,6},{5,7},{6,4},{7,5},{8,10},{9,11},{10,... | collective-permute-start | bytes 786440 | tf_op jit(solution)/shard_map/ppermute | solution.py:94
  365.3 16.2 %collective-permute-start.51 = (bf16[64,2048]{1,0:T(8,128)(2,1)S(1)}, bf16[64,2048]{1,0:T(8,128)(2,1)S(1)}, u32[]{:S(2)}, u32[]{:S(2)}) collective-permute-start(bf16[64,2048]{1,0:T(8,128)(2,1)S(1)} %copy-done.63), channel_id=1, source_target_pairs={{0,3},{1,2},{2,1},{3,0},{4,7},{5,6},{6,5},{7,4},{8,11},{9,10},{10,... | collective-permute-start | bytes 786440 | tf_op jit(solution)/shard_map/ppermute | solution.py:94
  384.8 17.0 %collective-permute-start.56 = (bf16[64,2048]{1,0:T(8,128)(2,1)}, bf16[64,2048]{1,0:T(8,128)(2,1)S(1)}, u32[]{:S(2)}, u32[]{:S(2)}) collective-permute-start(bf16[64,2048]{1,0:T(8,128)(2,1)} %outputs_own.1.refs_0_), channel_id=1, source_target_pairs={{0,1},{1,0},{2,3},{3,2},{4,5},{5,4},{6,7},{7,6},{8,9},{9,8},{10,11... | collective-permute-start | bytes 786440 | tf_op jit(solution)/shard_map/ppermute | solution.py:94
  385.2 16.6 %collective-permute-start.57 = (bf16[64,2048]{1,0:T(8,128)(2,1)}, bf16[64,2048]{1,0:T(8,128)(2,1)S(1)}, u32[]{:S(2)}, u32[]{:S(2)}) collective-permute-start(bf16[64,2048]{1,0:T(8,128)(2,1)} %outputs_own.1.refs_0_), channel_id=1, source_target_pairs={{0,2},{1,3},{2,0},{3,1},{4,6},{5,7},{6,4},{7,5},{8,10},{9,11},{10,... | collective-permute-start | bytes 786440 | tf_op jit(solution)/shard_map/ppermute | solution.py:94
  386.4 15.4 %collective-permute-start.58 = (bf16[64,2048]{1,0:T(8,128)(2,1)}, bf16[64,2048]{1,0:T(8,128)(2,1)S(1)}, u32[]{:S(2)}, u32[]{:S(2)}) collective-permute-start(bf16[64,2048]{1,0:T(8,128)(2,1)} %outputs_own.1.refs_0_), channel_id=1, source_target_pairs={{0,3},{1,2},{2,1},{3,0},{4,7},{5,6},{6,5},{7,4},{8,11},{9,10},{10,... | collective-permute-start | bytes 786440 | tf_op jit(solution)/shard_map/ppermute | solution.py:94
  (115 other events, 1002.6 us)

commit v7 on v6

--- a/solution.py
+++ b/solution.py
@@ -820,7 +820,7 @@
     narrow = jnp.concatenate([heads_grad[0], up_bias_grad[0]])
     rows = -(-narrow.shape[0] // features)
     narrow = jnp.pad(narrow, (0, rows * features - narrow.shape[0])).reshape(rows, features)
-    sums = at.sum_small(after(jnp.concatenate([sums_one[:2], sums_two[:4]]), input_others, grad_down, grad_up), narrow)
+    sums = at.sum_small(after(jnp.concatenate([sums_one[:2], sums_two[:4]]), outputs_own, grad_down, grad_up), narrow)
     narrow = sums[6:].reshape(-1)
     heads, hidden_units = 2 * heads, 2 * hidden_units
     return (

time: 413 us -> 418 us (1.012)
  waiting for transfers between devices: 146 us -> 153 us
    ppermute x47, waiting for transfers between devices: 108 us -> 119 us  [to_peer(): lax.ppermute(values, 'tensor', [(i, i ^ k) for i in range(self.tensor)])]
    unnamed x156 -> x158, local copies, waits for them, and re-layouts: 12.4 us -> 12.2 us
  transfers between devices with their start and end apart: 70 -> 70, of which waited for: 34 -> 39; matrix products, arithmetic and copies ran while one was open for 4% -> 4% of each run, Pallas kernels for 30% -> 30%
where the time goes in v7:
time: 418 us; the launch traced here: 415 us
  waiting for transfers between devices  153 us (37%)
  Pallas kernels  129 us (31%)
  starting transfers between devices  103 us (25%)
  local copies, waits for them, and re-layouts  21 us (5%)
  other arithmetic  7.54 us (2%)
    pallas_call x28, Pallas kernels, call(): pl.pallas_call(body, name=name, out_shape=outs, in_specs=in_specs, out_sp...  129 us
    ppermute x47, waiting for transfers between devices, to_peer(): lax.ppermute(values, 'tensor', [(i, i ^ k) for i in range(self.tensor)])  119 us
    ppermute x47, starting transfers between devices, to_peer(): lax.ppermute(values, 'tensor', [(i, i ^ k) for i in range(self.tensor)])  56.2 us
    all_to_all x6, starting transfers between devices, exchange(): lax.all_to_all(blocks, 'dp', 0, 0, axis_index_groups=groups, tiled=True)  34.8 us
    ppermute x10, waiting for transfers between devices, to_chip(): return lax.ppermute(values, 'dp', [(i, i ^ 2 * k) for i in range(self.dp)])  21.5 us
    unnamed x158, local copies, waits for them, and re-layouts  12.2 us
    ppermute x10, starting transfers between devices, to_chip(): return lax.ppermute(values, 'dp', [(i, i ^ 2 * k) for i in range(self.dp)])  11.6 us
    ppermute x7, waiting for transfers between devices, to_core(): return lax.ppermute(values, 'dp', self.swap)  9.91 us
  transfers between devices with their start and end apart: 70, of which 39 were waited for; matrix products, arithmetic and copies ran while one was open for 4% of the time, Pallas kernels for 30%

profile of v7, /device:TPU:8, one launch (start us, length us, event | category | flops | bytes accessed | tf_op | source)
XLA Modules:
  0.0 415.3 jit_solution(8364700555977629260)
XLA Ops:
  7.3 8.4 %collective-permute-done.4 = s32[256]{0:T(256)S(1)} collective-permute-done((s32[256]{0:T(256)S(1)}, s32[256]{0:T(256)S(1)}, u32[]{:S(2)}, u32[]{:S(2)}) %collective-permute-start.4) | collective-permute-done | bytes 1056 | tf_op jit(solution)/shard_map/ppermute | solution.py:88
  15.7 5.3 %all-to-all-start = ((bf16[4,4,256,256]{3,2,1,0:T(8,128)(2,1)}), bf16[4,4,256,256]{3,2,1,0:T(8,128)(2,1)S(1)}, u32[]{:S(2)}, u32[]{:S(2)}) async-start(bf16[4,4,256,256]{3,2,1,0:T(8,128)(2,1)} %pad_maximum_fusion.2), calls=%async_computation | async-start | bytes 4194304 | tf_op jit(solution)/shard_map/all_to_all | solution.py:105
  33.9 9.7 %collective-permute-done.1.refs_1_ = bf16[128,2048]{1,0:T(8,128)(2,1)S(1)} collective-permute-done((bf16[128,2048]{1,0:T(8,128)(2,1)S(1)}, bf16[128,2048]{1,0:T(8,128)(2,1)S(1)}, u32[]{:S(2)}, u32[]{:S(2)}) %collective-permute-start.1) | collective-permute-done | bytes 524320 | tf_op jit(solution)/shard_map/ppermute | solution.py:94
  43.6 9.9 %collective-permute-done.2.refs_2_ = bf16[128,2048]{1,0:T(8,128)(2,1)S(1)} collective-permute-done((bf16[128,2048]{1,0:T(8,128)(2,1)S(1)}, bf16[128,2048]{1,0:T(8,128)(2,1)S(1)}, u32[]{:S(2)}, u32[]{:S(2)}) %collective-permute-start.2) | collective-permute-done | bytes 524320 | tf_op jit(solution)/shard_map/ppermute | solution.py:94
  57.7 4.8 %first_norm.1.x.left = bf16[512,2048]{1,0:T(8,128)(2,1)} custom-call(s32[13]{0:T(128)} %pad_add_fusion.1.table, bf16[256,2048]{1,0:T(8,128)(2,1)} %own.2, f32[8,2048]{1,0:T(8,128)} %convert_element_type.8.vec, bf16[128,2048]{1,0:T(8,128)(2,1)} %copy-done.6, bf16[128,2048]{1,0:T(8,128)(2,1)} %copy-done.7, bf16[128,2048]{1,0:T(8,128)(2,1)} %copy-done.8, ...), custom_call_target="tpu_custom_call" | custom-call | flops 10485760 | bytes 5308468 | tf_op jit(solution)/shard_map/first_norm/pallas_call | solution.py:41
  65.1 7.7 %all-to-all-start.1 = ((bf16[4,256,1024]{2,1,0:T(8,128)(2,1)}), bf16[4,256,1024]{2,1,0:T(8,128)(2,1)}, u32[]{:S(2)}, u32[]{:S(2)}) async-start(bf16[4,256,1024]{2,1,0:T(8,128)(2,1)} %pad_maximum_fusion), calls=%async_computation.1 | async-start | bytes 4194304 | tf_op jit(solution)/shard_map/all_to_all | solution.py:105
  77.0 8.9 %attend.1 = (bf16[512,256]{1,0:T(8,128)(2,1)}, bf16[512,256]{1,0:T(8,128)(2,1)}, bf16[512,256]{1,0:T(8,128)(2,1)}, f32[4,256,256]{2,1,0:T(8,128)}, bf16[512,256]{1,0:T(8,128)(2,1)}) custom-call(s32[13]{0:T(128)} %pad_add_fusion.1.table, bf16[512,2048]{1,0:T(8,128)(2,1)} %first_norm.1.x.left, bf16[1,256]{1,0:T(2,128)(2,1)} %broadcast_in_dim.29.q_bias, ...), custom_call_target="tpu_custom_call" | custom-call | flops 1610612736 | bytes 8913972 | tf_op jit(solution)/shard_map/attend/pallas_call | solution.py:41
  86.0 4.8 %project_out.1 = (f32[64,2048]{1,0:T(8,128)}, f32[64,2048]{1,0:T(8,128)}, bf16[64,2048]{1,0:T(8,128)(2,1)}, bf16[64,2048]{1,0:T(8,128)(2,1)}, bf16[64,2048]{1,0:...) custom-call(s32[13]{0:T(128)} %pad_add_fusion.1.table, ...), custom_call_target="tpu_custom_call" | custom-call | flops 536870912 | bytes 7077940 | tf_op jit(solution)/shard_map/project_out/pallas_call | solution.py:41
  97.3 8.5 %collective-permute-done.10.refs_1_ = bf16[64,2048]{1,0:T(8,128)(2,1)S(1)} collective-permute-done((bf16[64,2048]{1,0:T(8,128)(2,1)}, bf16[64,2048]{1,0:T(8,128)(2,1)S(1)}, u32[]{:S(2)}, u32[]{:S(2)}) %collective-permute-start.10) | collective-permute-done | bytes 262176 | tf_op jit(solution)/shard_map/ppermute | solution.py:94
  112.9 5.5 %collective-permute-done.8.refs_2_ = bf16[64,2048]{1,0:T(8,128)(2,1)S(1)} collective-permute-done((bf16[64,2048]{1,0:T(8,128)(2,1)}, bf16[64,2048]{1,0:T(8,128)(2,1)S(1)}, u32[]{:S(2)}, u32[]{:S(2)}) %collective-permute-start.8) | collective-permute-done | bytes 262176 | tf_op jit(solution)/shard_map/ppermute | solution.py:94
  118.4 5.4 %collective-permute-done.12.refs_3_ = bf16[64,2048]{1,0:T(8,128)(2,1)S(1)} collective-permute-done((bf16[64,2048]{1,0:T(8,128)(2,1)}, bf16[64,2048]{1,0:T(8,128)(2,1)S(1)}, u32[]{:S(2)}, u32[]{:S(2)}) %collective-permute-start.12) | collective-permute-done | bytes 262176 | tf_op jit(solution)/shard_map/ppermute | solution.py:88
  138.8 6.2 %all-to-all-start.2 = ((bf16[4,1024,256]{2,1,0:T(8,128)(2,1)}), bf16[4,1024,256]{2,1,0:T(8,128)(2,1)}, u32[]{:S(2)}, u32[]{:S(2)}) async-start(bf16[4,1024,256]{2,1,0:T(8,128)(2,1)} %pad_maximum_fusion.1), calls=%async_computation.2 | async-start | bytes 4194304 | tf_op jit(solution)/shard_map/all_to_all | solution.py:105
  149.0 6.2 %collective-permute-done.15.refs_3_ = bf16[64,2048]{1,0:T(8,128)(2,1)S(1)} collective-permute-done((bf16[64,2048]{1,0:T(8,128)(2,1)S(1)}, bf16[64,2048]{1,0:T(8,128)(2,1)S(1)}, u32[]{:S(2)}, u32[]{:S(2)}) %collective-permute-start.15) | collective-permute-done | bytes 262176 | tf_op jit(solution)/shard_map/ppermute | solution.py:94
  155.1 4.7 %collective-permute-done.17.refs_5_ = bf16[64,2048]{1,0:T(8,128)(2,1)S(1)} collective-permute-done((bf16[64,2048]{1,0:T(8,128)(2,1)S(1)}, bf16[64,2048]{1,0:T(8,128)(2,1)S(1)}, u32[]{:S(2)}, u32[]{:S(2)}) %collective-permute-start.17) | collective-permute-done | bytes 262176 | tf_op jit(solution)/shard_map/ppermute | solution.py:94
  160.6 5.0 %collective-permute-done.19.refs_7_ = bf16[64,2048]{1,0:T(8,128)(2,1)S(1)} collective-permute-done((bf16[64,2048]{1,0:T(8,128)(2,1)S(1)}, bf16[64,2048]{1,0:T(8,128)(2,1)S(1)}, u32[]{:S(2)}, u32[]{:S(2)}) %collective-permute-start.19) | collective-permute-done | bytes 262176 | tf_op jit(solution)/shard_map/ppermute | solution.py:94
  167.7 8.6 %upper.1 = (bf16[512,2048]{1,0:T(8,128)(2,1)}, bf16[512,1024]{1,0:T(8,128)(2,1)}, f32[512,1024]{1,0:T(8,128)}) custom-call(s32[13]{0:T(128)} %pad_add_fusion.1.table, bf16[1,1024]{1,0:T(2,128)(2,1)} %broadcast_in_dim.28.bias, bf16[64,2048]{1,0:T(8,128)(2,1)} %get-tuple-element.124.refs_0_, bf16[64,2048]{1,0:T(8,128)(2,1)} %copy-done.69, ...), custom_call_target="tpu_custom_call" | custom-call | flops 2147483648 | bytes 11536436 | tf_op jit(solution)/shard_map/upper/pallas_call | solution.py:41
  186.5 5.2 %grad_down_near.1 = bf16[4,1024,256]{2,1,0:T(8,128)(2,1)} custom-call(s32[13]{0:T(128)} %pad_add_fusion.1.table, bf16[512,1024]{1,0:T(8,128)(2,1)} %get-tuple-element.149.left, bf16[512,2048]{1,0:T(8,128)(2,1)} %upstream.1.refs_0_.g, bf16[4,1024,256]{2,1,0:T(8,128)(2,1)} %copy-done.5), custom_call_target="tpu_custom_call" | custom-call | flops 1073741824 | bytes 7340084 | tf_op jit(solution)/shard_map/grad_down_near/pallas_call | solution.py:41
  191.9 6.0 %all-to-all-start.3 = ((bf16[4,1024,256]{2,1,0:T(8,128)(2,1)}), bf16[4,1024,256]{2,1,0:T(8,128)(2,1)S(1)}, u32[]{:S(2)}, u32[]{:S(2)}) async-start(bf16[4,1024,256]{2,1,0:T(8,128)(2,1)} %grad_down_near.1), calls=%async_computation.3 | async-start | bytes 4194304 | tf_op jit(solution)/shard_map/all_to_all | solution.py:105
  197.8 8.0 %upper_grad.1 = (bf16[512,1024]{1,0:T(8,128)(2,1)}, f32[1,2048]{1,0:T(1,128)}) custom-call(s32[13]{0:T(128)} %pad_add_fusion.1.table, bf16[512,2048]{1,0:T(8,128)(2,1)} %upstream.1.refs_0_.g, f32[512,1024]{1,0:T(8,128)} %get-tuple-element.129.slope, bf16[4,1024,256]{2,1,0:T(8,128)(2,1)} %all-to-all-done.2.refs_0_, ...), custom_call_target="tpu_custom_call" | custom-call | flops 2147483648 | bytes 9445428 | tf_op jit(solution)/shard_map/upper_grad/pallas_call | solution.py:41
  205.8 4.6 %grad_up_far.1 = bf16[4,256,1024]{2,1,0:T(8,128)(2,1)} custom-call(s32[13]{0:T(128)} %pad_add_fusion.1.table, bf16[512,2048]{1,0:T(8,128)(2,1)} %get-tuple-element.133.left, bf16[512,1024]{1,0:T(8,128)(2,1)} %get-tuple-element.144.refs_0_.left), custom_call_target="tpu_custom_call" | custom-call | flops 1073741824 | bytes 5242932 | tf_op jit(solution)/shard_map/grad_up_far/pallas_call | solution.py:41
  210.6 7.3 %second_part.1 = (f32[64,2048]{1,0:T(8,128)}, f32[64,2048]{1,0:T(8,128)}, bf16[64,2048]{1,0:T(8,128)(2,1)}, bf16[64,2048]{1,0:T(8,128)(2,1)}, bf16[64,2048]{1,0:...) custom-call(s32[13]{0:T(128)} %pad_add_fusion.1.table, ...), custom_call_target="tpu_custom_call" | custom-call | flops 2147483648 | bytes 7864372 | tf_op jit(solution)/shard_map/second_part/pallas_call | solution.py:41
  222.0 5.4 %collective-permute-done.23.refs_0_ = bf16[64,2048]{1,0:T(8,128)(2,1)S(1)} collective-permute-done((bf16[64,2048]{1,0:T(8,128)(2,1)}, bf16[64,2048]{1,0:T(8,128)(2,1)S(1)}, u32[]{:S(2)}, u32[]{:S(2)}) %collective-permute-start.23) | collective-permute-done | bytes 262176 | tf_op jit(solution)/shard_map/ppermute | solution.py:94
  227.9 4.8 %collective-permute-done.24.refs_1_ = bf16[64,2048]{1,0:T(8,128)(2,1)S(1)} collective-permute-done((bf16[64,2048]{1,0:T(8,128)(2,1)}, bf16[64,2048]{1,0:T(8,128)(2,1)S(1)}, u32[]{:S(2)}, u32[]{:S(2)}) %collective-permute-start.24) | collective-permute-done | bytes 262176 | tf_op jit(solution)/shard_map/ppermute | solution.py:94
  238.7 5.2 %collective-permute-done.27.refs_1_ = bf16[64,2048]{1,0:T(8,128)(2,1)S(1)} collective-permute-done((bf16[64,2048]{1,0:T(8,128)(2,1)}, bf16[64,2048]{1,0:T(8,128)(2,1)S(1)}, u32[]{:S(2)}, u32[]{:S(2)}) %collective-permute-start.27) | collective-permute-done | bytes 262176 | tf_op jit(solution)/shard_map/ppermute | solution.py:94
  243.9 5.4 %grad_up_near.1 = bf16[4,256,1024]{2,1,0:T(8,128)(2,1)} custom-call(s32[13]{0:T(128)} %pad_add_fusion.1.table, bf16[512,2048]{1,0:T(8,128)(2,1)} %get-tuple-element.133.left, bf16[512,1024]{1,0:T(8,128)(2,1)} %get-tuple-element.144.refs_0_.left, bf16[4,256,1024]{2,1,0:T(8,128)(2,1)} %collective-permute-done.29.refs_1_), custom_call_target="tpu_custom_call" | custom-call | flops 1073741824 | bytes 7340084 | tf_op jit(solution)/shard_map/grad_up_near/pallas_call | solution.py:41
  257.3 7.2 %feed.1 = (f32[64,2048]{1,0:T(8,128)}, f32[64,2048]{1,0:T(8,128)}, bf16[64,2048]{1,0:T(8,128)(2,1)}, bf16[64,2048]{1,0:T(8,128)(2,1)}, bf16[64,2048]{1,0:T(8,128...) custom-call(s32[13]{0:T(128)} %pad_add_fusion.1.table, ...), custom_call_target="tpu_custom_call" | custom-call | flops 2147483648 | bytes 7864372 | tf_op jit(solution)/shard_map/feed/pallas_call | solution.py:41
  279.4 5.7 %collective-permute-done.35.refs_5_ = bf16[64,2048]{1,0:T(8,128)(2,1)S(1)} collective-permute-done((bf16[64,2048]{1,0:T(8,128)(2,1)S(1)}, bf16[64,2048]{1,0:T(8,128)(2,1)S(1)}, u32[]{:S(2)}, u32[]{:S(2)}) %collective-permute-start.35) | collective-permute-done | bytes 262176 | tf_op jit(solution)/shard_map/ppermute | solution.py:94
  289.5 11.8 %attend_back.1 = (bf16[512,2048]{1,0:T(8,128)(2,1)}, bf16[512,256]{1,0:T(8,128)(2,1)}, bf16[512,256]{1,0:T(8,128)(2,1)}, bf16[512,256]{1,0:T(8,128)(2,1)}, f32[1...) custom-call(s32[13]{0:T(128)} %pad_add_fusion.1.table, ...), custom_call_target="tpu_custom_call" | custom-call | flops 2147483648 | bytes 13635636 | tf_op jit(solution)/shard_map/attend_back/pallas_call | solution.py:41
  301.3 5.2 %grad_attention_far.1 = bf16[4,256,1024]{2,1,0:T(8,128)(2,1)} custom-call(s32[13]{0:T(128)} %pad_add_fusion.1.table, bf16[512,2048]{1,0:T(8,128)(2,1)} %first_norm.1.x.left, bf16[512,256]{1,0:T(8,128)(2,1)} %get-tuple-element.115.left.other, bf16[512,256]{1,0:T(8,128)(2,1)} %get-tuple-element.187.refs_0_, bf16[512,256]{1,0:T(8,128)(2,1)} %get-tuple-element.188.refs_1_, ...), custom_call_target="tpu_custom_call" | custom-call | flops 1073741824 | bytes 7340084 | tf_op jit(solution)/shard_map/grad_attention_far/pallas_call | solution.py:41
  317.5 4.9 %collective-permute-done.43.refs_1_ = bf16[64,2048]{1,0:T(8,128)(2,1)S(1)} collective-permute-done((bf16[64,2048]{1,0:T(8,128)(2,1)}, bf16[64,2048]{1,0:T(8,128)(2,1)S(1)}, u32[]{:S(2)}, u32[]{:S(2)}) %collective-permute-start.43) | collective-permute-done | bytes 262176 | tf_op jit(solution)/shard_map/ppermute | solution.py:94
  330.2 5.8 %grad_attention_near.1 = bf16[4,256,1024]{2,1,0:T(8,128)(2,1)} custom-call(s32[13]{0:T(128)} %pad_add_fusion.1.table, bf16[512,2048]{1,0:T(8,128)(2,1)} %first_norm.1.x.left, bf16[512,256]{1,0:T(8,128)(2,1)} %get-tuple-element.115.left.other, bf16[512,256]{1,0:T(8,128)(2,1)} %get-tuple-element.187.refs_0_, bf16[512,256]{1,0:T(8,128)(2,1)} %get-tuple-element.188.refs_1_, ...), custom_call_target="tpu_custom_call" | custom-call | flops 1073741824 | bytes 9437236 | tf_op jit(solution)/shard_map/grad_attention_near/pallas_call | solution.py:41
  347.0 5.8 %all-to-all-start.5 = ((bf16[4,256,1024]{2,1,0:T(8,128)(2,1)}), bf16[4,256,1024]{2,1,0:T(8,128)(2,1)}, u32[]{:S(2)}, u32[]{:S(2)}) async-start(bf16[4,256,1024]{2,1,0:T(8,128)(2,1)} %grad_attention_near.1), calls=%async_computation.5 | async-start | bytes 4194304 | tf_op jit(solution)/shard_map/all_to_all | solution.py:105
  (350 shorter events, 206.4 us)
Async XLA Ops:
  15.7 49.3 %all-to-all-start = ((bf16[4,4,256,256]{3,2,1,0:T(8,128)(2,1)}), bf16[4,4,256,256]{3,2,1,0:T(8,128)(2,1)S(1)}, u32[]{:S(2)}, u32[]{:S(2)}) async-start(bf16[4,4,256,256]{3,2,1,0:T(8,128)(2,1)} %pad_maximum_fusion.2), calls=%async_computation | async-start | bytes 4194304 | tf_op jit(solution)/shard_map/all_to_all | solution.py:105
  28.7 14.9 %collective-permute-start.1 = (bf16[128,2048]{1,0:T(8,128)(2,1)S(1)}, bf16[128,2048]{1,0:T(8,128)(2,1)S(1)}, u32[]{:S(2)}, u32[]{:S(2)}) collective-permute-start(bf16[128,2048]{1,0:T(8,128)(2,1)S(1)} %collective-permute-done.refs_0_), channel_id=1, source_target_pairs={{0,1},{1,0},{2,3},{3,2},{4,5},{5,4},{6,7},{7,6},{8,9},{9,8},{10,11... | collective-permute-start | bytes 1572872 | tf_op jit(solution)/shard_map/ppermute | solution.py:94
  30.3 23.2 %collective-permute-start.2 = (bf16[128,2048]{1,0:T(8,128)(2,1)S(1)}, bf16[128,2048]{1,0:T(8,128)(2,1)S(1)}, u32[]{:S(2)}, u32[]{:S(2)}) collective-permute-start(bf16[128,2048]{1,0:T(8,128)(2,1)S(1)} %collective-permute-done.refs_0_), channel_id=1, source_target_pairs={{0,2},{1,3},{2,0},{3,1},{4,6},{5,7},{6,4},{7,5},{8,10},{9,11},{10,... | collective-permute-start | bytes 1572872 | tf_op jit(solution)/shard_map/ppermute | solution.py:94
  31.8 22.4 %collective-permute-start.3 = (bf16[128,2048]{1,0:T(8,128)(2,1)S(1)}, bf16[128,2048]{1,0:T(8,128)(2,1)}, u32[]{:S(2)}, u32[]{:S(2)}) collective-permute-start(bf16[128,2048]{1,0:T(8,128)(2,1)S(1)} %collective-permute-done.refs_0_), channel_id=1, source_target_pairs={{0,3},{1,2},{2,1},{3,0},{4,7},{5,6},{6,5},{7,4},{8,11},{9,10},{10,... | collective-permute-start | bytes 1572872 | tf_op jit(solution)/shard_map/ppermute | solution.py:94
  65.1 73.8 %all-to-all-start.1 = ((bf16[4,256,1024]{2,1,0:T(8,128)(2,1)}), bf16[4,256,1024]{2,1,0:T(8,128)(2,1)}, u32[]{:S(2)}, u32[]{:S(2)}) async-start(bf16[4,256,1024]{2,1,0:T(8,128)(2,1)} %pad_maximum_fusion), calls=%async_computation.1 | async-start | bytes 4194304 | tf_op jit(solution)/shard_map/all_to_all | solution.py:105
  90.7 15.1 %collective-permute-start.10 = (bf16[64,2048]{1,0:T(8,128)(2,1)}, bf16[64,2048]{1,0:T(8,128)(2,1)S(1)}, u32[]{:S(2)}, u32[]{:S(2)}) collective-permute-start(bf16[64,2048]{1,0:T(8,128)(2,1)} %get-tuple-element.122), channel_id=1, source_target_pairs={{0,2},{1,3},{2,0},{3,1},{4,6},{5,7},{6,4},{7,5},{8,10},{9,11},{10,... | collective-permute-start | bytes 786440 | tf_op jit(solution)/shard_map/ppermute | solution.py:94
  92.3 16.0 %collective-permute-start.11 = (bf16[64,2048]{1,0:T(8,128)(2,1)}, bf16[64,2048]{1,0:T(8,128)(2,1)S(1)}, u32[]{:S(2)}, u32[]{:S(2)}) collective-permute-start(bf16[64,2048]{1,0:T(8,128)(2,1)} %get-tuple-element.123), channel_id=1, source_target_pairs={{0,3},{1,2},{2,1},{3,0},{4,7},{5,6},{6,5},{7,4},{8,11},{9,10},{10,... | collective-permute-start | bytes 786440 | tf_op jit(solution)/shard_map/ppermute | solution.py:94
  93.7 14.5 %collective-permute-start.9 = (bf16[64,2048]{1,0:T(8,128)(2,1)}, bf16[64,2048]{1,0:T(8,128)(2,1)S(1)}, u32[]{:S(2)}, u32[]{:S(2)}) collective-permute-start(bf16[64,2048]{1,0:T(8,128)(2,1)} %get-tuple-element.121), channel_id=1, source_target_pairs={{0,1},{1,0},{2,3},{3,2},{4,5},{5,4},{6,7},{7,6},{8,9},{9,8},{10,11... | collective-permute-start | bytes 786440 | tf_op jit(solution)/shard_map/ppermute | solution.py:94
  94.3 18.6 %collective-permute-start.6 = (bf16[64,2048]{1,0:T(8,128)(2,1)}, bf16[64,2048]{1,0:T(8,128)(2,1)S(1)}, u32[]{:S(2)}, u32[]{:S(2)}) collective-permute-start(bf16[64,2048]{1,0:T(8,128)(2,1)} %get-tuple-element.117), channel_id=1, source_target_pairs={{0,1},{1,0},{2,3},{3,2},{4,5},{5,4},{6,7},{7,6},{8,9},{9,8},{10,11... | collective-permute-start | bytes 786440 | tf_op jit(solution)/shard_map/ppermute | solution.py:94
  95.8 17.1 %collective-permute-start.7 = (bf16[64,2048]{1,0:T(8,128)(2,1)}, bf16[64,2048]{1,0:T(8,128)(2,1)S(1)}, u32[]{:S(2)}, u32[]{:S(2)}) collective-permute-start(bf16[64,2048]{1,0:T(8,128)(2,1)} %get-tuple-element.118), channel_id=1, source_target_pairs={{0,2},{1,3},{2,0},{3,1},{4,6},{5,7},{6,4},{7,5},{8,10},{9,11},{10,... | collective-permute-start | bytes 786440 | tf_op jit(solution)/shard_map/ppermute | solution.py:94
  138.8 27.5 %collective-permute-start.20 = (bf16[4,256,1024]{2,1,0:T(8,128)(2,1)}, bf16[4,256,1024]{2,1,0:T(8,128)(2,1)S(1)}, u32[]{:S(2)}, u32[]{:S(2)}) collective-permute-start(bf16[4,256,1024]{2,1,0:T(8,128)(2,1)} %all-to-all-done.1.refs_8_.refs_0_), channel_id=1, source_target_pairs={{0,4},{4,0},{8,12},{12,8},{16,20},{20,16},{24,28},{28,24},{1,5},{5... | collective-permute-start | bytes 6291464 | tf_op jit(solution)/shard_map/ppermute | solution.py:85
  138.8 52.9 %all-to-all-start.2 = ((bf16[4,1024,256]{2,1,0:T(8,128)(2,1)}), bf16[4,1024,256]{2,1,0:T(8,128)(2,1)}, u32[]{:S(2)}, u32[]{:S(2)}) async-start(bf16[4,1024,256]{2,1,0:T(8,128)(2,1)} %pad_maximum_fusion.1), calls=%async_computation.2 | async-start | bytes 4194304 | tf_op jit(solution)/shard_map/all_to_all | solution.py:105
  145.5 14.3 %collective-permute-start.17 = (bf16[64,2048]{1,0:T(8,128)(2,1)S(1)}, bf16[64,2048]{1,0:T(8,128)(2,1)S(1)}, u32[]{:S(2)}, u32[]{:S(2)}) collective-permute-start(bf16[64,2048]{1,0:T(8,128)(2,1)S(1)} %collective-permute-done.16.refs_4_), channel_id=1, source_target_pairs={{0,1},{1,0},{2,3},{3,2},{4,5},{5,4},{6,7},{7,6},{8,9},{9,8},{10,11... | collective-permute-start | bytes 786440 | tf_op jit(solution)/shard_map/ppermute | solution.py:94
  148.5 17.1 %collective-permute-start.19 = (bf16[64,2048]{1,0:T(8,128)(2,1)S(1)}, bf16[64,2048]{1,0:T(8,128)(2,1)S(1)}, u32[]{:S(2)}, u32[]{:S(2)}) collective-permute-start(bf16[64,2048]{1,0:T(8,128)(2,1)S(1)} %collective-permute-done.16.refs_4_), channel_id=1, source_target_pairs={{0,3},{1,2},{2,1},{3,0},{4,7},{5,6},{6,5},{7,4},{8,11},{9,10},{10,... | collective-permute-start | bytes 786440 | tf_op jit(solution)/shard_map/ppermute | solution.py:94
  191.9 57.5 %all-to-all-start.3 = ((bf16[4,1024,256]{2,1,0:T(8,128)(2,1)}), bf16[4,1024,256]{2,1,0:T(8,128)(2,1)S(1)}, u32[]{:S(2)}, u32[]{:S(2)}) async-start(bf16[4,1024,256]{2,1,0:T(8,128)(2,1)} %grad_down_near.1), calls=%async_computation.3 | async-start | bytes 4194304 | tf_op jit(solution)/shard_map/all_to_all | solution.py:105
  210.4 33.5 %collective-permute-start.29 = (bf16[4,256,1024]{2,1,0:T(8,128)(2,1)}, bf16[4,256,1024]{2,1,0:T(8,128)(2,1)}, u32[]{:S(2)}, u32[]{:S(2)}) collective-permute-start(bf16[4,256,1024]{2,1,0:T(8,128)(2,1)} %grad_up_far.1), channel_id=1, source_target_pairs={{0,4},{4,0},{8,12},{12,8},{16,20},{20,16},{24,28},{28,24},{1,5},{5... | collective-permute-start | bytes 6291464 | tf_op jit(solution)/shard_map/ppermute | solution.py:85
  219.1 15.1 %collective-permute-start.25 = (bf16[64,2048]{1,0:T(8,128)(2,1)}, bf16[64,2048]{1,0:T(8,128)(2,1)}, u32[]{:S(2)}, u32[]{:S(2)}) collective-permute-start(bf16[64,2048]{1,0:T(8,128)(2,1)} %get-tuple-element.140), channel_id=1, source_target_pairs={{0,3},{1,2},{2,1},{3,0},{4,7},{5,6},{6,5},{7,4},{8,11},{9,10},{10,... | collective-permute-start | bytes 786440 | tf_op jit(solution)/shard_map/ppermute | solution.py:94
  221.5 17.2 %collective-permute-start.26 = (bf16[64,2048]{1,0:T(8,128)(2,1)}, bf16[64,2048]{1,0:T(8,128)(2,1)S(1)}, u32[]{:S(2)}, u32[]{:S(2)}) collective-permute-start(bf16[64,2048]{1,0:T(8,128)(2,1)} %get-tuple-element.141), channel_id=1, source_target_pairs={{0,1},{1,0},{2,3},{3,2},{4,5},{5,4},{6,7},{7,6},{8,9},{9,8},{10,11... | collective-permute-start | bytes 786440 | tf_op jit(solution)/shard_map/ppermute | solution.py:94
  227.4 16.4 %collective-permute-start.27 = (bf16[64,2048]{1,0:T(8,128)(2,1)}, bf16[64,2048]{1,0:T(8,128)(2,1)S(1)}, u32[]{:S(2)}, u32[]{:S(2)}) collective-permute-start(bf16[64,2048]{1,0:T(8,128)(2,1)} %get-tuple-element.142), channel_id=1, source_target_pairs={{0,2},{1,3},{2,0},{3,1},{4,6},{5,7},{6,4},{7,5},{8,10},{9,11},{10,... | collective-permute-start | bytes 786440 | tf_op jit(solution)/shard_map/ppermute | solution.py:94
  265.3 80.3 %all-to-all-start.4 = ((bf16[4,256,1024]{2,1,0:T(8,128)(2,1)}), bf16[4,256,1024]{2,1,0:T(8,128)(2,1)S(1)}, u32[]{:S(2)}, u32[]{:S(2)}) async-start(bf16[4,256,1024]{2,1,0:T(8,128)(2,1)} %grad_up_near.1), calls=%async_computation.4 | async-start | bytes 4194304 | tf_op jit(solution)/shard_map/all_to_all | solution.py:105
  272.7 16.1 %collective-permute-start.37 = (bf16[64,2048]{1,0:T(8,128)(2,1)S(1)}, bf16[64,2048]{1,0:T(8,128)(2,1)S(1)}, u32[]{:S(2)}, u32[]{:S(2)}) collective-permute-start(bf16[64,2048]{1,0:T(8,128)(2,1)S(1)} %collective-permute-done.34.refs_4_), channel_id=1, source_target_pairs={{0,3},{1,2},{2,1},{3,0},{4,7},{5,6},{6,5},{7,4},{8,11},{9,10},{10,... | collective-permute-start | bytes 786440 | tf_op jit(solution)/shard_map/ppermute | solution.py:94
  306.5 22.6 %collective-permute-start.52 = (bf16[4,256,1024]{2,1,0:T(8,128)(2,1)}, bf16[4,256,1024]{2,1,0:T(8,128)(2,1)}, u32[]{:S(2)}, u32[]{:S(2)}) collective-permute-start(bf16[4,256,1024]{2,1,0:T(8,128)(2,1)} %grad_attention_far.1), channel_id=1, source_target_pairs={{0,4},{4,0},{8,12},{12,8},{16,20},{20,16},{24,28},{28,24},{1,5},{5... | collective-permute-start | bytes 6291464 | tf_op jit(solution)/shard_map/ppermute | solution.py:85
  308.0 14.3 %collective-permute-start.43 = (bf16[64,2048]{1,0:T(8,128)(2,1)}, bf16[64,2048]{1,0:T(8,128)(2,1)S(1)}, u32[]{:S(2)}, u32[]{:S(2)}) collective-permute-start(bf16[64,2048]{1,0:T(8,128)(2,1)} %get-tuple-element.171), channel_id=1, source_target_pairs={{0,2},{1,3},{2,0},{3,1},{4,6},{5,7},{6,4},{7,5},{8,10},{9,11},{10,... | collective-permute-start | bytes 786440 | tf_op jit(solution)/shard_map/ppermute | solution.py:94
  309.6 14.5 %collective-permute-start.44 = (bf16[64,2048]{1,0:T(8,128)(2,1)}, bf16[64,2048]{1,0:T(8,128)(2,1)S(1)}, u32[]{:S(2)}, u32[]{:S(2)}) collective-permute-start(bf16[64,2048]{1,0:T(8,128)(2,1)} %get-tuple-element.172), channel_id=1, source_target_pairs={{0,3},{1,2},{2,1},{3,0},{4,7},{5,6},{6,5},{7,4},{8,11},{9,10},{10,... | collective-permute-start | bytes 786440 | tf_op jit(solution)/shard_map/ppermute | solution.py:94
  310.0 17.2 %collective-permute-start.38 = (bf16[64,2048]{1,0:T(8,128)(2,1)}, bf16[64,2048]{1,0:T(8,128)(2,1)S(1)}, u32[]{:S(2)}, u32[]{:S(2)}) collective-permute-start(bf16[64,2048]{1,0:T(8,128)(2,1)} %get-tuple-element.177), channel_id=1, source_target_pairs={{0,1},{1,0},{2,3},{3,2},{4,5},{5,4},{6,7},{7,6},{8,9},{9,8},{10,11... | collective-permute-start | bytes 786440 | tf_op jit(solution)/shard_map/ppermute | solution.py:94
  315.9 20.1 %collective-permute-start.53 = (bf16[64,2048]{1,0:T(8,128)(2,1)S(1)}, bf16[64,2048]{1,0:T(8,128)(2,1)}, u32[]{:S(2)}, u32[]{:S(2)}) collective-permute-start(bf16[64,2048]{1,0:T(8,128)(2,1)S(1)} %copy-done.67), channel_id=1, source_target_pairs={{0,2},{1,3},{2,0},{3,1},{4,6},{5,7},{6,4},{7,5},{8,10},{9,11},{10,... | collective-permute-start | bytes 786440 | tf_op jit(solution)/shard_map/ppermute | solution.py:94
  322.4 14.3 %collective-permute-start.54 = (bf16[64,2048]{1,0:T(8,128)(2,1)}, bf16[64,2048]{1,0:T(8,128)(2,1)}, u32[]{:S(2)}, u32[]{:S(2)}) collective-permute-start(bf16[64,2048]{1,0:T(8,128)(2,1)} %get-tuple-element.192), channel_id=1, source_target_pairs={{0,3},{1,2},{2,1},{3,0},{4,7},{5,6},{6,5},{7,4},{8,11},{9,10},{10,... | collective-permute-start | bytes 786440 | tf_op jit(solution)/shard_map/ppermute | solution.py:94
  329.1 15.6 %collective-permute-start.40 = (bf16[64,2048]{1,0:T(8,128)(2,1)}, bf16[64,2048]{1,0:T(8,128)(2,1)S(1)}, u32[]{:S(2)}, u32[]{:S(2)}) collective-permute-start(bf16[64,2048]{1,0:T(8,128)(2,1)} %get-tuple-element.179), channel_id=1, source_target_pairs={{0,2},{1,3},{2,0},{3,1},{4,6},{5,7},{6,4},{7,5},{8,10},{9,11},{10,... | collective-permute-start | bytes 786440 | tf_op jit(solution)/shard_map/ppermute | solution.py:94
  347.0 65.3 %all-to-all-start.5 = ((bf16[4,256,1024]{2,1,0:T(8,128)(2,1)}), bf16[4,256,1024]{2,1,0:T(8,128)(2,1)}, u32[]{:S(2)}, u32[]{:S(2)}) async-start(bf16[4,256,1024]{2,1,0:T(8,128)(2,1)} %grad_attention_near.1), calls=%async_computation.5 | async-start | bytes 4194304 | tf_op jit(solution)/shard_map/all_to_all | solution.py:105
  359.4 15.8 %collective-permute-start.49 = (bf16[64,2048]{1,0:T(8,128)(2,1)S(1)}, bf16[64,2048]{1,0:T(8,128)(2,1)S(1)}, u32[]{:S(2)}, u32[]{:S(2)}) collective-permute-start(bf16[64,2048]{1,0:T(8,128)(2,1)S(1)} %copy-done.66), channel_id=1, source_target_pairs={{0,1},{1,0},{2,3},{3,2},{4,5},{5,4},{6,7},{7,6},{8,9},{9,8},{10,11... | collective-permute-start | bytes 786440 | tf_op jit(solution)/shard_map/ppermute | solution.py:94
  361.3 16.4 %collective-permute-start.50 = (bf16[64,2048]{1,0:T(8,128)(2,1)S(1)}, bf16[64,2048]{1,0:T(8,128)(2,1)S(1)}, u32[]{:S(2)}, u32[]{:S(2)}) collective-permute-start(bf16[64,2048]{1,0:T(8,128)(2,1)S(1)} %copy-done.65), channel_id=1, source_target_pairs={{0,2},{1,3},{2,0},{3,1},{4,6},{5,7},{6,4},{7,5},{8,10},{9,11},{10,... | collective-permute-start | bytes 786440 | tf_op jit(solution)/shard_map/ppermute | solution.py:94
  390.9 15.8 %collective-permute-start.56 = (bf16[64,2048]{1,0:T(8,128)(2,1)S(1)}, bf16[64,2048]{1,0:T(8,128)(2,1)S(1)}, u32[]{:S(2)}, u32[]{:S(2)}) collective-permute-start(bf16[64,2048]{1,0:T(8,128)(2,1)S(1)} %copy-done.9), channel_id=1, source_target_pairs={{0,1},{1,0},{2,3},{3,2},{4,5},{5,4},{6,7},{7,6},{8,9},{9,8},{10,11... | collective-permute-start | bytes 786440 | tf_op jit(solution)/shard_map/ppermute | solution.py:94
  (116 other events, 970.6 us)
